TPU v7x, 32 devices: a whole 2x2x4 slice. The times are simulated.
32 devices in a mesh: dp: 8 (over z, y), tensor: 4 (over x, core).
Axes of the slice: x: 2, y: 2, z: 4, core: 2. Of those that a mesh axis runs over, the one named last changes fastest.
Arguments:
- embedded: bfloat16 [8192, 768], P(('dp', 'tensor')), may hold values from -6 to 6
- ids_two: int32 [8192], P('dp'), may hold values from 0 to 8191
- ids_three: int32 [8192], P('dp'), may hold values from 0 to 8191
- parents: int32 [8192], P('dp'), may hold values from 0 to 4, as said below
- table_two: float32 [8192, 192], P('dp', 'tensor'), may hold values from -6 to 6
- table_three: float32 [8192, 192], P('dp', 'tensor'), may hold values from -6 to 6
- w_two: float32 [192, 768], P('tensor', 'dp'), may hold values from -0.4375 to 0.4375
- w_three: float32 [192, 768], P('tensor', 'dp'), may hold values from -0.4375 to 0.4375
- norm_attn: float32 [768], replicated, may hold values from 0.5 to 1.5
- w_query: float32 [768, 768], P('dp', 'tensor'), may hold values from -0.21875 to 0.21875
- w_key: float32 [768, 768], P('dp', 'tensor'), may hold values from -0.21875 to 0.21875
- w_value: float32 [768, 768], P('dp', 'tensor'), may hold values from -0.21875 to 0.21875
- w_output: float32 [768, 768], P('tensor', 'dp'), may hold values from -0.875 to 0.875
- norm_ffn: float32 [768], replicated, may hold values from 0.5 to 1.5
- w_gate: float32 [768, 2048], P('dp', 'tensor'), may hold values from -0.21875 to 0.21875
- w_up: float32 [768, 2048], P('dp', 'tensor'), may hold values from -0.21875 to 0.21875
- w_down: float32 [2048, 768], P('tensor', 'dp'), may hold values from -0.125 to 0.125
- cotangent: bfloat16 [8192, 768], P(('dp', 'tensor')), may hold values from -6 to 6
Outputs:
- output: bfloat16 [8192, 768], P(('dp', 'tensor'))
- embed_grad: bfloat16 [8192, 768], P(('dp', 'tensor'))
- table_two_grad: float32 [8192, 192], P('dp', 'tensor')
- table_three_grad: float32 [8192, 192], P('dp', 'tensor')
- w_two_grad: float32 [192, 768], P('tensor', 'dp')
- w_three_grad: float32 [192, 768], P('tensor', 'dp')
- norm_attn_grad: float32 [768], replicated
- w_query_grad: float32 [768, 768], P('dp', 'tensor')
- w_key_grad: float32 [768, 768], P('dp', 'tensor')
- w_value_grad: float32 [768, 768], P('dp', 'tensor')
- w_output_grad: float32 [768, 768], P('tensor', 'dp')
- norm_ffn_grad: float32 [768], replicated
- w_gate_grad: float32 [768, 2048], P('dp', 'tensor')
- w_up_grad: float32 [768, 2048], P('dp', 'tensor')
- w_down_grad: float32 [2048, 768], P('tensor', 'dp')
Inputs may be any that keep to these rules, and one draw needn't show every extreme that they name: Every tree has seven blocks: the trunk, then six blocks that are two branches and their two leaves each, every leaf after its branch, in an order drawn for each tree. parents holds, for every token of a block, the index of the parent block: 0 for the trunk and for branches, the branch's block index for a leaf.
All inputs are finite; a program needn't handle non-finite values.
Results may differ from a plain program's by a relative error of at most 0.015.
Values may be sent and summed in bfloat16 or wider, within the bound.
No kernel may reach another device: no remote copies, remote signals or barrier semaphores. Data moves between devices by JAX's collectives and lax.ppermute only.
A program may use at most 192 MiB of HBM per device.

v0:
```python
import jax
import jax.numpy as jnp
from jax import lax
from jax.sharding import PartitionSpec as P

HD = 64
SEG = 128


epsilon = 1e-05
masked_score = -1e30
rope_base = 10000.0


def rms_norm(hidden, gain_vec):
    return (
        hidden * lax.rsqrt(jnp.mean(hidden * hidden, axis=-1, keepdims=True) + epsilon) * gain_vec
    )


def tree_layout(parents):
    length = parents.shape[0]
    token_index = jnp.arange(length, dtype=jnp.int32)
    trunk_len = 2 * SEG
    in_trunk = token_index < trunk_len
    block_of = jnp.where(in_trunk, 0, (token_index - trunk_len) // SEG + 1)
    offset = jnp.where(in_trunk, token_index, token_index - trunk_len - (block_of - 1) * SEG)
    position_base = jnp.where(in_trunk, 0, jnp.where(parents == 0, 2 * SEG, 3 * SEG))
    return (block_of, position_base + offset, token_index)


def rotary_tables(position):
    half_dim = HD // 2
    frequency = rope_base ** (-(jnp.arange(half_dim, dtype=jnp.float32) * 2.0 / HD))
    angles = position.astype(jnp.float32)[:, None] * frequency[None, :]
    return (jnp.cos(angles), jnp.sin(angles))


def rotate(values, cosine, sine_tab):
    rows_count = values.shape[0]
    shaped = values.reshape(rows_count, -1, HD)
    half_dim = HD // 2
    first_half = shaped[..., :half_dim]
    second_half = shaped[..., half_dim:]
    cosine_wide = cosine[:, None, :]
    sine_wide = sine_tab[:, None, :]
    turned = jnp.concatenate(
        [
            first_half * cosine_wide - second_half * sine_wide,
            first_half * sine_wide + second_half * cosine_wide,
        ],
        axis=-1,
    )
    return turned.reshape(rows_count, -1)


def allowed_keys(block_query, parent_query, index_query, block_of, token_index):
    same_block = block_of[None, :] == block_query[:, None]
    causal = token_index[None, :] <= index_query[:, None]
    ancestor = (block_of[None, :] == parent_query[:, None]) | (block_of[None, :] == 0)
    return same_block & causal | jnp.logical_not(same_block) & ancestor


def gather_ids(ids_two, ids_three):
    return (
        lax.all_gather(ids_two, "dp", axis=0, tiled=True),
        lax.all_gather(ids_three, "dp", axis=0, tiled=True),
    )


def shards(
    embedded,
    ids_two,
    ids_three,
    parents,
    table_two,
    table_three,
    w_two,
    w_three,
    norm_attn,
    w_query,
    w_key,
    w_value,
    w_output,
    norm_ffn,
    w_gate,
    w_up,
    w_down,
    cotangent,
):
    single = jnp.float32
    half_type = jnp.bfloat16
    length = ids_two.shape[0]
    all_ids = None
    (
        tab_two,
        tab_three,
        up_two,
        up_three,
        query_w,
        key_w,
        value_w,
        output_w,
        gate_w,
        upward_w,
        down_w,
    ) = (
        lax.all_gather(table_two.astype(half_type), "dp", axis=0, tiled=True),
        lax.all_gather(table_three.astype(half_type), "dp", axis=0, tiled=True),
        lax.all_gather(w_two.astype(half_type), "dp", axis=1, tiled=True),
        lax.all_gather(w_three.astype(half_type), "dp", axis=1, tiled=True),
        lax.all_gather(w_query.astype(half_type), "dp", axis=0, tiled=True),
        lax.all_gather(w_key.astype(half_type), "dp", axis=0, tiled=True),
        lax.all_gather(w_value.astype(half_type), "dp", axis=0, tiled=True),
        lax.all_gather(w_output.astype(half_type), "dp", axis=1, tiled=True),
        lax.all_gather(w_gate.astype(half_type), "dp", axis=0, tiled=True),
        lax.all_gather(w_up.astype(half_type), "dp", axis=0, tiled=True),
        lax.all_gather(w_down.astype(half_type), "dp", axis=1, tiled=True),
    )
    rows_two = jnp.take(tab_two, ids_two, axis=0)
    rows_three = jnp.take(tab_three, ids_three, axis=0)
    ngram = lax.psum_scatter(
        jnp.dot(rows_two, up_two, preferred_element_type=single)
        + jnp.dot(rows_three, up_three, preferred_element_type=single),
        "tensor",
        scatter_dimension=0,
        tiled=True,
    )
    resid_one = embedded.astype(single) + ngram
    normed = rms_norm(resid_one, norm_attn).astype(half_type)
    gathered = lax.all_gather(normed, "tensor", axis=0, tiled=True)
    qkv_w = jnp.concatenate([query_w, key_w, value_w], axis=1)
    width = query_w.shape[1]
    projected = jnp.dot(gathered, qkv_w, preferred_element_type=single)
    block_of, position, token_index = tree_layout(parents)
    cosine, sine_tab = rotary_tables(position)
    query = rotate(projected[:, :width], cosine, sine_tab).astype(half_type)
    keys_all = rotate(projected[:, width : 2 * width], cosine, sine_tab).astype(half_type)
    values = projected[:, 2 * width :].astype(half_type)
    heads_count = width // HD
    keys3 = keys_all.reshape(length, heads_count, HD)
    values3 = values.reshape(length, heads_count, HD)
    blocks = length // min(512, length)
    block_rows = length // blocks
    score_scale = HD ** (-0.5)
    query_blocks = query.reshape(blocks, block_rows, heads_count, HD)
    block_query_all = block_of.reshape(blocks, block_rows)
    parent_query_all = parents.reshape(blocks, block_rows)
    index_query_all = token_index.reshape(blocks, block_rows)

    def scores_of(query_block, block_query, parent_query, index_query):
        scores = (
            jnp.einsum("qhd,khd->hqk", query_block, keys3, preferred_element_type=single)
            * score_scale
        )
        allowed = allowed_keys(block_query, parent_query, index_query, block_of, token_index)
        return jnp.where(allowed[None], scores, masked_score)

    def attend(block):
        query_block, block_query, parent_query, index_query = block
        scores = scores_of(query_block, block_query, parent_query, index_query)
        top_score = jnp.max(scores, axis=-1, keepdims=True)
        log_total = top_score + jnp.log(
            jnp.sum(jnp.exp(scores - top_score), axis=-1, keepdims=True)
        )
        probs = jnp.exp(scores - log_total).astype(half_type)
        mixed_block = jnp.einsum("hqk,khd->qhd", probs, values3, preferred_element_type=single)
        return (mixed_block, log_total[..., 0])

    mixed_blocks, log_totals = lax.map(
        attend, (query_blocks, block_query_all, parent_query_all, index_query_all)
    )
    mixed = mixed_blocks.reshape(length, width).astype(half_type)
    attn_sum = lax.psum_scatter(
        jnp.dot(mixed, output_w, preferred_element_type=single).astype(jnp.bfloat16),
        "tensor",
        scatter_dimension=0,
        tiled=True,
    ).astype(jnp.float32)
    resid_two = resid_one + attn_sum
    normed_two = rms_norm(resid_two, norm_ffn).astype(half_type)
    gathered_two = lax.all_gather(normed_two, "tensor", axis=0, tiled=True)
    gate = jnp.dot(gathered_two, gate_w, preferred_element_type=single)
    upward = jnp.dot(gathered_two, upward_w, preferred_element_type=single)
    sigmoid_gate = jax.nn.sigmoid(gate)
    silu_gate = gate * sigmoid_gate
    hidden = (silu_gate * upward).astype(half_type)
    feed_sum = lax.psum_scatter(
        jnp.dot(hidden, down_w, preferred_element_type=single).astype(jnp.bfloat16),
        "tensor",
        scatter_dimension=0,
        tiled=True,
    ).astype(jnp.float32)
    output = (resid_two + feed_sum).astype(half_type)
    grad_top = cotangent.astype(single)
    grad_feed = lax.all_gather(cotangent, "tensor", axis=0, tiled=True)
    grad_hidden = jnp.dot(grad_feed, down_w.T, preferred_element_type=single)
    down_grad = jnp.dot(hidden.T, grad_feed, preferred_element_type=single)
    grad_gate = (grad_hidden * upward * sigmoid_gate * (1.0 + gate * (1.0 - sigmoid_gate))).astype(
        half_type
    )
    grad_upward = (grad_hidden * silu_gate).astype(half_type)
    grad_normed_two = lax.psum_scatter(
        (
            jnp.dot(grad_gate, gate_w.T, preferred_element_type=single)
            + jnp.dot(grad_upward, upward_w.T, preferred_element_type=single)
        ).astype(jnp.bfloat16),
        "tensor",
        scatter_dimension=0,
        tiled=True,
    ).astype(jnp.float32)
    gate_grad = jnp.dot(gathered_two.T, grad_gate, preferred_element_type=single)
    upward_grad = jnp.dot(gathered_two.T, grad_upward, preferred_element_type=single)
    unused_two, norm_pull_two = jax.vjp(rms_norm, resid_two, norm_ffn)
    resid_part_two, ffn_gain_part = norm_pull_two(grad_normed_two)
    grad_resid_two = grad_top + resid_part_two
    grad_attn = lax.all_gather(grad_resid_two.astype(half_type), "tensor", axis=0, tiled=True)
    output_grad = jnp.dot(mixed.T, grad_attn, preferred_element_type=single)
    grad_mixed = jnp.dot(grad_attn, output_w.T, preferred_element_type=single).astype(half_type)
    grad_mixed_blocks = grad_mixed.reshape(blocks, block_rows, heads_count, HD)

    def attend_back(carry, block):
        grad_keys_sum, grad_values_sum = carry
        query_block, block_query, parent_query, index_query, log_total, grad_block = block
        scores = scores_of(query_block, block_query, parent_query, index_query)
        probs = jnp.exp(scores - log_total[..., None])
        grad_values_sum = grad_values_sum + jnp.einsum(
            "hqk,qhd->khd", probs.astype(half_type), grad_block, preferred_element_type=single
        )
        grad_probs = jnp.einsum("qhd,khd->hqk", grad_block, values3, preferred_element_type=single)
        row_delta = jnp.sum(grad_probs * probs, axis=-1, keepdims=True)
        grad_scores = (probs * (grad_probs - row_delta)).astype(half_type)
        grad_query_block = (
            jnp.einsum("hqk,khd->qhd", grad_scores, keys3, preferred_element_type=single)
            * score_scale
        )
        grad_keys_sum = (
            grad_keys_sum
            + jnp.einsum("hqk,qhd->khd", grad_scores, query_block, preferred_element_type=single)
            * score_scale
        )
        return ((grad_keys_sum, grad_values_sum), grad_query_block)

    zero_heads = jnp.zeros((length, heads_count, HD), single)
    (grad_keys_sum, grad_values_sum), grad_query_blocks = lax.scan(
        attend_back,
        (zero_heads, zero_heads),
        (
            query_blocks,
            block_query_all,
            parent_query_all,
            index_query_all,
            log_totals,
            grad_mixed_blocks,
        ),
    )
    grad_query = rotate(grad_query_blocks.reshape(length, width), cosine, -sine_tab).astype(
        half_type
    )
    grad_keys = rotate(grad_keys_sum.reshape(length, width), cosine, -sine_tab).astype(half_type)
    grad_values = grad_values_sum.reshape(length, width).astype(half_type)
    grad_projected = jnp.concatenate([grad_query, grad_keys, grad_values], axis=1)
    grad_normed = lax.psum_scatter(
        jnp.dot(grad_projected, qkv_w.T, preferred_element_type=single).astype(jnp.bfloat16),
        "tensor",
        scatter_dimension=0,
        tiled=True,
    ).astype(jnp.float32)
    projected_grad = jnp.dot(gathered.T, grad_projected, preferred_element_type=single)
    query_grad = projected_grad[:, :width]
    key_grad = projected_grad[:, width : 2 * width]
    value_grad = projected_grad[:, 2 * width :]
    unused_one, norm_pull_one = jax.vjp(rms_norm, resid_one, norm_attn)
    resid_part_one, attn_gain_part = norm_pull_one(grad_normed)
    grad_resid_one = grad_resid_two + resid_part_one
    embed_grad = grad_resid_one.astype(half_type)
    grad_ngram = lax.all_gather(embed_grad, "tensor", axis=0, tiled=True)
    two_grad = jnp.dot(rows_two.T, grad_ngram, preferred_element_type=single)
    three_grad = jnp.dot(rows_three.T, grad_ngram, preferred_element_type=single)
    grad_rows_two = jnp.dot(grad_ngram, up_two.T, preferred_element_type=single)
    grad_rows_three = jnp.dot(grad_ngram, up_three.T, preferred_element_type=single)
    own_rows = table_two.shape[0]
    (
        w_two_grad,
        w_three_grad,
        w_query_grad,
        w_key_grad,
        w_value_grad,
        w_output_grad,
        w_gate_grad,
        w_up_grad,
        w_down_grad,
    ) = (
        lax.psum_scatter(two_grad, "dp", scatter_dimension=1, tiled=True),
        lax.psum_scatter(three_grad, "dp", scatter_dimension=1, tiled=True),
        lax.psum_scatter(query_grad, "dp", scatter_dimension=0, tiled=True),
        lax.psum_scatter(key_grad, "dp", scatter_dimension=0, tiled=True),
        lax.psum_scatter(value_grad, "dp", scatter_dimension=0, tiled=True),
        lax.psum_scatter(output_grad, "dp", scatter_dimension=1, tiled=True),
        lax.psum_scatter(gate_grad, "dp", scatter_dimension=0, tiled=True),
        lax.psum_scatter(upward_grad, "dp", scatter_dimension=0, tiled=True),
        lax.psum_scatter(down_grad, "dp", scatter_dimension=1, tiled=True),
    )
    all_ids = gather_ids(ids_two, ids_three)
    all_ids_two, all_ids_three = all_ids
    own_start = lax.axis_index("dp") * own_rows

    def rows_into(piece, row_ids):
        local_row = row_ids - own_start
        inside = (local_row >= 0) & (local_row < own_rows)
        target = jnp.where(inside, local_row, own_rows)
        return jax.ops.segment_sum(piece, target, num_segments=own_rows + 1)[:own_rows]

    zero_table = jnp.zeros((own_rows, grad_rows_two.shape[1]), single)
    carry = (zero_table, zero_table)
    table_two_grad = carry[0] + rows_into(
        lax.all_gather(grad_rows_two.astype(jnp.bfloat16), "dp", axis=0, tiled=True).astype(
            jnp.float32
        ),
        all_ids_two,
    )
    table_three_grad = carry[1] + rows_into(
        lax.all_gather(grad_rows_three.astype(jnp.bfloat16), "dp", axis=0, tiled=True).astype(
            jnp.float32
        ),
        all_ids_three,
    )
    norm_attn_grad, norm_ffn_grad = lax.psum((attn_gain_part, ffn_gain_part), ("dp", "tensor"))
    return (
        output,
        embed_grad,
        table_two_grad,
        table_three_grad,
        w_two_grad,
        w_three_grad,
        norm_attn_grad,
        w_query_grad,
        w_key_grad,
        w_value_grad,
        w_output_grad,
        norm_ffn_grad,
        w_gate_grad,
        w_up_grad,
        w_down_grad,
    )


def solution(mesh):
    in_specs = (
        P(("dp", "tensor"), None),
        P("dp"),
        P("dp"),
        P("dp"),
        P("dp", "tensor"),
        P("dp", "tensor"),
        P("tensor", "dp"),
        P("tensor", "dp"),
        P(),
        P("dp", "tensor"),
        P("dp", "tensor"),
        P("dp", "tensor"),
        P("tensor", "dp"),
        P(),
        P("dp", "tensor"),
        P("dp", "tensor"),
        P("tensor", "dp"),
        P(("dp", "tensor"), None),
    )
    out_specs = (
        P(("dp", "tensor"), None),
        P(("dp", "tensor"), None),
        P("dp", "tensor"),
        P("dp", "tensor"),
        P("tensor", "dp"),
        P("tensor", "dp"),
        P(),
        P("dp", "tensor"),
        P("dp", "tensor"),
        P("dp", "tensor"),
        P("tensor", "dp"),
        P(),
        P("dp", "tensor"),
        P("dp", "tensor"),
        P("tensor", "dp"),
    )
    return jax.shard_map(shards, mesh=mesh, in_specs=in_specs, out_specs=out_specs, check_vma=False)
```

profile of v0, /device:TPU:0, one launch (start us, length us, event | category | flops | bytes accessed | tf_op | source)
XLA Modules:
  0.0 1285.4 jit_solution(4678541448667562494)
XLA Ops:
  11.5 32.3 %all-gather.1 = bf16[8,96,48]{1,2,0:T(8,128)(2,1)S(1)} all-gather(bf16[1,96,48]{1,2,0:T(8,128)(2,1)S(1)} %convert_bitcast_fusion), channel_id=1, replica_groups=mesh['dp'=8,'tensor'=4] {'dp'}, dimensions={0}, use_global_device_ids=true | all-gather | bytes 82944 | tf_op jit(solution)/shard_map/all_gather | solution.py:111
  44.0 30.5 %all-gather = bf16[8,96,48]{1,2,0:T(8,128)(2,1)S(1)} all-gather(bf16[1,96,48]{1,2,0:T(8,128)(2,1)S(1)} %convert_bitcast_fusion.1), channel_id=1, replica_groups=mesh['dp'=8,'tensor'=4] {'dp'}, dimensions={0}, use_global_device_ids=true | all-gather | bytes 82944 | tf_op jit(solution)/shard_map/all_gather | solution.py:110
  76.6 32.0 %all_gather.62 = bf16[8192,48]{0,1:T(8,128)(2,1)S(1)} all-gather(bf16[1024,48]{0,1:T(8,128)(2,1)S(1)} %convert_element_type.145), channel_id=1, replica_groups=mesh['dp'=8,'tensor'=4] {'dp'}, dimensions={0}, use_global_device_ids=true | all-gather | bytes 884736 | tf_op jit(solution)/shard_map/all_gather | solution.py:109
  108.6 31.8 %all_gather.60 = bf16[8192,48]{0,1:T(8,128)(2,1)S(1)} all-gather(bf16[1024,48]{0,1:T(8,128)(2,1)S(1)} %convert_element_type.143), channel_id=1, replica_groups=mesh['dp'=8,'tensor'=4] {'dp'}, dimensions={0}, use_global_device_ids=true | all-gather | bytes 884736 | tf_op jit(solution)/shard_map/all_gather | solution.py:108
  143.2 4.7 gather_fusion
  147.9 3.2 gather_fusion.1
  154.3 39.1 %reduce-scatter.27.cloned.1.call-done = f32[256,768]{1,0:T(8,128)} async-done(((f32[1024,768]{1,0:T(8,128)}), f32[256,768]{1,0:T(8,128)}) %reduce-scatter.27.cloned.1.call-update) | async-done | bytes 786448 | tf_op jit(solution)/shard_map/reduce_scatter | solution.py:122
  196.0 31.4 %all_gather.68 = bf16[192,768]{0,1:T(8,128)(2,1)S(1)} all-gather(bf16[192,96]{0,1:T(8,128)(2,1)S(1)} %copy.80), channel_id=1, replica_groups=mesh['dp'=8,'tensor'=4] {'dp'}, dimensions={1}, use_global_device_ids=true | all-gather | bytes 331776 | tf_op jit(solution)/shard_map/all_gather | solution.py:115
  227.4 30.9 %all_gather.67 = bf16[768,192]{1,0:T(8,128)(2,1)S(1)} all-gather(bf16[96,192]{1,0:T(8,128)(2,1)S(1)} %convert_element_type.150), channel_id=1, replica_groups=mesh['dp'=8,'tensor'=4] {'dp'}, dimensions={0}, use_global_device_ids=true | all-gather | bytes 331776 | tf_op jit(solution)/shard_map/all_gather | solution.py:114
  258.3 31.3 %all_gather.66 = bf16[768,192]{1,0:T(8,128)(2,1)S(1)} all-gather(bf16[96,192]{1,0:T(8,128)(2,1)S(1)} %convert_element_type.149), channel_id=1, replica_groups=mesh['dp'=8,'tensor'=4] {'dp'}, dimensions={0}, use_global_device_ids=true | all-gather | bytes 331776 | tf_op jit(solution)/shard_map/all_gather | solution.py:113
  289.6 31.2 %all_gather.65 = bf16[768,192]{1,0:T(8,128)(2,1)S(1)} all-gather(bf16[96,192]{1,0:T(8,128)(2,1)S(1)} %convert_element_type.148), channel_id=1, replica_groups=mesh['dp'=8,'tensor'=4] {'dp'}, dimensions={0}, use_global_device_ids=true | all-gather | bytes 331776 | tf_op jit(solution)/shard_map/all_gather | solution.py:112
  326.9 12.6 while.30
  343.7 28.1 %reduce-scatter.29.cloned.1.call-done = bf16[256,768]{1,0:T(8,128)(2,1)} async-done(((bf16[1024,768]{1,0:T(8,128)(2,1)}), bf16[256,768]{1,0:T(8,128)(2,1)}) %reduce-scatter.29.cloned.1.call-update) | async-done | bytes 393232 | tf_op jit(solution)/shard_map/reduce_scatter | solution.py:174
  375.7 34.3 %all_gather.72 = bf16[512,768]{0,1:T(8,128)(2,1)} all-gather(bf16[512,96]{0,1:T(8,128)(2,1)S(1)} %convert_element_type.162), channel_id=1, replica_groups=mesh['dp'=8,'tensor'=4] {'dp'}, dimensions={1}, use_global_device_ids=true | all-gather | bytes 884736 | tf_op jit(solution)/shard_map/all_gather | solution.py:118
  409.9 31.8 %all_gather.71 = bf16[768,512]{1,0:T(8,128)(2,1)S(1)} all-gather(bf16[96,512]{1,0:T(8,128)(2,1)S(1)} %convert_element_type.160), channel_id=1, replica_groups=mesh['dp'=8,'tensor'=4] {'dp'}, dimensions={0}, use_global_device_ids=true | all-gather | bytes 884736 | tf_op jit(solution)/shard_map/all_gather | solution.py:117
  441.7 34.7 %all_gather.70 = bf16[768,512]{1,0:T(8,128)(2,1)} all-gather(bf16[96,512]{1,0:T(8,128)(2,1)S(1)} %convert_element_type.159), channel_id=1, replica_groups=mesh['dp'=8,'tensor'=4] {'dp'}, dimensions={0}, use_global_device_ids=true | all-gather | bytes 884736 | tf_op jit(solution)/shard_map/all_gather | solution.py:116
  476.4 3.9 fusion.121
  482.7 5.8 multiply_convert_fusion.1
  492.1 28.7 %reduce-scatter.33.cloned.1.call-done = bf16[256,768]{1,0:T(8,128)(2,1)} async-done(((bf16[1024,768]{1,0:T(8,128)(2,1)}), bf16[256,768]{1,0:T(8,128)(2,1)}) %reduce-scatter.33.cloned.1.call-update) | async-done | bytes 393232 | tf_op jit(solution)/shard_map/reduce_scatter | solution.py:203
  524.9 19.7 %all-gather.14.cloned.1.call-done = bf16[1024,768]{1,0:T(8,128)(2,1)} async-done(((bf16[256,768]{1,0:T(8,128)(2,1)}), bf16[1024,768]{1,0:T(8,128)(2,1)}) %all-gather.14.cloned.1.call-update) | async-done | bytes 1572880 | tf_op jit(solution)/shard_map/all_gather | solution.py:217
  549.5 44.9 %while.31 = (s32[]{:T(128)}, f32[1024,3,64]{0,2,1:T(8,128)S(1)}, f32[1024,3,64]{0,2,1:T(8,128)}, f32[2,512,3,64]{1,0,3,2:T(2,128)}, bf16[2,512,3,64]{1,3,2,0:T(8...) while((s32[]{:T(128)}, f32[1024,3,64]{0,2,1:T(8,128)S(1)}, ...), condition=%wide.region_13.15_spmd.clone.clone, body=%wide.region_11.14_spmd.clone.clone.sunk | while | flops 1035539968 | bytes 56432820 | solution.py:245
  552.4 3.8 fusion.207
  556.1 3.5 multiply_reduce_fusion.4
  563.8 8.0 dynamic_update_slice.24
  574.6 4.1 fusion.207
  578.7 3.5 multiply_reduce_fusion.4
  586.4 8.0 dynamic_update_slice.24
  601.7 3.4 convolution_convert_fusion.1
  605.4 24.6 %reduce-scatter.35.cloned.1.call-done = bf16[256,768]{1,0:T(8,128)(2,1)} async-done(((bf16[1024,768]{1,0:T(8,128)(2,1)}), bf16[256,768]{1,0:T(8,128)(2,1)}) %reduce-scatter.35.cloned.1.call-update) | async-done | bytes 393232 | tf_op jit(solution)/shard_map/reduce_scatter | solution.py:263
  631.3 29.5 %reduce-scatter.31.cloned.1.call-done = bf16[256,768]{1,0:T(8,128)(2,1)} async-done(((bf16[1024,768]{1,0:T(8,128)(2,1)}), bf16[256,768]{1,0:T(8,128)(2,1)}) %reduce-scatter.31.cloned.1.call-update) | async-done | bytes 393232 | tf_op jit(solution)/shard_map/reduce_scatter | solution.py:188
  663.4 3.0 convolution_bitcast_fusion
  666.5 16.6 %all-gather.16.cloned.1.call-done = bf16[1024,768]{1,0:T(8,128)(2,1)} async-done(((bf16[256,768]{1,0:T(8,128)(2,1)}), bf16[1024,768]{1,0:T(8,128)(2,1)}) %all-gather.16.cloned.1.call-update) | async-done | bytes 1572880 | tf_op jit(solution)/shard_map/all_gather | solution.py:277
  683.1 3.1 convolution_bitcast_fusion.2
  688.1 3.9 fusion.125
  692.1 4.0 fusion.123
  696.2 3.6 fusion.124
  705.2 30.5 %all_gather.75 = s32[8192]{0:T(1024)S(1)} all-gather(s32[1024]{0:T(1024)S(1)} %copy-done.44), channel_id=1, replica_groups=mesh['dp'=8,'tensor'=4] {'dp'}, dimensions={0}, use_global_device_ids=true | all-gather | bytes 36864 | tf_op jit(solution)/shard_map/all_gather | solution.py:66
  735.6 30.5 %all_gather.78 = s32[8192]{0:T(1024)S(1)} all-gather(s32[1024]{0:T(1024)S(1)} %copy-done.45), channel_id=1, replica_groups=mesh['dp'=8,'tensor'=4] {'dp'}, dimensions={0}, use_global_device_ids=true | all-gather | bytes 36864 | tf_op jit(solution)/shard_map/all_gather | solution.py:67
  769.1 38.6 %all-reduce = (f32[768]{0:T(1024)}, f32[768]{0:T(1024)}) all-reduce(f32[768]{0:T(1024)S(1)} %get-tuple-element.435, f32[768]{0:T(1024)S(1)} %copy-done.51), channel_id=1, replica_groups=mesh['dp'=8,'tensor'=4] {'dp','tensor'}, use_global_device_ids=true, to_apply=%region_21.23 | all-reduce | flops 1536 | bytes 12288 | tf_op jit(solution)/shard_map/psum | solution.py:328
  808.3 32.2 %all_gather.79 = bf16[8192,48]{0,1:T(8,128)(2,1)S(1)} all-gather(bf16[1024,48]{0,1:T(8,128)(2,1)S(1)} %convolution_convert_fusion.4), channel_id=1, replica_groups=mesh['dp'=8,'tensor'=4] {'dp'}, dimensions={0}, use_global_device_ids=true | all-gather | bytes 884736 | tf_op jit(solution)/shard_map/all_gather | solution.py:323
  842.9 50.4 %scatter_custom_fusion.1 = f32[1025,48]{1,0:T(8,128)S(1)} fusion(s32[8192]{0:T(1024)S(1)} %and_select_fusion, f32[8192,48]{1,0:T(8,128)} %copy.85, f32[]{:T(128)} %constant.79.clone.1), kind=kCustom, calls=%fused_computation.160 | custom fusion | flops 393216 | bytes 197312 | tf_op jit(solution)/shard_map/scatter-add | solution.py:312
  894.8 33.7 %all_gather.77 = bf16[8192,48]{0,1:T(8,128)(2,1)S(1)} all-gather(bf16[1024,48]{0,1:T(8,128)(2,1)S(1)} %convolution_convert_fusion.5), channel_id=1, replica_groups=mesh['dp'=8,'tensor'=4] {'dp'}, dimensions={0}, use_global_device_ids=true | all-gather | bytes 884736 | tf_op jit(solution)/shard_map/all_gather | solution.py:317
  930.9 50.3 %scatter_custom_fusion = f32[1025,48]{1,0:T(8,128)S(1)} fusion(s32[8192]{0:T(1024)S(1)} %and_select_fusion.1, f32[8192,48]{1,0:T(8,128)} %copy.84, f32[]{:T(128)} %constant.79.clone.1), kind=kCustom, calls=%fused_computation.162 | custom fusion | flops 393216 | bytes 197312 | tf_op jit(solution)/shard_map/scatter-add | solution.py:312
  985.0 29.5 %reduce-scatter.37.cloned.1.call-done = f32[96,512]{1,0:T(8,128)} async-done(((f32[768,512]{1,0:T(8,128)}), f32[96,512]{1,0:T(8,128)}) %reduce-scatter.37.cloned.1.call-update) | async-done | bytes 196624 | tf_op jit(solution)/shard_map/reduce_scatter | solution.py:300
  1014.5 67.6 %reduce-scatter.39.cloned.1.call-done = f32[96,512]{1,0:T(8,128)} async-done(((f32[768,512]{1,0:T(8,128)}), f32[96,512]{1,0:T(8,128)}) %reduce-scatter.39.cloned.1.call-update) | async-done | bytes 196624 | tf_op jit(solution)/shard_map/reduce_scatter | solution.py:301
  1082.1 65.5 %reduce-scatter.51.cloned.1.call-done = f32[96,192]{1,0:T(8,128)} async-done(((f32[768,192]{1,0:T(8,128)}), f32[96,192]{1,0:T(8,128)}) %reduce-scatter.51.cloned.1.call-update) | async-done | bytes 73744
  1147.6 65.3 %reduce-scatter.49.cloned.1.call-done = f32[96,192]{1,0:T(8,128)} async-done(((f32[768,192]{1,0:T(8,128)}), f32[96,192]{1,0:T(8,128)}) %reduce-scatter.49.cloned.1.call-update) | async-done | bytes 73744
  1212.9 65.7 %reduce-scatter.47.cloned.1.call-done = f32[96,192]{1,0:T(8,128)} async-done(((f32[768,192]{1,0:T(8,128)}), f32[96,192]{1,0:T(8,128)}) %reduce-scatter.47.cloned.1.call-update) | async-done | bytes 73744
  (302 shorter events, 102.0 us)
Async XLA Ops:
  7.2 186.2 %reduce-scatter.27.cloned.1.call-start = ((), (), s32[]{:S(2)}) async-start(), calls=%async_computation.14 | async-start | bytes 3932160 | tf_op jit(solution)/shard_map/reduce_scatter | solution.py:122
  7.9 143.2 %copy-start.55 = (pred[1024]{0:T(1024)(128)(4,1)}, pred[1024]{0:T(1024)(128)(4,1)S(1)}, u32[]{:S(2)}) copy-start(pred[1024]{0:T(1024)(128)(4,1)S(1)} %compare_and_fusion.3) | copy-start | bytes 3076
  9.3 142.5 %copy-start.61 = (pred[1024]{0:T(1024)(128)(4,1)}, pred[1024]{0:T(1024)(128)(4,1)S(1)}, u32[]{:S(2)}) copy-start(pred[1024]{0:T(1024)(128)(4,1)S(1)} %compare_and_fusion.2) | copy-start | bytes 3076
  44.0 107.9 %copy-start.21 = (bf16[768,48]{0,1:T(8,128)(2,1)}, bf16[768,48]{0,1:T(8,128)(2,1)S(1)}, u32[]{:S(2)}) copy-start(bf16[768,48]{0,1:T(8,128)(2,1)S(1)} %reshape.475) | copy-start | bytes 221188
  74.7 76.5 %copy-start.19 = (bf16[768,48]{0,1:T(8,128)(2,1)}, bf16[768,48]{0,1:T(8,128)(2,1)S(1)}, u32[]{:S(2)}) copy-start(bf16[768,48]{0,1:T(8,128)(2,1)S(1)} %reshape.473) | copy-start | bytes 221188
  154.1 39.3 %copy-start.25 = (bf16[256,768]{1,0:T(8,128)(2,1)S(1)}, bf16[256,768]{1,0:T(8,128)(2,1)}, u32[]{:S(2)}) copy-start(bf16[256,768]{1,0:T(8,128)(2,1)} %param.24) | copy-start | bytes 1179652
  154.1 40.6 %copy-start.46 = (f32[768]{0:T(1024)S(1)}, f32[768]{0:T(1024)}, u32[]{:S(2)}) copy-start(f32[768]{0:T(1024)} %param.32) | copy-start | bytes 9220
  154.1 41.6 %copy-start.52 = (s32[1024]{0:T(1024)S(1)}, s32[1024]{0:T(1024)}, u32[]{:S(2)}) copy-start(s32[1024]{0:T(1024)} %param.27) | copy-start | bytes 12292
  154.2 41.6 %copy-start.39 = (f32[96,192]{1,0:T(8,128)S(1)}, f32[96,192]{1,0:T(8,128)}, u32[]{:S(2)}) copy-start(f32[96,192]{1,0:T(8,128)} %param.33) | copy-start | bytes 221188
  154.2 41.6 %copy-start.40 = (f32[96,192]{1,0:T(8,128)S(1)}, f32[96,192]{1,0:T(8,128)}, u32[]{:S(2)}) copy-start(f32[96,192]{1,0:T(8,128)} %param.34) | copy-start | bytes 221188
  154.2 41.6 %copy-start.41 = (f32[96,192]{1,0:T(8,128)S(1)}, f32[96,192]{1,0:T(8,128)}, u32[]{:S(2)}) copy-start(f32[96,192]{1,0:T(8,128)} %param.35) | copy-start | bytes 221188
  154.2 41.6 %copy-start.42 = (f32[192,96]{1,0:T(8,128)S(1)}, f32[192,96]{1,0:T(8,128)}, u32[]{:S(2)}) copy-start(f32[192,96]{1,0:T(8,128)} %param.36) | copy-start | bytes 221188
  154.2 167.9 %all-gather.8.cloned.1.call-start = ((), (), s32[]{:S(2)}) async-start(), calls=%async_computation.15 | async-start | bytes 1966080 | tf_op jit(solution)/shard_map/all_gather | solution.py:131
  194.7 63.6 %copy-start.57 = (f32[256]{0:T(256)}, f32[256]{0:T(256)S(1)}, u32[]{:S(2)}) copy-start(f32[256]{0:T(256)S(1)} %get-tuple-element.483) | copy-start | bytes 3076
  194.7 63.6 %copy-start.53 = (f32[256]{0:T(256)}, f32[256]{0:T(256)S(1)}, u32[]{:S(2)}) copy-start(f32[256]{0:T(256)S(1)} %fusion.109) | copy-start | bytes 3076
  195.7 176.1 %reduce-scatter.29.cloned.1.call-start = ((), (), s32[]{:S(2)}) async-start(), calls=%async_computation.16 | async-start | bytes 1966080 | tf_op jit(solution)/shard_map/reduce_scatter | solution.py:174
  258.3 63.8 %copy-start.26 = (bf16[768,192]{1,0:T(8,128)(2,1)}, bf16[768,192]{1,0:T(8,128)(2,1)S(1)}, u32[]{:S(2)}) copy-start(bf16[768,192]{1,0:T(8,128)(2,1)S(1)} %all_gather.67) | copy-start | bytes 884740
  289.6 35.1 %copy-start.28 = (bf16[768,192]{1,0:T(8,128)(2,1)}, bf16[768,192]{1,0:T(8,128)(2,1)S(1)}, u32[]{:S(2)}) copy-start(bf16[768,192]{1,0:T(8,128)(2,1)S(1)} %all_gather.66) | copy-start | bytes 884740
  341.7 31.2 %copy-start.2 = (bf16[24,8,2,512]{3,1,2,0:T(8,128)(2,1)}, bf16[24,8,2,512]{3,1,2,0:T(8,128)(2,1)S(1)}, u32[]{:S(2)}) copy-start(bf16[24,8,2,512]{3,1,2,0:T(8,128)(2,1)S(1)} %copy.112) | copy-start | bytes 1179652
  341.7 31.2 %copy-start.43 = (f32[768]{0:T(1024)S(1)}, f32[768]{0:T(1024)}, u32[]{:S(2)}) copy-start(f32[768]{0:T(1024)} %param.37) | copy-start | bytes 9220
  343.6 31.9 %copy-start.35 = (f32[96,512]{1,0:T(8,128)S(1)}, f32[96,512]{1,0:T(8,128)}, u32[]{:S(2)}) copy-start(f32[96,512]{1,0:T(8,128)} %param.38) | copy-start | bytes 589828
  343.6 31.9 %copy-start.36 = (f32[96,512]{1,0:T(8,128)S(1)}, f32[96,512]{1,0:T(8,128)}, u32[]{:S(2)}) copy-start(f32[96,512]{1,0:T(8,128)} %param.39) | copy-start | bytes 589828
  343.6 32.0 %copy-start.37 = (f32[512,96]{0,1:T(8,128)S(1)}, f32[512,96]{0,1:T(8,128)}, u32[]{:S(2)}) copy-start(f32[512,96]{0,1:T(8,128)} %param.40) | copy-start | bytes 589828
  343.7 132.8 %all-gather.10.cloned.1.call-start = ((), (), s32[]{:S(2)}) async-start(), calls=%async_computation.17 | async-start | bytes 1966080 | tf_op jit(solution)/shard_map/all_gather | solution.py:182
  374.9 107.8 %all-gather.12.cloned.1.call-start = ((), (), s32[]{:S(2)}) async-start(), calls=%async_computation.19 | async-start | bytes 1966080 | tf_op jit(solution)/shard_map/all_gather | solution.py:196
  375.5 145.3 %reduce-scatter.33.cloned.1.call-start = ((), (), s32[]{:S(2)}) async-start(), calls=%async_computation.20 | async-start | bytes 1966080 | tf_op jit(solution)/shard_map/reduce_scatter | solution.py:203
  492.0 52.6 %all-gather.14.cloned.1.call-start = ((), (), s32[]{:S(2)}) async-start(), calls=%async_computation.21 | async-start | bytes 1966080 | tf_op jit(solution)/shard_map/all_gather | solution.py:217
  524.8 105.2 %reduce-scatter.35.cloned.1.call-start = ((), (), s32[]{:S(2)}) async-start(), calls=%async_computation.22 | async-start | bytes 1966080 | tf_op jit(solution)/shard_map/reduce_scatter | solution.py:263
  601.7 59.1 %reduce-scatter.31.cloned.1.call-start = ((), (), s32[]{:S(2)}) async-start(), calls=%async_computation.18 | async-start | bytes 1966080 | tf_op jit(solution)/shard_map/reduce_scatter | solution.py:188
  605.1 55.6 %copy-start.5 = (bf16[256,768]{1,0:T(8,128)(2,1)S(1)}, bf16[256,768]{1,0:T(8,128)(2,1)}, u32[]{:S(2)}) copy-start(bf16[256,768]{1,0:T(8,128)(2,1)} %param.41) | copy-start | bytes 1179652
  605.1 55.6 %copy-start.6 = (bf16[256,768]{1,0:T(8,128)(2,1)S(1)}, bf16[256,768]{1,0:T(8,128)(2,1)}, u32[]{:S(2)}) copy-start(bf16[256,768]{1,0:T(8,128)(2,1)} %reduce-scatter.33.cloned.1.call-done) | copy-start | bytes 1179652
  605.1 55.6 %copy-start.50 = (f32[256]{0:T(256)S(1)}, f32[256]{0:T(256)}, u32[]{:S(2)}) copy-start(f32[256]{0:T(256)} %copy-done.48) | copy-start | bytes 3076
  605.1 55.6 %copy-start.64 = (f32[256]{0:T(256)S(1)}, f32[256]{0:T(256)}, u32[]{:S(2)}) copy-start(f32[256]{0:T(256)} %copy-done.63) | copy-start | bytes 3076
  605.2 77.9 %all-gather.16.cloned.1.call-start = ((), (), s32[]{:S(2)}) async-start(), calls=%async_computation.23 | async-start | bytes 1966080 | tf_op jit(solution)/shard_map/all_gather | solution.py:277
  631.2 32.1 %copy-start.3 = (bf16[24,8,2,512]{3,1,2,0:T(8,128)(2,1)S(1)}, bf16[24,8,2,512]{3,1,2,0:T(8,128)(2,1)}, u32[]{:S(2)}) copy-start(bf16[24,8,2,512]{3,1,2,0:T(8,128)(2,1)} %copy-done.2) | copy-start | bytes 1179652
  663.3 104.1 %reduce-scatter.53.cloned.1.call-start = ((), (), s32[]{:S(2)}) async-start(), calls=%async_computation.32 | async-start | bytes 884736
  666.4 315.6 %reduce-scatter.43.cloned.1.call-start = ((), (), s32[]{:S(2)}) async-start(), calls=%async_computation.27 | async-start | bytes 442368
  686.3 297.2 %reduce-scatter.45.cloned.1.call-start = ((), (), s32[]{:S(2)}) async-start(), calls=%async_computation.28 | async-start | bytes 442368
  688.0 297.0 %reduce-scatter.41.cloned.1.call-start = ((), (), s32[]{:S(2)}) async-start(), calls=%async_computation.26 | async-start | bytes 1769472 | tf_op jit(solution)/shard_map/reduce_scatter | solution.py:302
  692.0 322.5 %reduce-scatter.37.cloned.1.call-start = ((), (), s32[]{:S(2)}) async-start(), calls=%async_computation.24 | async-start | bytes 1769472 | tf_op jit(solution)/shard_map/reduce_scatter | solution.py:300
  696.1 386.0 %reduce-scatter.39.cloned.1.call-start = ((), (), s32[]{:S(2)}) async-start(), calls=%async_computation.25 | async-start | bytes 1769472 | tf_op jit(solution)/shard_map/reduce_scatter | solution.py:301
  699.8 447.8 %reduce-scatter.51.cloned.1.call-start = ((), (), s32[]{:S(2)}) async-start(), calls=%async_computation.31 | async-start | bytes 884736
  702.6 33.0 %copy-start.45 = (s32[1024]{0:T(1024)S(1)}, s32[1024]{0:T(1024)}, u32[]{:S(2)}) copy-start(s32[1024]{0:T(1024)} %param.26) | copy-start | bytes 12292
  703.8 509.1 %reduce-scatter.49.cloned.1.call-start = ((), (), s32[]{:S(2)}) async-start(), calls=%async_computation.30 | async-start | bytes 884736
  703.9 65.2 %copy-start.51 = (f32[768]{0:T(1024)S(1)}, f32[768]{0:T(1024)}, u32[]{:S(2)}) copy-start(f32[768]{0:T(1024)} %get-tuple-element.433) | copy-start | bytes 9220
  703.9 103.8 %copy-start.22 = (bf16[768,48]{0,1:T(8,128)(2,1)S(1)}, bf16[768,48]{0,1:T(8,128)(2,1)}, u32[]{:S(2)}) copy-start(bf16[768,48]{0,1:T(8,128)(2,1)} %copy-done.21) | copy-start | bytes 221188
  705.1 573.5 %reduce-scatter.47.cloned.1.call-start = ((), (), s32[]{:S(2)}) async-start(), calls=%async_computation.29 | async-start | bytes 884736
  842.9 51.3 %copy-start.20 = (bf16[768,48]{0,1:T(8,128)(2,1)S(1)}, bf16[768,48]{0,1:T(8,128)(2,1)}, u32[]{:S(2)}) copy-start(bf16[768,48]{0,1:T(8,128)(2,1)} %copy-done.19) | copy-start | bytes 221188
  (37 other events, 351.8 us)
Sparse Core Ops, SparseCore 0:
  154.3 39.0 reduce-scatter.26
  195.8 19.6 all-gather.7
  343.7 27.9 reduce-scatter.28
  375.0 19.6 all-gather.9
  396.1 19.6 all-gather.11
  492.1 28.5 reduce-scatter.32
  524.9 19.6 all-gather.13
  601.8 28.1 reduce-scatter.34
  632.5 28.1 reduce-scatter.30
  663.4 19.6 all-gather.15
  686.8 62.4 reduce-scatter.52
  752.4 60.4 reduce-scatter.42
  816.2 60.4 reduce-scatter.44
  880.6 65.8 reduce-scatter.40
  950.7 63.7 reduce-scatter.36
  1018.4 63.6 reduce-scatter.38
  1086.2 61.4 reduce-scatter.50
  1151.4 61.4 reduce-scatter.48
  1217.1 61.4 reduce-scatter.46
where the time goes:
time: 1290 us
  blocking collectives  518 us (40%)
  waiting for transfers between devices  481 us (37%)
  other arithmetic  135 us (10%)
  matrix products  82.1 us (6%)
  local copies, waits for them, and re-layouts  53.9 us (4%)
  between operations  15.2 us (1%)
    unnamed x25, waiting for transfers between devices  197 us
    scatter-add x2, other arithmetic, rows_into(): jax.ops.segment_sum(piece, target, num_segments=own_rows + 1)[:own_rows]  101 us
    reduce_scatter x1, waiting for transfers between devices, shards(): lax.psum_scatter(upward_grad, 'dp', scatter_dimension=0, tiled=True)  67.6 us
    reduce_scatter x1, waiting for transfers between devices, shards(): lax.psum_scatter(jnp.dot(rows_two, up_two, preferred_element_type=single)...  39.1 us
    psum x1, blocking collectives, shards(): lax.psum((attn_gain_part, ffn_gain_part), ('dp', 'tensor'))  38.6 us
    all_gather x1, blocking collectives, shards(): lax.all_gather(w_gate.astype(half_type), 'dp', axis=0, tiled=True)  34.7 us
    all_gather x1, blocking collectives, shards(): lax.all_gather(w_down.astype(half_type), 'dp', axis=1, tiled=True)  34.3 us
    all_gather x1, blocking collectives, shards(): lax.all_gather(grad_rows_two.astype(jnp.bfloat16), 'dp', axis=0, tiled=True)  33.7 us
  transfers between devices with their start and end apart: 19, of which 12 were waited for; matrix products, arithmetic and copies ran while one was open for 12% of the time, Pallas kernels for 0%

commit v1 on v0

v1 whole, which is shorter than its diff:
```python
import functools

import jax
import jax.numpy as jnp
from jax import lax
from jax.experimental import pallas as pl
from jax.experimental.pallas import tpu as pltpu
from jax.sharding import PartitionSpec as P

HD = 64
SEG = 128
TILE = 2 * SEG
EPS = 1e-05
MASKED = -1e30
ROPE_BASE = 10000.0
F32 = jnp.float32
BF16 = jnp.bfloat16
VMEM = pltpu.VMEM


def xor_tensor(value, step):
    return lax.ppermute(value, "tensor", [(i, i ^ step) for i in range(4)])


def xor_dp(value, step, count):
    return lax.ppermute(value, "dp", [(i, i ^ step) for i in range(count)])


def gather_tensor(value):
    far = xor_tensor(value, 2)
    near = xor_tensor(value, 1)
    return [value, near, far, xor_tensor(far, 1)]


def add_round(one, two):
    return (one.astype(F32) + two.astype(F32)).astype(BF16)


def scatter_tensor(slots):
    three = xor_tensor(slots[3], 1)
    one = xor_tensor(slots[1], 1)
    far = xor_tensor(add_round(slots[2], three), 2)
    return slots[0].astype(F32) + one.astype(F32) + far.astype(F32)


def gather_dp(value, count, gate=None):
    if gate is not None:
        value, _ = lax.optimization_barrier((value, gate))
    zs = [value] + [xor_dp(value, step, count) for step in (2, 4, 6)]
    pieces = []
    for piece in zs:
        pieces += [piece, xor_dp(piece, 1, count)]
    return pieces


def scatter_dp(value, count):
    if count != 8:
        return lax.psum_scatter(
            value.astype(F32), "dp", scatter_dimension=0, tiled=True
        ).reshape(value.shape[1:])
    own = lax.axis_index("dp")
    y, z = own % 2, own // 2
    pairs = value.reshape((4, 2) + value.shape[1:])
    away = lax.dynamic_index_in_dim(pairs, 1 - y, 1, keepdims=False)
    keep = lax.dynamic_index_in_dim(pairs, y, 1, keepdims=False)
    both = add_round(keep, xor_dp(away, 1, count))
    total = lax.dynamic_index_in_dim(both, z, 0, keepdims=False).astype(F32)
    for j in (1, 2, 3):
        part = lax.dynamic_index_in_dim(both, z ^ j, 0, keepdims=False)
        total = total + xor_dp(part, 2 * j, count).astype(F32)
    return total


def assemble_kernel(count, turn, keep, info, *refs):
    pieces, out = refs[:count], refs[count]
    rows = pieces[0].shape[0]
    whole_ref = refs[count + 1] if turn else out
    for i in range(count):
        place = pl.ds(pl.multiple_of((info[1] ^ i) * rows, 16), rows)
        whole_ref[place, :] = pieces[i][...]
    if turn:
        out[...] = whole_ref[...].T[:keep, :]


def assemble(info, pieces, turn, block=0, keep=None):
    count = len(pieces)
    rows, lanes = pieces[0].shape
    if keep is None:
        keep, width = lanes, lanes
    else:
        width = SEG
    shape = (keep, count * rows) if turn else (count * rows, width)
    return pl.pallas_call(
        functools.partial(assemble_kernel, count, turn, keep),
        grid_spec=pltpu.PrefetchScalarGridSpec(
            num_scalar_prefetch=1,
            grid=(1,),
            in_specs=[pl.BlockSpec((rows, width), lambda *_: (0, block))] * count,
            out_specs=pl.BlockSpec(shape, lambda *_: (0, 0)),
            scratch_shapes=[VMEM((count * rows, width), BF16)] if turn else [],
        ),
        out_shape=jax.ShapeDtypeStruct(shape, BF16),
        name="assemble",
    )(info, *pieces)


def nn(a, b):
    return lax.dot_general(a, b, (((1,), (0,)), ((), ())), preferred_element_type=F32)


def nt(a, b):
    return lax.dot_general(a, b, (((1,), (1,)), ((), ())), preferred_element_type=F32)


def tn(a, b):
    return lax.dot_general(a, b, (((0,), (0,)), ((), ())), preferred_element_type=F32)


def lookup_kernel(owners, width, own_rows, start, *refs):
    info, ids = refs[0], refs[1]
    count = len(owners)
    pieces = refs[2 : 2 + count]
    prior = None if start else refs[2 + count]
    out = refs[-1]
    for half in range(2):
        lanes = slice(half * width, (half + 1) * width)
        if start:
            out[lanes, :] = jnp.zeros((width, out.shape[1]), BF16)
        else:
            out[lanes, :] = prior[lanes, :]
    for which in range(count):
        for half in range(2):
            wanted = ids[half : half + 1, :] - (info[1] ^ owners[which]) * own_rows

            def chunk(c, total):
                first = pl.multiple_of(c * TILE, TILE)
                rows = lax.broadcasted_iota(jnp.int32, (TILE, wanted.shape[1]), 0) + first
                hot = (rows == wanted).astype(F32).astype(BF16)
                part = pieces[which][half * width : (half + 1) * width, pl.ds(first, TILE)]
                return total + nn(part, hot)

            total = lax.fori_loop(
                0, own_rows // TILE, chunk, jnp.zeros((width, wanted.shape[1]), F32)
            )
            rows = slice(half * width, (half + 1) * width)
            out[rows, :] = (out[rows, :].astype(F32) + total).astype(BF16)


def lookup(info, pieces, owners, own_rows, ids, prior):
    count = len(pieces)
    width = pieces[0].shape[0] // 2
    operands = [info, ids, *pieces]
    specs = [pl.BlockSpec(memory_space=pltpu.SMEM)] + [pl.BlockSpec(memory_space=VMEM)] * (
        1 + count
    )
    if prior is not None:
        operands.append(prior)
        specs.append(pl.BlockSpec(memory_space=VMEM))
    return pl.pallas_call(
        functools.partial(lookup_kernel, tuple(owners), width, own_rows, prior is None),
        out_shape=jax.ShapeDtypeStruct((2 * width, ids.shape[1]), BF16),
        in_specs=specs,
        out_specs=pl.BlockSpec(memory_space=VMEM),
        name="lookup",
    )(*operands)


def spread_kernel(count, width, start, *refs):
    base = (refs[0][1] * refs[-1].shape[1]).astype(F32)
    pieces = refs[1 : 1 + count]
    prior = None if start else refs[1 + count]
    out = refs[-1]
    own_rows = out.shape[1]

    def chunk(c, carry):
        first = pl.multiple_of(c * TILE, TILE)
        rows = (
            lax.broadcasted_iota(jnp.int32, (TILE, pieces[0].shape[1]), 0).astype(F32)
            + base
            + first.astype(F32)
        )
        for half in range(2):
            lanes = slice(half * width, (half + 1) * width)
            total = (
                jnp.zeros((width, TILE), F32) if start else prior[lanes, pl.ds(first, TILE)]
            )
            for piece in pieces:
                digits = piece[2 * width : 2 * width + 16, :].astype(F32)
                ids = digits[2 * half : 2 * half + 1] * 256.0 + digits[2 * half + 1 : 2 * half + 2]
                hot = (rows == ids).astype(F32).astype(BF16)
                total = total + nt(piece[lanes, :], hot)
            out[lanes, pl.ds(first, TILE)] = total
        return carry

    lax.fori_loop(0, own_rows // TILE, chunk, 0)


def spread(info, pieces, own_rows, width, prior):
    count = len(pieces)
    operands = [info, *pieces]
    specs = [pl.BlockSpec(memory_space=pltpu.SMEM)] + [pl.BlockSpec(memory_space=VMEM)] * count
    if prior is not None:
        operands.append(prior)
        specs.append(pl.BlockSpec(memory_space=VMEM))
    return pl.pallas_call(
        functools.partial(spread_kernel, count, width, prior is None),
        out_shape=jax.ShapeDtypeStruct((2 * width, own_rows), F32),
        in_specs=specs,
        out_specs=pl.BlockSpec(memory_space=VMEM),
        name="spread",
    )(*operands)


def rope_into(out, row, values, cosine, sine, scale):
    half = HD // 2
    one, two = values[:half], values[half:]
    out[row : row + half, :] = (one * cosine - two * sine).astype(BF16) * scale
    out[row + half : row + HD, :] = (one * sine + two * cosine).astype(BF16) * scale


def key_offset(parent):
    return pl.multiple_of(jnp.where(parent > 0, parent + 1, 0) * SEG, SEG)


def front_kernel(
    par,
    row0,
    row1,
    row2,
    row3,
    up0,
    up1,
    up2,
    up3,
    emb,
    wqkv,
    gain,
    cos_ref,
    sin_ref,
    resid,
    normed,
    qkv,
    mixed,
    lse,
    keys,
    vals,
):
    tile = pl.program_id(0)
    rows = jnp.concatenate([row0[...], row1[...], row2[...], row3[...]], axis=0)
    ups = jnp.concatenate([up0[...], up1[...], up2[...], up3[...]], axis=0)
    hidden = emb[...].astype(F32) + tn(rows, ups)
    resid[...] = hidden
    rate = lax.rsqrt(jnp.mean(hidden * hidden, axis=-1, keepdims=True) + EPS)
    norm = (hidden * rate * gain[...]).astype(BF16)
    normed[...] = norm
    proj = nt(wqkv[...], norm)
    cosine, sine = cos_ref[...], sin_ref[...]
    width = keys.shape[0]
    heads = width // HD
    for h in range(heads):
        rope_into(qkv, h * HD, proj[h * HD : (h + 1) * HD], cosine, sine, BF16(HD**-0.5))
        low = width + h * HD
        rope_into(qkv, low, proj[low : low + HD], cosine, sine, BF16(1.0))
    qkv[2 * width :, :] = proj[2 * width :].astype(BF16)
    place = pl.ds(pl.multiple_of(tile * TILE, TILE), TILE)
    keys[:, place] = qkv[width : 2 * width, :]
    vals[:, place] = qkv[2 * width :, :]

    def finish(h, lanes, scores, value):
        top = jnp.max(scores, axis=0, keepdims=True)
        weights = jnp.exp(scores - top)
        total = jnp.sum(weights, axis=0, keepdims=True)
        got = nn(value, weights.astype(BF16))
        mixed[h * HD : (h + 1) * HD, lanes] = (got * (1.0 / total)).astype(BF16)
        lse[h : h + 1, lanes] = top + jnp.log(total)

    @pl.when(tile == 0)
    def _():
        key_at = lax.broadcasted_iota(jnp.int32, (TILE, TILE), 0)
        query_at = lax.broadcasted_iota(jnp.int32, (TILE, TILE), 1)
        for h in range(heads):
            hs = slice(h * HD, (h + 1) * HD)
            scores = tn(keys[hs, 0:TILE], qkv[hs, :])
            scores = jnp.where(key_at <= query_at, scores, MASKED)
            finish(h, slice(0, TILE), scores, vals[hs, 0:TILE])

    @pl.when(tile > 0)
    def _():
        key_at = lax.broadcasted_iota(jnp.int32, (4 * SEG, SEG), 0)
        query_at = lax.broadcasted_iota(jnp.int32, (4 * SEG, SEG), 1)
        for half in range(2):
            parent = par[2 + 2 * tile + half]
            mine = pl.ds(pl.multiple_of(tile * TILE + half * SEG, SEG), SEG)
            theirs = pl.ds(key_offset(parent), SEG)
            limit = jnp.where(parent > 0, 4 * SEG, 3 * SEG)
            seen = (key_at < TILE) | ((key_at - TILE <= query_at) & (key_at < 3 * SEG))
            seen = seen | ((key_at >= 3 * SEG) & (key_at < limit))
            lanes = slice(half * SEG, (half + 1) * SEG)
            for h in range(heads):
                hs = slice(h * HD, (h + 1) * HD)
                key = jnp.concatenate([keys[hs, 0:TILE], keys[hs, mine], keys[hs, theirs]], axis=1)
                value = jnp.concatenate(
                    [vals[hs, 0:TILE], vals[hs, mine], vals[hs, theirs]], axis=1
                )
                scores = jnp.where(seen, tn(key, qkv[hs, lanes]), MASKED)
                finish(h, lanes, scores, value)


def whole(shape):
    return pl.BlockSpec(shape, lambda *_: (0,) * len(shape))


def front(par, rows, ups, emb, wqkvo, gain, cosine, sine):
    length, dim = emb.shape
    width = wqkvo.shape[0] // 4
    ng = rows[0].shape[0]
    tall = lambda r, _: (r, 0)
    wide = lambda r, _: (0, r)
    return pl.pallas_call(
        front_kernel,
        grid_spec=pltpu.PrefetchScalarGridSpec(
            num_scalar_prefetch=1,
            grid=(length // TILE,),
            in_specs=[pl.BlockSpec((ng, TILE), wide)] * 4
            + [whole((ng, dim))] * 4
            + [
                pl.BlockSpec((TILE, dim), tall),
                whole((3 * width, dim)),
                whole((1, dim)),
                pl.BlockSpec((HD // 2, TILE), wide),
                pl.BlockSpec((HD // 2, TILE), wide),
            ],
            out_specs=[
                pl.BlockSpec((TILE, dim), tall),
                pl.BlockSpec((TILE, dim), tall),
                pl.BlockSpec((3 * width, TILE), wide),
                pl.BlockSpec((width, TILE), wide),
                pl.BlockSpec((8, TILE), wide),
            ],
            scratch_shapes=[VMEM((width, length), BF16), VMEM((width, length), BF16)],
        ),
        out_shape=[
            jax.ShapeDtypeStruct((length, dim), F32),
            jax.ShapeDtypeStruct((length, dim), BF16),
            jax.ShapeDtypeStruct((3 * width, length), BF16),
            jax.ShapeDtypeStruct((width, length), BF16),
            jax.ShapeDtypeStruct((8, length), F32),
        ],
        name="front",
    )(par, *rows, *ups, emb, wqkvo, gain, cosine, sine)


def middle_kernel(
    who,
    mix0,
    mix1,
    mix2,
    mix3,
    out0,
    out1,
    out2,
    out3,
    resid,
    gain,
    ffn,
    cot,
    feed,
    resid_own,
    normed,
    hidden,
    grads,
    grad_res,
    grad_mix,
    grad_gain,
):
    tile = pl.program_id(0)
    units = hidden.shape[1]
    outs = jnp.concatenate([out0[...], out1[...], out2[...], out3[...]], axis=0)
    mix = jnp.concatenate([mix0[...], mix1[...], mix2[...], mix3[...]], axis=0)
    res = resid[...] + tn(mix, outs)

    @pl.when(tile == who[0])
    def _():
        resid_own[...] = res

    rate = lax.rsqrt(jnp.mean(res * res, axis=-1, keepdims=True) + EPS)
    norm = (res * rate * gain[...]).astype(BF16)
    normed[...] = norm
    gate = nn(norm, ffn[:, :units])
    upward = nn(norm, ffn[:, units : 2 * units])
    sig = 1.0 / (1.0 + jnp.exp(-gate))
    silu = gate * sig
    hid = (silu * upward).astype(BF16)
    hidden[...] = hid
    feed[0] = nt(hid, ffn[:, 2 * units :]).astype(BF16)
    back = nn(cot[...], ffn[:, 2 * units :])
    grad_gate = (back * upward * sig * (1.0 + gate * (1.0 - sig))).astype(BF16)
    grad_up = (back * silu).astype(BF16)
    grads[:, :units] = grad_gate
    grads[:, units:] = grad_up
    pulled = nt(grad_gate, ffn[:, :units]) + nt(grad_up, ffn[:, units : 2 * units])
    scaled = pulled * gain[...]
    dots = jnp.mean(scaled * res, axis=-1, keepdims=True)
    part = rate * scaled - res * (rate * rate * rate * dots) + 0.25 * cot[...].astype(F32)
    part = part.astype(BF16)
    grad_res[...] = part
    grad_mix[...] = nt(outs, part).astype(BF16)
    gained = jnp.sum(pulled * res * rate, axis=0, keepdims=True)

    @pl.when(tile == 0)
    def _():
        grad_gain[...] = gained

    @pl.when(tile > 0)
    def _():
        grad_gain[...] += gained


def middle(who, mixes, outs, resid, gain, ffn, cot):
    length, dim = resid.shape
    width = mixes[0].shape[0]
    units = ffn.shape[1] // 3
    tiles = length // TILE
    tall = lambda r, _: (r, 0)
    wide = lambda r, _: (0, r)
    return pl.pallas_call(
        middle_kernel,
        grid_spec=pltpu.PrefetchScalarGridSpec(
            num_scalar_prefetch=1,
            grid=(tiles,),
            in_specs=[pl.BlockSpec((width, TILE), wide)] * 4
            + [whole((width, dim))] * 4
            + [
                pl.BlockSpec((TILE, dim), tall),
                whole((1, dim)),
                whole((dim, 3 * units)),
                pl.BlockSpec((TILE, dim), tall),
            ],
            out_specs=[
                pl.BlockSpec((1, TILE, dim), lambda r, who: (r ^ who[0], 0, 0)),
                whole((TILE, dim)),
                pl.BlockSpec((TILE, dim), tall),
                pl.BlockSpec((TILE, units), tall),
                pl.BlockSpec((TILE, 2 * units), tall),
                pl.BlockSpec((TILE, dim), tall),
                pl.BlockSpec((4 * width, TILE), wide),
                whole((1, dim)),
            ],
        ),
        out_shape=[
            jax.ShapeDtypeStruct((tiles, TILE, dim), BF16),
            jax.ShapeDtypeStruct((TILE, dim), F32),
            jax.ShapeDtypeStruct((length, dim), BF16),
            jax.ShapeDtypeStruct((length, units), BF16),
            jax.ShapeDtypeStruct((length, 2 * units), BF16),
            jax.ShapeDtypeStruct((length, dim), BF16),
            jax.ShapeDtypeStruct((4 * width, length), BF16),
            jax.ShapeDtypeStruct((1, dim), F32),
        ],
        name="middle",
    )(who, *mixes, *outs, resid, gain, ffn, cot)


def unrope_into(out, row, values, cosine, sine):
    half = HD // 2
    one, two = values[:half], values[half:]
    out[row : row + half, :] = (one * cosine + two * sine).astype(BF16)
    out[row + half : row + HD, :] = (two * cosine - one * sine).astype(BF16)


def back_kernel(
    info,
    qkv,
    gmix,
    mixed,
    lse,
    grad_res,
    resid,
    gain,
    wqkv,
    up0,
    up1,
    up2,
    up3,
    cos_ref,
    sin_ref,
    gproj,
    grad_slots,
    grad_emb,
    grad_rows,
    grad_gain,
    keys_sum,
    vals_sum,
    query_sum,
):
    step = pl.program_id(0)
    tile = pl.num_programs(0) - 1 - step
    width = gmix.shape[0]
    heads = width // HD

    @pl.when(step == 0)
    def _():
        keys_sum[...] = jnp.zeros_like(keys_sum)
        vals_sum[...] = jnp.zeros_like(vals_sum)

    base = pl.multiple_of(tile * TILE, TILE)

    def pull(h, lanes, query, key, value, seen):
        hs = slice(h * HD, (h + 1) * HD)
        grad = gmix[hs, lanes]
        delta = jnp.sum(grad.astype(F32) * mixed[hs, lanes].astype(F32), axis=0, keepdims=True)
        scores = jnp.where(seen, tn(key, query), MASKED)
        probs = jnp.exp(scores - lse[h : h + 1, lanes])
        dval = nt(grad, probs.astype(BF16))
        dscore = (probs * (tn(value, grad) - delta)).astype(BF16)
        query_sum[hs, lanes] = nn(key, dscore) * HD**-0.5
        return nt(query, dscore), dval

    @pl.when(tile == 0)
    def _():
        key_at = lax.broadcasted_iota(jnp.int32, (TILE, TILE), 0)
        query_at = lax.broadcasted_iota(jnp.int32, (TILE, TILE), 1)
        seen = key_at <= query_at
        for h in range(heads):
            hs = slice(h * HD, (h + 1) * HD)
            key = qkv[width + h * HD : width + (h + 1) * HD, 0:TILE]
            value = qkv[2 * width + h * HD : 2 * width + (h + 1) * HD, 0:TILE]
            dkey, dval = pull(h, slice(0, TILE), qkv[hs, 0:TILE], key, value, seen)
            keys_sum[hs, 0:TILE] += dkey
            vals_sum[hs, 0:TILE] += dval

    @pl.when(tile > 0)
    def _():
        key_at = lax.broadcasted_iota(jnp.int32, (4 * SEG, SEG), 0)
        query_at = lax.broadcasted_iota(jnp.int32, (4 * SEG, SEG), 1)
        for half in range(2):
            parent = info[2 + 2 * tile + half]
            mine = pl.ds(pl.multiple_of(base + half * SEG, SEG), SEG)
            theirs = pl.ds(key_offset(parent), SEG)
            limit = jnp.where(parent > 0, 4 * SEG, 3 * SEG)
            seen = (key_at < TILE) | ((key_at - TILE <= query_at) & (key_at < 3 * SEG))
            seen = seen | ((key_at >= 3 * SEG) & (key_at < limit))
            lanes = slice(half * SEG, (half + 1) * SEG)
            for h in range(heads):
                hs = slice(h * HD, (h + 1) * HD)
                ks = slice(width + h * HD, width + (h + 1) * HD)
                vs = slice(2 * width + h * HD, 2 * width + (h + 1) * HD)
                key = jnp.concatenate([qkv[ks, 0:TILE], qkv[ks, mine], qkv[ks, theirs]], axis=1)
                value = jnp.concatenate([qkv[vs, 0:TILE], qkv[vs, mine], qkv[vs, theirs]], axis=1)
                dkey, dval = pull(h, lanes, qkv[hs, mine], key, value, seen)
                for total, part in ((keys_sum, dkey), (vals_sum, dval)):
                    total[hs, 0:TILE] += part[:, 0:TILE]
                    total[hs, mine] += part[:, TILE : 3 * SEG]
                    total[hs, theirs] += part[:, 3 * SEG :]

    cosine, sine = cos_ref[...], sin_ref[...]
    place = pl.ds(base, TILE)
    for h in range(heads):
        hs = slice(h * HD, (h + 1) * HD)
        unrope_into(gproj, h * HD, query_sum[hs, :], cosine, sine)
        unrope_into(gproj, width + h * HD, keys_sum[hs, place], cosine, sine)
    gproj[2 * width :, :] = vals_sum[:, place].astype(BF16)
    pulled = tn(gproj[...], wqkv[...])
    hidden = resid[...]
    rate = lax.rsqrt(jnp.mean(hidden * hidden, axis=-1, keepdims=True) + EPS)
    scaled = pulled * gain[...]
    dots = jnp.mean(scaled * hidden, axis=-1, keepdims=True)
    part = grad_res[...].astype(F32) + rate * scaled - hidden * (rate * rate * rate * dots)
    part = part.astype(BF16)
    grad_slots[0] = part
    grad_emb[...] = part
    ups = jnp.concatenate([up0[...], up1[...], up2[...], up3[...]], axis=0)
    grad_rows[...] = nt(ups, part).astype(BF16)
    gained = jnp.sum(pulled * hidden * rate, axis=0, keepdims=True)

    @pl.when(step == 0)
    def _():
        grad_gain[...] = gained

    @pl.when(step > 0)
    def _():
        grad_gain[...] += gained


def back(info, qkv, gmix, mixed, lse, grad_res, resid, gain, wqkvo, ups, cosine, sine):
    length, dim = resid.shape
    width = gmix.shape[0]
    ng = ups[0].shape[0]
    tiles = length // TILE
    last = tiles - 1
    tall = lambda r, _: (last - r, 0)
    wide = lambda r, _: (0, last - r)
    return pl.pallas_call(
        back_kernel,
        grid_spec=pltpu.PrefetchScalarGridSpec(
            num_scalar_prefetch=1,
            grid=(tiles,),
            in_specs=[
                whole((3 * width, length)),
                pl.BlockSpec((width, TILE), wide),
                pl.BlockSpec((width, TILE), wide),
                pl.BlockSpec((8, TILE), wide),
                pl.BlockSpec((TILE, dim), tall),
                pl.BlockSpec((TILE, dim), tall),
                whole((1, dim)),
                whole((3 * width, dim)),
            ]
            + [whole((ng, dim))] * 4
            + [
                pl.BlockSpec((HD // 2, TILE), wide),
                pl.BlockSpec((HD // 2, TILE), wide),
            ],
            out_specs=[
                pl.BlockSpec((3 * width, TILE), wide),
                pl.BlockSpec((1, TILE, dim), lambda r, info: ((last - r) ^ info[0], 0, 0)),
                pl.BlockSpec((TILE, dim), tall),
                pl.BlockSpec((4 * ng, TILE), wide),
                whole((1, dim)),
            ],
            scratch_shapes=[
                VMEM((width, length), F32),
                VMEM((width, length), F32),
                VMEM((width, TILE), F32),
            ],
        ),
        out_shape=[
            jax.ShapeDtypeStruct((3 * width, length), BF16),
            jax.ShapeDtypeStruct((tiles, TILE, dim), BF16),
            jax.ShapeDtypeStruct((length, dim), BF16),
            jax.ShapeDtypeStruct((4 * ng, length), BF16),
            jax.ShapeDtypeStruct((1, dim), F32),
        ],
        name="back",
    )(info, qkv, gmix, mixed, lse, grad_res, resid, gain, wqkvo, *ups, cosine, sine)


def rotary(parents):
    length = parents.shape[0]
    token = jnp.arange(length, dtype=jnp.int32)
    trunk = 2 * SEG
    inside = token < trunk
    block = jnp.where(inside, 0, (token - trunk) // SEG + 1)
    offset = jnp.where(inside, token, token - trunk - (block - 1) * SEG)
    position = jnp.where(inside, 0, jnp.where(parents == 0, 2 * SEG, 3 * SEG)) + offset
    half = HD // 2
    frequency = ROPE_BASE ** (-(jnp.arange(half, dtype=F32) * 2.0 / HD))
    angles = frequency[:, None] * position.astype(F32)[None, :]
    return jnp.cos(angles), jnp.sin(angles)


def natural(slots, index):
    count = slots.shape[0]
    return jnp.concatenate(
        [lax.dynamic_index_in_dim(slots, r ^ index, 0, keepdims=False) for r in range(count)],
        axis=0,
    )


def shards(
    dp,
    embedded,
    ids_two,
    ids_three,
    parents,
    table_two,
    table_three,
    w_two,
    w_three,
    norm_attn,
    w_query,
    w_key,
    w_value,
    w_output,
    norm_ffn,
    w_gate,
    w_up,
    w_down,
    cotangent,
):
    own_d = lax.axis_index("dp")
    own_t = lax.axis_index("tensor")
    own_rows, ng = table_two.shape
    rows, dim = embedded.shape
    width = w_query.shape[1]
    units = w_gate.shape[1]
    own_dim = w_query.shape[0]
    gain_one = norm_attn.reshape(1, dim)
    gain_two = norm_ffn.reshape(1, dim)

    tables = jnp.concatenate([table_two.astype(BF16).T, table_three.astype(BF16).T], axis=0)
    small = jnp.concatenate([w_two.astype(BF16).T, w_three.astype(BF16).T], axis=1)
    attn_pack = jnp.concatenate(
        [
            w_query.astype(BF16),
            w_key.astype(BF16),
            w_value.astype(BF16),
            w_output.astype(BF16).T,
        ],
        axis=1,
    )
    ffn_pack = jnp.concatenate(
        [w_gate.astype(BF16), w_up.astype(BF16), w_down.astype(BF16).T], axis=1
    )
    ids = jnp.stack([ids_two, ids_three])
    info = jnp.concatenate(
        [jnp.stack([own_t, own_d]).astype(jnp.int32), parents.reshape(-1, SEG)[:, 0]]
    )

    token_slots = gather_tensor(jnp.stack([embedded, cotangent]))
    token_slots = jnp.stack(token_slots)
    emb_all = natural(token_slots[:, 0], own_t)
    cot_all = natural(token_slots[:, 1], own_t)

    if dp == 8:
        pad = jnp.zeros((own_dim, SEG - 2 * ng), BF16)
        first = jnp.concatenate([tables, small, pad], axis=1)
        pieces = gather_dp(first, dp)
        attn_pieces = gather_dp(attn_pack, dp, tuple(pieces[0::2]))
        ffn_pieces = gather_dp(ffn_pack, dp, tuple(attn_pieces[0::2]))
        got = None
        for j in range(0, dp, 2):
            got = lookup(info, pieces[j : j + 2], (j, j + 1), own_rows, ids, got)
        ups = assemble(info, pieces, True, own_rows // SEG, 2 * ng)
        wqkvo = assemble(info, attn_pieces, True)
        ffn_w = assemble(info, ffn_pieces, False)
    else:
        every = lax.all_gather(tables, "dp", axis=0)
        ups = lax.all_gather(small, "dp", axis=0, tiled=True).T
        wqkvo = lax.all_gather(attn_pack, "dp", axis=0, tiled=True).T
        ffn_w = lax.all_gather(ffn_pack, "dp", axis=0, tiled=True)

        def take(i, so_far):
            piece = lax.dynamic_index_in_dim(every, i, 0, keepdims=False)
            at = jnp.stack([own_t, i]).astype(jnp.int32)
            return lookup(at, [piece], (0,), own_rows, ids, so_far)

        got = lax.fori_loop(0, dp, take, jnp.zeros((2 * ng, ids.shape[1]), BF16))

    ups = gather_tensor(ups)
    outs = gather_tensor(wqkvo[3 * width :])
    row_sets = gather_tensor(got)

    cosine, sine = rotary(parents)
    resid, normed, qkv, mixed, lse = front(
        info, row_sets, ups, emb_all, wqkvo, gain_one, cosine, sine
    )
    mixes = gather_tensor(mixed)
    feed, resid_own, normed_two, hidden, grads, grad_res, grad_mix, gain_part_two = middle(
        info, mixes, outs, resid, gain_two, ffn_w, cot_all
    )
    gmix = scatter_tensor([grad_mix[k * width : (k + 1) * width] for k in range(4)]).astype(BF16)
    feed, grad_res_late, _ = lax.optimization_barrier((feed, grad_res, gmix))
    output = (resid_own + scatter_tensor([feed[k] for k in range(4)])).astype(BF16)
    out_parts = [nn(mixes[k], grad_res_late).astype(BF16) for k in range(4)]
    out_grad = scatter_tensor(out_parts).astype(BF16)

    gate_up = tn(normed_two, grads).astype(BF16)
    down = tn(cot_all, hidden).astype(BF16)
    ffn_grads = jnp.concatenate([gate_up, down], axis=1).reshape(dp, own_dim, 3 * units)
    ffn_total = scatter_dp(ffn_grads, dp)

    gproj, slots, grad_emb, grad_rows, gain_part_one = back(
        info, qkv, gmix, mixed, lse, grad_res, resid, gain_one, wqkvo, ups, cosine, sine
    )
    row_total = scatter_tensor([grad_rows[k * 2 * ng : (k + 1) * 2 * ng] for k in range(4)])
    slots, grad_emb, _ = lax.optimization_barrier((slots, grad_emb, row_total))
    embed_grad = scatter_tensor([slots[k] for k in range(4)]).astype(BF16)

    digits = jnp.stack([ids_two // 256, ids_two % 256, ids_three // 256, ids_three % 256])
    digits = jnp.concatenate([digits.astype(BF16), jnp.zeros((12, digits.shape[1]), BF16)])
    row_pack = jnp.concatenate([row_total.astype(BF16), digits], axis=0)
    if dp == 8:
        row_pieces = gather_dp(row_pack, dp)
        table_grad = None
        for j in range(0, dp, 2):
            table_grad = spread(info, row_pieces[j : j + 2], own_rows, ng, table_grad)
    else:
        every = lax.all_gather(row_pack, "dp", axis=0)

        def put(i, so_far):
            piece = lax.dynamic_index_in_dim(every, i, 0, keepdims=False)
            return spread(info, [piece], own_rows, ng, so_far)

        table_grad = lax.fori_loop(0, dp, put, jnp.zeros((2 * ng, own_rows), F32))

    up_parts = [nn(row_sets[k], grad_emb).astype(BF16) for k in range(4)]
    up_grad = scatter_tensor(up_parts).astype(BF16)
    proj_grad = lax.dot_general(
        normed, gproj, (((0,), (1,)), ((), ())), preferred_element_type=F32
    ).astype(BF16)
    attn_grads = jnp.concatenate([proj_grad, out_grad.T, up_grad.T], axis=1)
    attn_total = scatter_dp(attn_grads.reshape(dp, own_dim, attn_grads.shape[1]), dp)

    gains = jnp.concatenate([gain_part_one, gain_part_two], axis=0)
    gains = gains + xor_tensor(gains, 1)
    gains = gains + xor_tensor(gains, 2)
    step = 1
    while step < dp:
        gains = gains + xor_dp(gains, step, dp)
        step *= 2

    return (
        output,
        embed_grad,
        table_grad[:ng].T,
        table_grad[ng:].T,
        attn_total[:, 4 * width : 4 * width + ng].T,
        attn_total[:, 4 * width + ng :].T,
        gains[0],
        attn_total[:, :width],
        attn_total[:, width : 2 * width],
        attn_total[:, 2 * width : 3 * width],
        attn_total[:, 3 * width : 4 * width].T,
        gains[1],
        ffn_total[:, :units],
        ffn_total[:, units : 2 * units],
        ffn_total[:, 2 * units :].T,
    )


def solution(mesh):
    tokens = P(("dp", "tensor"), None)
    down, across = P("dp", "tensor"), P("tensor", "dp")
    in_specs = (
        (tokens, P("dp"), P("dp"), P("dp"), down, down, across, across, P())
        + (down, down, down, across, P(), down, down, across, tokens)
    )
    out_specs = (
        (tokens, tokens, down, down, across, across, P())
        + (down, down, down, across, P(), down, down, across)
    )
    body = functools.partial(shards, mesh.shape["dp"])
    return jax.shard_map(body, mesh=mesh, in_specs=in_specs, out_specs=out_specs, check_vma=False)
```

time: 1290 us -> 372 us (0.29)
  blocking collectives: 518 us -> 0 us
  waiting for transfers between devices: 481 us -> 132 us
  other arithmetic: 135 us -> 22.7 us
  Pallas kernels: 0 us -> 100 us
  starting transfers between devices: 0.96 us -> 70.5 us
  matrix products: 82.1 us -> 17.1 us
  local copies, waits for them, and re-layouts: 53.9 us -> 25.7 us
  between operations: 15.2 us -> 1.78 us
    all_gather x15 -> x0, blocking collectives: 479 us -> none  [the longest x1 34.7 us: shards(): lax.all_gather(w_gate.astype(half_type), 'dp', axis=0, tiled=True)]
    reduce_scatter x8 -> x0, waiting for transfers between devices: 247 us -> none  [the longest x1 67.6 us: shards(): lax.psum_scatter(upward_grad, 'dp', scatter_dimension=0, tiled=True)]
    unnamed x25 -> x0, waiting for transfers between devices: 197 us -> none
    ppermute x0 -> x74, waiting for transfers between devices: none -> 132 us  [the longest x39 113 us: xor_dp(): return lax.ppermute(value, 'dp', [(i, i ^ step) for i in range(count)])]
    scatter-add x2 -> x0, other arithmetic: 101 us -> none  [rows_into(): jax.ops.segment_sum(piece, target, num_segments=own_rows + 1)[:own_rows]]
    pallas_call x0 -> x14, Pallas kernels: none -> 100 us  [the longest x4 21.5 us: lookup(): pl.pallas_call(functools.partial(lookup_kernel, tuple(owners), width, own...]
    ppermute x0 -> x74, starting transfers between devices: none -> 70.5 us  [the longest x39 49.8 us: xor_dp(): return lax.ppermute(value, 'dp', [(i, i ^ step) for i in range(count)])]
    dot_general x32 -> x11, matrix products: 74.3 us -> 17.1 us  [the longest x8 10.5 us: nn(): lax.dot_general(a, b, (((1,), (0,)), ((), ())), preferred_element_type=F32)]
  transfers between devices with their start and end apart: 19 -> 74, of which waited for: 12 -> 24; matrix products, arithmetic and copies ran while one was open for 12% -> 15% of each run, Pallas kernels for 0% -> 22%
where the time goes in v1:
time: 372 us; the launch traced here: 371 us
  waiting for transfers between devices  132 us (35%)
  Pallas kernels  100 us (27%)
  starting transfers between devices  70.5 us (19%)
  local copies, waits for them, and re-layouts  25.7 us (7%)
  other arithmetic  22.7 us (6%)
  matrix products  17.1 us (5%)
    ppermute x39, waiting for transfers between devices, xor_dp(): return lax.ppermute(value, 'dp', [(i, i ^ step) for i in range(count)])  113 us
    ppermute x39, starting transfers between devices, xor_dp(): return lax.ppermute(value, 'dp', [(i, i ^ step) for i in range(count)])  49.8 us
    pallas_call x4, Pallas kernels, lookup(): pl.pallas_call(functools.partial(lookup_kernel, tuple(owners), width, own...  21.5 us
    ppermute x35, starting transfers between devices, xor_tensor(): return lax.ppermute(value, 'tensor', [(i, i ^ step) for i in range(4)])  20.7 us
    pallas_call x4, Pallas kernels, spread(): pl.pallas_call(functools.partial(spread_kernel, count, width, prior is No...  19.6 us
    ppermute x35, waiting for transfers between devices, xor_tensor(): return lax.ppermute(value, 'tensor', [(i, i ^ step) for i in range(4)])  19.4 us
    pallas_call x1, Pallas kernels, middle(): pl.pallas_call(middle_kernel, grid_spec=pltpu.PrefetchScalarGridSpec(num_...  18.3 us
    pallas_call x1, Pallas kernels, back(): pl.pallas_call(back_kernel, grid_spec=pltpu.PrefetchScalarGridSpec(num_sc...  17.5 us
  transfers between devices with their start and end apart: 74, of which 24 were waited for; matrix products, arithmetic and copies ran while one was open for 15% of the time, Pallas kernels for 22%

profile of v1, /device:TPU:0, one launch (start us, length us, event | category | flops | bytes accessed | tf_op | source)
XLA Modules:
  0.0 370.6 jit_solution(9423491107240958864)
XLA Ops:
  0.7 2.2 fusion.52
  2.9 2.9 collective-permute-start.14
  6.4 3.7 collective-permute-start
  12.8 3.9 %collective-permute-done.refs_2_.refs_6_ = bf16[96,1152]{1,0:T(8,128)(2,1)S(1)} collective-permute-done((bf16[96,1152]{1,0:T(8,128)(2,1)S(1)}, bf16[96,1152]{1,0:T(8,128)(2,1)S(1)}, u32[]{:S(2)}, u32[]{:S(2)}) %collective-permute-start) | collective-permute-done | bytes 221216 | tf_op jit(solution)/shard_map/ppermute | solution.py:26
  16.7 11.9 %collective-permute-done.2.refs_2_.refs_4_ = bf16[96,1152]{1,0:T(8,128)(2,1)S(1)} collective-permute-done((bf16[96,1152]{1,0:T(8,128)(2,1)S(1)}, bf16[96,1152]{1,0:T(8,128)(2,1)S(1)}, u32[]{:S(2)}, u32[]{:S(2)}) %collective-permute-start.2) | collective-permute-done | bytes 221216 | tf_op jit(solution)/shard_map/ppermute | solution.py:26
  28.6 3.0 collective-permute-start.19
  33.7 2.3 collective-permute-done.17.refs_2_
  37.5 4.7 %collective-permute-done.19.refs_4_ = bf16[96,768]{1,0:T(8,128)(2,1)S(1)} collective-permute-done((bf16[96,768]{1,0:T(8,128)(2,1)S(1)}, bf16[96,768]{1,0:T(8,128)(2,1)S(1)}, u32[]{:S(2)}, u32[]{:S(2)}) %collective-permute-start.19) | collective-permute-done | bytes 147488 | tf_op jit(solution)/shard_map/ppermute | solution.py:26
  45.9 4.7 %collective-permute-done.3.refs_3_.refs_5_ = bf16[96,1152]{1,0:T(8,128)(2,1)S(1)} collective-permute-done((bf16[96,1152]{1,0:T(8,128)(2,1)S(1)}, bf16[96,1152]{1,0:T(8,128)(2,1)S(1)}, u32[]{:S(2)}, u32[]{:S(2)}) %collective-permute-start.3) | collective-permute-done | bytes 221216 | tf_op jit(solution)/shard_map/ppermute | solution.py:26
  52.1 3.2 collective-permute-done.1.refs_3_.refs_7_
  58.6 5.3 %lookup.4.refs_4_ = bf16[96,1024]{1,0:T(8,128)(2,1)} custom-call(s32[10]{0:T(128)} %pad_add_fusion.1.refs_0_.info.par.who, s32[2,1024]{1,0:T(2,128)} %pad_add_fusion.refs_1_, bf16[96,1152]{1,0:T(8,128)(2,1)} %copy-done.6, bf16[96,1152]{1,0:T(8,128)(2,1)} %copy-done.30), custom_call_target="tpu_custom_call" | custom-call | tf_op jit(solution)/shard_map/lookup/pallas_call | solution.py:159
  63.9 5.4 %lookup.5.refs_4_ = bf16[96,1024]{1,0:T(8,128)(2,1)} custom-call(s32[10]{0:T(128)} %pad_add_fusion.1.refs_0_.info.par.who, s32[2,1024]{1,0:T(2,128)} %pad_add_fusion.refs_1_, bf16[96,1152]{1,0:T(8,128)(2,1)} %copy-done.29, bf16[96,1152]{1,0:T(8,128)(2,1)} %copy-done.31, bf16[96,1024]{1,0:T(8,128)(2,1)} %lookup.4.refs_4_), custom_call_target="tpu_custom_call" | custom-call | tf_op jit(solution)/shard_map/lookup/pallas_call | solution.py:159
  69.3 5.4 %lookup.6.refs_4_ = bf16[96,1024]{1,0:T(8,128)(2,1)} custom-call(s32[10]{0:T(128)} %pad_add_fusion.1.refs_0_.info.par.who, s32[2,1024]{1,0:T(2,128)} %pad_add_fusion.refs_1_, bf16[96,1152]{1,0:T(8,128)(2,1)} %copy-done.28, bf16[96,1152]{1,0:T(8,128)(2,1)} %copy-done.32, bf16[96,1024]{1,0:T(8,128)(2,1)} %lookup.5.refs_4_), custom_call_target="tpu_custom_call" | custom-call | tf_op jit(solution)/shard_map/lookup/pallas_call | solution.py:159
  74.8 2.3 assemble.3.up0
  77.1 5.4 %lookup.7.row0 = bf16[96,1024]{1,0:T(8,128)(2,1)} custom-call(s32[10]{0:T(128)} %pad_add_fusion.1.refs_0_.info.par.who, s32[2,1024]{1,0:T(2,128)} %pad_add_fusion.refs_1_, bf16[96,1152]{1,0:T(8,128)(2,1)} %copy-done.27, bf16[96,1152]{1,0:T(8,128)(2,1)} %copy-done.33, bf16[96,1024]{1,0:T(8,128)(2,1)} %lookup.6.refs_4_), custom_call_target="tpu_custom_call" | custom-call | tf_op jit(solution)/shard_map/lookup/pallas_call | solution.py:159
  88.6 3.5 assemble.4.wqkv
  93.2 1.8 pad_maximum_fusion
  97.5 13.9 %front.1 = (f32[1024,768]{1,0:T(8,128)}, bf16[1024,768]{1,0:T(8,128)(2,1)}, bf16[576,1024]{1,0:T(8,128)(2,1)}, bf16[192,1024]{1,0:T(8,128)(2,1)}, f32[8,1024]{1,0:T(8,128)}) custom-call(s32[10]{0:T(128)} %pad_add_fusion.1.refs_0_.info.par.who, bf16[96,1024]{1,0:T(8,128)(2,1)} %lookup.7.row0, bf16[96,1024]{1,0:T(8,128)(2,1)} %copy-done.34, ...), custom_call_target="tpu_custom_call" | custom-call | tf_op jit(solution)/shard_map/front/pallas_call | solution.py:319
  112.0 2.1 collective-permute-start.32
  119.5 15.7 %collective-permute-done.32.refs_4_ = bf16[96,1536]{1,0:T(8,128)(2,1)S(1)} collective-permute-done((bf16[96,1536]{1,0:T(8,128)(2,1)S(1)}, bf16[96,1536]{1,0:T(8,128)(2,1)S(1)}, u32[]{:S(2)}, u32[]{:S(2)}) %collective-permute-start.32) | collective-permute-done | bytes 294944 | tf_op jit(solution)/shard_map/ppermute | solution.py:26
  139.2 6.3 %collective-permute-done.31.refs_3_ = bf16[96,1536]{1,0:T(8,128)(2,1)} collective-permute-done((bf16[96,1536]{1,0:T(8,128)(2,1)}, bf16[96,1536]{1,0:T(8,128)(2,1)}, u32[]{:S(2)}, u32[]{:S(2)}) %collective-permute-start.31) | collective-permute-done | bytes 294944 | tf_op jit(solution)/shard_map/ppermute | solution.py:26
  145.5 6.3 %collective-permute-done.33.refs_5_ = bf16[96,1536]{1,0:T(8,128)(2,1)} collective-permute-done((bf16[96,1536]{1,0:T(8,128)(2,1)S(1)}, bf16[96,1536]{1,0:T(8,128)(2,1)}, u32[]{:S(2)}, u32[]{:S(2)}) %collective-permute-start.33) | collective-permute-done | bytes 294944 | tf_op jit(solution)/shard_map/ppermute | solution.py:26
  151.8 3.4 collective-permute-done.35.refs_7_
  156.0 3.8 %assemble.5.ffn = bf16[768,1536]{1,0:T(8,128)(2,1)} custom-call(s32[10]{0:T(128)} %pad_add_fusion.1.refs_0_.info.par.who, bf16[96,1536]{1,0:T(8,128)(2,1)} %copy-done.24, bf16[96,1536]{1,0:T(8,128)(2,1)} %copy-done.48, bf16[96,1536]{1,0:T(8,128)(2,1)} %collective-permute-done.30.refs_2_, bf16[96,1536]{1,0:T(8,128)(2,1)} %collective-permute-done.31.refs_3_, ...), custom_call_target="tpu_custom_call" | custom-call | tf_op jit(solution)/shard_map/assemble/pallas_call | solution.py:93
  162.2 18.3 %middle.1 = (bf16[4,256,768]{2,1,0:T(8,128)(2,1)}, f32[256,768]{1,0:T(8,128)}, bf16[1024,768]{1,0:T(8,128)(2,1)}, bf16[1024,512]{1,0:T(8,128)(2,1)}, bf16[1024,1...) custom-call(s32[10]{0:T(128)} %pad_add_fusion.1.refs_0_.info.par.who, ...), custom_call_target="tpu_custom_call" | custom-call | tf_op jit(solution)/shard_map/middle/pallas_call | solution.py:426
  182.4 3.6 convolution_convert_fusion
  191.0 7.7 %collective-permute-done.38 = bf16[192,1024]{1,0:T(8,128)(2,1)S(1)} collective-permute-done((bf16[192,1024]{1,0:T(8,128)(2,1)S(1)}, bf16[192,1024]{1,0:T(8,128)(2,1)S(1)}, u32[]{:S(2)}, u32[]{:S(2)}) %collective-permute-start.38) | collective-permute-done | bytes 393248 | tf_op jit(solution)/shard_map/ppermute | solution.py:22
  199.7 17.5 %back.1 = (bf16[576,1024]{1,0:T(8,128)(2,1)}, bf16[4,256,768]{2,1,0:T(8,128)(2,1)}, bf16[1024,768]{1,0:T(8,128)(2,1)}, bf16[384,1024]{1,0:T(8,128)(2,1)}, f32[1,768]{1,0:T(1,128)}) custom-call(s32[10]{0:T(128)} %pad_add_fusion.1.refs_0_.info.par.who, bf16[576,1024]{1,0:T(8,128)(2,1)} %get-tuple-element.48.qkv, bf16[192,1024]{1,0:T(8,128)(2,1)} %add_convert_fusion.gmix, ...), custom_call_target="tpu_custom_call" | custom-call | tf_op jit(solution)/shard_map/back/pallas_call | solution.py:593
  224.1 3.0 collective-permute-done.67
  227.6 2.0 convolution_convert_fusion.1
  233.0 2.4 collective-permute-done.69
  239.3 4.1 %collective-permute-done.44 = bf16[96,1024]{1,0:T(8,128)(2,1)S(1)} collective-permute-done((bf16[96,1024]{1,0:T(8,128)(2,1)S(1)}, bf16[96,1024]{1,0:T(8,128)(2,1)S(1)}, u32[]{:S(2)}, u32[]{:S(2)}) %collective-permute-start.44) | collective-permute-done | bytes 196640 | tf_op jit(solution)/shard_map/ppermute | solution.py:22
  251.2 2.8 concatenate.41.refs_1_
  255.6 2.0 fusion.21
  258.1 2.0 fusion.12
  260.7 2.3 fusion.9
  264.6 4.8 %spread.4.refs_3_ = f32[96,1024]{1,0:T(8,128)} custom-call(s32[10]{0:T(128)} %pad_add_fusion.1.refs_0_.info.par.who, bf16[112,1024]{1,0:T(8,128)(2,1)} %concatenate.41.refs_1_, bf16[112,1024]{1,0:T(8,128)(2,1)} %collective-permute-done.54.refs_2_), custom_call_target="tpu_custom_call" | custom-call | tf_op jit(solution)/shard_map/spread/pallas_call | solution.py:205
  276.8 20.9 %collective-permute-done.72 = bf16[96,1536]{1,0:T(8,128)(2,1)} collective-permute-done((bf16[96,1536]{1,0:T(8,128)(2,1)}, bf16[96,1536]{1,0:T(8,128)(2,1)}, u32[]{:S(2)}, u32[]{:S(2)}) %collective-permute-start.72) | collective-permute-done | bytes 294944 | tf_op jit(solution)/shard_map/ppermute | solution.py:26
  301.3 2.1 collective-permute-start.48
  303.4 6.0 %collective-permute-done.41 = bf16[256,768]{1,0:T(8,128)(2,1)S(1)} collective-permute-done((bf16[256,768]{1,0:T(8,128)(2,1)}, bf16[256,768]{1,0:T(8,128)(2,1)S(1)}, u32[]{:S(2)}, u32[]{:S(2)}) %collective-permute-start.41) | collective-permute-done | bytes 393248 | tf_op jit(solution)/shard_map/ppermute | solution.py:22
  310.9 2.0 fusion.24
  318.2 14.8 %collective-permute-done.53.refs_2_ = bf16[112,1024]{1,0:T(8,128)(2,1)} collective-permute-done((bf16[112,1024]{1,0:T(8,128)(2,1)}, bf16[112,1024]{1,0:T(8,128)(2,1)}, u32[]{:S(2)}, u32[]{:S(2)}) %collective-permute-start.53) | collective-permute-done | bytes 229408 | tf_op jit(solution)/shard_map/ppermute | solution.py:26
  334.4 4.9 %spread.5.refs_3_ = f32[96,1024]{1,0:T(8,128)} custom-call(s32[10]{0:T(128)} %pad_add_fusion.1.refs_0_.info.par.who, bf16[112,1024]{1,0:T(8,128)(2,1)} %collective-permute-done.52.refs_1_, bf16[112,1024]{1,0:T(8,128)(2,1)} %collective-permute-done.53.refs_2_, f32[96,1024]{1,0:T(8,128)} %spread.4.refs_3_), custom_call_target="tpu_custom_call" | custom-call | tf_op jit(solution)/shard_map/spread/pallas_call | solution.py:205
  339.4 4.9 %spread.6.refs_3_ = f32[96,1024]{1,0:T(8,128)} custom-call(s32[10]{0:T(128)} %pad_add_fusion.1.refs_0_.info.par.who, bf16[112,1024]{1,0:T(8,128)(2,1)} %collective-permute-done.50.refs_1_, bf16[112,1024]{1,0:T(8,128)(2,1)} %collective-permute-done.51.refs_2_, f32[96,1024]{1,0:T(8,128)} %spread.5.refs_3_), custom_call_target="tpu_custom_call" | custom-call | tf_op jit(solution)/shard_map/spread/pallas_call | solution.py:205
  344.3 4.9 %spread.7 = f32[96,1024]{1,0:T(8,128)} custom-call(s32[10]{0:T(128)} %pad_add_fusion.1.refs_0_.info.par.who, bf16[112,1024]{1,0:T(8,128)(2,1)} %collective-permute-done.48.refs_1_, bf16[112,1024]{1,0:T(8,128)(2,1)} %collective-permute-done.49.refs_2_, f32[96,1024]{1,0:T(8,128)} %spread.6.refs_3_), custom_call_target="tpu_custom_call" | custom-call | tf_op jit(solution)/shard_map/spread/pallas_call | solution.py:205
  352.3 5.2 %collective-permute-start.62 = (bf16[96,864]{1,0:T(8,128)(2,1)S(1)}, bf16[96,864]{1,0:T(8,128)(2,1)S(1)}, u32[]{:S(2)}, u32[]{:S(2)}) collective-permute-start(bf16[96,864]{1,0:T(8,128)(2,1)S(1)} %get-tuple-element.148), channel_id=1, source_target_pairs={{0,8},{4,12},{8,0},{12,4},{16,24},{20,28},{24,16},{28,20},{1,9},{5... | collective-permute-start | bytes 497672 | tf_op jit(solution)/shard_map/ppermute | solution.py:26
  360.0 2.0 fusion.20
  362.0 5.5 %collective-permute-done.63 = bf16[96,864]{1,0:T(8,128)(2,1)S(1)} collective-permute-done((bf16[96,864]{1,0:T(8,128)(2,1)S(1)}, bf16[96,864]{1,0:T(8,128)(2,1)S(1)}, u32[]{:S(2)}, u32[]{:S(2)}) %collective-permute-start.63) | collective-permute-done | bytes 165920 | tf_op jit(solution)/shard_map/ppermute | solution.py:26
  (354 shorter events, 100.2 us)
Async XLA Ops:
  2.9 30.3 %collective-permute-start.14 = (bf16[2,256,768]{2,1,0:T(8,128)(2,1)}, bf16[2,256,768]{2,1,0:T(8,128)(2,1)}, u32[]{:S(2)}, u32[]{:S(2)}) collective-permute-start(bf16[2,256,768]{2,1,0:T(8,128)(2,1)} %get-tuple-element.147), channel_id=1, source_target_pairs={{0,2},{1,3},{2,0},{3,1},{4,6},{5,7},{6,4},{7,5},{8,10},{9,11},{10,... | collective-permute-start | bytes 2359304 | tf_op jit(solution)/shard_map/ppermute | solution.py:22
  6.4 10.3 %collective-permute-start = (bf16[96,1152]{1,0:T(8,128)(2,1)S(1)}, bf16[96,1152]{1,0:T(8,128)(2,1)S(1)}, u32[]{:S(2)}, u32[]{:S(2)}) collective-permute-start(bf16[96,1152]{1,0:T(8,128)(2,1)S(1)} %concatenate.36.refs_2_.refs_0_), channel_id=1, source_target_pairs={{0,24},{4,28},{8,16},{12,20},{16,8},{20,12},{24,0},{28,4},{1,25},{... | collective-permute-start | bytes 663560 | tf_op jit(solution)/shard_map/ppermute | solution.py:26
  10.0 18.5 %collective-permute-start.2 = (bf16[96,1152]{1,0:T(8,128)(2,1)S(1)}, bf16[96,1152]{1,0:T(8,128)(2,1)S(1)}, u32[]{:S(2)}, u32[]{:S(2)}) collective-permute-start(bf16[96,1152]{1,0:T(8,128)(2,1)S(1)} %concatenate.36.refs_2_.refs_0_), channel_id=1, source_target_pairs={{0,16},{4,20},{8,24},{12,28},{16,0},{20,4},{24,8},{28,12},{1,17},{... | collective-permute-start | bytes 663560 | tf_op jit(solution)/shard_map/ppermute | solution.py:26
  10.0 18.5 %collective-permute-start.4 = (bf16[96,1152]{1,0:T(8,128)(2,1)S(1)}, bf16[96,1152]{1,0:T(8,128)(2,1)S(1)}, u32[]{:S(2)}, u32[]{:S(2)}) collective-permute-start(bf16[96,1152]{1,0:T(8,128)(2,1)S(1)} %concatenate.36.refs_2_.refs_0_), channel_id=1, source_target_pairs={{0,8},{4,12},{8,0},{12,4},{16,24},{20,28},{24,16},{28,20},{1,9},{5... | collective-permute-start | bytes 663560 | tf_op jit(solution)/shard_map/ppermute | solution.py:26
  10.8 22.3 %collective-permute-start.6 = (bf16[96,1152]{1,0:T(8,128)(2,1)S(1)}, bf16[96,1152]{1,0:T(8,128)(2,1)S(1)}, u32[]{:S(2)}, u32[]{:S(2)}) collective-permute-start(bf16[96,1152]{1,0:T(8,128)(2,1)S(1)} %concatenate.36.refs_2_.refs_0_), channel_id=1, source_target_pairs={{0,4},{4,0},{8,12},{12,8},{16,20},{20,16},{24,28},{28,24},{1,5},{5... | collective-permute-start | bytes 663560 | tf_op jit(solution)/shard_map/ppermute | solution.py:26
  28.6 13.6 %collective-permute-start.19 = (bf16[96,768]{1,0:T(8,128)(2,1)S(1)}, bf16[96,768]{1,0:T(8,128)(2,1)S(1)}, u32[]{:S(2)}, u32[]{:S(2)}) collective-permute-start(bf16[96,768]{1,0:T(8,128)(2,1)S(1)} %pad_maximum_fusion.8.refs_0_), channel_id=1, source_target_pairs={{0,16},{4,20},{8,24},{12,28},{16,0},{20,4},{24,8},{28,12},{1,17},{... | collective-permute-start | bytes 442376 | tf_op jit(solution)/shard_map/ppermute | solution.py:26
  31.6 12.1 %collective-permute-start.21 = (bf16[96,768]{1,0:T(8,128)(2,1)S(1)}, bf16[96,768]{1,0:T(8,128)(2,1)}, u32[]{:S(2)}, u32[]{:S(2)}) collective-permute-start(bf16[96,768]{1,0:T(8,128)(2,1)S(1)} %pad_maximum_fusion.8.refs_0_), channel_id=1, source_target_pairs={{0,24},{4,28},{8,16},{12,20},{16,8},{20,12},{24,0},{28,4},{1,25},{... | collective-permute-start | bytes 442376 | tf_op jit(solution)/shard_map/ppermute | solution.py:26
  33.1 59.6 %collective-permute-start.13 = (bf16[2,256,768]{2,1,0:T(8,128)(2,1)}, bf16[2,256,768]{2,1,0:T(8,128)(2,1)}, u32[]{:S(2)}, u32[]{:S(2)}) collective-permute-start(bf16[2,256,768]{2,1,0:T(8,128)(2,1)} %get-tuple-element.147), channel_id=1, source_target_pairs={{0,1},{1,0},{2,3},{3,2},{4,5},{5,4},{6,7},{7,6},{8,9},{9,8},{10,11... | collective-permute-start | bytes 2359304 | tf_op jit(solution)/shard_map/ppermute | solution.py:22
  33.2 59.6 %collective-permute-start.15 = (bf16[2,256,768]{2,1,0:T(8,128)(2,1)}, bf16[2,256,768]{2,1,0:T(8,128)(2,1)}, u32[]{:S(2)}, u32[]{:S(2)}) collective-permute-start(bf16[2,256,768]{2,1,0:T(8,128)(2,1)} %collective-permute-done.14), channel_id=1, source_target_pairs={{0,1},{1,0},{2,3},{3,2},{4,5},{5,4},{6,7},{7,6},{8,9},{9,8},{10,11... | collective-permute-start | bytes 2359304 | tf_op jit(solution)/shard_map/ppermute | solution.py:22
  43.7 11.6 %collective-permute-start.1 = (bf16[96,1152]{1,0:T(8,128)(2,1)S(1)}, bf16[96,1152]{1,0:T(8,128)(2,1)S(1)}, u32[]{:S(2)}, u32[]{:S(2)}) collective-permute-start(bf16[96,1152]{1,0:T(8,128)(2,1)S(1)} %collective-permute-done.refs_2_.refs_6_), channel_id=1, source_target_pairs={{0,4},{4,0},{8,12},{12,8},{16,20},{20,16},{24,28},{28,24},{1,5},{5... | collective-permute-start | bytes 663560 | tf_op jit(solution)/shard_map/ppermute | solution.py:26
  44.4 38.1 %collective-permute-start.16 = (bf16[96,768]{1,0:T(8,128)(2,1)S(1)}, bf16[96,768]{1,0:T(8,128)(2,1)S(1)}, u32[]{:S(2)}, u32[]{:S(2)}) collective-permute-start(bf16[96,768]{1,0:T(8,128)(2,1)S(1)} %pad_maximum_fusion.8.refs_0_), channel_id=1, source_target_pairs={{0,4},{4,0},{8,12},{12,8},{16,20},{20,16},{24,28},{28,24},{1,5},{5... | collective-permute-start | bytes 442376 | tf_op jit(solution)/shard_map/ppermute | solution.py:26
  50.6 32.5 %collective-permute-start.18 = (bf16[96,768]{1,0:T(8,128)(2,1)S(1)}, bf16[96,768]{1,0:T(8,128)(2,1)}, u32[]{:S(2)}, u32[]{:S(2)}) collective-permute-start(bf16[96,768]{1,0:T(8,128)(2,1)S(1)} %collective-permute-done.17.refs_2_), channel_id=1, source_target_pairs={{0,4},{4,0},{8,12},{12,8},{16,20},{20,16},{24,28},{28,24},{1,5},{5... | collective-permute-start | bytes 442376 | tf_op jit(solution)/shard_map/ppermute | solution.py:26
  55.3 28.3 %collective-permute-start.20 = (bf16[96,768]{1,0:T(8,128)(2,1)S(1)}, bf16[96,768]{1,0:T(8,128)(2,1)}, u32[]{:S(2)}, u32[]{:S(2)}) collective-permute-start(bf16[96,768]{1,0:T(8,128)(2,1)S(1)} %collective-permute-done.19.refs_4_), channel_id=1, source_target_pairs={{0,4},{4,0},{8,12},{12,8},{16,20},{20,16},{24,28},{28,24},{1,5},{5... | collective-permute-start | bytes 442376 | tf_op jit(solution)/shard_map/ppermute | solution.py:26
  87.9 30.1 %collective-permute-start.30 = (bf16[96,1536]{1,0:T(8,128)(2,1)S(1)}, bf16[96,1536]{1,0:T(8,128)(2,1)}, u32[]{:S(2)}, u32[]{:S(2)}) collective-permute-start(bf16[96,1536]{1,0:T(8,128)(2,1)S(1)} %pad_maximum_fusion.6.refs_0_), channel_id=1, source_target_pairs={{0,8},{4,12},{8,0},{12,4},{16,24},{20,28},{24,16},{28,20},{1,9},{5... | collective-permute-start | bytes 884744 | tf_op jit(solution)/shard_map/ppermute | solution.py:26
  111.4 26.6 %collective-permute-start.24 = (bf16[192,1024]{1,0:T(8,128)(2,1)}, bf16[192,1024]{1,0:T(8,128)(2,1)S(1)}, u32[]{:S(2)}, u32[]{:S(2)}) collective-permute-start(bf16[192,1024]{1,0:T(8,128)(2,1)} %get-tuple-element.40.mix0.mixed), channel_id=1, source_target_pairs={{0,2},{1,3},{2,0},{3,1},{4,6},{5,7},{6,4},{7,5},{8,10},{9,11},{10,... | collective-permute-start | bytes 1179656 | tf_op jit(solution)/shard_map/ppermute | solution.py:22
  112.0 23.2 %collective-permute-start.32 = (bf16[96,1536]{1,0:T(8,128)(2,1)S(1)}, bf16[96,1536]{1,0:T(8,128)(2,1)S(1)}, u32[]{:S(2)}, u32[]{:S(2)}) collective-permute-start(bf16[96,1536]{1,0:T(8,128)(2,1)S(1)} %pad_maximum_fusion.6.refs_0_), channel_id=1, source_target_pairs={{0,16},{4,20},{8,24},{12,28},{16,0},{20,4},{24,8},{28,12},{1,17},{... | collective-permute-start | bytes 884744 | tf_op jit(solution)/shard_map/ppermute | solution.py:26
  114.2 21.6 %collective-permute-start.34 = (bf16[96,1536]{1,0:T(8,128)(2,1)S(1)}, bf16[96,1536]{1,0:T(8,128)(2,1)}, u32[]{:S(2)}, u32[]{:S(2)}) collective-permute-start(bf16[96,1536]{1,0:T(8,128)(2,1)S(1)} %pad_maximum_fusion.6.refs_0_), channel_id=1, source_target_pairs={{0,24},{4,28},{8,16},{12,20},{16,8},{20,12},{24,0},{28,4},{1,25},{... | collective-permute-start | bytes 884744 | tf_op jit(solution)/shard_map/ppermute | solution.py:26
  115.8 21.5 %collective-permute-start.29 = (bf16[96,1536]{1,0:T(8,128)(2,1)S(1)}, bf16[96,1536]{1,0:T(8,128)(2,1)S(1)}, u32[]{:S(2)}, u32[]{:S(2)}) collective-permute-start(bf16[96,1536]{1,0:T(8,128)(2,1)S(1)} %pad_maximum_fusion.6.refs_0_), channel_id=1, source_target_pairs={{0,4},{4,0},{8,12},{12,8},{16,20},{20,16},{24,28},{28,24},{1,5},{5... | collective-permute-start | bytes 884744 | tf_op jit(solution)/shard_map/ppermute | solution.py:26
  118.0 20.0 %collective-permute-start.27 = (bf16[192,768]{1,0:T(8,128)(2,1)}, bf16[192,768]{1,0:T(8,128)(2,1)}, u32[]{:S(2)}, u32[]{:S(2)}) collective-permute-start(bf16[192,768]{1,0:T(8,128)(2,1)} %slice.133.out0), channel_id=1, source_target_pairs={{0,2},{1,3},{2,0},{3,1},{4,6},{5,7},{6,4},{7,5},{8,10},{9,11},{10,... | collective-permute-start | bytes 884744 | tf_op jit(solution)/shard_map/ppermute | solution.py:22
  135.7 16.1 %collective-permute-start.33 = (bf16[96,1536]{1,0:T(8,128)(2,1)S(1)}, bf16[96,1536]{1,0:T(8,128)(2,1)}, u32[]{:S(2)}, u32[]{:S(2)}) collective-permute-start(bf16[96,1536]{1,0:T(8,128)(2,1)S(1)} %collective-permute-done.32.refs_4_), channel_id=1, source_target_pairs={{0,4},{4,0},{8,12},{12,8},{16,20},{20,16},{24,28},{28,24},{1,5},{5... | collective-permute-start | bytes 884744 | tf_op jit(solution)/shard_map/ppermute | solution.py:26
  137.3 18.0 %collective-permute-start.35 = (bf16[96,1536]{1,0:T(8,128)(2,1)}, bf16[96,1536]{1,0:T(8,128)(2,1)S(1)}, u32[]{:S(2)}, u32[]{:S(2)}) collective-permute-start(bf16[96,1536]{1,0:T(8,128)(2,1)} %collective-permute-done.34.refs_6_), channel_id=1, source_target_pairs={{0,4},{4,0},{8,12},{12,8},{16,20},{20,16},{24,28},{28,24},{1,5},{5... | collective-permute-start | bytes 884744 | tf_op jit(solution)/shard_map/ppermute | solution.py:26
  138.0 23.3 %collective-permute-start.23 = (bf16[192,1024]{1,0:T(8,128)(2,1)}, bf16[192,1024]{1,0:T(8,128)(2,1)S(1)}, u32[]{:S(2)}, u32[]{:S(2)}) collective-permute-start(bf16[192,1024]{1,0:T(8,128)(2,1)} %get-tuple-element.40.mix0.mixed), channel_id=1, source_target_pairs={{0,1},{1,0},{2,3},{3,2},{4,5},{5,4},{6,7},{7,6},{8,9},{9,8},{10,11... | collective-permute-start | bytes 1179656 | tf_op jit(solution)/shard_map/ppermute | solution.py:22
  138.0 23.3 %collective-permute-start.25 = (bf16[192,1024]{1,0:T(8,128)(2,1)S(1)}, bf16[192,1024]{1,0:T(8,128)(2,1)S(1)}, u32[]{:S(2)}, u32[]{:S(2)}) collective-permute-start(bf16[192,1024]{1,0:T(8,128)(2,1)S(1)} %collective-permute-done.24.mix2), channel_id=1, source_target_pairs={{0,1},{1,0},{2,3},{3,2},{4,5},{5,4},{6,7},{7,6},{8,9},{9,8},{10,11... | collective-permute-start | bytes 1179656 | tf_op jit(solution)/shard_map/ppermute | solution.py:22
  145.5 15.8 %collective-permute-start.26 = (bf16[192,768]{1,0:T(8,128)(2,1)}, bf16[192,768]{1,0:T(8,128)(2,1)}, u32[]{:S(2)}, u32[]{:S(2)}) collective-permute-start(bf16[192,768]{1,0:T(8,128)(2,1)} %slice.133.out0), channel_id=1, source_target_pairs={{0,1},{1,0},{2,3},{3,2},{4,5},{5,4},{6,7},{7,6},{8,9},{9,8},{10,11... | collective-permute-start | bytes 884744 | tf_op jit(solution)/shard_map/ppermute | solution.py:22
  187.5 11.2 %collective-permute-start.38 = (bf16[192,1024]{1,0:T(8,128)(2,1)S(1)}, bf16[192,1024]{1,0:T(8,128)(2,1)S(1)}, u32[]{:S(2)}, u32[]{:S(2)}) collective-permute-start(bf16[192,1024]{1,0:T(8,128)(2,1)S(1)} %add_convert_fusion.1), channel_id=1, source_target_pairs={{0,2},{1,3},{2,0},{3,1},{4,6},{5,7},{6,4},{7,5},{8,10},{9,11},{10,... | collective-permute-start | bytes 1179656 | tf_op jit(solution)/shard_map/ppermute | solution.py:22
  190.5 56.5 %collective-permute-start.70 = (bf16[4,96,1536]{2,1,0:T(8,128)(2,1)}, bf16[4,96,1536]{2,1,0:T(8,128)(2,1)}, u32[]{:S(2)}, u32[]{:S(2)}) collective-permute-start(bf16[4,96,1536]{2,1,0:T(8,128)(2,1)} %dynamic-slice_bitcast_fusion), channel_id=1, source_target_pairs={{0,4},{4,0},{8,12},{12,8},{16,20},{20,16},{24,28},{28,24},{1,5},{5... | collective-permute-start | bytes 3538952 | tf_op jit(solution)/shard_map/ppermute | solution.py:26
  219.2 40.8 %collective-permute-start.55 = (bf16[192,768]{1,0:T(8,128)(2,1)}, bf16[192,768]{1,0:T(8,128)(2,1)}, u32[]{:S(2)}, u32[]{:S(2)}) collective-permute-start(bf16[192,768]{1,0:T(8,128)(2,1)} %convolution_convert_fusion.5), channel_id=1, source_target_pairs={{0,1},{1,0},{2,3},{3,2},{4,5},{5,4},{6,7},{7,6},{8,9},{9,8},{10,11... | collective-permute-start | bytes 884744 | tf_op jit(solution)/shard_map/ppermute | solution.py:22
  221.8 14.7 %collective-permute-start.56 = (bf16[192,768]{1,0:T(8,128)(2,1)S(1)}, bf16[192,768]{1,0:T(8,128)(2,1)S(1)}, u32[]{:S(2)}, u32[]{:S(2)}) collective-permute-start(bf16[192,768]{1,0:T(8,128)(2,1)S(1)} %convolution_convert_fusion.3), channel_id=1, source_target_pairs={{0,1},{1,0},{2,3},{3,2},{4,5},{5,4},{6,7},{7,6},{8,9},{9,8},{10,11... | collective-permute-start | bytes 884744 | tf_op jit(solution)/shard_map/ppermute | solution.py:22
  224.1 11.9 %collective-permute-start.43 = (bf16[96,1024]{1,0:T(8,128)(2,1)S(1)}, bf16[96,1024]{1,0:T(8,128)(2,1)S(1)}, u32[]{:S(2)}, u32[]{:S(2)}) collective-permute-start(bf16[96,1024]{1,0:T(8,128)(2,1)S(1)} %get-tuple-element.145), channel_id=1, source_target_pairs={{0,1},{1,0},{2,3},{3,2},{4,5},{5,4},{6,7},{7,6},{8,9},{9,8},{10,11... | collective-permute-start | bytes 589832 | tf_op jit(solution)/shard_map/ppermute | solution.py:22
  236.0 19.2 %collective-permute-start.40 = (bf16[256,768]{1,0:T(8,128)(2,1)}, bf16[256,768]{1,0:T(8,128)(2,1)}, u32[]{:S(2)}, u32[]{:S(2)}) collective-permute-start(bf16[256,768]{1,0:T(8,128)(2,1)} %get-tuple-element.130), channel_id=1, source_target_pairs={{0,1},{1,0},{2,3},{3,2},{4,5},{5,4},{6,7},{7,6},{8,9},{9,8},{10,11... | collective-permute-start | bytes 1179656 | tf_op jit(solution)/shard_map/ppermute | solution.py:22
  239.3 62.0 %collective-permute-start.39 = (bf16[256,768]{1,0:T(8,128)(2,1)}, bf16[256,768]{1,0:T(8,128)(2,1)}, u32[]{:S(2)}, u32[]{:S(2)}) collective-permute-start(bf16[256,768]{1,0:T(8,128)(2,1)} %get-tuple-element.129), channel_id=1, source_target_pairs={{0,1},{1,0},{2,3},{3,2},{4,5},{5,4},{6,7},{7,6},{8,9},{9,8},{10,11... | collective-permute-start | bytes 1179656 | tf_op jit(solution)/shard_map/ppermute | solution.py:22
  243.4 16.7 %collective-permute-start.57 = (bf16[192,768]{1,0:T(8,128)(2,1)}, bf16[192,768]{1,0:T(8,128)(2,1)}, u32[]{:S(2)}, u32[]{:S(2)}) collective-permute-start(bf16[192,768]{1,0:T(8,128)(2,1)} %fusion.7), channel_id=1, source_target_pairs={{0,2},{1,3},{2,0},{3,1},{4,6},{5,7},{6,4},{7,5},{8,10},{9,11},{10,... | collective-permute-start | bytes 884744 | tf_op jit(solution)/shard_map/ppermute | solution.py:22
  247.0 10.6 %collective-permute-start.59 = (bf16[96,768]{1,0:T(8,128)(2,1)}, bf16[96,768]{1,0:T(8,128)(2,1)}, u32[]{:S(2)}, u32[]{:S(2)}) collective-permute-start(bf16[96,768]{1,0:T(8,128)(2,1)} %convolution_convert_fusion.7), channel_id=1, source_target_pairs={{0,1},{1,0},{2,3},{3,2},{4,5},{5,4},{6,7},{7,6},{8,9},{9,8},{10,11... | collective-permute-start | bytes 442376 | tf_op jit(solution)/shard_map/ppermute | solution.py:22
  257.6 55.3 %collective-permute-start.52 = (bf16[112,1024]{1,0:T(8,128)(2,1)}, bf16[112,1024]{1,0:T(8,128)(2,1)}, u32[]{:S(2)}, u32[]{:S(2)}) collective-permute-start(bf16[112,1024]{1,0:T(8,128)(2,1)} %concatenate.41.refs_1_), channel_id=1, source_target_pairs={{0,8},{4,12},{8,0},{12,4},{16,24},{20,28},{24,16},{28,20},{1,9},{5... | collective-permute-start | bytes 688136 | tf_op jit(solution)/shard_map/ppermute | solution.py:26
  260.1 10.9 %collective-permute-start.60 = (bf16[96,768]{1,0:T(8,128)(2,1)}, bf16[96,768]{1,0:T(8,128)(2,1)}, u32[]{:S(2)}, u32[]{:S(2)}) collective-permute-start(bf16[96,768]{1,0:T(8,128)(2,1)} %fusion.12), channel_id=1, source_target_pairs={{0,2},{1,3},{2,0},{3,1},{4,6},{5,7},{6,4},{7,5},{8,10},{9,11},{10,... | collective-permute-start | bytes 442376 | tf_op jit(solution)/shard_map/ppermute | solution.py:22
  263.4 12.4 %collective-permute-start.71 = (bf16[96,1536]{1,0:T(8,128)(2,1)}, bf16[96,1536]{1,0:T(8,128)(2,1)}, u32[]{:S(2)}, u32[]{:S(2)}) collective-permute-start(bf16[96,1536]{1,0:T(8,128)(2,1)} %get-tuple-element.141), channel_id=1, source_target_pairs={{0,8},{4,12},{8,0},{12,4},{16,24},{20,28},{24,16},{28,20},{1,9},{5... | collective-permute-start | bytes 884744 | tf_op jit(solution)/shard_map/ppermute | solution.py:26
  269.4 28.3 %collective-permute-start.72 = (bf16[96,1536]{1,0:T(8,128)(2,1)}, bf16[96,1536]{1,0:T(8,128)(2,1)}, u32[]{:S(2)}, u32[]{:S(2)}) collective-permute-start(bf16[96,1536]{1,0:T(8,128)(2,1)} %get-tuple-element.143), channel_id=1, source_target_pairs={{0,16},{4,20},{8,24},{12,28},{16,0},{20,4},{24,8},{28,12},{1,17},{... | collective-permute-start | bytes 884744 | tf_op jit(solution)/shard_map/ppermute | solution.py:26
  271.0 26.6 %collective-permute-start.73 = (bf16[96,1536]{1,0:T(8,128)(2,1)}, bf16[96,1536]{1,0:T(8,128)(2,1)}, u32[]{:S(2)}, u32[]{:S(2)}) collective-permute-start(bf16[96,1536]{1,0:T(8,128)(2,1)} %get-tuple-element.142), channel_id=1, source_target_pairs={{0,24},{4,28},{8,16},{12,20},{16,8},{20,12},{24,0},{28,4},{1,25},{... | collective-permute-start | bytes 884744 | tf_op jit(solution)/shard_map/ppermute | solution.py:26
  275.8 38.0 %collective-permute-start.50 = (bf16[112,1024]{1,0:T(8,128)(2,1)}, bf16[112,1024]{1,0:T(8,128)(2,1)}, u32[]{:S(2)}, u32[]{:S(2)}) collective-permute-start(bf16[112,1024]{1,0:T(8,128)(2,1)} %concatenate.41.refs_1_), channel_id=1, source_target_pairs={{0,16},{4,20},{8,24},{12,28},{16,0},{20,4},{24,8},{28,12},{1,17},{... | collective-permute-start | bytes 688136 | tf_op jit(solution)/shard_map/ppermute | solution.py:26
  297.6 18.2 %collective-permute-start.46 = (bf16[256,768]{1,0:T(8,128)(2,1)}, bf16[256,768]{1,0:T(8,128)(2,1)S(1)}, u32[]{:S(2)}, u32[]{:S(2)}) collective-permute-start(bf16[256,768]{1,0:T(8,128)(2,1)} %get-tuple-element.128), channel_id=1, source_target_pairs={{0,1},{1,0},{2,3},{3,2},{4,5},{5,4},{6,7},{7,6},{8,9},{9,8},{10,11... | collective-permute-start | bytes 1179656 | tf_op jit(solution)/shard_map/ppermute | solution.py:22
  297.6 11.7 %collective-permute-start.41 = (bf16[256,768]{1,0:T(8,128)(2,1)}, bf16[256,768]{1,0:T(8,128)(2,1)S(1)}, u32[]{:S(2)}, u32[]{:S(2)}) collective-permute-start(bf16[256,768]{1,0:T(8,128)(2,1)} %fusion.21), channel_id=1, source_target_pairs={{0,2},{1,3},{2,0},{3,1},{4,6},{5,7},{6,4},{7,5},{8,10},{9,11},{10,... | collective-permute-start | bytes 1179656 | tf_op jit(solution)/shard_map/ppermute | solution.py:22
  301.3 14.0 %collective-permute-start.48 = (bf16[112,1024]{1,0:T(8,128)(2,1)}, bf16[112,1024]{1,0:T(8,128)(2,1)}, u32[]{:S(2)}, u32[]{:S(2)}) collective-permute-start(bf16[112,1024]{1,0:T(8,128)(2,1)} %concatenate.41.refs_1_), channel_id=1, source_target_pairs={{0,24},{4,28},{8,16},{12,20},{16,8},{20,12},{24,0},{28,4},{1,25},{... | collective-permute-start | bytes 688136 | tf_op jit(solution)/shard_map/ppermute | solution.py:26
  309.4 41.6 %collective-permute-start.61 = (bf16[4,96,864]{2,1,0:T(8,128)(2,1)}, bf16[4,96,864]{2,1,0:T(8,128)(2,1)}, u32[]{:S(2)}, u32[]{:S(2)}) collective-permute-start(bf16[4,96,864]{2,1,0:T(8,128)(2,1)} %dynamic-slice_bitcast_fusion.1), channel_id=1, source_target_pairs={{0,4},{4,0},{8,12},{12,8},{16,20},{20,16},{24,28},{28,24},{1,5},{5... | collective-permute-start | bytes 1990664 | tf_op jit(solution)/shard_map/ppermute | solution.py:26
  312.9 47.0 %collective-permute-start.45 = (bf16[256,768]{1,0:T(8,128)(2,1)S(1)}, bf16[256,768]{1,0:T(8,128)(2,1)}, u32[]{:S(2)}, u32[]{:S(2)}) collective-permute-start(bf16[256,768]{1,0:T(8,128)(2,1)S(1)} %copy-done.46), channel_id=1, source_target_pairs={{0,1},{1,0},{2,3},{3,2},{4,5},{5,4},{6,7},{7,6},{8,9},{9,8},{10,11... | collective-permute-start | bytes 1179656 | tf_op jit(solution)/shard_map/ppermute | solution.py:22
  313.8 19.1 %collective-permute-start.53 = (bf16[112,1024]{1,0:T(8,128)(2,1)}, bf16[112,1024]{1,0:T(8,128)(2,1)}, u32[]{:S(2)}, u32[]{:S(2)}) collective-permute-start(bf16[112,1024]{1,0:T(8,128)(2,1)} %collective-permute-done.52.refs_1_), channel_id=1, source_target_pairs={{0,4},{4,0},{8,12},{12,8},{16,20},{20,16},{24,28},{28,24},{1,5},{5... | collective-permute-start | bytes 688136 | tf_op jit(solution)/shard_map/ppermute | solution.py:26
  315.3 24.0 %collective-permute-start.51 = (bf16[112,1024]{1,0:T(8,128)(2,1)}, bf16[112,1024]{1,0:T(8,128)(2,1)}, u32[]{:S(2)}, u32[]{:S(2)}) collective-permute-start(bf16[112,1024]{1,0:T(8,128)(2,1)} %collective-permute-done.50.refs_1_), channel_id=1, source_target_pairs={{0,4},{4,0},{8,12},{12,8},{16,20},{20,16},{24,28},{28,24},{1,5},{5... | collective-permute-start | bytes 688136 | tf_op jit(solution)/shard_map/ppermute | solution.py:26
  315.8 28.5 %collective-permute-start.49 = (bf16[112,1024]{1,0:T(8,128)(2,1)}, bf16[112,1024]{1,0:T(8,128)(2,1)}, u32[]{:S(2)}, u32[]{:S(2)}) collective-permute-start(bf16[112,1024]{1,0:T(8,128)(2,1)} %collective-permute-done.48.refs_1_), channel_id=1, source_target_pairs={{0,4},{4,0},{8,12},{12,8},{16,20},{20,16},{24,28},{28,24},{1,5},{5... | collective-permute-start | bytes 688136 | tf_op jit(solution)/shard_map/ppermute | solution.py:26
  332.9 27.0 %collective-permute-start.47 = (bf16[256,768]{1,0:T(8,128)(2,1)}, bf16[256,768]{1,0:T(8,128)(2,1)}, u32[]{:S(2)}, u32[]{:S(2)}) collective-permute-start(bf16[256,768]{1,0:T(8,128)(2,1)} %fusion.18), channel_id=1, source_target_pairs={{0,2},{1,3},{2,0},{3,1},{4,6},{5,7},{6,4},{7,5},{8,10},{9,11},{10,... | collective-permute-start | bytes 1179656 | tf_op jit(solution)/shard_map/ppermute | solution.py:22
  (102 other events, 1366.3 us)

commit v2 on v1

v2 whole, which is shorter than its diff:
```python
import functools

import jax
import jax.numpy as jnp
from jax import lax
from jax.experimental import pallas as pl
from jax.experimental.pallas import tpu as pltpu
from jax.sharding import PartitionSpec as P

HD = 64
SEG = 128
TILE = 2 * SEG
EPS = 1e-05
MASKED = -1e30
ROPE_BASE = 10000.0
F32 = jnp.float32
BF16 = jnp.bfloat16
VMEM = pltpu.VMEM


def xor_tensor(value, step):
    return lax.ppermute(value, "tensor", [(i, i ^ step) for i in range(4)])


def xor_dp(value, step, count):
    return lax.ppermute(value, "dp", [(i, i ^ step) for i in range(count)])


def after(value, *others):
    return lax.optimization_barrier((value,) + others)[0]


def gather_tensor(value):
    far = xor_tensor(value, 2)
    near = xor_tensor(value, 1)
    return [value, near, far, xor_tensor(far, 1)]


def add_round(one, two):
    return (one.astype(F32) + two.astype(F32)).astype(BF16)


def scatter_tensor(stay, leave):
    come = xor_tensor(leave, 1)
    far = xor_tensor(add_round(stay[1], come[1]), 2)
    return stay[0], come[0], far


def total(terms):
    return terms[0].astype(F32) + terms[1].astype(F32) + terms[2].astype(F32)


def double_dp(value):
    zero = jnp.stack([value, xor_dp(value, 4, 8)])
    two = xor_dp(zero, 2, 8)
    return zero, two, xor_dp(zero, 1, 8), xor_dp(two, 1, 8)


DOUBLED = (0, 4, 2, 6, 1, 5, 3, 7)
HALVED = (0, 2, 1, 3)


def halve_first(keep, come):
    return add_round(keep[:2], come[:2]), add_round(keep[2:], come[2:])


def halve_second(stay, come):
    return add_round(stay[0], come[0]), add_round(stay[1], come[1])


def sum_dp(halves, count):
    if count != 8:
        return lax.psum_scatter(halves[0].astype(F32), "dp", scatter_dimension=0, tiled=True)[0]
    away, keep = halves
    stay, leave = halve_first(keep, xor_dp(away, 1, count))
    ours, leave = halve_second(stay, xor_dp(leave, 2, count))
    return ours.astype(F32) + xor_dp(leave, 4, count).astype(F32)


def entries(refs):
    out = []
    for ref in refs:
        out += [ref] if len(ref.shape) == 2 else [ref.at[i] for i in range(ref.shape[0])]
    return out


def place_rows(info, refs, lane, whole_ref):
    for piece, xor in zip(entries(refs), DOUBLED):
        rows = piece.shape[0]
        at = pl.ds(pl.multiple_of((info[1] ^ xor) * rows, 16), rows)
        whole_ref[at, :] = piece[:, lane : lane + whole_ref.shape[1]]


def assemble_kernel(turn, info, *refs):
    pieces, out = refs[:4], refs[4]
    whole_ref = refs[-1] if turn else out
    place_rows(info, pieces, 0, whole_ref)
    if turn:
        out[...] = whole_ref[...].T


def assemble(info, arrays, turn):
    rows, cols = arrays[0].shape[1:]
    shape = (cols, 8 * rows) if turn else (8 * rows, cols)
    return pl.pallas_call(
        functools.partial(assemble_kernel, turn),
        out_shape=jax.ShapeDtypeStruct(shape, BF16),
        in_specs=[pl.BlockSpec(memory_space=pltpu.SMEM)] + [pl.BlockSpec(memory_space=VMEM)] * 4,
        out_specs=pl.BlockSpec(memory_space=VMEM),
        scratch_shapes=[VMEM((8 * rows, cols), BF16)] if turn else [],
        name="assemble",
    )(info, *arrays)


def whole(shape):
    return pl.BlockSpec(shape, lambda *_: (0,) * len(shape))


def nn(a, b):
    return lax.dot_general(a, b, (((1,), (0,)), ((), ())), preferred_element_type=F32)


def nt(a, b):
    return lax.dot_general(a, b, (((1,), (1,)), ((), ())), preferred_element_type=F32)


def tn(a, b):
    return lax.dot_general(a, b, (((0,), (0,)), ((), ())), preferred_element_type=F32)


def pack_first_kernel(two, three, up_two, up_three, out):
    ng, rows = two.shape
    out[:ng, :rows] = two[...].astype(BF16)
    out[ng:, :rows] = three[...].astype(BF16)
    out[:, rows:] = jnp.zeros((2 * ng, SEG), BF16)
    if up_two.shape[1] == 2 * ng:
        small = jnp.concatenate([up_two[...], up_three[...]], axis=0)
        out[:, rows : rows + 2 * ng] = small.T.astype(BF16)


def pack_first(two, three, up_two, up_three):
    ng, rows = two.shape
    return pl.pallas_call(
        pack_first_kernel,
        out_shape=jax.ShapeDtypeStruct((2 * ng, rows + SEG), BF16),
        name="pack_first",
    )(two, three, up_two, up_three)


def pack_kernel(query, key, value, output, gate, up, down, attn, ffn):
    width, units = query.shape[1], gate.shape[1]
    for i, ref in enumerate((query, key, value)):
        attn[:, i * width : (i + 1) * width] = ref[...].astype(BF16)
    attn[:, 3 * width :] = output[...].T.astype(BF16)
    for i, ref in enumerate((gate, up, down)):
        ffn[:, i * units : (i + 1) * units] = ref[...].astype(BF16)


def pack(query, key, value, output, gate, up, down):
    rows, width = query.shape
    return pl.pallas_call(
        pack_kernel,
        out_shape=[
            jax.ShapeDtypeStruct((rows, 4 * width), BF16),
            jax.ShapeDtypeStruct((rows, 3 * gate.shape[1]), BF16),
        ],
        name="pack",
    )(query, key, value, output, gate, up, down)


def split_rows(info, whole_ref, outs, rows):
    if len(outs) == 1:
        for i in range(outs[0].shape[0]):
            outs[0][i] = whole_ref[i * rows : (i + 1) * rows, :]
        return
    for entry, xor in enumerate(HALVED):
        for out, other in zip(outs, (1, 0)):
            at = info[1] ^ (2 * xor + other)
            out[entry] = whole_ref[pl.ds(pl.multiple_of(at * rows, 16), rows), :]


def weigh_kernel(rows, halves, info, cot, hidden, norm, grads, *refs):
    mixes, grad, feed = refs[:4], refs[4], refs[5]
    downs, gates = refs[6 : 6 + halves], refs[6 + halves : 6 + 2 * halves]
    stay, leave, turned, down_whole, gate_whole = refs[6 + 2 * halves :]
    units = hidden.shape[1]
    turned[...] = cot[...].T
    down_whole[:, units:] = nn(turned[...], hidden[...]).astype(BF16)
    turned[...] = norm[...].T
    down_whole[:, :units] = nn(turned[...], grads[:, :units]).astype(BF16)
    split_rows(info, down_whole, downs, rows)
    gate_whole[...] = nn(turned[...], grads[:, units:]).astype(BF16)
    split_rows(info, gate_whole, gates, rows)
    for xor in range(4):
        out, at = (stay, leave)[xor % 2], xor // 2
        out[at, : feed.shape[1]] = feed[2 * (xor % 2) + at]
        out[at, feed.shape[1] :] = nn(mixes[xor][...], grad[...]).astype(BF16)


def weigh(info, cot, hidden, norm, grads, mixes, grad, feed, count, own_dim):
    vm = pl.BlockSpec(memory_space=VMEM)
    dim, length = cot.shape[1], cot.shape[0]
    lead = [4, 4] if count == 8 else [count]
    units = hidden.shape[1]
    shapes = [(n, own_dim, 2 * units) for n in lead]
    shapes += [(n, own_dim, units) for n in lead]
    shapes += [(2, feed.shape[1] + mixes[0].shape[0], dim)] * 2
    got = pl.pallas_call(
        functools.partial(weigh_kernel, own_dim, len(lead)),
        out_shape=[jax.ShapeDtypeStruct(shape, BF16) for shape in shapes],
        in_specs=[pl.BlockSpec(memory_space=pltpu.SMEM)] + [vm] * 10,
        out_specs=[vm] * len(shapes),
        scratch_shapes=[
            VMEM((dim, length), BF16),
            VMEM((dim, 2 * units), BF16),
            VMEM((dim, units), BF16),
        ],
        name="weigh",
    )(info, cot, hidden, norm, grads, *mixes, grad, feed)
    return got[: len(lead)], got[len(lead) : 2 * len(lead)], got[2 * len(lead) :]


def weigh_turned_kernel(rows, info, left, right, extra, *refs):
    outs, whole_ref = refs[:-1], refs[-1]
    wide = nn(right[...], left[...]).astype(BF16)
    whole_ref[...] = jnp.concatenate([wide, extra[...]], axis=0).T
    split_rows(info, whole_ref, outs, rows)


def turn_kernel(rows, info, extra, below, *refs):
    outs, whole_ref = refs[:-1], refs[-1]
    whole_ref[...] = extra[...].T
    split_rows(info, whole_ref, [out.at[:, :rows] for out in outs], rows)
    for out in outs:
        for z in range(out.shape[0]):
            out[z, rows:] = below[...]


def split_call(body, info, operands, count, own_dim, cols, below=0):
    vm = pl.BlockSpec(memory_space=VMEM)
    lead = [4, 4] if count == 8 else [count]
    shapes = [jax.ShapeDtypeStruct((n, own_dim + below, cols), BF16) for n in lead]
    return pl.pallas_call(
        functools.partial(body, own_dim),
        out_shape=shapes,
        in_specs=[pl.BlockSpec(memory_space=pltpu.SMEM)] + [vm] * len(operands),
        out_specs=[vm] * len(shapes),
        scratch_shapes=[VMEM((count * own_dim, cols), BF16)],
        name="split",
    )(info, *operands)


def weigh_turned(info, left, right, extra, count, own_dim):
    cols = right.shape[0] + extra.shape[0]
    return split_call(weigh_turned_kernel, info, [left, right, extra], count, own_dim, cols)


def turn(info, extra, below, count, own_dim):
    return split_call(
        turn_kernel, info, [extra, below], count, own_dim, extra.shape[0], below.shape[0]
    )


def steps(length):
    return lax.broadcasted_iota(jnp.int32, (TILE, SEG), 0).astype(F32).astype(BF16)


def one_hot(places, wanted):
    near = jnp.clip(wanted, -1.0, float(TILE)).astype(BF16)
    parts = [
        jnp.where(places == near[:, c : c + SEG], BF16(1.0), BF16(0.0))
        for c in range(0, wanted.shape[1], SEG)
    ]
    return jnp.concatenate(parts, axis=1)


def lookup_kernel(owners, arrays, width, own_rows, start, end, *refs):
    info, ids = refs[0], refs[1]
    arrays, refs = refs[2 : 2 + arrays], refs[2 + arrays :]
    pieces = entries(arrays)
    count = len(owners)
    at = 0
    if end:
        ups, refs, out, whole_ref = refs[:4], refs[4:-2], refs[-2], refs[-1]
        at = out.shape[1] - ids.shape[1]
        place_rows(info, ups, own_rows, whole_ref)
        out[:, :at] = whole_ref[...].T[: 2 * width]
    else:
        out = refs[-1]
    prior = None if start else refs[0]
    places = steps(TILE)
    for half in range(2):
        lanes = slice(half * width, (half + 1) * width)
        wanted = [
            (ids[half : half + 1, :] - (info[1] ^ owner) * own_rows).astype(F32) for owner in owners
        ]

        def chunk(c, sofar):
            first = pl.multiple_of(c * TILE, TILE)
            for which in range(count):
                hot = one_hot(places, wanted[which] - first.astype(F32))
                sofar = sofar + nn(pieces[which][lanes, pl.ds(first, TILE)], hot)
            return sofar

        empty = jnp.zeros((width, ids.shape[1]), F32) if start else prior[lanes, :].astype(F32)
        out[lanes, at:] = lax.fori_loop(0, own_rows // TILE, chunk, empty).astype(BF16)


def lookup(info, pieces, owners, own_rows, ids, prior, ups=()):
    width = pieces[0].shape[-2] // 2
    vm = pl.BlockSpec(memory_space=VMEM)
    operands = [info, ids, *pieces, *ups] + ([] if prior is None else [prior])
    at = 8 * ups[0].shape[1] if ups else 0
    return pl.pallas_call(
        functools.partial(
            lookup_kernel, owners, len(pieces), width, own_rows, prior is None, bool(ups)
        ),
        out_shape=jax.ShapeDtypeStruct((2 * width, at + ids.shape[1]), BF16),
        in_specs=[pl.BlockSpec(memory_space=pltpu.SMEM)] + [vm] * (len(operands) - 1),
        out_specs=vm,
        scratch_shapes=[VMEM((at, SEG), BF16)] if ups else [],
        name="lookup",
    )(*operands)


def spread_kernel(arrays, width, start, end, *refs):
    outs = refs[-3:-1] if end else refs[-2:-1]
    turned = refs[-1]
    info, pieces = refs[0], entries(refs[1 : 1 + arrays])
    own_rows = outs[0].shape[-1] if end else outs[0].shape[1]
    length = pieces[0].shape[1]
    places = steps(TILE)
    wanted = []
    for i, piece in enumerate(pieces):
        turned[i * length : (i + 1) * length, :] = piece[: 2 * width, :].T
        digits = piece[2 * width :, :].astype(F32)
        wanted.append(
            [
                digits[d : d + 1] * 256.0 + digits[d + 1 : d + 2] - (info[1] * own_rows).astype(F32)
                for d in (0, 2)
            ]
        )

    def chunk(c, carry):
        first = pl.multiple_of(c * TILE, TILE)
        for half in range(2):
            hot = [one_hot(places, want[half] - first.astype(F32)) for want in wanted]
            hot = jnp.concatenate(hot, axis=1) if len(hot) > 1 else hot[0]
            part = nn(hot, turned[: len(pieces) * length, half * width : (half + 1) * width])
            cut = pl.ds(first, TILE)
            if not start:
                part = part + refs[1 + arrays][half, cut, :]
            if end:
                outs[half][:, cut] = part.T
            else:
                outs[0][half, cut, :] = part
        return carry

    lax.fori_loop(0, own_rows // TILE, chunk, 0)


def spread(info, pieces, own_rows, width, prior, end):
    operands = [info, *pieces] + ([] if prior is None else [prior])
    vm = pl.BlockSpec(memory_space=VMEM)
    shapes = [(width, own_rows)] * 2 if end else [(2, own_rows, width)]
    length = pieces[0].shape[-1]
    count = sum(1 if piece.ndim == 2 else piece.shape[0] for piece in pieces)
    got = pl.pallas_call(
        functools.partial(spread_kernel, len(pieces), width, prior is None, end),
        out_shape=[jax.ShapeDtypeStruct(shape, F32) for shape in shapes],
        in_specs=[pl.BlockSpec(memory_space=pltpu.SMEM)] + [vm] * (len(operands) - 1),
        out_specs=[vm] * len(shapes),
        scratch_shapes=[VMEM((count * length, 2 * width), BF16)],
        name="spread",
    )(*operands)
    return got if end else got[0]


def rope_into(out, row, values, cosine, sine, scale):
    half = HD // 2
    one, two = values[:half], values[half:]
    out[row : row + half, :] = (one * cosine - two * sine).astype(BF16) * scale
    out[row + half : row + HD, :] = (one * sine + two * cosine).astype(BF16) * scale


def key_offset(parent):
    return pl.multiple_of(jnp.where(parent > 0, parent + 1, 0) * SEG, SEG)


def pick(refs, which):
    value = refs[3][0]
    for k in range(3):
        value = jnp.where(which == k, refs[k][0], value)
    return value


def front_kernel(
    par,
    row0,
    row1,
    row2,
    row3,
    up0,
    up1,
    up2,
    up3,
    emb0,
    emb1,
    emb2,
    emb3,
    wqkv,
    gain,
    cos_ref,
    sin_ref,
    resid,
    normed,
    qkv,
    mixed,
    lse,
    keys,
    vals,
):
    tile = pl.program_id(0)
    rows = jnp.concatenate([row0[...], row1[...], row2[...], row3[...]], axis=0)
    ups = jnp.concatenate([up0[...], up1[...], up2[...], up3[...]], axis=0)
    own = pick((emb0, emb1, emb2, emb3), tile ^ par[0])
    hidden = own.astype(F32) + tn(rows, ups)
    resid[...] = hidden
    rate = lax.rsqrt(jnp.mean(hidden * hidden, axis=-1, keepdims=True) + EPS)
    norm = (hidden * rate * gain[...]).astype(BF16)
    normed[...] = norm
    proj = nt(wqkv[...], norm)
    cosine, sine = cos_ref[...], sin_ref[...]
    width = keys.shape[0]
    heads = width // HD
    for h in range(heads):
        rope_into(qkv, h * HD, proj[h * HD : (h + 1) * HD], cosine, sine, BF16(HD**-0.5))
        low = width + h * HD
        rope_into(qkv, low, proj[low : low + HD], cosine, sine, BF16(1.0))
    qkv[2 * width :, :] = proj[2 * width :].astype(BF16)
    place = pl.ds(pl.multiple_of(tile * TILE, TILE), TILE)
    keys[:, place] = qkv[width : 2 * width, :]
    vals[:, place] = qkv[2 * width :, :]

    def finish(h, lanes, scores, value):
        top = jnp.max(scores, axis=0, keepdims=True)
        weights = jnp.exp(scores - top)
        total = jnp.sum(weights, axis=0, keepdims=True)
        got = nn(value, weights.astype(BF16))
        mixed[h * HD : (h + 1) * HD, lanes] = (got * (1.0 / total)).astype(BF16)
        lse[h : h + 1, lanes] = top + jnp.log(total)

    @pl.when(tile == 0)
    def _():
        key_at = lax.broadcasted_iota(jnp.int32, (TILE, TILE), 0)
        query_at = lax.broadcasted_iota(jnp.int32, (TILE, TILE), 1)
        for h in range(heads):
            hs = slice(h * HD, (h + 1) * HD)
            scores = tn(keys[hs, 0:TILE], qkv[hs, :])
            scores = jnp.where(key_at <= query_at, scores, MASKED)
            finish(h, slice(0, TILE), scores, vals[hs, 0:TILE])

    @pl.when(tile > 0)
    def _():
        key_at = lax.broadcasted_iota(jnp.int32, (4 * SEG, SEG), 0)
        query_at = lax.broadcasted_iota(jnp.int32, (4 * SEG, SEG), 1)
        for half in range(2):
            parent = par[2 + 2 * tile + half]
            mine = pl.ds(pl.multiple_of(tile * TILE + half * SEG, SEG), SEG)
            theirs = pl.ds(key_offset(parent), SEG)
            limit = jnp.where(parent > 0, 4 * SEG, 3 * SEG)
            seen = (key_at < TILE) | ((key_at - TILE <= query_at) & (key_at < 3 * SEG))
            seen = seen | ((key_at >= 3 * SEG) & (key_at < limit))
            lanes = slice(half * SEG, (half + 1) * SEG)
            for h in range(heads):
                hs = slice(h * HD, (h + 1) * HD)
                key = jnp.concatenate([keys[hs, 0:TILE], keys[hs, mine], keys[hs, theirs]], axis=1)
                value = jnp.concatenate(
                    [vals[hs, 0:TILE], vals[hs, mine], vals[hs, theirs]], axis=1
                )
                scores = jnp.where(seen, tn(key, qkv[hs, lanes]), MASKED)
                finish(h, lanes, scores, value)


def front(par, sets, tokens, wqkvo, gain, cosine, sine):
    dim = tokens[0].shape[2]
    length = sets[0].shape[1] - dim
    width = wqkvo.shape[0] // 4
    ng = sets[0].shape[0]
    tall = lambda r, _: (r, 0)
    wide = lambda r, _: (0, r)
    return pl.pallas_call(
        front_kernel,
        grid_spec=pltpu.PrefetchScalarGridSpec(
            num_scalar_prefetch=1,
            grid=(length // TILE,),
            in_specs=[pl.BlockSpec((ng, TILE), lambda r, _: (0, r + dim // TILE))] * 4
            + [whole((ng, dim))] * 4
            + [whole((1, TILE, dim))] * 4
            + [
                whole((3 * width, dim)),
                whole((1, dim)),
                pl.BlockSpec((HD // 2, TILE), wide),
                pl.BlockSpec((HD // 2, TILE), wide),
            ],
            out_specs=[
                pl.BlockSpec((TILE, dim), tall),
                pl.BlockSpec((TILE, dim), tall),
                pl.BlockSpec((3 * width, TILE), wide),
                pl.BlockSpec((width, TILE), wide),
                pl.BlockSpec((8, TILE), wide),
            ],
            scratch_shapes=[VMEM((width, length), BF16), VMEM((width, length), BF16)],
        ),
        out_shape=[
            jax.ShapeDtypeStruct((length, dim), F32),
            jax.ShapeDtypeStruct((length, dim), BF16),
            jax.ShapeDtypeStruct((3 * width, length), BF16),
            jax.ShapeDtypeStruct((width, length), BF16),
            jax.ShapeDtypeStruct((8, length), F32),
        ],
        name="front",
    )(par, *sets, *sets, *tokens, wqkvo, gain, cosine, sine)


def middle_kernel(
    who,
    mix0,
    mix1,
    mix2,
    mix3,
    out0,
    out1,
    out2,
    out3,
    resid,
    gain,
    ffn,
    cot0,
    cot1,
    cot2,
    cot3,
    feed,
    resid_own,
    normed,
    hidden,
    grads,
    grad_res,
    mix_stay,
    mix_leave,
    grad_gain,
    cot_all,
):
    tile = pl.program_id(0)
    units = hidden.shape[1]
    outs = jnp.concatenate([out0[...], out1[...], out2[...], out3[...]], axis=0)
    mix = jnp.concatenate([mix0[...], mix1[...], mix2[...], mix3[...]], axis=0)
    res = resid[...] + tn(mix, outs)

    @pl.when(tile == who[0])
    def _():
        resid_own[...] = res

    rate = lax.rsqrt(jnp.mean(res * res, axis=-1, keepdims=True) + EPS)
    norm = (res * rate * gain[...]).astype(BF16)
    normed[...] = norm
    gate = nn(norm, ffn[:, :units])
    upward = nn(norm, ffn[:, units : 2 * units])
    sig = 1.0 / (1.0 + jnp.exp(-gate))
    silu = gate * sig
    hid = (silu * upward).astype(BF16)
    hidden[...] = hid
    feed[0] = nt(hid, ffn[:, 2 * units :]).astype(BF16)
    cot = pick((cot0, cot1, cot2, cot3), tile ^ who[0])
    cot_all[...] = cot
    back = nn(cot, ffn[:, 2 * units :])
    grad_gate = (back * upward * sig * (1.0 + gate * (1.0 - sig))).astype(BF16)
    grad_up = (back * silu).astype(BF16)
    grads[:, :units] = grad_gate
    grads[:, units:] = grad_up
    pulled = nt(grad_gate, ffn[:, :units]) + nt(grad_up, ffn[:, units : 2 * units])
    scaled = pulled * gain[...]
    dots = jnp.mean(scaled * res, axis=-1, keepdims=True)
    part = rate * scaled - res * (rate * rate * rate * dots) + 0.25 * cot.astype(F32)
    part = part.astype(BF16)
    grad_res[...] = part
    by_head = nt(outs, part).astype(BF16)
    width = out0.shape[0]
    for k in range(4):
        out = (mix_stay, mix_leave)[k % 2]
        out[k // 2] = by_head[k * width : (k + 1) * width]
    gained = jnp.sum(pulled * res * rate, axis=0, keepdims=True)

    @pl.when(tile == 0)
    def _():
        grad_gain[...] = gained

    @pl.when(tile > 0)
    def _():
        grad_gain[...] += gained


def slot_of(xor):
    return (xor & 1) * 2 + (xor >> 1)


def middle(who, mixes, outs, resid, gain, ffn, tokens):
    length, dim = resid.shape
    width = mixes[0].shape[0]
    units = ffn.shape[1] // 3
    tiles = length // TILE
    tall = lambda r, _: (r, 0)
    wide = lambda r, _: (0, r)
    return pl.pallas_call(
        middle_kernel,
        grid_spec=pltpu.PrefetchScalarGridSpec(
            num_scalar_prefetch=1,
            grid=(tiles,),
            in_specs=[pl.BlockSpec((width, TILE), wide)] * 4
            + [whole((width, dim))] * 4
            + [
                pl.BlockSpec((TILE, dim), tall),
                whole((1, dim)),
                whole((dim, 3 * units)),
            ]
            + [pl.BlockSpec((1, TILE, dim), lambda *_: (1, 0, 0))] * 4,
            out_specs=[
                pl.BlockSpec((1, TILE, dim), lambda r, who: (slot_of(r ^ who[0]), 0, 0)),
                whole((TILE, dim)),
                pl.BlockSpec((TILE, dim), tall),
                pl.BlockSpec((TILE, units), tall),
                pl.BlockSpec((TILE, 2 * units), tall),
                pl.BlockSpec((TILE, dim), tall),
                pl.BlockSpec((2, width, TILE), lambda r, _: (0, 0, r)),
                pl.BlockSpec((2, width, TILE), lambda r, _: (0, 0, r)),
                whole((1, dim)),
                pl.BlockSpec((TILE, dim), tall),
            ],
        ),
        out_shape=[
            jax.ShapeDtypeStruct((tiles, TILE, dim), BF16),
            jax.ShapeDtypeStruct((TILE, dim), F32),
            jax.ShapeDtypeStruct((length, dim), BF16),
            jax.ShapeDtypeStruct((length, units), BF16),
            jax.ShapeDtypeStruct((length, 2 * units), BF16),
            jax.ShapeDtypeStruct((length, dim), BF16),
            jax.ShapeDtypeStruct((2, width, length), BF16),
            jax.ShapeDtypeStruct((2, width, length), BF16),
            jax.ShapeDtypeStruct((1, dim), F32),
            jax.ShapeDtypeStruct((length, dim), BF16),
        ],
        name="middle",
    )(who, *mixes, *outs, resid, gain, ffn, *tokens)


def unrope_into(out, row, values, cosine, sine):
    half = HD // 2
    one, two = values[:half], values[half:]
    out[row : row + half, :] = (one * cosine + two * sine).astype(BF16)
    out[row + half : row + HD, :] = (two * cosine - one * sine).astype(BF16)


def back_kernel(
    info,
    qkv,
    gmix,
    mixed,
    lse,
    grad_res,
    resid,
    gain,
    gain_two,
    wqkv,
    up0,
    up1,
    up2,
    up3,
    row0,
    row1,
    row2,
    row3,
    cos_ref,
    sin_ref,
    gproj,
    stay,
    leave,
    row_stay,
    row_leave,
    keys_sum,
    vals_sum,
    query_sum,
    grad_gain,
    grad_ups,
):
    step = pl.program_id(0)
    tile = pl.num_programs(0) - 1 - step
    width = gmix.shape[0]
    heads = width // HD

    @pl.when(step == 0)
    def _():
        keys_sum[...] = jnp.zeros_like(keys_sum)
        vals_sum[...] = jnp.zeros_like(vals_sum)

    base = pl.multiple_of(tile * TILE, TILE)

    def pull(h, lanes, query, key, value, seen):
        hs = slice(h * HD, (h + 1) * HD)
        grad = gmix[hs, lanes]
        delta = jnp.sum(grad.astype(F32) * mixed[hs, lanes].astype(F32), axis=0, keepdims=True)
        scores = jnp.where(seen, tn(key, query), MASKED)
        probs = jnp.exp(scores - lse[h : h + 1, lanes])
        dval = nt(grad, probs.astype(BF16))
        dscore = (probs * (tn(value, grad) - delta)).astype(BF16)
        query_sum[hs, lanes] = nn(key, dscore) * HD**-0.5
        return nt(query, dscore), dval

    @pl.when(tile == 0)
    def _():
        key_at = lax.broadcasted_iota(jnp.int32, (TILE, TILE), 0)
        query_at = lax.broadcasted_iota(jnp.int32, (TILE, TILE), 1)
        seen = key_at <= query_at
        for h in range(heads):
            hs = slice(h * HD, (h + 1) * HD)
            key = qkv[width + h * HD : width + (h + 1) * HD, 0:TILE]
            value = qkv[2 * width + h * HD : 2 * width + (h + 1) * HD, 0:TILE]
            dkey, dval = pull(h, slice(0, TILE), qkv[hs, 0:TILE], key, value, seen)
            keys_sum[hs, 0:TILE] += dkey
            vals_sum[hs, 0:TILE] += dval

    @pl.when(tile > 0)
    def _():
        key_at = lax.broadcasted_iota(jnp.int32, (4 * SEG, SEG), 0)
        query_at = lax.broadcasted_iota(jnp.int32, (4 * SEG, SEG), 1)
        for half in range(2):
            parent = info[2 + 2 * tile + half]
            mine = pl.ds(pl.multiple_of(base + half * SEG, SEG), SEG)
            theirs = pl.ds(key_offset(parent), SEG)
            limit = jnp.where(parent > 0, 4 * SEG, 3 * SEG)
            seen = (key_at < TILE) | ((key_at - TILE <= query_at) & (key_at < 3 * SEG))
            seen = seen | ((key_at >= 3 * SEG) & (key_at < limit))
            lanes = slice(half * SEG, (half + 1) * SEG)
            for h in range(heads):
                hs = slice(h * HD, (h + 1) * HD)
                ks = slice(width + h * HD, width + (h + 1) * HD)
                vs = slice(2 * width + h * HD, 2 * width + (h + 1) * HD)
                key = jnp.concatenate([qkv[ks, 0:TILE], qkv[ks, mine], qkv[ks, theirs]], axis=1)
                value = jnp.concatenate([qkv[vs, 0:TILE], qkv[vs, mine], qkv[vs, theirs]], axis=1)
                dkey, dval = pull(h, lanes, qkv[hs, mine], key, value, seen)
                for total, part in ((keys_sum, dkey), (vals_sum, dval)):
                    total[hs, 0:TILE] += part[:, 0:TILE]
                    total[hs, mine] += part[:, TILE : 3 * SEG]
                    total[hs, theirs] += part[:, 3 * SEG :]

    cosine, sine = cos_ref[...], sin_ref[...]
    place = pl.ds(base, TILE)
    for h in range(heads):
        hs = slice(h * HD, (h + 1) * HD)
        unrope_into(gproj, h * HD, query_sum[hs, :], cosine, sine)
        unrope_into(gproj, width + h * HD, keys_sum[hs, place], cosine, sine)
    gproj[2 * width :, :] = vals_sum[:, place].astype(BF16)
    pulled = tn(gproj[...], wqkv[...])
    hidden = resid[...]
    rate = lax.rsqrt(jnp.mean(hidden * hidden, axis=-1, keepdims=True) + EPS)
    scaled = pulled * gain[...]
    dots = jnp.mean(scaled * hidden, axis=-1, keepdims=True)
    part = grad_res[...].astype(F32) + rate * scaled - hidden * (rate * rate * rate * dots)
    part = part.astype(BF16)
    slot = slot_of(tile ^ info[0])

    @pl.when(slot < 2)
    def _():
        stay[slot, :TILE, :] = part

    @pl.when(slot >= 2)
    def _():
        leave[slot - 2, :TILE, :] = part

    rows = jnp.concatenate([row0[...], row1[...], row2[...], row3[...]], axis=0)
    up_part = nn(rows, part)
    ups = jnp.concatenate([up0[...], up1[...], up2[...], up3[...]], axis=0)
    by_column = nt(ups, part).astype(BF16)
    wide = up0.shape[0]
    for k in range(4):
        (row_stay, row_leave)[k % 2][k // 2] = by_column[k * wide : (k + 1) * wide]
    gained = jnp.sum(pulled * hidden * rate, axis=0, keepdims=True)

    @pl.when(step == 0)
    def _():
        grad_gain[...] = gained
        grad_ups[...] = up_part

    @pl.when(step > 0)
    def _():
        grad_gain[...] += gained
        grad_ups[...] += up_part

    @pl.when(tile == 0)
    def _():
        dim = grad_gain.shape[1]
        gains = jnp.concatenate(
            [grad_gain[...], gain_two[...], jnp.zeros((14, dim), F32)], axis=0
        ).astype(BF16)
        for k in range(4):
            out = (stay, leave)[k % 2]
            out[k // 2, TILE : TILE + wide, :] = grad_ups[k * wide : (k + 1) * wide, :].astype(BF16)
            out[k // 2, TILE + wide :, :] = gains


def back(info, qkv, gmix, mixed, lse, grad_res, resid, gain, gain_part, wqkvo, sets, cosine, sine):
    length, dim = resid.shape
    width = gmix.shape[0]
    ng = sets[0].shape[0]
    tiles = length // TILE
    last = tiles - 1
    tall = lambda r, _: (last - r, 0)
    wide = lambda r, _: (0, last - r)
    return pl.pallas_call(
        back_kernel,
        grid_spec=pltpu.PrefetchScalarGridSpec(
            num_scalar_prefetch=1,
            grid=(tiles,),
            in_specs=[
                whole((3 * width, length)),
                pl.BlockSpec((width, TILE), wide),
                pl.BlockSpec((width, TILE), wide),
                pl.BlockSpec((8, TILE), wide),
                pl.BlockSpec((TILE, dim), tall),
                pl.BlockSpec((TILE, dim), tall),
                whole((1, dim)),
                whole((1, dim)),
                whole((3 * width, dim)),
            ]
            + [whole((ng, dim))] * 4
            + [pl.BlockSpec((ng, TILE), lambda r, _: (0, last - r + dim // TILE))] * 4
            + [
                pl.BlockSpec((HD // 2, TILE), wide),
                pl.BlockSpec((HD // 2, TILE), wide),
            ],
            out_specs=[
                pl.BlockSpec((3 * width, TILE), wide),
                whole((2, TILE + ng + 16, dim)),
                whole((2, TILE + ng + 16, dim)),
                pl.BlockSpec((2, ng, TILE), lambda r, _: (0, 0, last - r)),
                pl.BlockSpec((2, ng, TILE), lambda r, _: (0, 0, last - r)),
            ],
            scratch_shapes=[
                VMEM((width, length), F32),
                VMEM((width, length), F32),
                VMEM((width, TILE), F32),
                VMEM((1, dim), F32),
                VMEM((4 * ng, dim), F32),
            ],
        ),
        out_shape=[
            jax.ShapeDtypeStruct((3 * width, length), BF16),
            jax.ShapeDtypeStruct((2, TILE + ng + 16, dim), BF16),
            jax.ShapeDtypeStruct((2, TILE + ng + 16, dim), BF16),
            jax.ShapeDtypeStruct((2, ng, length), BF16),
            jax.ShapeDtypeStruct((2, ng, length), BF16),
        ],
        name="back",
    )(info, qkv, gmix, mixed, lse, grad_res, resid, gain, gain_part, wqkvo, *sets, *sets, cosine, sine)


def rotary(parents):
    length = parents.shape[0]
    token = jnp.arange(length, dtype=jnp.int32)
    trunk = 2 * SEG
    inside = token < trunk
    block = jnp.where(inside, 0, (token - trunk) // SEG + 1)
    offset = jnp.where(inside, token, token - trunk - (block - 1) * SEG)
    position = jnp.where(inside, 0, jnp.where(parents == 0, 2 * SEG, 3 * SEG)) + offset
    half = HD // 2
    frequency = ROPE_BASE ** (-(jnp.arange(half, dtype=F32) * 2.0 / HD))
    angles = frequency[:, None] * position.astype(F32)[None, :]
    return jnp.cos(angles), jnp.sin(angles)


def shards(
    dp,
    embedded,
    ids_two,
    ids_three,
    parents,
    table_two,
    table_three,
    w_two,
    w_three,
    norm_attn,
    w_query,
    w_key,
    w_value,
    w_output,
    norm_ffn,
    w_gate,
    w_up,
    w_down,
    cotangent,
):
    own_d = lax.axis_index("dp")
    own_t = lax.axis_index("tensor")
    own_rows, ng = table_two.shape
    rows, dim = embedded.shape
    width = w_query.shape[1]
    units = w_gate.shape[1]
    own_dim = w_query.shape[0]
    gain_one = norm_attn.reshape(1, dim)
    gain_two = norm_ffn.reshape(1, dim)

    ids = jnp.stack([ids_two, ids_three])
    info = jnp.concatenate(
        [jnp.stack([own_t, own_d]).astype(jnp.int32), parents.reshape(-1, SEG)[:, 0]]
    )
    cosine, sine = rotary(parents)

    first = pack_first(table_two.T, table_three.T, w_two, w_three)
    attn_pack, ffn_pack = pack(w_query, w_key, w_value, w_output, w_gate, w_up, w_down.T)
    token_pair = jnp.stack([embedded, cotangent])
    if dp == 8:
        zero, two, one, three = arrays = double_dp(first)
        got = lookup(info, [zero], (0, 4), own_rows, ids, None)
        got = lookup(info, [two, one], (2, 6, 1, 5), own_rows, ids, got)
        got = lookup(info, [three], (3, 7), own_rows, ids, got, arrays)
        token_pair = after(token_pair, zero)
        attn_arrays = double_dp(after(attn_pack, zero))
        wqkvo = assemble(info, attn_arrays, True)
        ffn_arrays = double_dp(after(ffn_pack, attn_arrays[0]))
        ffn_w = assemble(info, ffn_arrays, False)
    else:
        every = lax.all_gather(first[:, :own_rows], "dp", axis=0)
        small = jnp.concatenate([w_two.astype(BF16).T, w_three.astype(BF16).T], axis=1)
        ups = lax.all_gather(small, "dp", axis=0, tiled=True).T
        wqkvo = lax.all_gather(attn_pack, "dp", axis=0, tiled=True).T
        ffn_w = lax.all_gather(ffn_pack, "dp", axis=0, tiled=True)

        def take(i, so_far):
            piece = lax.dynamic_index_in_dim(every, i, 0, keepdims=False)
            at = jnp.stack([own_t, i]).astype(jnp.int32)
            return lookup(at, [piece], (0,), own_rows, ids, so_far)

        got = lax.fori_loop(0, dp, take, jnp.zeros((2 * ng, ids.shape[1]), BF16))
        got = jnp.concatenate([ups, got], axis=1)

    tokens = gather_tensor(token_pair)
    sets = gather_tensor(got)
    outs = gather_tensor(after(wqkvo[3 * width :], sets[2]))

    resid, normed, qkv, mixed, lse = front(info, sets, tokens, wqkvo, gain_one, cosine, sine)
    mixes = gather_tensor(mixed)
    feed, resid_own, normed_two, hidden, grads, grad_res, stay, leave, gain_part_two, cot_all = (
        middle(info, mixes, outs, resid, gain_two, ffn_w, tokens)
    )
    near, near_far = xor_tensor(leave, 1), None
    near_far = add_round(stay[1], near[1])
    gmix = total((stay[0], near[0], xor_tensor(near_far, 2))).astype(BF16)

    cot_all, _ = lax.optimization_barrier((cot_all, near_far))
    down_halves, up_halves, halves = weigh(
        info, cot_all, hidden, normed_two, grads, mixes, grad_res, feed, dp, own_dim
    )
    down_total, up_total = sum_dp(down_halves, dp), sum_dp(up_halves, dp)
    gmix, *halves = lax.optimization_barrier((gmix, *halves))
    feed_terms = scatter_tensor(*halves)
    output = (resid_own + total([term[:rows] for term in feed_terms])).astype(BF16)
    out_grad = total([term[rows:] for term in feed_terms]).astype(BF16)

    gproj, stay, leave, row_stay, row_leave = back(
        info, qkv, gmix, mixed, lse, grad_res, resid, gain_one, gain_part_two, wqkvo, sets,
        cosine, sine,
    )

    near = xor_tensor(row_leave, 1)
    near_far = add_round(row_stay[1], near[1])
    far = xor_tensor(near_far, 2)
    row_total = total((row_stay[0], near[0], far)).astype(BF16)
    digits = jnp.stack([ids_two // 256, ids_two % 256, ids_three // 256, ids_three % 256])
    digits = jnp.pad(digits.astype(BF16), ((0, 12), (0, 0)))
    row_pack = jnp.concatenate([row_total, digits], axis=0)
    if dp == 8:
        zero, two, one, three = double_dp(row_pack)
        table_grad = spread(info, [zero], own_rows, ng, None, False)
        table_grad = spread(info, [two, one], own_rows, ng, table_grad, False)
        table_grad = spread(info, [three], own_rows, ng, table_grad, True)
    else:
        every = lax.all_gather(row_pack, "dp", axis=0)

        def put(i, so_far):
            piece = lax.dynamic_index_in_dim(every, i, 0, keepdims=False)
            return spread(info, [piece], own_rows, ng, so_far, False)

        table_grad = lax.fori_loop(0, dp, put, jnp.zeros((2, own_rows, ng), F32))
        table_grad = table_grad[0].T, table_grad[1].T

    gproj, _ = lax.optimization_barrier((gproj, near_far))
    attn_total = sum_dp(weigh_turned(info, normed, gproj, out_grad, dp, own_dim), dp)

    stay, leave, _ = lax.optimization_barrier((stay, leave, far))
    terms = scatter_tensor(stay, leave)
    embed_grad = total([term[:rows] for term in terms]).astype(BF16)
    below = add_round(add_round(terms[0][rows:], terms[1][rows:]), terms[2][rows:])
    proj_up_grad, gains = below[: 2 * ng], below[2 * ng : 2 * ng + 2]
    if dp == 8:
        folded = gains.reshape(2 * dim // (2 * ng), 2 * ng)
        proj_up_total = sum_dp(turn(info, proj_up_grad, folded, dp, own_dim), dp)
        gains = proj_up_total[own_dim:].reshape(2, dim)
    else:
        empty = jnp.zeros((16, 2 * ng), BF16)
        halves = turn(info, proj_up_grad, empty, dp, own_dim)[0][:, :own_dim]
        proj_up_total = sum_dp([halves], dp)
        gains = lax.psum(gains.astype(F32), "dp")

    return (
        output,
        embed_grad,
        table_grad[0].T,
        table_grad[1].T,
        proj_up_total[:own_dim, :ng].T,
        proj_up_total[:own_dim, ng:].T,
        gains[0],
        attn_total[:, :width],
        attn_total[:, width : 2 * width],
        attn_total[:, 2 * width : 3 * width],
        attn_total[:, 3 * width :].T,
        gains[1],
        down_total[:, :units],
        up_total,
        down_total[:, units:].T,
    )


def solution(mesh):
    tokens = P(("dp", "tensor"), None)
    down, across = P("dp", "tensor"), P("tensor", "dp")
    in_specs = (
        (tokens, P("dp"), P("dp"), P("dp"), down, down, across, across, P())
        + (down, down, down, across, P(), down, down, across, tokens)
    )
    out_specs = (
        (tokens, tokens, down, down, across, across, P())
        + (down, down, down, across, P(), down, down, across)
    )
    body = functools.partial(shards, mesh.shape["dp"])
    return jax.shard_map(body, mesh=mesh, in_specs=in_specs, out_specs=out_specs, check_vma=False)
```

time: 372 us -> 285 us (0.77)
  waiting for transfers between devices: 132 us -> 87.7 us
  starting transfers between devices: 70.5 us -> 45.7 us
  matrix products: 17.1 us -> 0 us
  local copies, waits for them, and re-layouts: 25.7 us -> 13.7 us
  Pallas kernels: 100 us -> 111 us
    ppermute x39 -> x28, waiting for transfers between devices: 113 us -> 68.4 us  [xor_dp(): return lax.ppermute(value, 'dp', [(i, i ^ step) for i in range(count)])]
    dot_general x11 -> x0, matrix products: 17.1 us -> none  [the longest x8 10.5 us: nn(): lax.dot_general(a, b, (((1,), (0,)), ((), ())), preferred_element_type=F32)]
    ppermute x39 -> x28, starting transfers between devices: 49.8 us -> 34.3 us  [xor_dp(): return lax.ppermute(value, 'dp', [(i, i ^ step) for i in range(count)])]
    ppermute x35 -> x20, starting transfers between devices: 20.7 us -> 11.4 us  [xor_tensor(): return lax.ppermute(value, 'tensor', [(i, i ^ step) for i in range(4)])]
    pallas_call x11 -> x13, Pallas kernels: 50.7 us -> 58.8 us  [the longest x3 18.3 us: spread(): pl.pallas_call(functools.partial(spread_kernel, len(pieces), width, prior...]
    squeeze x8 -> x2, local copies, waits for them, and re-layouts: 5.3 us -> 1.33 us  [the longest x1 0.67 us: shards(): gains[0]]
    concatenate x8 -> x0, other arithmetic: 3.78 us -> none  [the longest x2 2.64 us: natural(): jnp.concatenate([lax.dynamic_index_in_dim(slots, r ^ index, 0, keepdims=F...]
    concatenate x3 -> x0, local copies, waits for them, and re-layouts: 3.77 us -> none  [the longest x1 2.81 us: shards(): row_pack = jnp.concatenate([row_total.astype(BF16), digits], axis=0)]
  transfers between devices with their start and end apart: 74 -> 48, of which waited for: 24 -> 19; matrix products, arithmetic and copies ran while one was open for 15% -> 10% of each run, Pallas kernels for 22% -> 32%
where the time goes in v2:
time: 285 us; the launch traced here: 284 us
  Pallas kernels  111 us (39%)
  waiting for transfers between devices  87.7 us (31%)
  starting transfers between devices  45.7 us (16%)
  other arithmetic  24.5 us (9%)
  local copies, waits for them, and re-layouts  13.7 us (5%)
    ppermute x28, waiting for transfers between devices, xor_dp(): return lax.ppermute(value, 'dp', [(i, i ^ step) for i in range(count)])  68.4 us
    ppermute x28, starting transfers between devices, xor_dp(): return lax.ppermute(value, 'dp', [(i, i ^ step) for i in range(count)])  34.3 us
    ppermute x20, waiting for transfers between devices, xor_tensor(): return lax.ppermute(value, 'tensor', [(i, i ^ step) for i in range(4)])  19.4 us
    pallas_call x1, Pallas kernels, back(): pl.pallas_call(back_kernel, grid_spec=pltpu.PrefetchScalarGridSpec(num_sc...  19 us
    pallas_call x1, Pallas kernels, middle(): pl.pallas_call(middle_kernel, grid_spec=pltpu.PrefetchScalarGridSpec(num_...  18.6 us
    pallas_call x3, Pallas kernels, spread(): pl.pallas_call(functools.partial(spread_kernel, len(pieces), width, prior...  18.3 us
    pallas_call x3, Pallas kernels, lookup(): pl.pallas_call(functools.partial(lookup_kernel, owners, len(pieces), widt...  15.1 us
    pallas_call x1, Pallas kernels, front(): pl.pallas_call(front_kernel, grid_spec=pltpu.PrefetchScalarGridSpec(num_s...  14.4 us
  transfers between devices with their start and end apart: 48, of which 19 were waited for; matrix products, arithmetic and copies ran while one was open for 10% of the time, Pallas kernels for 32%

profile of v2, /device:TPU:0, one launch (start us, length us, event | category | flops | bytes accessed | tf_op | source)
XLA Modules:
  0.0 283.7 jit_solution(12998132523391839817)
XLA Ops:
  0.7 1.9 pack_first.1
  2.5 4.0 %collective-permute-start = (bf16[96,1152]{1,0:T(8,128)(2,1)}, bf16[96,1152]{1,0:T(8,128)(2,1)S(1)}, u32[]{:S(2)}, u32[]{:S(2)}) collective-permute-start(bf16[96,1152]{1,0:T(8,128)(2,1)} %pack_first.1), channel_id=1, source_target_pairs={{0,16},{4,20},{8,24},{12,28},{16,0},{20,4},{24,8},{28,12},{1,17},{... | collective-permute-start | bytes 663560 | tf_op jit(solution)/shard_map/ppermute | solution.py:26
  6.6 10.4 %collective-permute-done = bf16[96,1152]{1,0:T(8,128)(2,1)S(1)} collective-permute-done((bf16[96,1152]{1,0:T(8,128)(2,1)}, bf16[96,1152]{1,0:T(8,128)(2,1)S(1)}, u32[]{:S(2)}, u32[]{:S(2)}) %collective-permute-start) | collective-permute-done | bytes 221216 | tf_op jit(solution)/shard_map/ppermute | solution.py:26
  20.5 2.1 pack.1
  22.7 3.3 %collective-permute-start.10 = (bf16[96,768]{1,0:T(8,128)(2,1)}, bf16[96,768]{1,0:T(8,128)(2,1)S(1)}, u32[]{:S(2)}, u32[]{:S(2)}) collective-permute-start(bf16[96,768]{1,0:T(8,128)(2,1)} %get-tuple-element.62), channel_id=1, source_target_pairs={{0,16},{4,20},{8,24},{12,28},{16,0},{20,4},{24,8},{28,12},{1,17},{... | collective-permute-start | bytes 442376 | tf_op jit(solution)/shard_map/ppermute | solution.py:26
  27.5 5.1 %collective-permute-done.1.refs_2_.refs_4_ = bf16[2,96,1152]{2,1,0:T(8,128)(2,1)S(1)} collective-permute-done((bf16[2,96,1152]{2,1,0:T(8,128)(2,1)S(1)}, bf16[2,96,1152]{2,1,0:T(8,128)(2,1)S(1)}, u32[]{:S(2)}, u32[]{:S(2)}) %collective-permute-start.1) | collective-permute-done | bytes 442400 | tf_op jit(solution)/shard_map/ppermute | solution.py:26
  34.8 1.8 collective-permute-start.11
  36.7 3.3 %collective-permute-start.20 = (bf16[96,1536]{1,0:T(8,128)(2,1)}, bf16[96,1536]{1,0:T(8,128)(2,1)}, u32[]{:S(2)}, u32[]{:S(2)}) collective-permute-start(bf16[96,1536]{1,0:T(8,128)(2,1)} %get-tuple-element.67), channel_id=1, source_target_pairs={{0,16},{4,20},{8,24},{12,28},{16,0},{20,4},{24,8},{28,12},{1,17},{... | collective-permute-start | bytes 884744 | tf_op jit(solution)/shard_map/ppermute | solution.py:26
  41.3 4.2 %lookup.3.refs_4_ = bf16[96,1024]{1,0:T(8,128)(2,1)} custom-call(s32[10]{0:T(128)} %pad_add_fusion.1.refs_0_.info.par.who, s32[2,1024]{1,0:T(2,128)} %pad_add_fusion.refs_1_, bf16[2,96,1152]{2,1,0:T(8,128)(2,1)} %copy-done.4), custom_call_target="tpu_custom_call" | custom-call | tf_op jit(solution)/shard_map/lookup/pallas_call | solution.py:314
  45.6 5.8 %lookup.4.refs_7_ = bf16[96,1024]{1,0:T(8,128)(2,1)} custom-call(s32[10]{0:T(128)} %pad_add_fusion.1.refs_0_.info.par.who, s32[2,1024]{1,0:T(2,128)} %pad_add_fusion.refs_1_, bf16[2,96,1152]{2,1,0:T(8,128)(2,1)} %copy-done.8, bf16[2,96,1152]{2,1,0:T(8,128)(2,1)} %copy-done.9, bf16[96,1024]{1,0:T(8,128)(2,1)} %lookup.3.refs_4_), custom_call_target="tpu_custom_call" | custom-call | tf_op jit(solution)/shard_map/lookup/pallas_call | solution.py:314
  51.4 5.0 %lookup.5.row0.up0 = bf16[96,1792]{1,0:T(8,128)(2,1)} custom-call(s32[10]{0:T(128)} %pad_add_fusion.1.refs_0_.info.par.who, s32[2,1024]{1,0:T(2,128)} %pad_add_fusion.refs_1_, bf16[2,96,1152]{2,1,0:T(8,128)(2,1)} %collective-permute-done.2.refs_2_.refs_6_, bf16[2,96,1152]{2,1,0:T(8,128)(2,1)} %copy-done.4, bf16[2,96,1152]{2,1,0:T(8,128)(2,1)} %copy-done.8, ...), custom_call_target="tpu_custom_call" | custom-call | tf_op jit(solution)/shard_map/lookup/pallas_call | solution.py:314
  60.0 2.2 pad_maximum_fusion.1.refs_0_
  62.2 5.6 %collective-permute-done.12.refs_2_ = bf16[2,96,768]{2,1,0:T(8,128)(2,1)S(1)} collective-permute-done((bf16[2,96,768]{2,1,0:T(8,128)(2,1)S(1)}, bf16[2,96,768]{2,1,0:T(8,128)(2,1)S(1)}, u32[]{:S(2)}, u32[]{:S(2)}) %collective-permute-start.12) | collective-permute-done | bytes 294944 | tf_op jit(solution)/shard_map/ppermute | solution.py:26
  68.5 4.8 %collective-permute-done.13.refs_3_ = bf16[2,96,768]{2,1,0:T(8,128)(2,1)S(1)} collective-permute-done((bf16[2,96,768]{2,1,0:T(8,128)(2,1)}, bf16[2,96,768]{2,1,0:T(8,128)(2,1)S(1)}, u32[]{:S(2)}, u32[]{:S(2)}) %collective-permute-start.13) | collective-permute-done | bytes 294944 | tf_op jit(solution)/shard_map/ppermute | solution.py:26
  76.3 2.7 assemble.2.wqkv
  79.9 14.4 %front.1 = (f32[1024,768]{1,0:T(8,128)}, bf16[1024,768]{1,0:T(8,128)(2,1)}, bf16[576,1024]{1,0:T(8,128)(2,1)}, bf16[192,1024]{1,0:T(8,128)(2,1)}, f32[8,1024]{1,0:T(8,128)}) custom-call(s32[10]{0:T(128)} %pad_add_fusion.1.refs_0_.info.par.who, bf16[96,1792]{1,0:T(8,128)(2,1)} %lookup.5.row0.up0, bf16[96,1792]{1,0:T(8,128)(2,1)} %copy-done.2, ...), custom_call_target="tpu_custom_call" | custom-call | tf_op jit(solution)/shard_map/front/pallas_call | solution.py:492
  95.8 1.6 collective-permute-start.23
  98.9 7.6 %collective-permute-done.15.mix2.refs_2_ = bf16[192,1024]{1,0:T(8,128)(2,1)S(1)} collective-permute-done((bf16[192,1024]{1,0:T(8,128)(2,1)}, bf16[192,1024]{1,0:T(8,128)(2,1)S(1)}, u32[]{:S(2)}, u32[]{:S(2)}) %collective-permute-start.15) | collective-permute-done | bytes 393248 | tf_op jit(solution)/shard_map/ppermute | solution.py:22
  107.1 4.6 %collective-permute-done.18.out2 = bf16[192,768]{1,0:T(8,128)(2,1)S(1)} collective-permute-done((bf16[192,768]{1,0:T(8,128)(2,1)S(1)}, bf16[192,768]{1,0:T(8,128)(2,1)S(1)}, u32[]{:S(2)}, u32[]{:S(2)}) %collective-permute-start.18) | collective-permute-done | bytes 294944 | tf_op jit(solution)/shard_map/ppermute | solution.py:22
  113.1 3.2 %assemble.3.ffn = bf16[768,1536]{1,0:T(8,128)(2,1)} custom-call(s32[10]{0:T(128)} %pad_add_fusion.1.refs_0_.info.par.who, bf16[2,96,1536]{2,1,0:T(8,128)(2,1)} %pad_maximum_fusion.1.refs_0_, bf16[2,96,1536]{2,1,0:T(8,128)(2,1)} %collective-permute-done.21.refs_1_, bf16[2,96,1536]{2,1,0:T(8,128)(2,1)} %collective-permute-done.22.refs_2_, ...), custom_call_target="tpu_custom_call" | custom-call | tf_op jit(solution)/shard_map/assemble/pallas_call | solution.py:105
  117.4 18.6 %middle.1 = (bf16[4,256,768]{2,1,0:T(8,128)(2,1)}, f32[256,768]{1,0:T(8,128)}, bf16[1024,768]{1,0:T(8,128)(2,1)}, bf16[1024,512]{1,0:T(8,128)(2,1)}, bf16[1024,1...) custom-call(s32[10]{0:T(128)} %pad_add_fusion.1.refs_0_.info.par.who, ...), custom_call_target="tpu_custom_call" | custom-call | tf_op jit(solution)/shard_map/middle/pallas_call | solution.py:614
  136.5 2.1 collective-permute-done.24
  138.6 1.9 fusion.7
  141.1 9.7 %weigh.1 = (bf16[4,96,1024]{2,1,0:T(8,128)(2,1)}, bf16[4,96,1024]{2,1,0:T(8,128)(2,1)}, bf16[4,96,512]{2,1,0:T(8,128)(2,1)}, bf16[4,96,512]{2,1,0:T(8,128)(2,1)}...) custom-call(s32[10]{0:T(128)} %pad_add_fusion.1.refs_0_.info.par.who, ...), custom_call_target="tpu_custom_call" | custom-call | tf_op jit(solution)/shard_map/weigh/pallas_call | solution.py:208
  153.8 19.0 %back.1 = (bf16[576,1024]{1,0:T(8,128)(2,1)}, bf16[2,368,768]{2,1,0:T(8,128)(2,1)}, bf16[2,368,768]{2,1,0:T(8,128)(2,1)}, bf16[2,96,1024]{2,1,0:T(8,128)(2,1)}, bf16[2,96,1024]{2,1,0:T(8,128)(2,1)}) custom-call(s32[10]{0:T(128)} %pad_add_fusion.1.refs_0_.info.par.who, bf16[576,1024]{1,0:T(8,128)(2,1)} %get-tuple-element.82.qkv, ...), custom_call_target="tpu_custom_call" | custom-call | tf_op jit(solution)/shard_map/back/pallas_call | solution.py:818
  174.9 1.6 collective-permute-start.29
  176.5 2.5 collective-permute-done.42
  179.4 2.5 collective-permute-done.29
  182.8 2.3 collective-permute-start.47
  185.1 13.3 %collective-permute-done.32 = bf16[112,1024]{1,0:T(8,128)(2,1)S(1)} collective-permute-done((bf16[112,1024]{1,0:T(8,128)(2,1)S(1)}, bf16[112,1024]{1,0:T(8,128)(2,1)S(1)}, u32[]{:S(2)}, u32[]{:S(2)}) %collective-permute-start.32) | collective-permute-done | bytes 229408 | tf_op jit(solution)/shard_map/ppermute | solution.py:26
  198.6 1.6 collective-permute-done.47
  201.8 5.0 %spread.3.refs_3_ = f32[2,1024,48]{2,1,0:T(8,128)} custom-call(s32[10]{0:T(128)} %pad_add_fusion.1.refs_0_.info.par.who, bf16[2,112,1024]{2,1,0:T(8,128)(2,1)} %copy-done.7), custom_call_target="tpu_custom_call" | custom-call | tf_op jit(solution)/shard_map/spread/pallas_call | solution.py:368
  208.3 6.4 %collective-permute-done.33.refs_1_ = bf16[2,112,1024]{2,1,0:T(8,128)(2,1)} collective-permute-done((bf16[2,112,1024]{2,1,0:T(8,128)(2,1)S(1)}, bf16[2,112,1024]{2,1,0:T(8,128)(2,1)}, u32[]{:S(2)}, u32[]{:S(2)}) %collective-permute-start.33) | collective-permute-done | bytes 458784 | tf_op jit(solution)/shard_map/ppermute | solution.py:26
  216.2 2.1 fusion.4
  219.8 2.0 fusion.6
  224.1 8.1 %spread.4.refs_2_ = f32[2,1024,48]{2,1,0:T(8,128)} custom-call(s32[10]{0:T(128)} %pad_add_fusion.1.refs_0_.info.par.who, bf16[2,112,1024]{2,1,0:T(8,128)(2,1)} %collective-permute-done.33.refs_1_, bf16[2,112,1024]{2,1,0:T(8,128)(2,1)} %collective-permute-done.35.refs_2_, f32[2,1024,48]{2,1,0:T(8,128)} %spread.3.refs_3_), custom_call_target="tpu_custom_call" | custom-call | tf_op jit(solution)/shard_map/spread/pallas_call | solution.py:368
  233.0 5.2 %spread.5 = (f32[48,1024]{1,0:T(8,128)}, f32[48,1024]{1,0:T(8,128)}) custom-call(s32[10]{0:T(128)} %pad_add_fusion.1.refs_0_.info.par.who, bf16[2,112,1024]{2,1,0:T(8,128)(2,1)} %copy-done.22, f32[2,1024,48]{2,1,0:T(8,128)} %spread.4.refs_2_), custom_call_target="tpu_custom_call" | custom-call | tf_op jit(solution)/shard_map/spread/pallas_call | solution.py:368
  238.2 1.9 fusion.5.extra
  240.1 4.1 %split.3 = (bf16[4,96,768]{2,1,0:T(8,128)(2,1)}, bf16[4,96,768]{2,1,0:T(8,128)(2,1)}) custom-call(s32[10]{0:T(128)} %pad_add_fusion.1.refs_0_.info.par.who, bf16[1024,768]{1,0:T(8,128)(2,1)} %get-tuple-element.96.left, bf16[576,1024]{1,0:T(8,128)(2,1)} %get-tuple-element.98.right, bf16[192,768]{1,0:T(8,128)(2,1)} %fusion.5.extra), custom_call_target="tpu_custom_call" | custom-call | tf_op jit(solution)/shard_map/split/pallas_call | solution.py:243
  248.7 1.7 split.2
  250.9 2.0 fusion.2
  252.9 6.8 %collective-permute-done.36 = bf16[4,112,96]{2,1,0:T(8,128)(2,1)S(1)} collective-permute-done((bf16[4,112,96]{2,1,0:T(8,128)(2,1)}, bf16[4,112,96]{2,1,0:T(8,128)(2,1)S(1)}, u32[]{:S(2)}, u32[]{:S(2)}) %collective-permute-start.36) | collective-permute-done | bytes 86048 | tf_op jit(solution)/shard_map/ppermute | solution.py:26
  259.8 2.0 fusion
  261.8 2.5 collective-permute-done.37
  267.2 1.9 collective-permute-done.38
  270.6 3.8 %collective-permute-done.40 = bf16[2,96,768]{2,1,0:T(8,128)(2,1)S(1)} collective-permute-done((bf16[2,96,768]{2,1,0:T(8,128)(2,1)S(1)}, bf16[2,96,768]{2,1,0:T(8,128)(2,1)S(1)}, u32[]{:S(2)}, u32[]{:S(2)}) %collective-permute-start.40) | collective-permute-done | bytes 294944 | tf_op jit(solution)/shard_map/ppermute | solution.py:26
  274.4 2.5 collective-permute-start.41
  278.3 3.8 %collective-permute-done.41 = bf16[96,768]{1,0:T(8,128)(2,1)S(1)} collective-permute-done((bf16[96,768]{1,0:T(8,128)(2,1)S(1)}, bf16[96,768]{1,0:T(8,128)(2,1)S(1)}, u32[]{:S(2)}, u32[]{:S(2)}) %collective-permute-start.41) | collective-permute-done | bytes 147488 | tf_op jit(solution)/shard_map/ppermute | solution.py:26
  (200 shorter events, 52.0 us)
Async XLA Ops:
  2.5 14.4 %collective-permute-start = (bf16[96,1152]{1,0:T(8,128)(2,1)}, bf16[96,1152]{1,0:T(8,128)(2,1)S(1)}, u32[]{:S(2)}, u32[]{:S(2)}) collective-permute-start(bf16[96,1152]{1,0:T(8,128)(2,1)} %pack_first.1), channel_id=1, source_target_pairs={{0,16},{4,20},{8,24},{12,28},{16,0},{20,4},{24,8},{28,12},{1,17},{... | collective-permute-start | bytes 663560 | tf_op jit(solution)/shard_map/ppermute | solution.py:26
  17.9 14.6 %collective-permute-start.1 = (bf16[2,96,1152]{2,1,0:T(8,128)(2,1)S(1)}, bf16[2,96,1152]{2,1,0:T(8,128)(2,1)S(1)}, u32[]{:S(2)}, u32[]{:S(2)}) collective-permute-start(bf16[2,96,1152]{2,1,0:T(8,128)(2,1)S(1)} %pad_maximum_fusion.3.refs_2_.refs_3_), channel_id=1, source_target_pairs={{0,8},{4,12},{8,0},{12,4},{16,24},{20,28},{24,16},{28,20},{1,9},{5... | collective-permute-start | bytes 1327112 | tf_op jit(solution)/shard_map/ppermute | solution.py:26
  19.0 41.0 %collective-permute-start.8 = (bf16[2,256,768]{2,1,0:T(8,128)(2,1)S(1)}, bf16[2,256,768]{2,1,0:T(8,128)(2,1)S(1)}, u32[]{:S(2)}, u32[]{:S(2)}) collective-permute-start(bf16[2,256,768]{2,1,0:T(8,128)(2,1)S(1)} %pad_maximum_fusion.emb0.cot0), channel_id=1, source_target_pairs={{0,2},{1,3},{2,0},{3,1},{4,6},{5,7},{6,4},{7,5},{8,10},{9,11},{10,... | collective-permute-start | bytes 2359304 | tf_op jit(solution)/shard_map/ppermute | solution.py:22
  22.7 11.2 %collective-permute-start.10 = (bf16[96,768]{1,0:T(8,128)(2,1)}, bf16[96,768]{1,0:T(8,128)(2,1)S(1)}, u32[]{:S(2)}, u32[]{:S(2)}) collective-permute-start(bf16[96,768]{1,0:T(8,128)(2,1)} %get-tuple-element.62), channel_id=1, source_target_pairs={{0,16},{4,20},{8,24},{12,28},{16,0},{20,4},{24,8},{28,12},{1,17},{... | collective-permute-start | bytes 442376 | tf_op jit(solution)/shard_map/ppermute | solution.py:26
  25.9 14.7 %collective-permute-start.3 = (bf16[2,96,1152]{2,1,0:T(8,128)(2,1)S(1)}, bf16[2,96,1152]{2,1,0:T(8,128)(2,1)S(1)}, u32[]{:S(2)}, u32[]{:S(2)}) collective-permute-start(bf16[2,96,1152]{2,1,0:T(8,128)(2,1)S(1)} %pad_maximum_fusion.3.refs_2_.refs_3_), channel_id=1, source_target_pairs={{0,4},{4,0},{8,12},{12,8},{16,20},{20,16},{24,28},{28,24},{1,5},{5... | collective-permute-start | bytes 1327112 | tf_op jit(solution)/shard_map/ppermute | solution.py:26
  32.5 18.9 %collective-permute-start.2 = (bf16[2,96,1152]{2,1,0:T(8,128)(2,1)S(1)}, bf16[2,96,1152]{2,1,0:T(8,128)(2,1)}, u32[]{:S(2)}, u32[]{:S(2)}) collective-permute-start(bf16[2,96,1152]{2,1,0:T(8,128)(2,1)S(1)} %collective-permute-done.1.refs_2_.refs_4_), channel_id=1, source_target_pairs={{0,4},{4,0},{8,12},{12,8},{16,20},{20,16},{24,28},{28,24},{1,5},{5... | collective-permute-start | bytes 1327112 | tf_op jit(solution)/shard_map/ppermute | solution.py:26
  34.8 23.1 %collective-permute-start.11 = (bf16[2,96,768]{2,1,0:T(8,128)(2,1)S(1)}, bf16[2,96,768]{2,1,0:T(8,128)(2,1)}, u32[]{:S(2)}, u32[]{:S(2)}) collective-permute-start(bf16[2,96,768]{2,1,0:T(8,128)(2,1)S(1)} %pad_maximum_fusion.4.refs_0_), channel_id=1, source_target_pairs={{0,8},{4,12},{8,0},{12,4},{16,24},{20,28},{24,16},{28,20},{1,9},{5... | collective-permute-start | bytes 884744 | tf_op jit(solution)/shard_map/ppermute | solution.py:26
  36.7 21.7 %collective-permute-start.20 = (bf16[96,1536]{1,0:T(8,128)(2,1)}, bf16[96,1536]{1,0:T(8,128)(2,1)}, u32[]{:S(2)}, u32[]{:S(2)}) collective-permute-start(bf16[96,1536]{1,0:T(8,128)(2,1)} %get-tuple-element.67), channel_id=1, source_target_pairs={{0,16},{4,20},{8,24},{12,28},{16,0},{20,4},{24,8},{28,12},{1,17},{... | collective-permute-start | bytes 884744 | tf_op jit(solution)/shard_map/ppermute | solution.py:26
  40.7 33.2 %collective-permute-start.7 = (bf16[2,256,768]{2,1,0:T(8,128)(2,1)S(1)}, bf16[2,256,768]{2,1,0:T(8,128)(2,1)S(1)}, u32[]{:S(2)}, u32[]{:S(2)}) collective-permute-start(bf16[2,256,768]{2,1,0:T(8,128)(2,1)S(1)} %pad_maximum_fusion.emb0.cot0), channel_id=1, source_target_pairs={{0,1},{1,0},{2,3},{3,2},{4,5},{5,4},{6,7},{7,6},{8,9},{9,8},{10,11... | collective-permute-start | bytes 2359304 | tf_op jit(solution)/shard_map/ppermute | solution.py:22
  56.4 16.9 %collective-permute-start.5 = (bf16[96,1792]{1,0:T(8,128)(2,1)}, bf16[96,1792]{1,0:T(8,128)(2,1)S(1)}, u32[]{:S(2)}, u32[]{:S(2)}) collective-permute-start(bf16[96,1792]{1,0:T(8,128)(2,1)} %lookup.5.row0.up0), channel_id=1, source_target_pairs={{0,2},{1,3},{2,0},{3,1},{4,6},{5,7},{6,4},{7,5},{8,10},{9,11},{10,... | collective-permute-start | bytes 1032200 | tf_op jit(solution)/shard_map/ppermute | solution.py:22
  57.9 9.9 %collective-permute-start.12 = (bf16[2,96,768]{2,1,0:T(8,128)(2,1)S(1)}, bf16[2,96,768]{2,1,0:T(8,128)(2,1)S(1)}, u32[]{:S(2)}, u32[]{:S(2)}) collective-permute-start(bf16[2,96,768]{2,1,0:T(8,128)(2,1)S(1)} %pad_maximum_fusion.4.refs_0_), channel_id=1, source_target_pairs={{0,4},{4,0},{8,12},{12,8},{16,20},{20,16},{24,28},{28,24},{1,5},{5... | collective-permute-start | bytes 884744 | tf_op jit(solution)/shard_map/ppermute | solution.py:26
  58.4 14.9 %collective-permute-start.13 = (bf16[2,96,768]{2,1,0:T(8,128)(2,1)}, bf16[2,96,768]{2,1,0:T(8,128)(2,1)S(1)}, u32[]{:S(2)}, u32[]{:S(2)}) collective-permute-start(bf16[2,96,768]{2,1,0:T(8,128)(2,1)} %collective-permute-done.11.refs_1_), channel_id=1, source_target_pairs={{0,4},{4,0},{8,12},{12,8},{16,20},{20,16},{24,28},{28,24},{1,5},{5... | collective-permute-start | bytes 884744 | tf_op jit(solution)/shard_map/ppermute | solution.py:26
  60.0 19.1 %collective-permute-start.9 = (bf16[2,256,768]{2,1,0:T(8,128)(2,1)S(1)}, bf16[2,256,768]{2,1,0:T(8,128)(2,1)}, u32[]{:S(2)}, u32[]{:S(2)}) collective-permute-start(bf16[2,256,768]{2,1,0:T(8,128)(2,1)S(1)} %collective-permute-done.8.emb2.cot2), channel_id=1, source_target_pairs={{0,1},{1,0},{2,3},{3,2},{4,5},{5,4},{6,7},{7,6},{8,9},{9,8},{10,11... | collective-permute-start | bytes 2359304 | tf_op jit(solution)/shard_map/ppermute | solution.py:22
  67.8 28.0 %collective-permute-start.21 = (bf16[2,96,1536]{2,1,0:T(8,128)(2,1)}, bf16[2,96,1536]{2,1,0:T(8,128)(2,1)}, u32[]{:S(2)}, u32[]{:S(2)}) collective-permute-start(bf16[2,96,1536]{2,1,0:T(8,128)(2,1)} %pad_maximum_fusion.1.refs_0_), channel_id=1, source_target_pairs={{0,8},{4,12},{8,0},{12,4},{16,24},{20,28},{24,16},{28,20},{1,9},{5... | collective-permute-start | bytes 1769480 | tf_op jit(solution)/shard_map/ppermute | solution.py:26
  73.3 5.7 %collective-permute-start.4 = (bf16[96,1792]{1,0:T(8,128)(2,1)}, bf16[96,1792]{1,0:T(8,128)(2,1)S(1)}, u32[]{:S(2)}, u32[]{:S(2)}) collective-permute-start(bf16[96,1792]{1,0:T(8,128)(2,1)} %lookup.5.row0.up0), channel_id=1, source_target_pairs={{0,1},{1,0},{2,3},{3,2},{4,5},{5,4},{6,7},{7,6},{8,9},{9,8},{10,11... | collective-permute-start | bytes 1032200 | tf_op jit(solution)/shard_map/ppermute | solution.py:22
  73.3 5.7 %collective-permute-start.6 = (bf16[96,1792]{1,0:T(8,128)(2,1)S(1)}, bf16[96,1792]{1,0:T(8,128)(2,1)S(1)}, u32[]{:S(2)}, u32[]{:S(2)}) collective-permute-start(bf16[96,1792]{1,0:T(8,128)(2,1)S(1)} %collective-permute-done.5.row2.up2), channel_id=1, source_target_pairs={{0,1},{1,0},{2,3},{3,2},{4,5},{5,4},{6,7},{7,6},{8,9},{9,8},{10,11... | collective-permute-start | bytes 1032200 | tf_op jit(solution)/shard_map/ppermute | solution.py:22
  74.0 32.5 %collective-permute-start.22 = (bf16[2,96,1536]{2,1,0:T(8,128)(2,1)}, bf16[2,96,1536]{2,1,0:T(8,128)(2,1)}, u32[]{:S(2)}, u32[]{:S(2)}) collective-permute-start(bf16[2,96,1536]{2,1,0:T(8,128)(2,1)} %pad_maximum_fusion.1.refs_0_), channel_id=1, source_target_pairs={{0,4},{4,0},{8,12},{12,8},{16,20},{20,16},{24,28},{28,24},{1,5},{5... | collective-permute-start | bytes 1769480 | tf_op jit(solution)/shard_map/ppermute | solution.py:26
  94.2 12.3 %collective-permute-start.15 = (bf16[192,1024]{1,0:T(8,128)(2,1)}, bf16[192,1024]{1,0:T(8,128)(2,1)S(1)}, u32[]{:S(2)}, u32[]{:S(2)}) collective-permute-start(bf16[192,1024]{1,0:T(8,128)(2,1)} %get-tuple-element.63.mix0.refs_0_.mixed), channel_id=1, source_target_pairs={{0,2},{1,3},{2,0},{3,1},{4,6},{5,7},{6,4},{7,5},{8,10},{9,11},{10,... | collective-permute-start | bytes 1179656 | tf_op jit(solution)/shard_map/ppermute | solution.py:22
  95.8 16.4 %collective-permute-start.23 = (bf16[2,96,1536]{2,1,0:T(8,128)(2,1)}, bf16[2,96,1536]{2,1,0:T(8,128)(2,1)S(1)}, u32[]{:S(2)}, u32[]{:S(2)}) collective-permute-start(bf16[2,96,1536]{2,1,0:T(8,128)(2,1)} %collective-permute-done.21.refs_1_), channel_id=1, source_target_pairs={{0,4},{4,0},{8,12},{12,8},{16,20},{20,16},{24,28},{28,24},{1,5},{5... | collective-permute-start | bytes 1769480 | tf_op jit(solution)/shard_map/ppermute | solution.py:26
  97.4 14.2 %collective-permute-start.18 = (bf16[192,768]{1,0:T(8,128)(2,1)S(1)}, bf16[192,768]{1,0:T(8,128)(2,1)S(1)}, u32[]{:S(2)}, u32[]{:S(2)}) collective-permute-start(bf16[192,768]{1,0:T(8,128)(2,1)S(1)} %slice.305.out0), channel_id=1, source_target_pairs={{0,2},{1,3},{2,0},{3,1},{4,6},{5,7},{6,4},{7,5},{8,10},{9,11},{10,... | collective-permute-start | bytes 884744 | tf_op jit(solution)/shard_map/ppermute | solution.py:22
  98.9 17.4 %collective-permute-start.14 = (bf16[192,1024]{1,0:T(8,128)(2,1)}, bf16[192,1024]{1,0:T(8,128)(2,1)S(1)}, u32[]{:S(2)}, u32[]{:S(2)}) collective-permute-start(bf16[192,1024]{1,0:T(8,128)(2,1)} %get-tuple-element.63.mix0.refs_0_.mixed), channel_id=1, source_target_pairs={{0,1},{1,0},{2,3},{3,2},{4,5},{5,4},{6,7},{7,6},{8,9},{9,8},{10,11... | collective-permute-start | bytes 1179656 | tf_op jit(solution)/shard_map/ppermute | solution.py:22
  106.5 9.8 %collective-permute-start.16 = (bf16[192,1024]{1,0:T(8,128)(2,1)S(1)}, bf16[192,1024]{1,0:T(8,128)(2,1)S(1)}, u32[]{:S(2)}, u32[]{:S(2)}) collective-permute-start(bf16[192,1024]{1,0:T(8,128)(2,1)S(1)} %collective-permute-done.15.mix2.refs_2_), channel_id=1, source_target_pairs={{0,1},{1,0},{2,3},{3,2},{4,5},{5,4},{6,7},{7,6},{8,9},{9,8},{10,11... | collective-permute-start | bytes 1179656 | tf_op jit(solution)/shard_map/ppermute | solution.py:22
  106.5 9.7 %collective-permute-start.17 = (bf16[192,768]{1,0:T(8,128)(2,1)S(1)}, bf16[192,768]{1,0:T(8,128)(2,1)S(1)}, u32[]{:S(2)}, u32[]{:S(2)}) collective-permute-start(bf16[192,768]{1,0:T(8,128)(2,1)S(1)} %slice.305.out0), channel_id=1, source_target_pairs={{0,1},{1,0},{2,3},{3,2},{4,5},{5,4},{6,7},{7,6},{8,9},{9,8},{10,11... | collective-permute-start | bytes 884744 | tf_op jit(solution)/shard_map/ppermute | solution.py:22
  111.6 4.7 %collective-permute-start.19 = (bf16[192,768]{1,0:T(8,128)(2,1)S(1)}, bf16[192,768]{1,0:T(8,128)(2,1)S(1)}, u32[]{:S(2)}, u32[]{:S(2)}) collective-permute-start(bf16[192,768]{1,0:T(8,128)(2,1)S(1)} %collective-permute-done.18.out2), channel_id=1, source_target_pairs={{0,1},{1,0},{2,3},{3,2},{4,5},{5,4},{6,7},{7,6},{8,9},{9,8},{10,11... | collective-permute-start | bytes 884744 | tf_op jit(solution)/shard_map/ppermute | solution.py:22
  136.0 2.6 collective-permute-start.24
  140.5 12.3 %collective-permute-start.25 = (bf16[192,1024]{1,0:T(8,128)(2,1)}, bf16[192,1024]{1,0:T(8,128)(2,1)S(1)}, u32[]{:S(2)}, u32[]{:S(2)}) collective-permute-start(bf16[192,1024]{1,0:T(8,128)(2,1)} %fusion.7), channel_id=1, source_target_pairs={{0,2},{1,3},{2,0},{3,1},{4,6},{5,7},{6,4},{7,5},{8,10},{9,11},{10,... | collective-permute-start | bytes 1179656 | tf_op jit(solution)/shard_map/ppermute | solution.py:22
  150.8 22.2 %collective-permute-start.45 = (bf16[4,96,512]{2,1,0:T(8,128)(2,1)}, bf16[4,96,512]{2,1,0:T(8,128)(2,1)S(1)}, u32[]{:S(2)}, u32[]{:S(2)}) collective-permute-start(bf16[4,96,512]{2,1,0:T(8,128)(2,1)} %get-tuple-element.104), channel_id=1, source_target_pairs={{0,4},{4,0},{8,12},{12,8},{16,20},{20,16},{24,28},{28,24},{1,5},{5... | collective-permute-start | bytes 1179656 | tf_op jit(solution)/shard_map/ppermute | solution.py:26
  152.3 26.6 %collective-permute-start.42 = (bf16[4,96,1024]{2,1,0:T(8,128)(2,1)}, bf16[4,96,1024]{2,1,0:T(8,128)(2,1)S(1)}, u32[]{:S(2)}, u32[]{:S(2)}) collective-permute-start(bf16[4,96,1024]{2,1,0:T(8,128)(2,1)} %get-tuple-element.102), channel_id=1, source_target_pairs={{0,4},{4,0},{8,12},{12,8},{16,20},{20,16},{24,28},{28,24},{1,5},{5... | collective-permute-start | bytes 2359304 | tf_op jit(solution)/shard_map/ppermute | solution.py:26
  172.8 2.0 collective-permute-start.28
  173.2 9.6 %collective-permute-start.46 = (bf16[2,96,512]{2,1,0:T(8,128)(2,1)S(1)}, bf16[2,96,512]{2,1,0:T(8,128)(2,1)S(1)}, u32[]{:S(2)}, u32[]{:S(2)}) collective-permute-start(bf16[2,96,512]{2,1,0:T(8,128)(2,1)S(1)} %get-tuple-element.155), channel_id=1, source_target_pairs={{0,8},{4,12},{8,0},{12,4},{16,24},{20,28},{24,16},{28,20},{1,9},{5... | collective-permute-start | bytes 589832 | tf_op jit(solution)/shard_map/ppermute | solution.py:26
  173.3 42.9 %collective-permute-start.26 = (bf16[2,448,768]{2,1,0:T(8,128)(2,1)}, bf16[2,448,768]{2,1,0:T(8,128)(2,1)}, u32[]{:S(2)}, u32[]{:S(2)}) collective-permute-start(bf16[2,448,768]{2,1,0:T(8,128)(2,1)} %get-tuple-element.81), channel_id=1, source_target_pairs={{0,1},{1,0},{2,3},{3,2},{4,5},{5,4},{6,7},{7,6},{8,9},{9,8},{10,11... | collective-permute-start | bytes 4128776 | tf_op jit(solution)/shard_map/ppermute | solution.py:22
  174.9 7.0 %collective-permute-start.29 = (bf16[96,1024]{1,0:T(8,128)(2,1)S(1)}, bf16[96,1024]{1,0:T(8,128)(2,1)S(1)}, u32[]{:S(2)}, u32[]{:S(2)}) collective-permute-start(bf16[96,1024]{1,0:T(8,128)(2,1)S(1)} %fusion.10), channel_id=1, source_target_pairs={{0,2},{1,3},{2,0},{3,1},{4,6},{5,7},{6,4},{7,5},{8,10},{9,11},{10,... | collective-permute-start | bytes 589832 | tf_op jit(solution)/shard_map/ppermute | solution.py:22
  179.3 21.6 %collective-permute-start.43 = (bf16[2,96,1024]{2,1,0:T(8,128)(2,1)S(1)}, bf16[2,96,1024]{2,1,0:T(8,128)(2,1)S(1)}, u32[]{:S(2)}, u32[]{:S(2)}) collective-permute-start(bf16[2,96,1024]{2,1,0:T(8,128)(2,1)S(1)} %get-tuple-element.151), channel_id=1, source_target_pairs={{0,8},{4,12},{8,0},{12,4},{16,24},{20,28},{24,16},{28,20},{1,9},{5... | collective-permute-start | bytes 1179656 | tf_op jit(solution)/shard_map/ppermute | solution.py:26
  181.9 37.9 %collective-permute-start.30 = (bf16[2,368,768]{2,1,0:T(8,128)(2,1)}, bf16[2,368,768]{2,1,0:T(8,128)(2,1)}, u32[]{:S(2)}, u32[]{:S(2)}) collective-permute-start(bf16[2,368,768]{2,1,0:T(8,128)(2,1)} %get-tuple-element.91), channel_id=1, source_target_pairs={{0,1},{1,0},{2,3},{3,2},{4,5},{5,4},{6,7},{7,6},{8,9},{9,8},{10,11... | collective-permute-start | bytes 3391496 | tf_op jit(solution)/shard_map/ppermute | solution.py:22
  182.0 16.4 %collective-permute-start.32 = (bf16[112,1024]{1,0:T(8,128)(2,1)S(1)}, bf16[112,1024]{1,0:T(8,128)(2,1)S(1)}, u32[]{:S(2)}, u32[]{:S(2)}) collective-permute-start(bf16[112,1024]{1,0:T(8,128)(2,1)S(1)} %get-tuple-element.165), channel_id=1, source_target_pairs={{0,16},{4,20},{8,24},{12,28},{16,0},{20,4},{24,8},{28,12},{1,17},{... | collective-permute-start | bytes 688136 | tf_op jit(solution)/shard_map/ppermute | solution.py:26
  182.8 17.4 %collective-permute-start.47 = (bf16[96,512]{1,0:T(8,128)(2,1)S(1)}, bf16[96,512]{1,0:T(8,128)(2,1)S(1)}, u32[]{:S(2)}, u32[]{:S(2)}) collective-permute-start(bf16[96,512]{1,0:T(8,128)(2,1)S(1)} %fusion.17), channel_id=1, source_target_pairs={{0,16},{4,20},{8,24},{12,28},{16,0},{20,4},{24,8},{28,12},{1,17},{... | collective-permute-start | bytes 294920 | tf_op jit(solution)/shard_map/ppermute | solution.py:26
  198.5 16.2 %collective-permute-start.33 = (bf16[2,112,1024]{2,1,0:T(8,128)(2,1)S(1)}, bf16[2,112,1024]{2,1,0:T(8,128)(2,1)}, u32[]{:S(2)}, u32[]{:S(2)}) collective-permute-start(bf16[2,112,1024]{2,1,0:T(8,128)(2,1)S(1)} %pad_maximum_fusion.2.refs_1_), channel_id=1, source_target_pairs={{0,8},{4,12},{8,0},{12,4},{16,24},{20,28},{24,16},{28,20},{1,9},{5... | collective-permute-start | bytes 1376264 | tf_op jit(solution)/shard_map/ppermute | solution.py:26
  201.7 20.6 %collective-permute-start.44 = (bf16[96,1024]{1,0:T(8,128)(2,1)S(1)}, bf16[96,1024]{1,0:T(8,128)(2,1)}, u32[]{:S(2)}, u32[]{:S(2)}) collective-permute-start(bf16[96,1024]{1,0:T(8,128)(2,1)S(1)} %fusion.12), channel_id=1, source_target_pairs={{0,16},{4,20},{8,24},{12,28},{16,0},{20,4},{24,8},{28,12},{1,17},{... | collective-permute-start | bytes 589832 | tf_op jit(solution)/shard_map/ppermute | solution.py:26
  206.8 17.3 %collective-permute-start.35 = (bf16[2,112,1024]{2,1,0:T(8,128)(2,1)}, bf16[2,112,1024]{2,1,0:T(8,128)(2,1)}, u32[]{:S(2)}, u32[]{:S(2)}) collective-permute-start(bf16[2,112,1024]{2,1,0:T(8,128)(2,1)} %copy-done.7), channel_id=1, source_target_pairs={{0,4},{4,0},{8,12},{12,8},{16,20},{20,16},{24,28},{28,24},{1,5},{5... | collective-permute-start | bytes 1376264 | tf_op jit(solution)/shard_map/ppermute | solution.py:26
  214.7 17.5 %collective-permute-start.34 = (bf16[2,112,1024]{2,1,0:T(8,128)(2,1)}, bf16[2,112,1024]{2,1,0:T(8,128)(2,1)S(1)}, u32[]{:S(2)}, u32[]{:S(2)}) collective-permute-start(bf16[2,112,1024]{2,1,0:T(8,128)(2,1)} %collective-permute-done.33.refs_1_), channel_id=1, source_target_pairs={{0,4},{4,0},{8,12},{12,8},{16,20},{20,16},{24,28},{28,24},{1,5},{5... | collective-permute-start | bytes 1376264 | tf_op jit(solution)/shard_map/ppermute | solution.py:26
  218.3 19.9 %collective-permute-start.27 = (bf16[448,768]{1,0:T(8,128)(2,1)}, bf16[448,768]{1,0:T(8,128)(2,1)}, u32[]{:S(2)}, u32[]{:S(2)}) collective-permute-start(bf16[448,768]{1,0:T(8,128)(2,1)} %fusion.4), channel_id=1, source_target_pairs={{0,2},{1,3},{2,0},{3,1},{4,6},{5,7},{6,4},{7,5},{8,10},{9,11},{10,... | collective-permute-start | bytes 2064392 | tf_op jit(solution)/shard_map/ppermute | solution.py:22
  221.8 24.5 %collective-permute-start.31 = (bf16[368,768]{1,0:T(8,128)(2,1)}, bf16[368,768]{1,0:T(8,128)(2,1)}, u32[]{:S(2)}, u32[]{:S(2)}) collective-permute-start(bf16[368,768]{1,0:T(8,128)(2,1)} %fusion.6), channel_id=1, source_target_pairs={{0,2},{1,3},{2,0},{3,1},{4,6},{5,7},{6,4},{7,5},{8,10},{9,11},{10,... | collective-permute-start | bytes 1695752 | tf_op jit(solution)/shard_map/ppermute | solution.py:22
  244.2 20.6 %collective-permute-start.39 = (bf16[4,96,768]{2,1,0:T(8,128)(2,1)}, bf16[4,96,768]{2,1,0:T(8,128)(2,1)}, u32[]{:S(2)}, u32[]{:S(2)}) collective-permute-start(bf16[4,96,768]{2,1,0:T(8,128)(2,1)} %get-tuple-element.100), channel_id=1, source_target_pairs={{0,4},{4,0},{8,12},{12,8},{16,20},{20,16},{24,28},{28,24},{1,5},{5... | collective-permute-start | bytes 1769480 | tf_op jit(solution)/shard_map/ppermute | solution.py:26
  250.4 9.3 %collective-permute-start.36 = (bf16[4,112,96]{2,1,0:T(8,128)(2,1)}, bf16[4,112,96]{2,1,0:T(8,128)(2,1)S(1)}, u32[]{:S(2)}, u32[]{:S(2)}) collective-permute-start(bf16[4,112,96]{2,1,0:T(8,128)(2,1)} %get-tuple-element.95), channel_id=1, source_target_pairs={{0,4},{4,0},{8,12},{12,8},{16,20},{20,16},{24,28},{28,24},{1,5},{5... | collective-permute-start | bytes 258056 | tf_op jit(solution)/shard_map/ppermute | solution.py:26
  259.7 4.6 %collective-permute-start.37 = (bf16[2,112,96]{2,1,0:T(8,128)(2,1)S(1)}, bf16[2,112,96]{2,1,0:T(8,128)(2,1)S(1)}, u32[]{:S(2)}, u32[]{:S(2)}) collective-permute-start(bf16[2,112,96]{2,1,0:T(8,128)(2,1)S(1)} %get-tuple-element.163), channel_id=1, source_target_pairs={{0,8},{4,12},{8,0},{12,4},{16,24},{20,28},{24,16},{28,20},{1,9},{5... | collective-permute-start | bytes 129032 | tf_op jit(solution)/shard_map/ppermute | solution.py:26
  264.3 4.8 %collective-permute-start.38 = (bf16[112,96]{1,0:T(8,128)(2,1)S(1)}, bf16[112,96]{1,0:T(8,128)(2,1)S(1)}, u32[]{:S(2)}, u32[]{:S(2)}) collective-permute-start(bf16[112,96]{1,0:T(8,128)(2,1)S(1)} %fusion.26), channel_id=1, source_target_pairs={{0,16},{4,20},{8,24},{12,28},{16,0},{20,4},{24,8},{28,12},{1,17},{... | collective-permute-start | bytes 64520 | tf_op jit(solution)/shard_map/ppermute | solution.py:26
  266.0 8.4 %collective-permute-start.40 = (bf16[2,96,768]{2,1,0:T(8,128)(2,1)S(1)}, bf16[2,96,768]{2,1,0:T(8,128)(2,1)S(1)}, u32[]{:S(2)}, u32[]{:S(2)}) collective-permute-start(bf16[2,96,768]{2,1,0:T(8,128)(2,1)S(1)} %get-tuple-element.153), channel_id=1, source_target_pairs={{0,8},{4,12},{8,0},{12,4},{16,24},{20,28},{24,16},{28,20},{1,9},{5... | collective-permute-start | bytes 884744 | tf_op jit(solution)/shard_map/ppermute | solution.py:26
  274.4 7.7 %collective-permute-start.41 = (bf16[96,768]{1,0:T(8,128)(2,1)S(1)}, bf16[96,768]{1,0:T(8,128)(2,1)S(1)}, u32[]{:S(2)}, u32[]{:S(2)}) collective-permute-start(bf16[96,768]{1,0:T(8,128)(2,1)S(1)} %fusion.15), channel_id=1, source_target_pairs={{0,16},{4,20},{8,24},{12,28},{16,0},{20,4},{24,8},{28,12},{1,17},{... | collective-permute-start | bytes 442376 | tf_op jit(solution)/shard_map/ppermute | solution.py:26
  (40 other events, 451.0 us)

commit v3 on v2

--- a/solution.py
+++ b/solution.py
@@ -50,10 +50,11 @@
     return terms[0].astype(F32) + terms[1].astype(F32) + terms[2].astype(F32)
 
 
-def double_dp(value):
-    zero = jnp.stack([value, xor_dp(value, 4, 8)])
-    two = xor_dp(zero, 2, 8)
-    return zero, two, xor_dp(zero, 1, 8), xor_dp(two, 1, 8)
+def double_dp(value, others=(), window=lambda zero: ()):
+    zero = jnp.stack([value, after(xor_dp(value, 4, 8), *others)])
+    made = window(zero)
+    two, one, *made = lax.optimization_barrier((xor_dp(zero, 2, 8), xor_dp(zero, 1, 8), *made))
+    return (zero, two, one, xor_dp(two, 1, 8)), made
 
 
 DOUBLED = (0, 4, 2, 6, 1, 5, 3, 7)
@@ -68,13 +69,28 @@
     return add_round(stay[0], come[0]), add_round(stay[1], come[1])
 
 
-def sum_dp(halves, count):
-    if count != 8:
-        return lax.psum_scatter(halves[0].astype(F32), "dp", scatter_dimension=0, tiled=True)[0]
-    away, keep = halves
-    stay, leave = halve_first(keep, xor_dp(away, 1, count))
-    ours, leave = halve_second(stay, xor_dp(leave, 2, count))
-    return ours.astype(F32) + xor_dp(leave, 4, count).astype(F32)
+class SumDp:
+    def __init__(self, halves, count):
+        self.count, self.halves = count, halves
+        if count == 8:
+            away, self.keep = halves
+            self.first = xor_dp(away, 1, count)
+
+    def across(self):
+        if self.count == 8:
+            self.stay, leave = halve_first(self.keep, self.first)
+            self.second = xor_dp(leave, 2, self.count)
+
+    def total(self):
+        if self.count != 8:
+            values = self.halves[0].astype(F32)
+            return lax.psum_scatter(values, "dp", scatter_dimension=0, tiled=True)[0]
+        return self.ours.astype(F32) + self.third.astype(F32)
+
+    def between(self):
+        if self.count == 8:
+            self.ours, leave = halve_second(self.stay, self.second)
+            self.third = xor_dp(leave, 4, self.count)
 
 
 def entries(refs):
@@ -96,17 +112,21 @@
     whole_ref = refs[-1] if turn else out
     place_rows(info, pieces, 0, whole_ref)
     if turn:
-        out[...] = whole_ref[...].T
+        turned = whole_ref[...].T
+        out[...] = turned[: out.shape[0]]
+        refs[5][...] = turned[out.shape[0] :]
 
 
 def assemble(info, arrays, turn):
     rows, cols = arrays[0].shape[1:]
-    shape = (cols, 8 * rows) if turn else (8 * rows, cols)
+    shapes = [(8 * rows, cols)]
+    if turn:
+        shapes = [(cols - cols // 4, 8 * rows), (cols // 4, 8 * rows)]
     return pl.pallas_call(
         functools.partial(assemble_kernel, turn),
-        out_shape=jax.ShapeDtypeStruct(shape, BF16),
+        out_shape=[jax.ShapeDtypeStruct(shape, BF16) for shape in shapes],
         in_specs=[pl.BlockSpec(memory_space=pltpu.SMEM)] + [pl.BlockSpec(memory_space=VMEM)] * 4,
-        out_specs=pl.BlockSpec(memory_space=VMEM),
+        out_specs=[pl.BlockSpec(memory_space=VMEM)] * len(shapes),
         scratch_shapes=[VMEM((8 * rows, cols), BF16)] if turn else [],
         name="assemble",
     )(info, *arrays)
@@ -180,60 +200,53 @@
 
 
 def weigh_kernel(rows, halves, info, cot, hidden, norm, grads, *refs):
-    mixes, grad, feed = refs[:4], refs[4], refs[5]
-    downs, gates = refs[6 : 6 + halves], refs[6 + halves : 6 + 2 * halves]
-    stay, leave, turned, down_whole, gate_whole = refs[6 + 2 * halves :]
-    units = hidden.shape[1]
+    mixes, grad, refs = refs[:4], refs[4], refs[5:]
+    outs, (stay, leave, turned, whole_ref) = refs[:halves], refs[halves:]
+    at = grads.shape[1]
     turned[...] = cot[...].T
-    down_whole[:, units:] = nn(turned[...], hidden[...]).astype(BF16)
+    whole_ref[:, at:] = nn(turned[...], hidden[...]).astype(BF16)
     turned[...] = norm[...].T
-    down_whole[:, :units] = nn(turned[...], grads[:, :units]).astype(BF16)
-    split_rows(info, down_whole, downs, rows)
-    gate_whole[...] = nn(turned[...], grads[:, units:]).astype(BF16)
-    split_rows(info, gate_whole, gates, rows)
+    whole_ref[:, :at] = nn(turned[...], grads[...]).astype(BF16)
+    split_rows(info, whole_ref, outs, rows)
     for xor in range(4):
-        out, at = (stay, leave)[xor % 2], xor // 2
-        out[at, : feed.shape[1]] = feed[2 * (xor % 2) + at]
-        out[at, feed.shape[1] :] = nn(mixes[xor][...], grad[...]).astype(BF16)
-
-
-def weigh(info, cot, hidden, norm, grads, mixes, grad, feed, count, own_dim):
+        (stay, leave)[xor % 2][xor // 2] = nn(mixes[xor][...], grad[...]).astype(BF16)
+
+
+def weigh(info, cot, hidden, norm, grads, mixes, grad, count, own_dim):
     vm = pl.BlockSpec(memory_space=VMEM)
     dim, length = cot.shape[1], cot.shape[0]
     lead = [4, 4] if count == 8 else [count]
-    units = hidden.shape[1]
-    shapes = [(n, own_dim, 2 * units) for n in lead]
-    shapes += [(n, own_dim, units) for n in lead]
-    shapes += [(2, feed.shape[1] + mixes[0].shape[0], dim)] * 2
+    cols = hidden.shape[1] + grads.shape[1]
+    shapes = [(n, own_dim, cols) for n in lead] + [(2, mixes[0].shape[0], dim)] * 2
     got = pl.pallas_call(
         functools.partial(weigh_kernel, own_dim, len(lead)),
         out_shape=[jax.ShapeDtypeStruct(shape, BF16) for shape in shapes],
-        in_specs=[pl.BlockSpec(memory_space=pltpu.SMEM)] + [vm] * 10,
+        in_specs=[pl.BlockSpec(memory_space=pltpu.SMEM)] + [vm] * 9,
         out_specs=[vm] * len(shapes),
-        scratch_shapes=[
-            VMEM((dim, length), BF16),
-            VMEM((dim, 2 * units), BF16),
-            VMEM((dim, units), BF16),
-        ],
+        scratch_shapes=[VMEM((dim, length), BF16), VMEM((dim, cols), BF16)],
         name="weigh",
-    )(info, cot, hidden, norm, grads, *mixes, grad, feed)
-    return got[: len(lead)], got[len(lead) : 2 * len(lead)], got[2 * len(lead) :]
-
-
-def weigh_turned_kernel(rows, info, left, right, extra, *refs):
+    )(info, cot, hidden, norm, grads, *mixes, grad)
+    return got[: len(lead)], got[len(lead) :]
+
+
+def weigh_turned_kernel(rows, info, left, right, *refs):
     outs, whole_ref = refs[:-1], refs[-1]
-    wide = nn(right[...], left[...]).astype(BF16)
-    whole_ref[...] = jnp.concatenate([wide, extra[...]], axis=0).T
+    whole_ref[...] = nn(right[...], left[...]).astype(BF16).T
     split_rows(info, whole_ref, outs, rows)
 
 
-def turn_kernel(rows, info, extra, below, *refs):
+def turn_kernel(rows, info, wide, *refs):
     outs, whole_ref = refs[:-1], refs[-1]
-    whole_ref[...] = extra[...].T
-    split_rows(info, whole_ref, [out.at[:, :rows] for out in outs], rows)
+    whole_ref[...] = wide[...].T
+    split_rows(info, whole_ref, outs, rows)
+
+
+def turn_below_kernel(rows, info, wide, below, *refs):
+    outs = refs[:-1]
+    turn_kernel(rows, info, wide, *(out.at[:, :rows] for out in outs), refs[-1])
     for out in outs:
         for z in range(out.shape[0]):
-            out[z, rows:] = below[...]
+            out[z, rows:, : below.shape[1]] = below[...]
 
 
 def split_call(body, info, operands, count, own_dim, cols, below=0):
@@ -250,14 +263,15 @@
     )(info, *operands)
 
 
-def weigh_turned(info, left, right, extra, count, own_dim):
-    cols = right.shape[0] + extra.shape[0]
-    return split_call(weigh_turned_kernel, info, [left, right, extra], count, own_dim, cols)
-
-
-def turn(info, extra, below, count, own_dim):
+def weigh_turned(info, left, right, count, own_dim):
+    return split_call(weigh_turned_kernel, info, [left, right], count, own_dim, right.shape[0])
+
+
+def turn(info, wide, below, count, own_dim):
+    if below is None:
+        return split_call(turn_kernel, info, [wide], count, own_dim, wide.shape[0])
     return split_call(
-        turn_kernel, info, [extra, below], count, own_dim, extra.shape[0], below.shape[0]
+        turn_below_kernel, info, [wide, below], count, own_dim, wide.shape[0], below.shape[0]
     )
 
 
@@ -324,36 +338,30 @@
 
 
 def spread_kernel(arrays, width, start, end, *refs):
-    outs = refs[-3:-1] if end else refs[-2:-1]
-    turned = refs[-1]
+    outs = refs[-2:] if end else refs[-1:]
     info, pieces = refs[0], entries(refs[1 : 1 + arrays])
-    own_rows = outs[0].shape[-1] if end else outs[0].shape[1]
-    length = pieces[0].shape[1]
+    prior = None if start else refs[1 + arrays]
+    own_rows = outs[0].shape[1]
+    base = (info[1] * own_rows).astype(F32)
     places = steps(TILE)
     wanted = []
-    for i, piece in enumerate(pieces):
-        turned[i * length : (i + 1) * length, :] = piece[: 2 * width, :].T
+    for piece in pieces:
         digits = piece[2 * width :, :].astype(F32)
-        wanted.append(
-            [
-                digits[d : d + 1] * 256.0 + digits[d + 1 : d + 2] - (info[1] * own_rows).astype(F32)
-                for d in (0, 2)
-            ]
-        )
+        wanted.append([digits[d : d + 1] * 256.0 + digits[d + 1 : d + 2] - base for d in (0, 2)])
 
     def chunk(c, carry):
         first = pl.multiple_of(c * TILE, TILE)
+        cut = pl.ds(first, TILE)
         for half in range(2):
-            hot = [one_hot(places, want[half] - first.astype(F32)) for want in wanted]
-            hot = jnp.concatenate(hot, axis=1) if len(hot) > 1 else hot[0]
-            part = nn(hot, turned[: len(pieces) * length, half * width : (half + 1) * width])
-            cut = pl.ds(first, TILE)
-            if not start:
-                part = part + refs[1 + arrays][half, cut, :]
+            lanes = slice(half * width, (half + 1) * width)
+            sofar = jnp.zeros((width, TILE), F32) if start else prior[lanes, cut]
+            for piece, want in zip(pieces, wanted):
+                hot = one_hot(places, want[half] - first.astype(F32))
+                sofar = sofar + nt(piece[lanes, :], hot)
             if end:
-                outs[half][:, cut] = part.T
+                outs[half][:, cut] = sofar
             else:
-                outs[0][half, cut, :] = part
+                outs[0][lanes, cut] = sofar
         return carry
 
     lax.fori_loop(0, own_rows // TILE, chunk, 0)
@@ -362,15 +370,12 @@
 def spread(info, pieces, own_rows, width, prior, end):
     operands = [info, *pieces] + ([] if prior is None else [prior])
     vm = pl.BlockSpec(memory_space=VMEM)
-    shapes = [(width, own_rows)] * 2 if end else [(2, own_rows, width)]
-    length = pieces[0].shape[-1]
-    count = sum(1 if piece.ndim == 2 else piece.shape[0] for piece in pieces)
+    shapes = [(width, own_rows)] * 2 if end else [(2 * width, own_rows)]
     got = pl.pallas_call(
         functools.partial(spread_kernel, len(pieces), width, prior is None, end),
         out_shape=[jax.ShapeDtypeStruct(shape, F32) for shape in shapes],
         in_specs=[pl.BlockSpec(memory_space=pltpu.SMEM)] + [vm] * (len(operands) - 1),
         out_specs=[vm] * len(shapes),
-        scratch_shapes=[VMEM((count * length, 2 * width), BF16)],
         name="spread",
     )(*operands)
     return got if end else got[0]
@@ -485,7 +490,7 @@
 def front(par, sets, tokens, wqkvo, gain, cosine, sine):
     dim = tokens[0].shape[2]
     length = sets[0].shape[1] - dim
-    width = wqkvo.shape[0] // 4
+    width = wqkvo.shape[0] // 3
     ng = sets[0].shape[0]
     tall = lambda r, _: (r, 0)
     wide = lambda r, _: (0, r)
@@ -523,6 +528,10 @@
     )(par, *sets, *sets, *tokens, wqkvo, gain, cosine, sine)
 
 
+def slot_of(xor):
+    return (xor & 1) * 2 + (xor >> 1)
+
+
 def middle_kernel(
     who,
     mix0,
@@ -535,12 +544,16 @@
     out3,
     resid,
     gain,
-    ffn,
+    ffn0,
+    ffn1,
+    ffn2,
+    ffn3,
     cot0,
     cot1,
     cot2,
     cot3,
-    feed,
+    feed_stay,
+    feed_leave,
     resid_own,
     normed,
     hidden,
@@ -550,9 +563,18 @@
     mix_leave,
     grad_gain,
     cot_all,
+    ffn,
 ):
     tile = pl.program_id(0)
     units = hidden.shape[1]
+
+    @pl.when(tile == 0)
+    def _():
+        if len(ffn0.shape) == 3:
+            place_rows(who, (ffn0, ffn1, ffn2, ffn3), 0, ffn)
+        else:
+            ffn[...] = ffn0[...]
+
     outs = jnp.concatenate([out0[...], out1[...], out2[...], out3[...]], axis=0)
     mix = jnp.concatenate([mix0[...], mix1[...], mix2[...], mix3[...]], axis=0)
     res = resid[...] + tn(mix, outs)
@@ -570,7 +592,17 @@
     silu = gate * sig
     hid = (silu * upward).astype(BF16)
     hidden[...] = hid
-    feed[0] = nt(hid, ffn[:, 2 * units :]).astype(BF16)
+    fed = nt(hid, ffn[:, 2 * units :]).astype(BF16)
+    slot = slot_of(tile ^ who[0])
+
+    @pl.when(slot < 2)
+    def _():
+        feed_stay[0] = fed
+
+    @pl.when(slot >= 2)
+    def _():
+        feed_leave[0] = fed
+
     cot = pick((cot0, cot1, cot2, cot3), tile ^ who[0])
     cot_all[...] = cot
     back = nn(cot, ffn[:, 2 * units :])
@@ -600,14 +632,10 @@
         grad_gain[...] += gained
 
 
-def slot_of(xor):
-    return (xor & 1) * 2 + (xor >> 1)
-
-
-def middle(who, mixes, outs, resid, gain, ffn, tokens):
+def middle(who, mixes, outs, resid, gain, ffns, tokens):
     length, dim = resid.shape
     width = mixes[0].shape[0]
-    units = ffn.shape[1] // 3
+    units = ffns[0].shape[-1] // 3
     tiles = length // TILE
     tall = lambda r, _: (r, 0)
     wide = lambda r, _: (0, r)
@@ -621,11 +649,13 @@
             + [
                 pl.BlockSpec((TILE, dim), tall),
                 whole((1, dim)),
-                whole((dim, 3 * units)),
             ]
+            + [whole(array.shape) for array in ffns]
             + [pl.BlockSpec((1, TILE, dim), lambda *_: (1, 0, 0))] * 4,
+            scratch_shapes=[VMEM((dim, 3 * units), BF16)],
             out_specs=[
-                pl.BlockSpec((1, TILE, dim), lambda r, who: (slot_of(r ^ who[0]), 0, 0)),
+                pl.BlockSpec((1, TILE, dim), lambda r, who: ((r >> 1) ^ (who[0] >> 1), 0, 0)),
+                pl.BlockSpec((1, TILE, dim), lambda r, who: ((r >> 1) ^ (who[0] >> 1), 0, 0)),
                 whole((TILE, dim)),
                 pl.BlockSpec((TILE, dim), tall),
                 pl.BlockSpec((TILE, units), tall),
@@ -638,7 +668,8 @@
             ],
         ),
         out_shape=[
-            jax.ShapeDtypeStruct((tiles, TILE, dim), BF16),
+            jax.ShapeDtypeStruct((tiles // 2, TILE, dim), BF16),
+            jax.ShapeDtypeStruct((tiles // 2, TILE, dim), BF16),
             jax.ShapeDtypeStruct((TILE, dim), F32),
             jax.ShapeDtypeStruct((length, dim), BF16),
             jax.ShapeDtypeStruct((length, units), BF16),
@@ -650,7 +681,7 @@
             jax.ShapeDtypeStruct((length, dim), BF16),
         ],
         name="middle",
-    )(who, *mixes, *outs, resid, gain, ffn, *tokens)
+    )(who, *mixes, *outs, resid, gain, *ffns, *tokens)
 
 
 def unrope_into(out, row, values, cosine, sine):
@@ -681,9 +712,15 @@
     row3,
     cos_ref,
     sin_ref,
+    feed_stay,
+    feed_leave,
+    out_stay,
+    out_leave,
     gproj,
     stay,
     leave,
+    up_stay,
+    up_leave,
     row_stay,
     row_leave,
     keys_sum,
@@ -770,11 +807,13 @@
 
     @pl.when(slot < 2)
     def _():
-        stay[slot, :TILE, :] = part
+        stay[0, :TILE] = part
+        stay[0, TILE:] = feed_stay[0]
 
     @pl.when(slot >= 2)
     def _():
-        leave[slot - 2, :TILE, :] = part
+        leave[0, :TILE] = part
+        leave[0, TILE:] = feed_leave[0]
 
     rows = jnp.concatenate([row0[...], row1[...], row2[...], row3[...]], axis=0)
     up_part = nn(rows, part)
@@ -802,17 +841,20 @@
             [grad_gain[...], gain_two[...], jnp.zeros((14, dim), F32)], axis=0
         ).astype(BF16)
         for k in range(4):
-            out = (stay, leave)[k % 2]
-            out[k // 2, TILE : TILE + wide, :] = grad_ups[k * wide : (k + 1) * wide, :].astype(BF16)
-            out[k // 2, TILE + wide :, :] = gains
-
-
-def back(info, qkv, gmix, mixed, lse, grad_res, resid, gain, gain_part, wqkvo, sets, cosine, sine):
+            out = (up_stay, up_leave)[k % 2]
+            other = (out_stay, out_leave)[k % 2][k // 2]
+            out[k // 2, :wide, :] = grad_ups[k * wide : (k + 1) * wide, :].astype(BF16)
+            out[k // 2, wide : wide + width, :] = other
+            out[k // 2, wide + width :, :] = gains
+
+
+def back(info, qkv, gmix, mixed, lse, grad_res, resid, gain, gain_part, wqkvo, sets, cosine, sine, feeds, outs):
     length, dim = resid.shape
     width = gmix.shape[0]
     ng = sets[0].shape[0]
     tiles = length // TILE
     last = tiles - 1
+    token_slot = lambda r, info: (((last - r) >> 1) ^ (info[0] >> 1), 0, 0)
     tall = lambda r, _: (last - r, 0)
     wide = lambda r, _: (0, last - r)
     return pl.pallas_call(
@@ -836,11 +878,17 @@
             + [
                 pl.BlockSpec((HD // 2, TILE), wide),
                 pl.BlockSpec((HD // 2, TILE), wide),
+                pl.BlockSpec((1, TILE, dim), token_slot),
+                pl.BlockSpec((1, TILE, dim), token_slot),
+                whole((2, width, dim)),
+                whole((2, width, dim)),
             ],
             out_specs=[
                 pl.BlockSpec((3 * width, TILE), wide),
-                whole((2, TILE + ng + 16, dim)),
-                whole((2, TILE + ng + 16, dim)),
+                pl.BlockSpec((1, 2 * TILE, dim), token_slot),
+                pl.BlockSpec((1, 2 * TILE, dim), token_slot),
+                whole((2, ng + width + 16, dim)),
+                whole((2, ng + width + 16, dim)),
                 pl.BlockSpec((2, ng, TILE), lambda r, _: (0, 0, last - r)),
                 pl.BlockSpec((2, ng, TILE), lambda r, _: (0, 0, last - r)),
             ],
@@ -854,13 +902,15 @@
         ),
         out_shape=[
             jax.ShapeDtypeStruct((3 * width, length), BF16),
-            jax.ShapeDtypeStruct((2, TILE + ng + 16, dim), BF16),
-            jax.ShapeDtypeStruct((2, TILE + ng + 16, dim), BF16),
+            jax.ShapeDtypeStruct((2, 2 * TILE, dim), BF16),
+            jax.ShapeDtypeStruct((2, 2 * TILE, dim), BF16),
+            jax.ShapeDtypeStruct((2, ng + width + 16, dim), BF16),
+            jax.ShapeDtypeStruct((2, ng + width + 16, dim), BF16),
             jax.ShapeDtypeStruct((2, ng, length), BF16),
             jax.ShapeDtypeStruct((2, ng, length), BF16),
         ],
         name="back",
-    )(info, qkv, gmix, mixed, lse, grad_res, resid, gain, gain_part, wqkvo, *sets, *sets, cosine, sine)
+    )(info, qkv, gmix, mixed, lse, grad_res, resid, gain, gain_part, wqkvo, *sets, *sets, cosine, sine, *feeds, *outs)
 
 
 def rotary(parents):
@@ -914,25 +964,39 @@
     )
     cosine, sine = rotary(parents)
 
+    digits = jnp.stack([ids_two // 256, ids_two % 256, ids_three // 256, ids_three % 256])
+    digits = jnp.pad(digits.astype(BF16), ((0, 12), (0, 0)))
     first = pack_first(table_two.T, table_three.T, w_two, w_three)
     attn_pack, ffn_pack = pack(w_query, w_key, w_value, w_output, w_gate, w_up, w_down.T)
     token_pair = jnp.stack([embedded, cotangent])
+    token_near = xor_tensor(token_pair, 1)
     if dp == 8:
-        zero, two, one, three = arrays = double_dp(first)
-        got = lookup(info, [zero], (0, 4), own_rows, ids, None)
+        arrays, (got, token_near) = double_dp(
+            first,
+            (attn_pack, ffn_pack, cosine, sine, gain_one, gain_two, digits),
+            lambda zero: [lookup(info, [zero], (0, 4), own_rows, ids, None), token_near],
+        )
+        _, two, one, three = arrays
+        token_far = xor_tensor(after(token_pair, arrays[0]), 2)
         got = lookup(info, [two, one], (2, 6, 1, 5), own_rows, ids, got)
-        got = lookup(info, [three], (3, 7), own_rows, ids, got, arrays)
-        token_pair = after(token_pair, zero)
-        attn_arrays = double_dp(after(attn_pack, zero))
-        wqkvo = assemble(info, attn_arrays, True)
-        ffn_arrays = double_dp(after(ffn_pack, attn_arrays[0]))
-        ffn_w = assemble(info, ffn_arrays, False)
+        attn_arrays, (got, token_far) = double_dp(
+            after(attn_pack, arrays[0]),
+            (got,),
+            lambda zero: [lookup(info, [three], (3, 7), own_rows, ids, got, arrays), token_far],
+        )
+        wqkv, wo = assemble(info, attn_arrays, True)
+        ffn_arrays, _ = double_dp(after(ffn_pack, two), (attn_arrays[1],))
+        wqkv, ffn_zero = lax.optimization_barrier((wqkv, ffn_arrays[0]))
+        ffns = (ffn_zero, *ffn_arrays[1:])
     else:
         every = lax.all_gather(first[:, :own_rows], "dp", axis=0)
         small = jnp.concatenate([w_two.astype(BF16).T, w_three.astype(BF16).T], axis=1)
         ups = lax.all_gather(small, "dp", axis=0, tiled=True).T
         wqkvo = lax.all_gather(attn_pack, "dp", axis=0, tiled=True).T
-        ffn_w = lax.all_gather(ffn_pack, "dp", axis=0, tiled=True)
+        wqkv, wo = wqkvo[: 3 * width], wqkvo[3 * width :]
+        ffns = [lax.all_gather(ffn_pack, "dp", axis=0, tiled=True)]
+        ffns += [jnp.zeros((8, SEG), BF16)] * 3
+        token_far = xor_tensor(token_pair, 2)
 
         def take(i, so_far):
             piece = lax.dynamic_index_in_dim(every, i, 0, keepdims=False)
@@ -942,46 +1006,78 @@
         got = lax.fori_loop(0, dp, take, jnp.zeros((2 * ng, ids.shape[1]), BF16))
         got = jnp.concatenate([ups, got], axis=1)
 
-    tokens = gather_tensor(token_pair)
+    tokens = [token_pair, token_near, token_far, xor_tensor(token_far, 1)]
     sets = gather_tensor(got)
-    outs = gather_tensor(after(wqkvo[3 * width :], sets[2]))
-
-    resid, normed, qkv, mixed, lse = front(info, sets, tokens, wqkvo, gain_one, cosine, sine)
+    outs = gather_tensor(after(wo, sets[2]))
+
+    resid, normed, qkv, mixed, lse = front(info, sets, tokens, wqkv, gain_one, cosine, sine)
+    mixed = after(mixed, outs[2])
     mixes = gather_tensor(mixed)
-    feed, resid_own, normed_two, hidden, grads, grad_res, stay, leave, gain_part_two, cot_all = (
-        middle(info, mixes, outs, resid, gain_two, ffn_w, tokens)
+    (
+        feed_stay, feed_leave, resid_own, normed_two, hidden, grads, grad_res, stay, leave,
+        gain_part_two, cot_all,
+    ) = middle(info, mixes, outs, resid, gain_two, ffns, tokens)
+    near = xor_tensor(leave, 1)
+    near_far = add_round(stay[1], near[1])
+    far = xor_tensor(near_far, 2)
+    halves, out_pair = weigh(
+        info, cot_all, after(hidden, near_far), normed_two, grads, mixes, grad_res, dp, own_dim
     )
-    near, near_far = xor_tensor(leave, 1), None
-    near_far = add_round(stay[1], near[1])
-    gmix = total((stay[0], near[0], xor_tensor(near_far, 2))).astype(BF16)
-
-    cot_all, _ = lax.optimization_barrier((cot_all, near_far))
-    down_halves, up_halves, halves = weigh(
-        info, cot_all, hidden, normed_two, grads, mixes, grad_res, feed, dp, own_dim
-    )
-    down_total, up_total = sum_dp(down_halves, dp), sum_dp(up_halves, dp)
-    gmix, *halves = lax.optimization_barrier((gmix, *halves))
-    feed_terms = scatter_tensor(*halves)
-    output = (resid_own + total([term[:rows] for term in feed_terms])).astype(BF16)
-    out_grad = total([term[rows:] for term in feed_terms]).astype(BF16)
-
-    gproj, stay, leave, row_stay, row_leave = back(
-        info, qkv, gmix, mixed, lse, grad_res, resid, gain_one, gain_part_two, wqkvo, sets,
-        cosine, sine,
+    ffn_sum = SumDp(halves, dp)
+    far, _ = lax.optimization_barrier((far, halves))
+    gmix = total((stay[0], near[0], far)).astype(BF16)
+
+    gproj, stay, leave, up_stay, up_leave, row_stay, row_leave = back(
+        info, qkv, gmix, mixed, lse, grad_res, resid, gain_one, gain_part_two, wqkv, sets,
+        cosine, sine, (feed_stay, feed_leave), out_pair,
     )
 
     near = xor_tensor(row_leave, 1)
     near_far = add_round(row_stay[1], near[1])
+    if dp == 8:
+        near_far, ffn_sum.first = lax.optimization_barrier((near_far, ffn_sum.first))
+        ffn_sum.across()
     far = xor_tensor(near_far, 2)
+    gproj = after(gproj, near_far)
+    attn_halves = weigh_turned(info, normed, gproj, dp, own_dim)
+    attn_sum = SumDp(attn_halves, dp)
+    far, _ = lax.optimization_barrier((far, attn_halves))
     row_total = total((row_stay[0], near[0], far)).astype(BF16)
-    digits = jnp.stack([ids_two // 256, ids_two % 256, ids_three // 256, ids_three % 256])
-    digits = jnp.pad(digits.astype(BF16), ((0, 12), (0, 0)))
     row_pack = jnp.concatenate([row_total, digits], axis=0)
+    up_near = xor_tensor(after(up_leave, near_far), 1)
+    up_near_far = after(add_round(up_stay[1], up_near[1]), far)
+    up_far = xor_tensor(up_near_far, 2)
+    below = add_round(add_round(up_stay[0], up_near[0]), up_far)
+    wide_grad, gains = below[: 2 * ng + width], below[2 * ng + width : 2 * ng + width + 2]
+    token_near = xor_tensor(after(leave, far), 1)
+    token_far = xor_tensor(after(add_round(stay[1], token_near[1]), up_near_far), 2)
     if dp == 8:
-        zero, two, one, three = double_dp(row_pack)
-        table_grad = spread(info, [zero], own_rows, ng, None, False)
+        folded = gains.reshape(2 * dim // (2 * ng), 2 * ng)
+        proj_sum = SumDp(turn(info, wide_grad, folded, dp, own_dim), dp)
+
+        def own_rows_first(zero):
+            zero, attn_sum.first, ffn_sum.second = lax.optimization_barrier(
+                (zero, attn_sum.first, ffn_sum.second)
+            )
+            ffn_sum.between()
+            return [spread(info, [zero], own_rows, ng, None, False)]
+
+        (_, two, one, three), (table_grad,) = double_dp(row_pack, (up_far,), own_rows_first)
         table_grad = spread(info, [two, one], own_rows, ng, table_grad, False)
+        attn_sum.first, token_far, table_grad = lax.optimization_barrier(
+            (attn_sum.first, token_far, table_grad)
+        )
+        attn_sum.across()
         table_grad = spread(info, [three], own_rows, ng, table_grad, True)
+        attn_sum.second, proj_sum.first = (
+            after(x, *table_grad) for x in (attn_sum.second, proj_sum.first)
+        )
+        attn_sum.between()
+        proj_sum.across()
+        ffn_sum.third, token_far, proj_sum.second = (
+            after(x, attn_sum.second) for x in (ffn_sum.third, token_far, proj_sum.second)
+        )
+        proj_sum.between()
     else:
         every = lax.all_gather(row_pack, "dp", axis=0)
 
@@ -989,25 +1085,17 @@
             piece = lax.dynamic_index_in_dim(every, i, 0, keepdims=False)
             return spread(info, [piece], own_rows, ng, so_far, False)
 
-        table_grad = lax.fori_loop(0, dp, put, jnp.zeros((2, own_rows, ng), F32))
-        table_grad = table_grad[0].T, table_grad[1].T
-
-    gproj, _ = lax.optimization_barrier((gproj, near_far))
-    attn_total = sum_dp(weigh_turned(info, normed, gproj, out_grad, dp, own_dim), dp)
-
-    stay, leave, _ = lax.optimization_barrier((stay, leave, far))
-    terms = scatter_tensor(stay, leave)
-    embed_grad = total([term[:rows] for term in terms]).astype(BF16)
-    below = add_round(add_round(terms[0][rows:], terms[1][rows:]), terms[2][rows:])
-    proj_up_grad, gains = below[: 2 * ng], below[2 * ng : 2 * ng + 2]
+        table_grad = lax.fori_loop(0, dp, put, jnp.zeros((2 * ng, own_rows), F32))
+        table_grad = table_grad[:ng], table_grad[ng:]
+    ffn_total, attn_total = ffn_sum.total(), attn_sum.total()
+    sums = total((stay[0], token_near[0], token_far))
+    embed_grad = sums[:rows].astype(BF16)
+    output = (resid_own + sums[rows:]).astype(BF16)
     if dp == 8:
-        folded = gains.reshape(2 * dim // (2 * ng), 2 * ng)
-        proj_up_total = sum_dp(turn(info, proj_up_grad, folded, dp, own_dim), dp)
-        gains = proj_up_total[own_dim:].reshape(2, dim)
+        proj_up_total = proj_sum.total()
+        gains = proj_up_total[own_dim:, : 2 * ng].reshape(2, dim)
     else:
-        empty = jnp.zeros((16, 2 * ng), BF16)
-        halves = turn(info, proj_up_grad, empty, dp, own_dim)[0][:, :own_dim]
-        proj_up_total = sum_dp([halves], dp)
+        proj_up_total = SumDp(turn(info, wide_grad, None, dp, own_dim), dp).total()
         gains = lax.psum(gains.astype(F32), "dp")
 
     return (
@@ -1016,16 +1104,16 @@
         table_grad[0].T,
         table_grad[1].T,
         proj_up_total[:own_dim, :ng].T,
-        proj_up_total[:own_dim, ng:].T,
+        proj_up_total[:own_dim, ng : 2 * ng].T,
         gains[0],
         attn_total[:, :width],
         attn_total[:, width : 2 * width],
         attn_total[:, 2 * width : 3 * width],
-        attn_total[:, 3 * width :].T,
+        proj_up_total[:own_dim, 2 * ng :].T,
         gains[1],
-        down_total[:, :units],
-        up_total,
-        down_total[:, units:].T,
+        ffn_total[:, :units],
+        ffn_total[:, units : 2 * units],
+        ffn_total[:, 2 * units :].T,
     )
 
 

time: 285 us -> 250 us (0.88)
  waiting for transfers between devices: 87.7 us -> 60.6 us
  Pallas kernels: 111 us -> 107 us
    ppermute x28 -> x25, waiting for transfers between devices: 68.4 us -> 39.9 us  [xor_dp(): return lax.ppermute(value, 'dp', [(i, i ^ step) for i in range(count)])]
    convert_element_type x4 -> x2, other arithmetic: 6.85 us -> 1.76 us  [the longest x1 0.94 us: shards(): gmix = total((stay[0], near[0], far)).astype(BF16)]
    pallas_call x2 -> x1, Pallas kernels: 5.89 us -> 2.84 us  [assemble(): pl.pallas_call(functools.partial(assemble_kernel, turn), out_shape=[jax.S...]
    ppermute x28 -> x25, starting transfers between devices: 34.3 us -> 32.9 us  [xor_dp(): return lax.ppermute(value, 'dp', [(i, i ^ step) for i in range(count)])]
    unnamed x83 -> x89, local copies, waits for them, and re-layouts: 7.1 us -> 8.09 us
    convert_element_type x13 -> x11, other arithmetic: 8.86 us -> 9.75 us  [add_round(): return (one.astype(F32) + two.astype(F32)).astype(BF16)]
  transfers between devices with their start and end apart: 48 -> 45, of which waited for: 19 -> 19; matrix products, arithmetic and copies ran while one was open for 10% -> 11% of each run, Pallas kernels for 32% -> 34%
where the time goes in v3:
time: 250 us
  Pallas kernels  107 us (43%)
  waiting for transfers between devices  60.6 us (24%)
  starting transfers between devices  44 us (18%)
  other arithmetic  21.7 us (9%)
  local copies, waits for them, and re-layouts  14.7 us (6%)
    ppermute x25, waiting for transfers between devices, xor_dp(): return lax.ppermute(value, 'dp', [(i, i ^ step) for i in range(count)])  39.9 us
    ppermute x25, starting transfers between devices, xor_dp(): return lax.ppermute(value, 'dp', [(i, i ^ step) for i in range(count)])  32.9 us
    ppermute x20, waiting for transfers between devices, xor_tensor(): return lax.ppermute(value, 'tensor', [(i, i ^ step) for i in range(4)])  20.7 us
    pallas_call x1, Pallas kernels, back(): pl.pallas_call(back_kernel, grid_spec=pltpu.PrefetchScalarGridSpec(num_sc...  20.1 us
    pallas_call x1, Pallas kernels, middle(): pl.pallas_call(middle_kernel, grid_spec=pltpu.PrefetchScalarGridSpec(num_...  19.8 us
    pallas_call x3, Pallas kernels, spread(): pl.pallas_call(functools.partial(spread_kernel, len(pieces), width, prior...  16.8 us
    pallas_call x3, Pallas kernels, lookup(): pl.pallas_call(functools.partial(lookup_kernel, owners, len(pieces), widt...  15 us
    pallas_call x1, Pallas kernels, front(): pl.pallas_call(front_kernel, grid_spec=pltpu.PrefetchScalarGridSpec(num_s...  14.2 us
  transfers between devices with their start and end apart: 45, of which 19 were waited for; matrix products, arithmetic and copies ran while one was open for 11% of the time, Pallas kernels for 34%

profile of v3, /device:TPU:0, one launch (start us, length us, event | category | flops | bytes accessed | tf_op | source)
XLA Modules:
  0.0 249.5 jit_solution(17658212990746866652)
XLA Ops:
  0.7 1.8 pack_first.1
  2.5 4.0 %collective-permute-start = (bf16[96,1152]{1,0:T(8,128)(2,1)}, bf16[96,1152]{1,0:T(8,128)(2,1)S(1)}, u32[]{:S(2)}, u32[]{:S(2)}) collective-permute-start(bf16[96,1152]{1,0:T(8,128)(2,1)} %pack_first.1), channel_id=1, source_target_pairs={{0,16},{4,20},{8,24},{12,28},{16,0},{20,4},{24,8},{28,12},{1,17},{... | collective-permute-start | bytes 663560 | tf_op jit(solution)/shard_map/ppermute | solution.py:26
  10.4 2.1 pack.1
  13.2 3.8 %collective-permute-done = bf16[96,1152]{1,0:T(8,128)(2,1)S(1)} collective-permute-done((bf16[96,1152]{1,0:T(8,128)(2,1)}, bf16[96,1152]{1,0:T(8,128)(2,1)S(1)}, u32[]{:S(2)}, u32[]{:S(2)}) %collective-permute-start) | collective-permute-done | bytes 221216 | tf_op jit(solution)/shard_map/ppermute | solution.py:26
  17.1 1.6 collective-permute-start.3
  19.4 1.5 collective-permute-start.8
  21.0 3.3 %collective-permute-start.1 = (bf16[96,768]{1,0:T(8,128)(2,1)}, bf16[96,768]{1,0:T(8,128)(2,1)}, u32[]{:S(2)}, u32[]{:S(2)}) collective-permute-start(bf16[96,768]{1,0:T(8,128)(2,1)} %get-tuple-element.100), channel_id=1, source_target_pairs={{0,16},{4,20},{8,24},{12,28},{16,0},{20,4},{24,8},{28,12},{1,17},{... | collective-permute-start | bytes 442376 | tf_op jit(solution)/shard_map/ppermute | solution.py:26
  25.6 4.2 %lookup.3.refs_4_ = bf16[96,1024]{1,0:T(8,128)(2,1)} custom-call(s32[10]{0:T(128)} %pad_add_fusion.1.refs_0_.info.par.who, s32[2,1024]{1,0:T(2,128)} %pad_add_fusion.refs_1_, bf16[2,96,1152]{2,1,0:T(8,128)(2,1)} %copy-done.4), custom_call_target="tpu_custom_call" | custom-call | tf_op jit(solution)/shard_map/lookup/pallas_call | solution.py:328
  29.8 3.0 %collective-permute-done.2.refs_2_.refs_4_ = bf16[2,96,1152]{2,1,0:T(8,128)(2,1)} collective-permute-done((bf16[2,96,1152]{2,1,0:T(8,128)(2,1)S(1)}, bf16[2,96,1152]{2,1,0:T(8,128)(2,1)}, u32[]{:S(2)}, u32[]{:S(2)}) %collective-permute-start.2) | collective-permute-done | bytes 442400 | tf_op jit(solution)/shard_map/ppermute | solution.py:26
  33.5 5.8 %lookup.4.refs_7_ = bf16[96,1024]{1,0:T(8,128)(2,1)} custom-call(s32[10]{0:T(128)} %pad_add_fusion.1.refs_0_.info.par.who, s32[2,1024]{1,0:T(2,128)} %pad_add_fusion.refs_1_, bf16[2,96,1152]{2,1,0:T(8,128)(2,1)} %collective-permute-done.2.refs_2_.refs_4_, bf16[2,96,1152]{2,1,0:T(8,128)(2,1)} %copy-done.10, bf16[96,1024]{1,0:T(8,128)(2,1)} %lookup.3.refs_4_), custom_call_target="tpu_custom_call" | custom-call | tf_op jit(solution)/shard_map/lookup/pallas_call | solution.py:328
  41.7 5.0 %collective-permute-start.14 = (bf16[96,1536]{1,0:T(8,128)(2,1)S(1)}, bf16[96,1536]{1,0:T(8,128)(2,1)}, u32[]{:S(2)}, u32[]{:S(2)}) collective-permute-start(bf16[96,1536]{1,0:T(8,128)(2,1)S(1)} %copy-done.35), channel_id=1, source_target_pairs={{0,16},{4,20},{8,24},{12,28},{16,0},{20,4},{24,8},{28,12},{1,17},{... | collective-permute-start | bytes 884744 | tf_op jit(solution)/shard_map/ppermute | solution.py:26
  47.5 5.0 %lookup.5.row0.up0 = bf16[96,1792]{1,0:T(8,128)(2,1)} custom-call(s32[10]{0:T(128)} %pad_add_fusion.1.refs_0_.info.par.who, s32[2,1024]{1,0:T(2,128)} %pad_add_fusion.refs_1_, bf16[2,96,1152]{2,1,0:T(8,128)(2,1)} %copy-done.11, bf16[2,96,1152]{2,1,0:T(8,128)(2,1)} %copy-done.4, bf16[2,96,1152]{2,1,0:T(8,128)(2,1)} %collective-permute-done.2.refs_2_.refs_4_, ...), custom_call_target="tpu_custom_call" | custom-call | tf_op jit(solution)/shard_map/lookup/pallas_call | solution.py:328
  52.5 2.1 collective-permute-done.5.refs_1_
  54.7 1.5 collective-permute-start.10
  56.6 1.8 collective-permute-done.14
  60.1 6.1 %collective-permute-done.13.refs_3_ = bf16[2,96,768]{2,1,0:T(8,128)(2,1)S(1)} collective-permute-done((bf16[2,96,768]{2,1,0:T(8,128)(2,1)}, bf16[2,96,768]{2,1,0:T(8,128)(2,1)S(1)}, u32[]{:S(2)}, u32[]{:S(2)}) %collective-permute-start.13) | collective-permute-done | bytes 294944 | tf_op jit(solution)/shard_map/ppermute | solution.py:26
  66.9 2.8 %assemble.1 = (bf16[576,768]{1,0:T(8,128)(2,1)}, bf16[192,768]{1,0:T(8,128)(2,1)}) custom-call(s32[10]{0:T(128)} %pad_add_fusion.1.refs_0_.info.par.who, bf16[2,96,768]{2,1,0:T(8,128)(2,1)} %copy-done.21, bf16[2,96,768]{2,1,0:T(8,128)(2,1)} %collective-permute-done.5.refs_1_, bf16[2,96,768]{2,1,0:T(8,128)(2,1)} %collective-permute-done.6.refs_2_, ...), custom_call_target="tpu_custom_call" | custom-call | tf_op jit(solution)/shard_map/assemble/pallas_call | solution.py:125
  72.0 14.2 %front.1 = (f32[1024,768]{1,0:T(8,128)}, bf16[1024,768]{1,0:T(8,128)(2,1)}, bf16[576,1024]{1,0:T(8,128)(2,1)}, bf16[192,1024]{1,0:T(8,128)(2,1)}, f32[8,1024]{1,0:T(8,128)}) custom-call(s32[10]{0:T(128)} %pad_add_fusion.1.refs_0_.info.par.who, bf16[96,1792]{1,0:T(8,128)(2,1)} %lookup.5.row0.up0, bf16[96,1792]{1,0:T(8,128)(2,1)} %copy-done.2, ...), custom_call_target="tpu_custom_call" | custom-call | tf_op jit(solution)/shard_map/front/pallas_call | solution.py:497
  86.3 1.6 collective-permute-start.17
  88.4 9.3 %collective-permute-done.17.mix2.refs_2_ = bf16[192,1024]{1,0:T(8,128)(2,1)S(1)} collective-permute-done((bf16[192,1024]{1,0:T(8,128)(2,1)}, bf16[192,1024]{1,0:T(8,128)(2,1)S(1)}, u32[]{:S(2)}, u32[]{:S(2)}) %collective-permute-start.17) | collective-permute-done | bytes 393248 | tf_op jit(solution)/shard_map/ppermute | solution.py:22
  98.2 1.7 collective-permute-done.19.out1
  100.5 2.6 %collective-permute-done.23.ffn3 = bf16[2,96,1536]{2,1,0:T(8,128)(2,1)S(1)} collective-permute-done((bf16[2,96,1536]{2,1,0:T(8,128)(2,1)}, bf16[2,96,1536]{2,1,0:T(8,128)(2,1)S(1)}, u32[]{:S(2)}, u32[]{:S(2)}) %collective-permute-start.23) | collective-permute-done | bytes 589856 | tf_op jit(solution)/shard_map/ppermute | solution.py:26
  104.1 19.8 %middle.1 = (bf16[2,256,768]{2,1,0:T(8,128)(2,1)}, bf16[2,256,768]{2,1,0:T(8,128)(2,1)}, f32[256,768]{1,0:T(8,128)}, bf16[1024,768]{1,0:T(8,128)(2,1)}, bf16[102...) custom-call(s32[10]{0:T(128)} %pad_add_fusion.1.refs_0_.info.par.who, ...), custom_call_target="tpu_custom_call" | custom-call | tf_op jit(solution)/shard_map/middle/pallas_call | solution.py:642
  124.0 2.5 collective-permute-done.24
  128.2 8.5 %weigh.1 = (bf16[4,96,1536]{2,1,0:T(8,128)(2,1)}, bf16[4,96,1536]{2,1,0:T(8,128)(2,1)}, bf16[2,192,768]{2,1,0:T(8,128)(2,1)}, bf16[2,192,768]{2,1,0:T(8,128)(2,1)}) custom-call(s32[10]{0:T(128)} %pad_add_fusion.1.refs_0_.info.par.who, bf16[1024,768]{1,0:T(8,128)(2,1)} %get-tuple-element.127.cot, bf16[1024,512]{1,0:T(8,128)(2,1)} %get-tuple-element.129.hidden, ...), custom_call_target="tpu_custom_call" | custom-call | tf_op jit(solution)/shard_map/weigh/pallas_call | solution.py:221
  139.7 20.1 %back.1 = (bf16[576,1024]{1,0:T(8,128)(2,1)}, bf16[2,512,768]{2,1,0:T(8,128)(2,1)}, bf16[2,512,768]{2,1,0:T(8,128)(2,1)}, bf16[2,304,768]{2,1,0:T(8,128)(2,1)}, ...) custom-call(s32[10]{0:T(128)} %pad_add_fusion.1.refs_0_.info.par.who, ...), custom_call_target="tpu_custom_call" | custom-call | tf_op jit(solution)/shard_map/back/pallas_call | solution.py:860
  159.9 1.9 collective-permute-done.26
  161.8 1.8 fusion.10
  164.7 1.6 collective-permute-start.28
  166.2 4.0 %split.2 = (bf16[4,96,576]{2,1,0:T(8,128)(2,1)}, bf16[4,96,576]{2,1,0:T(8,128)(2,1)}) custom-call(s32[10]{0:T(128)} %pad_add_fusion.1.refs_0_.info.par.who, bf16[1024,768]{1,0:T(8,128)(2,1)} %get-tuple-element.147.left, bf16[576,1024]{1,0:T(8,128)(2,1)} %get-tuple-element.149.right), custom_call_target="tpu_custom_call" | custom-call | tf_op jit(solution)/shard_map/split/pallas_call | solution.py:256
  170.2 2.0 collective-permute-done.28
  176.7 1.5 collective-permute-start.32
  179.3 8.7 %collective-permute-done.30 = bf16[112,1024]{1,0:T(8,128)(2,1)S(1)} collective-permute-done((bf16[112,1024]{1,0:T(8,128)(2,1)S(1)}, bf16[112,1024]{1,0:T(8,128)(2,1)S(1)}, u32[]{:S(2)}, u32[]{:S(2)}) %collective-permute-start.30) | collective-permute-done | bytes 229408 | tf_op jit(solution)/shard_map/ppermute | solution.py:26
  189.4 1.8 collective-permute-start.37
  193.1 1.5 collective-permute-start.35
  195.6 3.4 %collective-permute-done.34 = bf16[2,96,1536]{2,1,0:T(8,128)(2,1)} collective-permute-done((bf16[2,96,1536]{2,1,0:T(8,128)(2,1)S(1)}, bf16[2,96,1536]{2,1,0:T(8,128)(2,1)}, u32[]{:S(2)}, u32[]{:S(2)}) %collective-permute-start.34) | collective-permute-done | bytes 589856 | tf_op jit(solution)/shard_map/ppermute | solution.py:26
  199.6 2.1 split.3
  201.7 1.7 collective-permute-start.40
  203.4 4.7 %spread.3.refs_3_ = f32[96,1024]{1,0:T(8,128)} custom-call(s32[10]{0:T(128)} %pad_add_fusion.1.refs_0_.info.par.who, bf16[2,112,1024]{2,1,0:T(8,128)(2,1)} %copy-done.9), custom_call_target="tpu_custom_call" | custom-call | tf_op jit(solution)/shard_map/spread/pallas_call | solution.py:374
  209.1 1.8 fusion.9
  210.9 7.3 %spread.4.refs_2_ = f32[96,1024]{1,0:T(8,128)} custom-call(s32[10]{0:T(128)} %pad_add_fusion.1.refs_0_.info.par.who, bf16[2,112,1024]{2,1,0:T(8,128)(2,1)} %collective-permute-done.36.refs_1_, bf16[2,112,1024]{2,1,0:T(8,128)(2,1)} %collective-permute-done.37.refs_2_, f32[96,1024]{1,0:T(8,128)} %spread.3.refs_3_), custom_call_target="tpu_custom_call" | custom-call | tf_op jit(solution)/shard_map/spread/pallas_call | solution.py:374
  218.2 1.9 add_convert_fusion.8
  220.9 4.8 %spread.5 = (f32[48,1024]{1,0:T(8,128)}, f32[48,1024]{1,0:T(8,128)}) custom-call(s32[10]{0:T(128)} %pad_add_fusion.1.refs_0_.info.par.who, bf16[2,112,1024]{2,1,0:T(8,128)(2,1)} %copy-done.30, f32[96,1024]{1,0:T(8,128)} %spread.4.refs_2_), custom_call_target="tpu_custom_call" | custom-call | tf_op jit(solution)/shard_map/spread/pallas_call | solution.py:374
  225.7 2.6 %collective-permute-start.38 = (bf16[2,96,576]{2,1,0:T(8,128)(2,1)}, bf16[2,96,576]{2,1,0:T(8,128)(2,1)S(1)}, u32[]{:S(2)}, u32[]{:S(2)}) collective-permute-start(bf16[2,96,576]{2,1,0:T(8,128)(2,1)} %get-tuple-element.227), channel_id=1, source_target_pairs={{0,8},{4,12},{8,0},{12,4},{16,24},{20,28},{24,16},{28,20},{1,9},{5... | collective-permute-start | bytes 663560 | tf_op jit(solution)/shard_map/ppermute | solution.py:26
  229.6 5.0 %collective-permute-done.38 = bf16[2,96,576]{2,1,0:T(8,128)(2,1)S(1)} collective-permute-done((bf16[2,96,576]{2,1,0:T(8,128)(2,1)}, bf16[2,96,576]{2,1,0:T(8,128)(2,1)S(1)}, u32[]{:S(2)}, u32[]{:S(2)}) %collective-permute-start.38) | collective-permute-done | bytes 221216 | tf_op jit(solution)/shard_map/ppermute | solution.py:26
  236.7 2.1 collective-permute-start.42
  238.8 1.4 bitcast_add_fusion
  246.4 2.3 collective-permute-done.43
  (196 shorter events, 46.6 us)
Async XLA Ops:
  2.5 14.5 %collective-permute-start = (bf16[96,1152]{1,0:T(8,128)(2,1)}, bf16[96,1152]{1,0:T(8,128)(2,1)S(1)}, u32[]{:S(2)}, u32[]{:S(2)}) collective-permute-start(bf16[96,1152]{1,0:T(8,128)(2,1)} %pack_first.1), channel_id=1, source_target_pairs={{0,16},{4,20},{8,24},{12,28},{16,0},{20,4},{24,8},{28,12},{1,17},{... | collective-permute-start | bytes 663560 | tf_op jit(solution)/shard_map/ppermute | solution.py:26
  7.8 31.6 %copy-start = (bf16[2,256,768]{2,1,0:T(8,128)(2,1)}, bf16[2,256,768]{2,1,0:T(8,128)(2,1)S(1)}, u32[]{:S(2)}) copy-start(bf16[2,256,768]{2,1,0:T(8,128)(2,1)S(1)} %pad_maximum_fusion.emb0.cot0) | copy-start | bytes 2359300
  7.8 25.0 %collective-permute-start.4 = (bf16[2,256,768]{2,1,0:T(8,128)(2,1)S(1)}, bf16[2,256,768]{2,1,0:T(8,128)(2,1)S(1)}, u32[]{:S(2)}, u32[]{:S(2)}) collective-permute-start(bf16[2,256,768]{2,1,0:T(8,128)(2,1)S(1)} %pad_maximum_fusion.emb0.cot0), channel_id=1, source_target_pairs={{0,1},{1,0},{2,3},{3,2},{4,5},{5,4},{6,7},{7,6},{8,9},{9,8},{10,11... | collective-permute-start | bytes 2359304 | tf_op jit(solution)/shard_map/ppermute | solution.py:22
  17.0 24.7 %copy-start.35 = (bf16[96,1536]{1,0:T(8,128)(2,1)S(1)}, bf16[96,1536]{1,0:T(8,128)(2,1)}, u32[]{:S(2)}) copy-start(bf16[96,1536]{1,0:T(8,128)(2,1)} %get-tuple-element.112) | copy-start | bytes 884740
  17.1 12.7 %collective-permute-start.3 = (bf16[2,96,1152]{2,1,0:T(8,128)(2,1)S(1)}, bf16[2,96,1152]{2,1,0:T(8,128)(2,1)S(1)}, u32[]{:S(2)}, u32[]{:S(2)}) collective-permute-start(bf16[2,96,1152]{2,1,0:T(8,128)(2,1)S(1)} %pad_maximum_fusion.3.refs_2_.refs_3_), channel_id=1, source_target_pairs={{0,4},{4,0},{8,12},{12,8},{16,20},{20,16},{24,28},{28,24},{1,5},{5... | collective-permute-start | bytes 1327112 | tf_op jit(solution)/shard_map/ppermute | solution.py:26
  18.7 14.1 %collective-permute-start.2 = (bf16[2,96,1152]{2,1,0:T(8,128)(2,1)S(1)}, bf16[2,96,1152]{2,1,0:T(8,128)(2,1)}, u32[]{:S(2)}, u32[]{:S(2)}) collective-permute-start(bf16[2,96,1152]{2,1,0:T(8,128)(2,1)S(1)} %pad_maximum_fusion.3.refs_2_.refs_3_), channel_id=1, source_target_pairs={{0,8},{4,12},{8,0},{12,4},{16,24},{20,28},{24,16},{28,20},{1,9},{5... | collective-permute-start | bytes 1327112 | tf_op jit(solution)/shard_map/ppermute | solution.py:26
  19.4 33.1 %collective-permute-start.8 = (bf16[2,256,768]{2,1,0:T(8,128)(2,1)S(1)}, bf16[2,256,768]{2,1,0:T(8,128)(2,1)S(1)}, u32[]{:S(2)}, u32[]{:S(2)}) collective-permute-start(bf16[2,256,768]{2,1,0:T(8,128)(2,1)S(1)} %pad_maximum_fusion.emb0.cot0), channel_id=1, source_target_pairs={{0,2},{1,3},{2,0},{3,1},{4,6},{5,7},{6,4},{7,5},{8,10},{9,11},{10,... | collective-permute-start | bytes 2359304 | tf_op jit(solution)/shard_map/ppermute | solution.py:22
  21.0 18.3 %collective-permute-start.1 = (bf16[96,768]{1,0:T(8,128)(2,1)}, bf16[96,768]{1,0:T(8,128)(2,1)}, u32[]{:S(2)}, u32[]{:S(2)}) collective-permute-start(bf16[96,768]{1,0:T(8,128)(2,1)} %get-tuple-element.100), channel_id=1, source_target_pairs={{0,16},{4,20},{8,24},{12,28},{16,0},{20,4},{24,8},{28,12},{1,17},{... | collective-permute-start | bytes 442376 | tf_op jit(solution)/shard_map/ppermute | solution.py:26
  32.8 14.0 %collective-permute-start.7 = (bf16[2,96,1152]{2,1,0:T(8,128)(2,1)}, bf16[2,96,1152]{2,1,0:T(8,128)(2,1)S(1)}, u32[]{:S(2)}, u32[]{:S(2)}) collective-permute-start(bf16[2,96,1152]{2,1,0:T(8,128)(2,1)} %collective-permute-done.2.refs_2_.refs_4_), channel_id=1, source_target_pairs={{0,4},{4,0},{8,12},{12,8},{16,20},{20,16},{24,28},{28,24},{1,5},{5... | collective-permute-start | bytes 1327112 | tf_op jit(solution)/shard_map/ppermute | solution.py:26
  40.4 12.1 %collective-permute-start.6 = (bf16[2,96,768]{2,1,0:T(8,128)(2,1)S(1)}, bf16[2,96,768]{2,1,0:T(8,128)(2,1)}, u32[]{:S(2)}, u32[]{:S(2)}) collective-permute-start(bf16[2,96,768]{2,1,0:T(8,128)(2,1)S(1)} %pad_maximum_fusion.4.refs_0_), channel_id=1, source_target_pairs={{0,4},{4,0},{8,12},{12,8},{16,20},{20,16},{24,28},{28,24},{1,5},{5... | collective-permute-start | bytes 884744 | tf_op jit(solution)/shard_map/ppermute | solution.py:26
  41.7 12.9 %collective-permute-start.5 = (bf16[2,96,768]{2,1,0:T(8,128)(2,1)S(1)}, bf16[2,96,768]{2,1,0:T(8,128)(2,1)}, u32[]{:S(2)}, u32[]{:S(2)}) collective-permute-start(bf16[2,96,768]{2,1,0:T(8,128)(2,1)S(1)} %pad_maximum_fusion.4.refs_0_), channel_id=1, source_target_pairs={{0,8},{4,12},{8,0},{12,4},{16,24},{20,28},{24,16},{28,20},{1,9},{5... | collective-permute-start | bytes 884744 | tf_op jit(solution)/shard_map/ppermute | solution.py:26
  41.7 16.7 %collective-permute-start.14 = (bf16[96,1536]{1,0:T(8,128)(2,1)S(1)}, bf16[96,1536]{1,0:T(8,128)(2,1)}, u32[]{:S(2)}, u32[]{:S(2)}) collective-permute-start(bf16[96,1536]{1,0:T(8,128)(2,1)S(1)} %copy-done.35), channel_id=1, source_target_pairs={{0,16},{4,20},{8,24},{12,28},{16,0},{20,4},{24,8},{28,12},{1,17},{... | collective-permute-start | bytes 884744 | tf_op jit(solution)/shard_map/ppermute | solution.py:26
  54.7 15.7 %collective-permute-start.12 = (bf16[2,256,768]{2,1,0:T(8,128)(2,1)S(1)}, bf16[2,256,768]{2,1,0:T(8,128)(2,1)S(1)}, u32[]{:S(2)}, u32[]{:S(2)}) collective-permute-start(bf16[2,256,768]{2,1,0:T(8,128)(2,1)S(1)} %collective-permute-done.8.emb2.cot2), channel_id=1, source_target_pairs={{0,1},{1,0},{2,3},{3,2},{4,5},{5,4},{6,7},{7,6},{8,9},{9,8},{10,11... | collective-permute-start | bytes 2359304 | tf_op jit(solution)/shard_map/ppermute | solution.py:22
  54.7 12.3 %collective-permute-start.10 = (bf16[96,1792]{1,0:T(8,128)(2,1)}, bf16[96,1792]{1,0:T(8,128)(2,1)S(1)}, u32[]{:S(2)}, u32[]{:S(2)}) collective-permute-start(bf16[96,1792]{1,0:T(8,128)(2,1)} %lookup.5.row0.up0), channel_id=1, source_target_pairs={{0,2},{1,3},{2,0},{3,1},{4,6},{5,7},{6,4},{7,5},{8,10},{9,11},{10,... | collective-permute-start | bytes 1032200 | tf_op jit(solution)/shard_map/ppermute | solution.py:22
  56.1 10.1 %collective-permute-start.13 = (bf16[2,96,768]{2,1,0:T(8,128)(2,1)}, bf16[2,96,768]{2,1,0:T(8,128)(2,1)S(1)}, u32[]{:S(2)}, u32[]{:S(2)}) collective-permute-start(bf16[2,96,768]{2,1,0:T(8,128)(2,1)} %collective-permute-done.5.refs_1_), channel_id=1, source_target_pairs={{0,4},{4,0},{8,12},{12,8},{16,20},{20,16},{24,28},{28,24},{1,5},{5... | collective-permute-start | bytes 884744 | tf_op jit(solution)/shard_map/ppermute | solution.py:26
  56.6 13.1 %collective-permute-start.9 = (bf16[96,1792]{1,0:T(8,128)(2,1)}, bf16[96,1792]{1,0:T(8,128)(2,1)S(1)}, u32[]{:S(2)}, u32[]{:S(2)}) collective-permute-start(bf16[96,1792]{1,0:T(8,128)(2,1)} %lookup.5.row0.up0), channel_id=1, source_target_pairs={{0,1},{1,0},{2,3},{3,2},{4,5},{5,4},{6,7},{7,6},{8,9},{9,8},{10,11... | collective-permute-start | bytes 1032200 | tf_op jit(solution)/shard_map/ppermute | solution.py:22
  59.4 26.8 %copy-start.8 = (bf16[2,96,1536]{2,1,0:T(8,128)(2,1)}, bf16[2,96,1536]{2,1,0:T(8,128)(2,1)S(1)}, u32[]{:S(2)}) copy-start(bf16[2,96,1536]{2,1,0:T(8,128)(2,1)S(1)} %pad_maximum_fusion.1.ffn0) | copy-start | bytes 1769476
  59.4 28.4 %collective-permute-start.22 = (bf16[2,96,1536]{2,1,0:T(8,128)(2,1)S(1)}, bf16[2,96,1536]{2,1,0:T(8,128)(2,1)}, u32[]{:S(2)}, u32[]{:S(2)}) collective-permute-start(bf16[2,96,1536]{2,1,0:T(8,128)(2,1)S(1)} %pad_maximum_fusion.1.ffn0), channel_id=1, source_target_pairs={{0,4},{4,0},{8,12},{12,8},{16,20},{20,16},{24,28},{28,24},{1,5},{5... | collective-permute-start | bytes 1769480 | tf_op jit(solution)/shard_map/ppermute | solution.py:26
  66.2 21.6 %collective-permute-start.21 = (bf16[2,96,1536]{2,1,0:T(8,128)(2,1)S(1)}, bf16[2,96,1536]{2,1,0:T(8,128)(2,1)}, u32[]{:S(2)}, u32[]{:S(2)}) collective-permute-start(bf16[2,96,1536]{2,1,0:T(8,128)(2,1)S(1)} %pad_maximum_fusion.1.ffn0), channel_id=1, source_target_pairs={{0,8},{4,12},{8,0},{12,4},{16,24},{20,28},{24,16},{28,20},{1,9},{5... | collective-permute-start | bytes 1769480 | tf_op jit(solution)/shard_map/ppermute | solution.py:26
  66.9 3.5 %collective-permute-start.11 = (bf16[96,1792]{1,0:T(8,128)(2,1)S(1)}, bf16[96,1792]{1,0:T(8,128)(2,1)S(1)}, u32[]{:S(2)}, u32[]{:S(2)}) collective-permute-start(bf16[96,1792]{1,0:T(8,128)(2,1)S(1)} %collective-permute-done.10.row2.up2), channel_id=1, source_target_pairs={{0,1},{1,0},{2,3},{3,2},{4,5},{5,4},{6,7},{7,6},{8,9},{9,8},{10,11... | collective-permute-start | bytes 1032200 | tf_op jit(solution)/shard_map/ppermute | solution.py:22
  69.8 16.5 %collective-permute-start.15 = (bf16[192,768]{1,0:T(8,128)(2,1)}, bf16[192,768]{1,0:T(8,128)(2,1)}, u32[]{:S(2)}, u32[]{:S(2)}) collective-permute-start(bf16[192,768]{1,0:T(8,128)(2,1)} %get-tuple-element.117.out0), channel_id=1, source_target_pairs={{0,2},{1,3},{2,0},{3,1},{4,6},{5,7},{6,4},{7,5},{8,10},{9,11},{10,... | collective-permute-start | bytes 884744 | tf_op jit(solution)/shard_map/ppermute | solution.py:22
  86.3 11.4 %collective-permute-start.17 = (bf16[192,1024]{1,0:T(8,128)(2,1)}, bf16[192,1024]{1,0:T(8,128)(2,1)S(1)}, u32[]{:S(2)}, u32[]{:S(2)}) collective-permute-start(bf16[192,1024]{1,0:T(8,128)(2,1)} %get-tuple-element.118.mix0.refs_0_.mixed), channel_id=1, source_target_pairs={{0,2},{1,3},{2,0},{3,1},{4,6},{5,7},{6,4},{7,5},{8,10},{9,11},{10,... | collective-permute-start | bytes 1179656 | tf_op jit(solution)/shard_map/ppermute | solution.py:22
  87.8 15.2 %collective-permute-start.23 = (bf16[2,96,1536]{2,1,0:T(8,128)(2,1)}, bf16[2,96,1536]{2,1,0:T(8,128)(2,1)S(1)}, u32[]{:S(2)}, u32[]{:S(2)}) collective-permute-start(bf16[2,96,1536]{2,1,0:T(8,128)(2,1)} %collective-permute-done.21.ffn1), channel_id=1, source_target_pairs={{0,4},{4,0},{8,12},{12,8},{16,20},{20,16},{24,28},{28,24},{1,5},{5... | collective-permute-start | bytes 1769480 | tf_op jit(solution)/shard_map/ppermute | solution.py:26
  88.3 12.1 %collective-permute-start.16 = (bf16[192,1024]{1,0:T(8,128)(2,1)}, bf16[192,1024]{1,0:T(8,128)(2,1)S(1)}, u32[]{:S(2)}, u32[]{:S(2)}) collective-permute-start(bf16[192,1024]{1,0:T(8,128)(2,1)} %get-tuple-element.118.mix0.refs_0_.mixed), channel_id=1, source_target_pairs={{0,1},{1,0},{2,3},{3,2},{4,5},{5,4},{6,7},{7,6},{8,9},{9,8},{10,11... | collective-permute-start | bytes 1179656 | tf_op jit(solution)/shard_map/ppermute | solution.py:22
  97.7 5.4 %collective-permute-start.18 = (bf16[192,1024]{1,0:T(8,128)(2,1)S(1)}, bf16[192,1024]{1,0:T(8,128)(2,1)S(1)}, u32[]{:S(2)}, u32[]{:S(2)}) collective-permute-start(bf16[192,1024]{1,0:T(8,128)(2,1)S(1)} %collective-permute-done.17.mix2.refs_2_), channel_id=1, source_target_pairs={{0,1},{1,0},{2,3},{3,2},{4,5},{5,4},{6,7},{7,6},{8,9},{9,8},{10,11... | collective-permute-start | bytes 1179656 | tf_op jit(solution)/shard_map/ppermute | solution.py:22
  97.7 2.2 collective-permute-start.19
  98.2 2.3 collective-permute-start.20
  123.9 2.6 %collective-permute-start.24 = (bf16[2,192,1024]{2,1,0:T(8,128)(2,1)}, bf16[2,192,1024]{2,1,0:T(8,128)(2,1)S(1)}, u32[]{:S(2)}, u32[]{:S(2)}) collective-permute-start(bf16[2,192,1024]{2,1,0:T(8,128)(2,1)} %get-tuple-element.126), channel_id=1, source_target_pairs={{0,1},{1,0},{2,3},{3,2},{4,5},{5,4},{6,7},{7,6},{8,9},{9,8},{10,11... | collective-permute-start | bytes 2359304 | tf_op jit(solution)/shard_map/ppermute | solution.py:22
  127.6 11.2 %collective-permute-start.25 = (bf16[192,1024]{1,0:T(8,128)(2,1)S(1)}, bf16[192,1024]{1,0:T(8,128)(2,1)S(1)}, u32[]{:S(2)}, u32[]{:S(2)}) collective-permute-start(bf16[192,1024]{1,0:T(8,128)(2,1)S(1)} %fusion.6), channel_id=1, source_target_pairs={{0,2},{1,3},{2,0},{3,1},{4,6},{5,7},{6,4},{7,5},{8,10},{9,11},{10,... | collective-permute-start | bytes 1179656 | tf_op jit(solution)/shard_map/ppermute | solution.py:22
  136.7 27.9 %collective-permute-start.27 = (bf16[4,96,1536]{2,1,0:T(8,128)(2,1)}, bf16[4,96,1536]{2,1,0:T(8,128)(2,1)S(1)}, u32[]{:S(2)}, u32[]{:S(2)}) collective-permute-start(bf16[4,96,1536]{2,1,0:T(8,128)(2,1)} %get-tuple-element.133), channel_id=1, source_target_pairs={{0,4},{4,0},{8,12},{12,8},{16,20},{20,16},{24,28},{28,24},{1,5},{5... | collective-permute-start | bytes 3538952 | tf_op jit(solution)/shard_map/ppermute | solution.py:26
  159.8 2.0 collective-permute-start.26
  164.7 11.0 %collective-permute-start.31 = (bf16[2,304,768]{2,1,0:T(8,128)(2,1)}, bf16[2,304,768]{2,1,0:T(8,128)(2,1)S(1)}, u32[]{:S(2)}, u32[]{:S(2)}) collective-permute-start(bf16[2,304,768]{2,1,0:T(8,128)(2,1)} %get-tuple-element.156), channel_id=1, source_target_pairs={{0,1},{1,0},{2,3},{3,2},{4,5},{5,4},{6,7},{7,6},{8,9},{9,8},{10,11... | collective-permute-start | bytes 2801672 | tf_op jit(solution)/shard_map/ppermute | solution.py:22
  164.7 7.6 %collective-permute-start.28 = (bf16[96,1024]{1,0:T(8,128)(2,1)}, bf16[96,1024]{1,0:T(8,128)(2,1)}, u32[]{:S(2)}, u32[]{:S(2)}) collective-permute-start(bf16[96,1024]{1,0:T(8,128)(2,1)} %fusion.10), channel_id=1, source_target_pairs={{0,2},{1,3},{2,0},{3,1},{4,6},{5,7},{6,4},{7,5},{8,10},{9,11},{10,... | collective-permute-start | bytes 589832 | tf_op jit(solution)/shard_map/ppermute | solution.py:22
  172.3 19.5 %collective-permute-start.29 = (bf16[2,512,768]{2,1,0:T(8,128)(2,1)}, bf16[2,512,768]{2,1,0:T(8,128)(2,1)S(1)}, u32[]{:S(2)}, u32[]{:S(2)}) collective-permute-start(bf16[2,512,768]{2,1,0:T(8,128)(2,1)} %get-tuple-element.153), channel_id=1, source_target_pairs={{0,1},{1,0},{2,3},{3,2},{4,5},{5,4},{6,7},{7,6},{8,9},{9,8},{10,11... | collective-permute-start | bytes 4718600 | tf_op jit(solution)/shard_map/ppermute | solution.py:22
  172.3 23.3 %collective-permute-start.33 = (bf16[4,96,576]{2,1,0:T(8,128)(2,1)}, bf16[4,96,576]{2,1,0:T(8,128)(2,1)}, u32[]{:S(2)}, u32[]{:S(2)}) collective-permute-start(bf16[4,96,576]{2,1,0:T(8,128)(2,1)} %get-tuple-element.150), channel_id=1, source_target_pairs={{0,4},{4,0},{8,12},{12,8},{16,20},{20,16},{24,28},{28,24},{1,5},{5... | collective-permute-start | bytes 1327112 | tf_op jit(solution)/shard_map/ppermute | solution.py:26
  174.2 13.7 %collective-permute-start.30 = (bf16[112,1024]{1,0:T(8,128)(2,1)S(1)}, bf16[112,1024]{1,0:T(8,128)(2,1)S(1)}, u32[]{:S(2)}, u32[]{:S(2)}) collective-permute-start(bf16[112,1024]{1,0:T(8,128)(2,1)S(1)} %get-tuple-element.237), channel_id=1, source_target_pairs={{0,16},{4,20},{8,24},{12,28},{16,0},{20,4},{24,8},{28,12},{1,17},{... | collective-permute-start | bytes 688136 | tf_op jit(solution)/shard_map/ppermute | solution.py:26
  176.7 12.6 %collective-permute-start.32 = (bf16[304,768]{1,0:T(8,128)(2,1)S(1)}, bf16[304,768]{1,0:T(8,128)(2,1)S(1)}, u32[]{:S(2)}, u32[]{:S(2)}) collective-permute-start(bf16[304,768]{1,0:T(8,128)(2,1)S(1)} %fusion.4), channel_id=1, source_target_pairs={{0,2},{1,3},{2,0},{3,1},{4,6},{5,7},{6,4},{7,5},{8,10},{9,11},{10,... | collective-permute-start | bytes 1400840 | tf_op jit(solution)/shard_map/ppermute | solution.py:22
  178.6 20.4 %collective-permute-start.34 = (bf16[2,96,1536]{2,1,0:T(8,128)(2,1)S(1)}, bf16[2,96,1536]{2,1,0:T(8,128)(2,1)}, u32[]{:S(2)}, u32[]{:S(2)}) collective-permute-start(bf16[2,96,1536]{2,1,0:T(8,128)(2,1)S(1)} %get-tuple-element.225), channel_id=1, source_target_pairs={{0,8},{4,12},{8,0},{12,4},{16,24},{20,28},{24,16},{28,20},{1,9},{5... | collective-permute-start | bytes 1769480 | tf_op jit(solution)/shard_map/ppermute | solution.py:26
  189.4 18.7 %collective-permute-start.37 = (bf16[2,112,1024]{2,1,0:T(8,128)(2,1)S(1)}, bf16[2,112,1024]{2,1,0:T(8,128)(2,1)}, u32[]{:S(2)}, u32[]{:S(2)}) collective-permute-start(bf16[2,112,1024]{2,1,0:T(8,128)(2,1)S(1)} %pad_maximum_fusion.2.refs_1_), channel_id=1, source_target_pairs={{0,4},{4,0},{8,12},{12,8},{16,20},{20,16},{24,28},{28,24},{1,5},{5... | collective-permute-start | bytes 1376264 | tf_op jit(solution)/shard_map/ppermute | solution.py:26
  191.2 16.9 %collective-permute-start.36 = (bf16[2,112,1024]{2,1,0:T(8,128)(2,1)S(1)}, bf16[2,112,1024]{2,1,0:T(8,128)(2,1)}, u32[]{:S(2)}, u32[]{:S(2)}) collective-permute-start(bf16[2,112,1024]{2,1,0:T(8,128)(2,1)S(1)} %pad_maximum_fusion.2.refs_1_), channel_id=1, source_target_pairs={{0,8},{4,12},{8,0},{12,4},{16,24},{20,28},{24,16},{28,20},{1,9},{5... | collective-permute-start | bytes 1376264 | tf_op jit(solution)/shard_map/ppermute | solution.py:26
  193.1 25.1 %collective-permute-start.35 = (bf16[512,768]{1,0:T(8,128)(2,1)}, bf16[512,768]{1,0:T(8,128)(2,1)}, u32[]{:S(2)}, u32[]{:S(2)}) collective-permute-start(bf16[512,768]{1,0:T(8,128)(2,1)} %fusion.1), channel_id=1, source_target_pairs={{0,2},{1,3},{2,0},{3,1},{4,6},{5,7},{6,4},{7,5},{8,10},{9,11},{10,... | collective-permute-start | bytes 2359304 | tf_op jit(solution)/shard_map/ppermute | solution.py:22
  201.7 24.0 %collective-permute-start.40 = (bf16[4,112,288]{2,1,0:T(8,128)(2,1)}, bf16[4,112,288]{2,1,0:T(8,128)(2,1)}, u32[]{:S(2)}, u32[]{:S(2)}) collective-permute-start(bf16[4,112,288]{2,1,0:T(8,128)(2,1)} %get-tuple-element.174), channel_id=1, source_target_pairs={{0,4},{4,0},{8,12},{12,8},{16,20},{20,16},{24,28},{28,24},{1,5},{5... | collective-permute-start | bytes 774152 | tf_op jit(solution)/shard_map/ppermute | solution.py:26
  208.1 12.0 %collective-permute-start.39 = (bf16[2,112,1024]{2,1,0:T(8,128)(2,1)}, bf16[2,112,1024]{2,1,0:T(8,128)(2,1)S(1)}, u32[]{:S(2)}, u32[]{:S(2)}) collective-permute-start(bf16[2,112,1024]{2,1,0:T(8,128)(2,1)} %collective-permute-done.36.refs_1_), channel_id=1, source_target_pairs={{0,4},{4,0},{8,12},{12,8},{16,20},{20,16},{24,28},{28,24},{1,5},{5... | collective-permute-start | bytes 1376264 | tf_op jit(solution)/shard_map/ppermute | solution.py:26
  210.9 23.8 %collective-permute-start.44 = (bf16[96,1536]{1,0:T(8,128)(2,1)}, bf16[96,1536]{1,0:T(8,128)(2,1)}, u32[]{:S(2)}, u32[]{:S(2)}) collective-permute-start(bf16[96,1536]{1,0:T(8,128)(2,1)} %fusion.9), channel_id=1, source_target_pairs={{0,16},{4,20},{8,24},{12,28},{16,0},{20,4},{24,8},{28,12},{1,17},{... | collective-permute-start | bytes 884744 | tf_op jit(solution)/shard_map/ppermute | solution.py:26
  225.7 9.0 %collective-permute-start.38 = (bf16[2,96,576]{2,1,0:T(8,128)(2,1)}, bf16[2,96,576]{2,1,0:T(8,128)(2,1)S(1)}, u32[]{:S(2)}, u32[]{:S(2)}) collective-permute-start(bf16[2,96,576]{2,1,0:T(8,128)(2,1)} %get-tuple-element.227), channel_id=1, source_target_pairs={{0,8},{4,12},{8,0},{12,4},{16,24},{20,28},{24,16},{28,20},{1,9},{5... | collective-permute-start | bytes 663560 | tf_op jit(solution)/shard_map/ppermute | solution.py:26
  229.5 7.1 %collective-permute-start.41 = (bf16[2,112,288]{2,1,0:T(8,128)(2,1)S(1)}, bf16[2,112,288]{2,1,0:T(8,128)(2,1)S(1)}, u32[]{:S(2)}, u32[]{:S(2)}) collective-permute-start(bf16[2,112,288]{2,1,0:T(8,128)(2,1)S(1)} %get-tuple-element.228), channel_id=1, source_target_pairs={{0,8},{4,12},{8,0},{12,4},{16,24},{20,28},{24,16},{28,20},{1,9},{5... | collective-permute-start | bytes 387080 | tf_op jit(solution)/shard_map/ppermute | solution.py:26
  236.7 6.0 %collective-permute-start.42 = (bf16[112,288]{1,0:T(8,128)(2,1)S(1)}, bf16[112,288]{1,0:T(8,128)(2,1)S(1)}, u32[]{:S(2)}, u32[]{:S(2)}) collective-permute-start(bf16[112,288]{1,0:T(8,128)(2,1)S(1)} %fusion.14), channel_id=1, source_target_pairs={{0,16},{4,20},{8,24},{12,28},{16,0},{20,4},{24,8},{28,12},{1,17},{... | collective-permute-start | bytes 193544 | tf_op jit(solution)/shard_map/ppermute | solution.py:26
  241.9 6.8 %collective-permute-start.43 = (bf16[96,576]{1,0:T(8,128)(2,1)S(1)}, bf16[96,576]{1,0:T(8,128)(2,1)S(1)}, u32[]{:S(2)}, u32[]{:S(2)}) collective-permute-start(bf16[96,576]{1,0:T(8,128)(2,1)S(1)} %fusion.12), channel_id=1, source_target_pairs={{0,16},{4,20},{8,24},{12,28},{16,0},{20,4},{24,8},{28,12},{1,17},{... | collective-permute-start | bytes 331784 | tf_op jit(solution)/shard_map/ppermute | solution.py:26
  (40 other events, 270.6 us)

commit v4 on v3

v4 whole, which is shorter than its diff:
```python
import functools

import jax
import jax.numpy as jnp
from jax import lax
from jax.experimental import pallas as pl
from jax.experimental.pallas import tpu as pltpu
from jax.sharding import PartitionSpec as P

HD = 64
SEG = 128
TILE = 2 * SEG
EPS = 1e-05
MASKED = -1e30
ROPE_BASE = 10000.0
F32 = jnp.float32
BF16 = jnp.bfloat16
VMEM = pltpu.VMEM


def xor_tensor(value, step):
    return lax.ppermute(value, "tensor", [(i, i ^ step) for i in range(4)])


def xor_dp(value, step, count):
    return lax.ppermute(value, "dp", [(i, i ^ step) for i in range(count)])


def after(value, *others):
    return lax.optimization_barrier((value,) + others)[0]


def gather_tensor(value):
    far = xor_tensor(value, 2)
    near = xor_tensor(value, 1)
    return [value, near, far, xor_tensor(far, 1)]


def add_round(one, two):
    return (one.astype(F32) + two.astype(F32)).astype(BF16)


def scatter_tensor(stay, leave):
    come = xor_tensor(leave, 1)
    far = xor_tensor(add_round(stay[1], come[1]), 2)
    return stay[0], come[0], far


def total(terms):
    return terms[0].astype(F32) + terms[1].astype(F32) + terms[2].astype(F32)


def double_dp(value, others=(), window=lambda zero: ()):
    zero = jnp.stack([value, after(xor_dp(value, 4, 8), *others)])
    made = window(zero)
    two, one, *made = lax.optimization_barrier((xor_dp(zero, 2, 8), xor_dp(zero, 1, 8), *made))
    return (zero, two, one, xor_dp(two, 1, 8)), made


DOUBLED = (0, 4, 2, 6, 1, 5, 3, 7)
HALVED = (0, 2, 1, 3)


def halve_first(keep, come):
    return add_round(keep[:2], come[:2]), add_round(keep[2:], come[2:])


def halve_second(stay, come):
    return add_round(stay[0], come[0]), add_round(stay[1], come[1])


class SumDp:
    def __init__(self, halves, count):
        self.count, self.halves = count, halves
        if count == 8:
            away, self.keep = halves
            self.first = xor_dp(away, 1, count)

    def across(self):
        if self.count == 8:
            self.stay, leave = halve_first(self.keep, self.first)
            self.second = xor_dp(leave, 2, self.count)

    def total(self):
        if self.count != 8:
            values = self.halves[0].astype(F32)
            return lax.psum_scatter(values, "dp", scatter_dimension=0, tiled=True)[0]
        return self.ours.astype(F32) + self.third.astype(F32)

    def between(self):
        if self.count == 8:
            self.ours, leave = halve_second(self.stay, self.second)
            self.third = xor_dp(leave, 4, self.count)


def entries(refs):
    out = []
    for ref in refs:
        out += [ref] if len(ref.shape) == 2 else [ref.at[i] for i in range(ref.shape[0])]
    return out


def place_rows(info, refs, lane, whole_ref):
    for piece, xor in zip(entries(refs), DOUBLED):
        rows = piece.shape[0]
        at = pl.ds(pl.multiple_of((info[1] ^ xor) * rows, 16), rows)
        whole_ref[at, :] = piece[:, lane : lane + whole_ref.shape[1]]


def assemble_kernel(turn, info, *refs):
    pieces, out = refs[:4], refs[4]
    whole_ref = refs[-1] if turn else out
    place_rows(info, pieces, 0, whole_ref)
    if turn:
        turned = whole_ref[...].T
        out[...] = turned[: out.shape[0]]
        refs[5][...] = turned[out.shape[0] :]


def assemble(info, arrays, turn):
    rows, cols = arrays[0].shape[1:]
    shapes = [(8 * rows, cols)]
    if turn:
        shapes = [(cols - cols // 4, 8 * rows), (cols // 4, 8 * rows)]
    return pl.pallas_call(
        functools.partial(assemble_kernel, turn),
        out_shape=[jax.ShapeDtypeStruct(shape, BF16) for shape in shapes],
        in_specs=[pl.BlockSpec(memory_space=pltpu.SMEM)] + [pl.BlockSpec(memory_space=VMEM)] * 4,
        out_specs=[pl.BlockSpec(memory_space=VMEM)] * len(shapes),
        scratch_shapes=[VMEM((8 * rows, cols), BF16)] if turn else [],
        name="assemble",
    )(info, *arrays)


def pick(refs, which):
    value = refs[3][0]
    for k in range(3):
        value = jnp.where(which == k, refs[k][0], value)
    return value


def whole(shape):
    return pl.BlockSpec(shape, lambda *_: (0,) * len(shape))


def nn(a, b):
    return lax.dot_general(a, b, (((1,), (0,)), ((), ())), preferred_element_type=F32)


def nt(a, b):
    return lax.dot_general(a, b, (((1,), (1,)), ((), ())), preferred_element_type=F32)


def tn(a, b):
    return lax.dot_general(a, b, (((0,), (0,)), ((), ())), preferred_element_type=F32)


def pack_first_kernel(two, three, up_two, up_three, out):
    ng, rows = two.shape
    out[:ng, :rows] = two[...].astype(BF16)
    out[ng:, :rows] = three[...].astype(BF16)
    out[:, rows:] = jnp.zeros((2 * ng, SEG), BF16)
    if up_two.shape[1] == 2 * ng:
        small = jnp.concatenate([up_two[...], up_three[...]], axis=0)
        out[:, rows : rows + 2 * ng] = small.T.astype(BF16)


def pack_first(two, three, up_two, up_three):
    ng, rows = two.shape
    return pl.pallas_call(
        pack_first_kernel,
        out_shape=jax.ShapeDtypeStruct((2 * ng, rows + SEG), BF16),
        name="pack_first",
    )(two, three, up_two, up_three)


def pack_kernel(query, key, value, output, gate, up, down, attn, ffn):
    width, units = query.shape[1], gate.shape[1]
    for i, ref in enumerate((query, key, value)):
        attn[:, i * width : (i + 1) * width] = ref[...].astype(BF16)
    attn[:, 3 * width :] = output[...].T.astype(BF16)
    for i, ref in enumerate((gate, up, down)):
        ffn[:, i * units : (i + 1) * units] = ref[...].astype(BF16)


def pack(query, key, value, output, gate, up, down):
    rows, width = query.shape
    return pl.pallas_call(
        pack_kernel,
        out_shape=[
            jax.ShapeDtypeStruct((rows, 4 * width), BF16),
            jax.ShapeDtypeStruct((rows, 3 * gate.shape[1]), BF16),
        ],
        name="pack",
    )(query, key, value, output, gate, up, down)


def split_rows(info, whole_ref, outs, rows):
    if len(outs) == 1:
        for i in range(outs[0].shape[0]):
            outs[0][i] = whole_ref[i * rows : (i + 1) * rows, :]
        return
    for entry, xor in enumerate(HALVED):
        for out, other in zip(outs, (1, 0)):
            at = info[1] ^ (2 * xor + other)
            out[entry] = whole_ref[pl.ds(pl.multiple_of(at * rows, 16), rows), :]


def weigh_kernel(rows, halves, info, hidden, norm, grads, *refs):
    cots, mixes, grad, refs = refs[:4], refs[4:8], refs[8], refs[9:]
    outs, (stay, leave, turned, whole_ref) = refs[:halves], refs[halves:]
    at = grads.shape[1]
    for tile in range(4):
        cot = pick([ref.at[1:2] for ref in cots], tile ^ info[0])
        turned[:, tile * TILE : (tile + 1) * TILE] = cot.T
    whole_ref[:, at:] = nn(turned[...], hidden[...]).astype(BF16)
    turned[...] = norm[...].T
    whole_ref[:, :at] = nn(turned[...], grads[...]).astype(BF16)
    split_rows(info, whole_ref, outs, rows)
    for xor in range(4):
        (stay, leave)[xor % 2][xor // 2] = nn(mixes[xor][...], grad[...]).astype(BF16)


def weigh(info, tokens, hidden, norm, grads, mixes, grad, count, own_dim):
    length, dim = norm.shape
    lead = [4, 4] if count == 8 else [count]
    cols = hidden.shape[1] + grads.shape[1]
    shapes = [(n, own_dim, cols) for n in lead] + [(2, mixes[0].shape[0], dim)] * 2
    operands = [hidden, norm, grads, *tokens, *mixes, grad]
    vm = pl.BlockSpec(memory_space=VMEM)
    got = pl.pallas_call(
        functools.partial(weigh_kernel, own_dim, len(lead)),
        in_specs=[pl.BlockSpec(memory_space=pltpu.SMEM)] + [vm] * len(operands),
        out_specs=[vm] * len(shapes),
        scratch_shapes=[VMEM((dim, length), BF16), VMEM((dim, cols), BF16)],
        out_shape=[jax.ShapeDtypeStruct(shape, BF16) for shape in shapes],
        name="weigh",
    )(info, *operands)
    return got[: len(lead)], got[len(lead) :]


def weigh_turned_kernel(rows, info, left, right, *refs):
    outs, whole_ref = refs[:-1], refs[-1]
    whole_ref[...] = nn(right[...], left[...]).astype(BF16).T
    split_rows(info, whole_ref, outs, rows)


def turn_kernel(rows, info, wide, *refs):
    outs, whole_ref = refs[:-1], refs[-1]
    whole_ref[...] = wide[...].T
    split_rows(info, whole_ref, outs, rows)


def turn_below_kernel(rows, info, wide, below, *refs):
    outs = refs[:-1]
    turn_kernel(rows, info, wide, *(out.at[:, :rows] for out in outs), refs[-1])
    for out in outs:
        for z in range(out.shape[0]):
            out[z, rows:, : below.shape[1]] = below[...]


def split_call(body, info, operands, count, own_dim, cols, below=0):
    vm = pl.BlockSpec(memory_space=VMEM)
    lead = [4, 4] if count == 8 else [count]
    shapes = [jax.ShapeDtypeStruct((n, own_dim + below, cols), BF16) for n in lead]
    return pl.pallas_call(
        functools.partial(body, own_dim),
        out_shape=shapes,
        in_specs=[pl.BlockSpec(memory_space=pltpu.SMEM)] + [vm] * len(operands),
        out_specs=[vm] * len(shapes),
        scratch_shapes=[VMEM((count * own_dim, cols), BF16)],
        name="split",
    )(info, *operands)


def weigh_turned(info, left, right, count, own_dim):
    return split_call(weigh_turned_kernel, info, [left, right], count, own_dim, right.shape[0])


def turn(info, wide, below, count, own_dim):
    if below is None:
        return split_call(turn_kernel, info, [wide], count, own_dim, wide.shape[0])
    return split_call(
        turn_below_kernel, info, [wide, below], count, own_dim, wide.shape[0], below.shape[0]
    )


def finish_kernel(attn, attn_come, wide, wide_come, query, key, value, two, three, output, gains):
    width, ng = query.shape[1], two.shape[0]
    rows = query.shape[0]
    sums = attn[...].astype(F32) + attn_come[...].astype(F32)
    for i, out in enumerate((query, key, value)):
        out[...] = sums[:, i * width : (i + 1) * width]
    sums = wide[...].astype(F32) + wide_come[...].astype(F32)
    turned = sums[:rows].T
    two[...] = turned[:ng]
    three[...] = turned[ng : 2 * ng]
    output[...] = turned[2 * ng :]
    gains[...] = sums[rows:, : gains.shape[1]]


def finish(attn_sum, wide_sum, ng):
    rows, cols = attn_sum.ours.shape
    width = cols // 3
    operands = [attn_sum.ours, attn_sum.third, wide_sum.ours, wide_sum.third]
    below = wide_sum.ours.shape[0] - rows
    shapes = [(rows, width)] * 3 + [(ng, rows)] * 2 + [(width, rows), (below, 2 * ng)]
    vm = pl.BlockSpec(memory_space=VMEM)
    return pl.pallas_call(
        finish_kernel,
        out_shape=[jax.ShapeDtypeStruct(shape, F32) for shape in shapes],
        in_specs=[vm] * 4,
        out_specs=[vm] * 7,
        name="finish",
    )(*operands)


def one_hot(low):
    rows = lax.broadcasted_iota(jnp.int32, (TILE, SEG), 0).astype(F32).astype(BF16)
    parts = [
        jnp.where(rows == low[:, c : c + SEG], BF16(1.0), BF16(0.0))
        for c in range(0, low.shape[1], SEG)
    ]
    return jnp.concatenate(parts, axis=1)


def lookup_kernel(owners, arrays, width, own_rows, start, end, *refs):
    info, ids = refs[0], refs[1]
    arrays, refs = refs[2 : 2 + arrays], refs[2 + arrays :]
    pieces = entries(arrays)
    count = len(owners)
    at = 0
    if end:
        ups, refs, out, whole_ref = refs[:4], refs[4:-2], refs[-2], refs[-1]
        at = out.shape[1] - ids.shape[1]
        place_rows(info, ups, own_rows, whole_ref)
        out[:, :at] = whole_ref[...].T[: 2 * width]
    else:
        out = refs[-1]
    prior = None if start else refs[0]
    chunks = own_rows // TILE
    for half in range(2):
        lanes = slice(half * width, (half + 1) * width)
        stacks = [
            jnp.concatenate([piece[lanes, c * TILE : (c + 1) * TILE] for c in range(chunks)], axis=0)
            for piece in pieces
        ]

        def part(n, carry):
            cut = pl.ds(pl.multiple_of(n * TILE, TILE), TILE)
            wanted = ids[half : half + 1, cut]
            high = wanted // TILE
            low = (wanted - high * TILE).astype(F32).astype(BF16)
            hot = one_hot(low)
            sofar = jnp.zeros((width, TILE), F32) if start else prior[lanes, cut].astype(F32)
            for stack, owner in zip(stacks, owners):
                got = nn(stack, hot)
                first = (info[1] ^ owner) * chunks
                for c in range(chunks):
                    mine = got[c * width : (c + 1) * width]
                    sofar = sofar + jnp.where(high == first + c, mine, 0.0)
            out[lanes, pl.ds(pl.multiple_of(at + n * TILE, TILE), TILE)] = sofar.astype(BF16)
            return carry

        lax.fori_loop(0, ids.shape[1] // TILE, part, 0)


def lookup(info, pieces, owners, own_rows, ids, prior, ups=()):
    width = pieces[0].shape[-2] // 2
    vm = pl.BlockSpec(memory_space=VMEM)
    operands = [info, ids, *pieces, *ups] + ([] if prior is None else [prior])
    at = 8 * ups[0].shape[1] if ups else 0
    return pl.pallas_call(
        functools.partial(
            lookup_kernel, owners, len(pieces), width, own_rows, prior is None, bool(ups)
        ),
        out_shape=jax.ShapeDtypeStruct((2 * width, at + ids.shape[1]), BF16),
        in_specs=[pl.BlockSpec(memory_space=pltpu.SMEM)] + [vm] * (len(operands) - 1),
        out_specs=vm,
        scratch_shapes=[VMEM((at, SEG), BF16)] if ups else [],
        name="lookup",
    )(*operands)


def spread_kernel(arrays, width, start, end, *refs):
    outs = refs[-2:] if end else refs[-1:]
    info, pieces = refs[0], entries(refs[1 : 1 + arrays])
    prior = None if start else refs[1 + arrays]
    own_rows = outs[0].shape[1]
    chunks = own_rows // TILE
    for half in range(2):
        lanes = slice(half * width, (half + 1) * width)
        sofar = None
        for piece in pieces:
            digits = piece[2 * width :, :]
            high, low = digits[2 * half : 2 * half + 1], digits[2 * half + 1 : 2 * half + 2]
            grads = piece[lanes, :]
            stack = [
                jnp.where(high == (info[1] * chunks + c).astype(F32).astype(BF16), grads, BF16(0.0))
                for c in range(chunks)
            ]
            got = nt(jnp.concatenate(stack, axis=0), one_hot(low))
            sofar = got if sofar is None else sofar + got
        for c in range(chunks):
            cut = slice(c * TILE, (c + 1) * TILE)
            part = sofar[c * width : (c + 1) * width]
            if not start:
                part = part + prior[lanes, cut]
            if end:
                outs[half][:, cut] = part
            else:
                outs[0][lanes, cut] = part


def spread(info, pieces, own_rows, width, prior, end):
    operands = [info, *pieces] + ([] if prior is None else [prior])
    vm = pl.BlockSpec(memory_space=VMEM)
    shapes = [(width, own_rows)] * 2 if end else [(2 * width, own_rows)]
    got = pl.pallas_call(
        functools.partial(spread_kernel, len(pieces), width, prior is None, end),
        out_shape=[jax.ShapeDtypeStruct(shape, F32) for shape in shapes],
        in_specs=[pl.BlockSpec(memory_space=pltpu.SMEM)] + [vm] * (len(operands) - 1),
        out_specs=[vm] * len(shapes),
        name="spread",
    )(*operands)
    return got if end else got[0]


def rope_into(out, row, values, cosine, sine, scale):
    half = HD // 2
    one, two = values[:half], values[half:]
    out[row : row + half, :] = (one * cosine - two * sine).astype(BF16) * scale
    out[row + half : row + HD, :] = (one * sine + two * cosine).astype(BF16) * scale


def key_offset(parent):
    return pl.multiple_of(jnp.where(parent > 0, parent + 1, 0) * SEG, SEG)


def block_keys(parent, start):
    key_at = lax.broadcasted_iota(jnp.int32, (4 * SEG, SEG), 0)
    query_at = lax.broadcasted_iota(jnp.int32, (4 * SEG, SEG), 1)
    limit = jnp.where(parent > 0, 4 * SEG, 3 * SEG)
    seen = (key_at < TILE) | ((key_at - TILE <= query_at) & (key_at < 3 * SEG))
    seen = seen | ((key_at >= 3 * SEG) & (key_at < limit))
    mine = pl.ds(pl.multiple_of(start, SEG), SEG)
    return (slice(0, TILE), mine, pl.ds(key_offset(parent), SEG)), seen


def trunk_seen():
    key_at = lax.broadcasted_iota(jnp.int32, (TILE, TILE), 0)
    return key_at <= lax.broadcasted_iota(jnp.int32, (TILE, TILE), 1)


def front_kernel(
    info,
    set0,
    set1,
    set2,
    set3,
    emb0,
    emb1,
    emb2,
    emb3,
    wqkv,
    gain,
    cos_ref,
    sin_ref,
    resid,
    normed,
    qkv,
    mixed,
    lse,
):
    length, dim = resid.shape
    sets = (set0, set1, set2, set3)
    rows = jnp.concatenate([ref[:, dim:] for ref in sets], axis=0)
    ups = jnp.concatenate([ref[:, :dim] for ref in sets], axis=0)
    own = [pick((emb0, emb1, emb2, emb3), i ^ info[0]) for i in range(length // TILE)]
    hidden = jnp.concatenate(own, axis=0).astype(F32) + tn(rows, ups)
    resid[...] = hidden
    rate = lax.rsqrt(jnp.mean(hidden * hidden, axis=-1, keepdims=True) + EPS)
    norm = (hidden * rate * gain[...]).astype(BF16)
    normed[...] = norm
    proj = nt(wqkv[...], norm)
    cosine, sine = cos_ref[...], sin_ref[...]
    width = mixed.shape[0]
    heads = width // HD
    for h in range(heads):
        rope_into(qkv, h * HD, proj[h * HD : (h + 1) * HD], cosine, sine, BF16(HD**-0.5))
        low = width + h * HD
        rope_into(qkv, low, proj[low : low + HD], cosine, sine, BF16(1.0))
    qkv[2 * width :, :] = proj[2 * width :].astype(BF16)

    def attend(h, lanes, cuts, seen):
        hs = slice(h * HD, (h + 1) * HD)
        ks = slice(width + h * HD, width + (h + 1) * HD)
        vs = slice(2 * width + h * HD, 2 * width + (h + 1) * HD)
        key = jnp.concatenate([qkv[ks, cut] for cut in cuts], axis=1)
        value = jnp.concatenate([qkv[vs, cut] for cut in cuts], axis=1)
        scores = jnp.where(seen, tn(key, qkv[hs, lanes]), MASKED)
        top = jnp.max(scores, axis=0, keepdims=True)
        weights = jnp.exp(scores - top)
        sums = jnp.sum(weights, axis=0, keepdims=True)
        got = nn(value, weights.astype(BF16))
        mixed[hs, lanes] = (got * (1.0 / sums)).astype(BF16)
        lse[h : h + 1, lanes] = top + jnp.log(sums)

    for h in range(heads):
        attend(h, slice(0, TILE), (slice(0, TILE),), trunk_seen())

    def block(j, carry):
        cuts, seen = block_keys(info[2 + j], j * SEG)
        for h in range(heads):
            attend(h, cuts[1], cuts, seen)
        return carry

    lax.fori_loop(TILE // SEG, length // SEG, block, 0)


def front(info, sets, tokens, wqkv, gain, cosine, sine):
    dim = tokens[0].shape[2]
    length = sets[0].shape[1] - dim
    width = wqkv.shape[0] // 3
    vm = pl.BlockSpec(memory_space=VMEM)
    operands = [*sets, *tokens, wqkv, gain, cosine, sine]
    shapes = [
        ((length, dim), F32),
        ((length, dim), BF16),
        ((3 * width, length), BF16),
        ((width, length), BF16),
        ((8, length), F32),
    ]
    return pl.pallas_call(
        front_kernel,
        out_shape=[jax.ShapeDtypeStruct(*shape) for shape in shapes],
        in_specs=[pl.BlockSpec(memory_space=pltpu.SMEM)] + [vm] * len(operands),
        out_specs=[vm] * len(shapes),
        name="front",
    )(info, *operands)


def slot_of(xor):
    return (xor & 1) * 2 + (xor >> 1)


def middle_kernel(
    who,
    mix0,
    mix1,
    mix2,
    mix3,
    out0,
    out1,
    out2,
    out3,
    resid,
    gain,
    ffn0,
    ffn1,
    ffn2,
    ffn3,
    cot0,
    cot1,
    cot2,
    cot3,
    feed_stay,
    feed_leave,
    resid_own,
    normed,
    hidden,
    grads,
    grad_res,
    mix_stay,
    mix_leave,
    grad_gain,
    ffn,
):
    units = hidden.shape[1]
    if len(ffn0.shape) == 3:
        place_rows(who, (ffn0, ffn1, ffn2, ffn3), 0, ffn)
    else:
        ffn[...] = ffn0[...]
    outs = jnp.concatenate([out0[...], out1[...], out2[...], out3[...]], axis=0)
    mix = jnp.concatenate([mix0[...], mix1[...], mix2[...], mix3[...]], axis=0)
    res = resid[...] + tn(mix, outs)
    tiles = range(res.shape[0] // TILE)
    for i in tiles:

        @pl.when(who[0] == i)
        def _():
            resid_own[...] = res[i * TILE : (i + 1) * TILE]

    rate = lax.rsqrt(jnp.mean(res * res, axis=-1, keepdims=True) + EPS)
    norm = (res * rate * gain[...]).astype(BF16)
    normed[...] = norm
    gate = nn(norm, ffn[:, :units])
    upward = nn(norm, ffn[:, units : 2 * units])
    sig = 1.0 / (1.0 + jnp.exp(-gate))
    silu = gate * sig
    hid = (silu * upward).astype(BF16)
    hidden[...] = hid
    fed = nt(hid, ffn[:, 2 * units :]).astype(BF16)
    for i in tiles:
        slot = slot_of(i ^ who[0])
        part = fed[i * TILE : (i + 1) * TILE]

        @pl.when(slot < 2)
        def _():
            feed_stay[slot % 2] = part

        @pl.when(slot >= 2)
        def _():
            feed_leave[slot % 2] = part

    cots = [ref.at[1:2] for ref in (cot0, cot1, cot2, cot3)]
    cot = jnp.concatenate([pick(cots, i ^ who[0]) for i in tiles], axis=0)
    back = nn(cot, ffn[:, 2 * units :])
    grad_gate = (back * upward * sig * (1.0 + gate * (1.0 - sig))).astype(BF16)
    grad_up = (back * silu).astype(BF16)
    grads[:, :units] = grad_gate
    grads[:, units:] = grad_up
    pulled = nt(grad_gate, ffn[:, :units]) + nt(grad_up, ffn[:, units : 2 * units])
    scaled = pulled * gain[...]
    dots = jnp.mean(scaled * res, axis=-1, keepdims=True)
    part = rate * scaled - res * (rate * rate * rate * dots) + 0.25 * cot.astype(F32)
    part = part.astype(BF16)
    grad_res[...] = part
    by_head = nt(outs, part).astype(BF16)
    width = out0.shape[0]
    for k in range(4):
        (mix_stay, mix_leave)[k % 2][k // 2] = by_head[k * width : (k + 1) * width]
    grad_gain[...] = jnp.sum(pulled * res * rate, axis=0, keepdims=True)


def middle(info, mixes, outs, resid, gain, ffns, tokens):
    length, dim = resid.shape
    width = mixes[0].shape[0]
    units = ffns[0].shape[-1] // 3
    vm = pl.BlockSpec(memory_space=VMEM)
    operands = [*mixes, *outs, resid, gain, *ffns, *tokens]
    shapes = [
        ((2, TILE, dim), BF16),
        ((2, TILE, dim), BF16),
        ((TILE, dim), F32),
        ((length, dim), BF16),
        ((length, units), BF16),
        ((length, 2 * units), BF16),
        ((length, dim), BF16),
        ((2, width, length), BF16),
        ((2, width, length), BF16),
        ((1, dim), F32),
    ]
    return pl.pallas_call(
        middle_kernel,
        in_specs=[pl.BlockSpec(memory_space=pltpu.SMEM)] + [vm] * len(operands),
        out_specs=[vm] * len(shapes),
        scratch_shapes=[VMEM((dim, 3 * units), BF16)],
        out_shape=[jax.ShapeDtypeStruct(*shape) for shape in shapes],
        name="middle",
    )(info, *operands)


def unrope_into(out, row, values, cosine, sine):
    half = HD // 2
    one, two = values[:half], values[half:]
    out[row : row + half, :] = (one * cosine + two * sine).astype(BF16)
    out[row + half : row + HD, :] = (two * cosine - one * sine).astype(BF16)


def back_kernel(
    info,
    qkv,
    gmix,
    mixed,
    lse,
    grad_res,
    resid,
    gain,
    gain_two,
    wqkv,
    set0,
    set1,
    set2,
    set3,
    cos_ref,
    sin_ref,
    feed_stay,
    feed_leave,
    out_stay,
    out_leave,
    gproj,
    stay,
    leave,
    up_stay,
    up_leave,
    row_stay,
    row_leave,
    keys_sum,
    vals_sum,
    query_sum,
):
    length, dim = resid.shape
    width = gmix.shape[0]
    heads = width // HD
    keys_sum[...] = jnp.zeros_like(keys_sum)
    vals_sum[...] = jnp.zeros_like(vals_sum)

    def pull(h, lanes, cuts, seen):
        hs = slice(h * HD, (h + 1) * HD)
        ks = slice(width + h * HD, width + (h + 1) * HD)
        vs = slice(2 * width + h * HD, 2 * width + (h + 1) * HD)
        query, grad = qkv[hs, lanes], gmix[hs, lanes]
        key = jnp.concatenate([qkv[ks, cut] for cut in cuts], axis=1)
        value = jnp.concatenate([qkv[vs, cut] for cut in cuts], axis=1)
        delta = jnp.sum(grad.astype(F32) * mixed[hs, lanes].astype(F32), axis=0, keepdims=True)
        scores = jnp.where(seen, tn(key, query), MASKED)
        probs = jnp.exp(scores - lse[h : h + 1, lanes])
        dval = nt(grad, probs.astype(BF16))
        dscore = (probs * (tn(value, grad) - delta)).astype(BF16)
        query_sum[hs, lanes] = nn(key, dscore) * HD**-0.5
        dkey = nt(query, dscore)
        at = 0
        for cut, size in zip(cuts, (TILE, SEG, SEG)):
            keys_sum[hs, cut] += dkey[:, at : at + size]
            vals_sum[hs, cut] += dval[:, at : at + size]
            at += size

    for h in range(heads):
        pull(h, slice(0, TILE), (slice(0, TILE),), trunk_seen())

    def tile(r, carry):
        for half in range(2):
            start = r * TILE + half * SEG
            cuts, seen = block_keys(info[2 + 2 * r + half], start)
            for h in range(heads):
                pull(h, cuts[1], cuts, seen)
        return carry

    lax.fori_loop(1, length // TILE, tile, 0)

    cosine, sine = cos_ref[...], sin_ref[...]
    for h in range(heads):
        hs = slice(h * HD, (h + 1) * HD)
        unrope_into(gproj, h * HD, query_sum[hs, :], cosine, sine)
        unrope_into(gproj, width + h * HD, keys_sum[hs, :], cosine, sine)
    gproj[2 * width :, :] = vals_sum[...].astype(BF16)
    pulled = tn(gproj[...], wqkv[...])
    hidden = resid[...]
    rate = lax.rsqrt(jnp.mean(hidden * hidden, axis=-1, keepdims=True) + EPS)
    scaled = pulled * gain[...]
    dots = jnp.mean(scaled * hidden, axis=-1, keepdims=True)
    part = grad_res[...].astype(F32) + rate * scaled - hidden * (rate * rate * rate * dots)
    part = part.astype(BF16)
    for i in range(length // TILE):
        slot = slot_of(i ^ info[0])
        piece = part[i * TILE : (i + 1) * TILE]

        @pl.when(slot < 2)
        def _():
            stay[slot % 2, :TILE] = piece

        @pl.when(slot >= 2)
        def _():
            leave[slot % 2, :TILE] = piece

    stay[:, TILE:] = feed_stay[...]
    leave[:, TILE:] = feed_leave[...]
    sets = (set0, set1, set2, set3)
    ng = set0.shape[0]
    ups = jnp.concatenate([ref[:, :dim] for ref in sets], axis=0)
    by_column = nt(ups, part).astype(BF16)
    rows = jnp.concatenate([ref[:, dim:] for ref in sets], axis=0)
    grad_ups = nn(rows, part).astype(BF16)
    grad_gain = jnp.sum(pulled * hidden * rate, axis=0, keepdims=True)
    gains = jnp.concatenate([grad_gain, gain_two[...], jnp.zeros((14, dim), F32)], axis=0)
    gains = gains.astype(BF16)
    for k in range(4):
        (row_stay, row_leave)[k % 2][k // 2] = by_column[k * ng : (k + 1) * ng]
        out = (up_stay, up_leave)[k % 2]
        out[k // 2, :ng, :] = grad_ups[k * ng : (k + 1) * ng]
        out[k // 2, ng : ng + width, :] = (out_stay, out_leave)[k % 2][k // 2]
        out[k // 2, ng + width :, :] = gains


def back(
    info, qkv, gmix, mixed, lse, grad_res, resid, gain, gain_part, wqkv, sets, cosine, sine, feeds, outs
):
    length, dim = resid.shape
    width = gmix.shape[0]
    ng = sets[0].shape[0]
    vm = pl.BlockSpec(memory_space=VMEM)
    operands = [qkv, gmix, mixed, lse, grad_res, resid, gain, gain_part, wqkv, *sets, cosine, sine]
    operands += [*feeds, *outs]
    shapes = [(3 * width, length)] + [(2, 2 * TILE, dim)] * 2
    shapes += [(2, ng + width + 16, dim)] * 2 + [(2, ng, length)] * 2
    return pl.pallas_call(
        back_kernel,
        out_shape=[jax.ShapeDtypeStruct(shape, BF16) for shape in shapes],
        in_specs=[pl.BlockSpec(memory_space=pltpu.SMEM)] + [vm] * len(operands),
        out_specs=[vm] * len(shapes),
        scratch_shapes=[VMEM((width, length), F32)] * 3,
        name="back",
    )(info, *operands)


def rotary(parents):
    length = parents.shape[0]
    token = jnp.arange(length, dtype=jnp.int32)
    trunk = 2 * SEG
    inside = token < trunk
    block = jnp.where(inside, 0, (token - trunk) // SEG + 1)
    offset = jnp.where(inside, token, token - trunk - (block - 1) * SEG)
    position = jnp.where(inside, 0, jnp.where(parents == 0, 2 * SEG, 3 * SEG)) + offset
    half = HD // 2
    frequency = ROPE_BASE ** (-(jnp.arange(half, dtype=F32) * 2.0 / HD))
    angles = frequency[:, None] * position.astype(F32)[None, :]
    return jnp.cos(angles), jnp.sin(angles)


def shards(
    dp,
    embedded,
    ids_two,
    ids_three,
    parents,
    table_two,
    table_three,
    w_two,
    w_three,
    norm_attn,
    w_query,
    w_key,
    w_value,
    w_output,
    norm_ffn,
    w_gate,
    w_up,
    w_down,
    cotangent,
):
    own_d = lax.axis_index("dp")
    own_t = lax.axis_index("tensor")
    own_rows, ng = table_two.shape
    rows, dim = embedded.shape
    width = w_query.shape[1]
    units = w_gate.shape[1]
    own_dim = w_query.shape[0]
    gain_one = norm_attn.reshape(1, dim)
    gain_two = norm_ffn.reshape(1, dim)

    ids = jnp.stack([ids_two, ids_three])
    info = jnp.concatenate(
        [jnp.stack([own_t, own_d]).astype(jnp.int32), parents.reshape(-1, SEG)[:, 0]]
    )
    cosine, sine = rotary(parents)

    digits = jnp.stack([ids_two // 256, ids_two % 256, ids_three // 256, ids_three % 256])
    digits = jnp.pad(digits.astype(BF16), ((0, 12), (0, 0)))
    first = pack_first(table_two.T, table_three.T, w_two, w_three)
    attn_pack, ffn_pack = pack(w_query, w_key, w_value, w_output, w_gate, w_up, w_down.T)
    token_pair = jnp.stack([embedded, cotangent])
    token_near = xor_tensor(token_pair, 1)
    if dp == 8:
        arrays, (got, token_near) = double_dp(
            first,
            (attn_pack, ffn_pack, cosine, sine, gain_one, gain_two, digits),
            lambda zero: [lookup(info, [zero], (0, 4), own_rows, ids, None), token_near],
        )
        _, two, one, three = arrays
        token_far = xor_tensor(after(token_pair, arrays[0]), 2)
        got = lookup(info, [two, one], (2, 6, 1, 5), own_rows, ids, got)
        attn_arrays, (got, token_far) = double_dp(
            after(attn_pack, arrays[0]),
            (got,),
            lambda zero: [lookup(info, [three], (3, 7), own_rows, ids, got, arrays), token_far],
        )
        wqkv, wo = assemble(info, attn_arrays, True)
        ffn_arrays, _ = double_dp(after(ffn_pack, two), (attn_arrays[1],))
        wqkv, ffn_zero = lax.optimization_barrier((wqkv, ffn_arrays[0]))
        ffns = (ffn_zero, *ffn_arrays[1:])
    else:
        every = lax.all_gather(first[:, :own_rows], "dp", axis=0)
        small = jnp.concatenate([w_two.astype(BF16).T, w_three.astype(BF16).T], axis=1)
        ups = lax.all_gather(small, "dp", axis=0, tiled=True).T
        wqkvo = lax.all_gather(attn_pack, "dp", axis=0, tiled=True).T
        wqkv, wo = wqkvo[: 3 * width], wqkvo[3 * width :]
        ffns = [lax.all_gather(ffn_pack, "dp", axis=0, tiled=True)]
        ffns += [jnp.zeros((8, SEG), BF16)] * 3
        token_far = xor_tensor(token_pair, 2)

        def take(i, so_far):
            piece = lax.dynamic_index_in_dim(every, i, 0, keepdims=False)
            at = jnp.stack([own_t, i]).astype(jnp.int32)
            return lookup(at, [piece], (0,), own_rows, ids, so_far)

        got = lax.fori_loop(0, dp, take, jnp.zeros((2 * ng, ids.shape[1]), BF16))
        got = jnp.concatenate([ups, got], axis=1)

    tokens = [token_pair, token_near, token_far, xor_tensor(token_far, 1)]
    sets = gather_tensor(got)
    outs = gather_tensor(after(wo, sets[2]))

    resid, normed, qkv, mixed, lse = front(info, sets, tokens, wqkv, gain_one, cosine, sine)
    mixed = after(mixed, outs[2])
    mixes = gather_tensor(mixed)
    (
        feed_stay, feed_leave, resid_own, normed_two, hidden, grads, grad_res, stay, leave,
        gain_part_two,
    ) = middle(info, mixes, outs, resid, gain_two, ffns, tokens)
    near = xor_tensor(leave, 1)
    near_far = add_round(stay[1], near[1])
    far = xor_tensor(near_far, 2)
    halves, out_pair = weigh(
        info, tokens, after(hidden, near_far), normed_two, grads, mixes, grad_res, dp, own_dim
    )
    ffn_sum = SumDp(halves, dp)
    far, _ = lax.optimization_barrier((far, halves))
    gmix = total((stay[0], near[0], far)).astype(BF16)

    gproj, stay, leave, up_stay, up_leave, row_stay, row_leave = back(
        info, qkv, gmix, mixed, lse, grad_res, resid, gain_one, gain_part_two, wqkv, sets,
        cosine, sine, (feed_stay, feed_leave), out_pair,
    )

    near = xor_tensor(row_leave, 1)
    near_far = add_round(row_stay[1], near[1])
    if dp == 8:
        near_far, ffn_sum.first = lax.optimization_barrier((near_far, ffn_sum.first))
        ffn_sum.across()
    far = xor_tensor(near_far, 2)
    gproj = after(gproj, near_far)
    attn_halves = weigh_turned(info, normed, gproj, dp, own_dim)
    attn_sum = SumDp(attn_halves, dp)
    far, _ = lax.optimization_barrier((far, attn_halves))
    row_total = total((row_stay[0], near[0], far)).astype(BF16)
    row_pack = jnp.concatenate([row_total, digits], axis=0)
    up_near = xor_tensor(after(up_leave, near_far), 1)
    up_near_far = after(add_round(up_stay[1], up_near[1]), far)
    up_far = xor_tensor(up_near_far, 2)
    token_near = xor_tensor(after(leave, far), 1)
    token_far = xor_tensor(after(add_round(stay[1], token_near[1]), up_near_far), 2)
    if dp == 8:
        zero = jnp.stack([row_pack, xor_dp(row_pack, 4, dp)])
        zero, attn_sum.first, up_far, ffn_sum.second = lax.optimization_barrier(
            (zero, attn_sum.first, up_far, ffn_sum.second)
        )
    below = add_round(add_round(up_stay[0], up_near[0]), up_far)
    wide_grad, gains = below[: 2 * ng + width], below[2 * ng + width : 2 * ng + width + 2]
    if dp == 8:
        folded = gains.reshape(2 * dim // (2 * ng), 2 * ng)
        halves = turn(info, wide_grad, folded, dp, own_dim)
        two, one, ffn_sum.second, halves = lax.optimization_barrier(
            (xor_dp(zero, 2, dp), xor_dp(zero, 1, dp), ffn_sum.second, halves)
        )
        three = xor_dp(two, 1, dp)
        proj_sum = SumDp(halves, dp)
        ffn_sum.between()
        attn_sum.first = after(attn_sum.first, two)
        attn_sum.across()
        table_grad = spread(info, [zero, two, one], own_rows, ng, None, False)
        proj_sum.first, token_far, table_grad = lax.optimization_barrier(
            (proj_sum.first, token_far, table_grad)
        )
        proj_sum.across()
        ffn_total = ffn_sum.total()
        sums = total((stay[0], token_near[0], token_far))
        embed_grad = sums[:rows].astype(BF16)
        output = (resid_own + sums[rows:]).astype(BF16)
        gate_grad, up_grad, down_grad = (
            ffn_total[:, i * units : (i + 1) * units] for i in range(3)
        )
        attn_sum.second, proj_sum.second, embed_grad, output, table_grad = (
            lax.optimization_barrier(
                (attn_sum.second, proj_sum.second, embed_grad, output, table_grad)
            )
        )
        proj_sum.between()
        attn_sum.between()
        table_grad = spread(info, [three], own_rows, ng, table_grad, True)
        *grads_done, folded = finish(attn_sum, proj_sum, ng)
        gains = folded.reshape(2, dim)
    else:
        every = lax.all_gather(row_pack, "dp", axis=0)

        def put(i, so_far):
            piece = lax.dynamic_index_in_dim(every, i, 0, keepdims=False)
            return spread(info, [piece], own_rows, ng, so_far, False)

        table_grad = lax.fori_loop(0, dp, put, jnp.zeros((2 * ng, own_rows), F32))
        table_grad = table_grad[:ng], table_grad[ng:]
        sums = total((stay[0], token_near[0], token_far))
        embed_grad = sums[:rows].astype(BF16)
        output = (resid_own + sums[rows:]).astype(BF16)
        ffn_total = ffn_sum.total()
        gate_grad, up_grad, down_grad = (
            ffn_total[:, i * units : (i + 1) * units] for i in range(3)
        )
        attn_total = attn_sum.total()
        wide_total = SumDp(turn(info, wide_grad, None, dp, own_dim), dp).total()
        grads_done = [attn_total[:, i * width : (i + 1) * width] for i in range(3)]
        grads_done += [wide_total[:, :ng].T, wide_total[:, ng : 2 * ng].T, wide_total[:, 2 * ng :].T]
        gains = lax.psum(gains.astype(F32), "dp")
    query_grad, key_grad, value_grad, two_grad, three_grad, output_grad = grads_done

    return (
        output,
        embed_grad,
        table_grad[0].T,
        table_grad[1].T,
        two_grad,
        three_grad,
        gains[0],
        query_grad,
        key_grad,
        value_grad,
        output_grad,
        gains[1],
        gate_grad,
        up_grad,
        down_grad.T,
    )


def solution(mesh):
    tokens = P(("dp", "tensor"), None)
    down, across = P("dp", "tensor"), P("tensor", "dp")
    in_specs = (
        (tokens, P("dp"), P("dp"), P("dp"), down, down, across, across, P())
        + (down, down, down, across, P(), down, down, across, tokens)
    )
    out_specs = (
        (tokens, tokens, down, down, across, across, P())
        + (down, down, down, across, P(), down, down, across)
    )
    body = functools.partial(shards, mesh.shape["dp"])
    return jax.shard_map(body, mesh=mesh, in_specs=in_specs, out_specs=out_specs, check_vma=False)
```

time: 250 us -> 243 us (0.972)
  Pallas kernels: 107 us -> 91.9 us
  waiting for transfers between devices: 60.6 us -> 67.5 us
  local copies, waits for them, and re-layouts: 14.7 us -> 11.3 us
  starting transfers between devices: 44 us -> 46.6 us
    ppermute x25, waiting for transfers between devices: 39.9 us -> 50.4 us  [xor_dp(): return lax.ppermute(value, 'dp', [(i, i ^ step) for i in range(count)])]
    pallas_call x3 -> x2, Pallas kernels: 16.8 us -> 7 us  [spread(): pl.pallas_call(functools.partial(spread_kernel, len(pieces), width, prior...]
    ppermute x25, starting transfers between devices: 32.9 us -> 36.6 us  [xor_dp(): return lax.ppermute(value, 'dp', [(i, i ^ step) for i in range(count)])]
    ppermute x20, waiting for transfers between devices: 20.7 us -> 17.1 us  [xor_tensor(): return lax.ppermute(value, 'tensor', [(i, i ^ step) for i in range(4)])]
    unnamed x89 -> x82, local copies, waits for them, and re-layouts: 8.09 us -> 4.88 us
    pallas_call x4 -> x5, Pallas kernels: 62.6 us -> 59.6 us  [the longest x1 19.7 us: back(): pl.pallas_call(back_kernel, out_shape=[jax.ShapeDtypeStruct(shape, BF16)...]
    pallas_call x3, Pallas kernels: 15 us -> 12.3 us  [lookup(): pl.pallas_call(functools.partial(lookup_kernel, owners, len(pieces), widt...]
  transfers between devices with their start and end apart: 45 -> 45, of which waited for: 19 -> 22; matrix products, arithmetic and copies ran while one was open for 11% -> 11% of each run, Pallas kernels for 34% -> 30%
where the time goes in v4:
time: 243 us; the launch traced here: 242 us
  Pallas kernels  91.9 us (38%)
  waiting for transfers between devices  67.5 us (28%)
  starting transfers between devices  46.6 us (19%)
  other arithmetic  23.4 us (10%)
  local copies, waits for them, and re-layouts  11.3 us (5%)
    ppermute x25, waiting for transfers between devices, xor_dp(): return lax.ppermute(value, 'dp', [(i, i ^ step) for i in range(count)])  50.4 us
    ppermute x25, starting transfers between devices, xor_dp(): return lax.ppermute(value, 'dp', [(i, i ^ step) for i in range(count)])  36.6 us
    pallas_call x1, Pallas kernels, back(): pl.pallas_call(back_kernel, out_shape=[jax.ShapeDtypeStruct(shape, BF16)...  19.7 us
    ppermute x20, waiting for transfers between devices, xor_tensor(): return lax.ppermute(value, 'tensor', [(i, i ^ step) for i in range(4)])  17.1 us
    pallas_call x1, Pallas kernels, middle(): pl.pallas_call(middle_kernel, in_specs=[pl.BlockSpec(memory_space=pltpu.S...  16.2 us
    pallas_call x1, Pallas kernels, front(): pl.pallas_call(front_kernel, out_shape=[jax.ShapeDtypeStruct(*shape) for...  12.9 us
    pallas_call x3, Pallas kernels, lookup(): pl.pallas_call(functools.partial(lookup_kernel, owners, len(pieces), widt...  12.3 us
    convert_element_type x11, other arithmetic, add_round(): return (one.astype(F32) + two.astype(F32)).astype(BF16)  11.4 us
  transfers between devices with their start and end apart: 45, of which 22 were waited for; matrix products, arithmetic and copies ran while one was open for 11% of the time, Pallas kernels for 30%

profile of v4, /device:TPU:0, one launch (start us, length us, event | category | flops | bytes accessed | tf_op | source)
XLA Modules:
  0.0 241.8 jit_solution(2288708349936299511)
XLA Ops:
  0.7 1.8 pack_first.1
  2.5 4.0 %collective-permute-start = (bf16[96,1152]{1,0:T(8,128)(2,1)}, bf16[96,1152]{1,0:T(8,128)(2,1)S(1)}, u32[]{:S(2)}, u32[]{:S(2)}) collective-permute-start(bf16[96,1152]{1,0:T(8,128)(2,1)} %pack_first.1), channel_id=1, source_target_pairs={{0,16},{4,20},{8,24},{12,28},{16,0},{20,4},{24,8},{28,12},{1,17},{... | collective-permute-start | bytes 663560 | tf_op jit(solution)/shard_map/ppermute | solution.py:26
  10.4 2.1 pack.1
  13.2 3.8 %collective-permute-done = bf16[96,1152]{1,0:T(8,128)(2,1)S(1)} collective-permute-done((bf16[96,1152]{1,0:T(8,128)(2,1)}, bf16[96,1152]{1,0:T(8,128)(2,1)S(1)}, u32[]{:S(2)}, u32[]{:S(2)}) %collective-permute-start) | collective-permute-done | bytes 221216 | tf_op jit(solution)/shard_map/ppermute | solution.py:26
  17.1 1.6 collective-permute-start.3
  19.4 1.5 collective-permute-start.8
  21.0 3.3 %collective-permute-start.1 = (bf16[96,768]{1,0:T(8,128)(2,1)}, bf16[96,768]{1,0:T(8,128)(2,1)}, u32[]{:S(2)}, u32[]{:S(2)}) collective-permute-start(bf16[96,768]{1,0:T(8,128)(2,1)} %get-tuple-element.109), channel_id=1, source_target_pairs={{0,16},{4,20},{8,24},{12,28},{16,0},{20,4},{24,8},{28,12},{1,17},{... | collective-permute-start | bytes 442376 | tf_op jit(solution)/shard_map/ppermute | solution.py:26
  25.6 3.6 %lookup.3.refs_4_ = bf16[96,1024]{1,0:T(8,128)(2,1)} custom-call(s32[10]{0:T(128)} %pad_add_fusion.1.refs_0_.info.who, s32[2,1024]{1,0:T(2,128)} %pad_add_fusion.refs_1_, bf16[2,96,1152]{2,1,0:T(8,128)(2,1)} %copy-done.4), custom_call_target="tpu_custom_call" | custom-call | tf_op jit(solution)/shard_map/lookup/pallas_call | solution.py:373
  29.2 3.6 %collective-permute-done.2.refs_2_.refs_4_ = bf16[2,96,1152]{2,1,0:T(8,128)(2,1)} collective-permute-done((bf16[2,96,1152]{2,1,0:T(8,128)(2,1)S(1)}, bf16[2,96,1152]{2,1,0:T(8,128)(2,1)}, u32[]{:S(2)}, u32[]{:S(2)}) %collective-permute-start.2) | collective-permute-done | bytes 442400 | tf_op jit(solution)/shard_map/ppermute | solution.py:26
  33.5 4.3 %lookup.4.refs_7_ = bf16[96,1024]{1,0:T(8,128)(2,1)} custom-call(s32[10]{0:T(128)} %pad_add_fusion.1.refs_0_.info.who, s32[2,1024]{1,0:T(2,128)} %pad_add_fusion.refs_1_, bf16[2,96,1152]{2,1,0:T(8,128)(2,1)} %collective-permute-done.2.refs_2_.refs_4_, bf16[2,96,1152]{2,1,0:T(8,128)(2,1)} %copy-done.7, bf16[96,1024]{1,0:T(8,128)(2,1)} %lookup.3.refs_4_), custom_call_target="tpu_custom_call" | custom-call | tf_op jit(solution)/shard_map/lookup/pallas_call | solution.py:373
  40.2 5.0 %collective-permute-start.14 = (bf16[96,1536]{1,0:T(8,128)(2,1)S(1)}, bf16[96,1536]{1,0:T(8,128)(2,1)}, u32[]{:S(2)}, u32[]{:S(2)}) collective-permute-start(bf16[96,1536]{1,0:T(8,128)(2,1)S(1)} %copy-done.31), channel_id=1, source_target_pairs={{0,16},{4,20},{8,24},{12,28},{16,0},{20,4},{24,8},{28,12},{1,17},{... | collective-permute-start | bytes 884744 | tf_op jit(solution)/shard_map/ppermute | solution.py:26
  46.8 4.4 %lookup.5.set0 = bf16[96,1792]{1,0:T(8,128)(2,1)} custom-call(s32[10]{0:T(128)} %pad_add_fusion.1.refs_0_.info.who, s32[2,1024]{1,0:T(2,128)} %pad_add_fusion.refs_1_, bf16[2,96,1152]{2,1,0:T(8,128)(2,1)} %copy-done.8, bf16[2,96,1152]{2,1,0:T(8,128)(2,1)} %copy-done.4, bf16[2,96,1152]{2,1,0:T(8,128)(2,1)} %collective-permute-done.2.refs_2_.refs_4_, ...), custom_call_target="tpu_custom_call" | custom-call | tf_op jit(solution)/shard_map/lookup/pallas_call | solution.py:373
  51.3 1.8 collective-permute-done.5.refs_1_
  53.1 1.5 collective-permute-start.10
  55.1 1.7 collective-permute-done.14
  58.5 6.1 %collective-permute-done.13.refs_3_ = bf16[2,96,768]{2,1,0:T(8,128)(2,1)S(1)} collective-permute-done((bf16[2,96,768]{2,1,0:T(8,128)(2,1)}, bf16[2,96,768]{2,1,0:T(8,128)(2,1)S(1)}, u32[]{:S(2)}, u32[]{:S(2)}) %collective-permute-start.13) | collective-permute-done | bytes 294944 | tf_op jit(solution)/shard_map/ppermute | solution.py:26
  65.4 2.9 %assemble.1 = (bf16[576,768]{1,0:T(8,128)(2,1)}, bf16[192,768]{1,0:T(8,128)(2,1)}) custom-call(s32[10]{0:T(128)} %pad_add_fusion.1.refs_0_.info.who, bf16[2,96,768]{2,1,0:T(8,128)(2,1)} %copy-done.17, bf16[2,96,768]{2,1,0:T(8,128)(2,1)} %collective-permute-done.5.refs_1_, bf16[2,96,768]{2,1,0:T(8,128)(2,1)} %collective-permute-done.6.refs_2_, ...), custom_call_target="tpu_custom_call" | custom-call | tf_op jit(solution)/shard_map/assemble/pallas_call | solution.py:125
  70.5 12.9 %front.1 = (f32[1024,768]{1,0:T(8,128)}, bf16[1024,768]{1,0:T(8,128)(2,1)}, bf16[576,1024]{1,0:T(8,128)(2,1)}, bf16[192,1024]{1,0:T(8,128)(2,1)}, f32[8,1024]{1,0:T(8,128)}) custom-call(s32[10]{0:T(128)} %pad_add_fusion.1.refs_0_.info.who, bf16[96,1792]{1,0:T(8,128)(2,1)} %lookup.5.set0, bf16[96,1792]{1,0:T(8,128)(2,1)} %copy-done.14, ...), custom_call_target="tpu_custom_call" | custom-call | tf_op jit(solution)/shard_map/front/pallas_call | solution.py:534
  83.4 1.6 collective-permute-start.17
  85.4 9.3 %collective-permute-done.17.mix2.refs_6_ = bf16[192,1024]{1,0:T(8,128)(2,1)S(1)} collective-permute-done((bf16[192,1024]{1,0:T(8,128)(2,1)}, bf16[192,1024]{1,0:T(8,128)(2,1)S(1)}, u32[]{:S(2)}, u32[]{:S(2)}) %collective-permute-start.17) | collective-permute-done | bytes 393248 | tf_op jit(solution)/shard_map/ppermute | solution.py:22
  95.3 1.7 collective-permute-done.19.out1
  97.5 2.6 %collective-permute-done.23.ffn3 = bf16[2,96,1536]{2,1,0:T(8,128)(2,1)S(1)} collective-permute-done((bf16[2,96,1536]{2,1,0:T(8,128)(2,1)}, bf16[2,96,1536]{2,1,0:T(8,128)(2,1)S(1)}, u32[]{:S(2)}, u32[]{:S(2)}) %collective-permute-start.23) | collective-permute-done | bytes 589856 | tf_op jit(solution)/shard_map/ppermute | solution.py:26
  101.2 16.2 %middle.1 = (bf16[2,256,768]{2,1,0:T(8,128)(2,1)}, bf16[2,256,768]{2,1,0:T(8,128)(2,1)}, f32[256,768]{1,0:T(8,128)}, bf16[1024,768]{1,0:T(8,128)(2,1)}, bf16[102...) custom-call(s32[10]{0:T(128)} %pad_add_fusion.1.refs_0_.info.who, ...), custom_call_target="tpu_custom_call" | custom-call | tf_op jit(solution)/shard_map/middle/pallas_call | solution.py:654
  117.5 2.5 %collective-permute-done.24 = bf16[2,192,1024]{2,1,0:T(8,128)(2,1)S(1)} collective-permute-done((bf16[2,192,1024]{2,1,0:T(8,128)(2,1)}, bf16[2,192,1024]{2,1,0:T(8,128)(2,1)S(1)}, u32[]{:S(2)}, u32[]{:S(2)}) %collective-permute-start.24) | collective-permute-done | bytes 786464 | tf_op jit(solution)/shard_map/ppermute | solution.py:22
  120.0 1.9 fusion.6
  122.4 9.0 %weigh.1 = (bf16[4,96,1536]{2,1,0:T(8,128)(2,1)}, bf16[4,96,1536]{2,1,0:T(8,128)(2,1)}, bf16[2,192,768]{2,1,0:T(8,128)(2,1)}, bf16[2,192,768]{2,1,0:T(8,128)(2,1)}) custom-call(s32[10]{0:T(128)} %pad_add_fusion.1.refs_0_.info.who, bf16[1024,512]{1,0:T(8,128)(2,1)} %get-tuple-element.137.hidden, bf16[1024,768]{1,0:T(8,128)(2,1)} %get-tuple-element.138.norm, ...), custom_call_target="tpu_custom_call" | custom-call | tf_op jit(solution)/shard_map/weigh/pallas_call | solution.py:231
  134.2 19.7 %back.1 = (bf16[576,1024]{1,0:T(8,128)(2,1)}, bf16[2,512,768]{2,1,0:T(8,128)(2,1)}, bf16[2,512,768]{2,1,0:T(8,128)(2,1)}, bf16[2,304,768]{2,1,0:T(8,128)(2,1)}, ...) custom-call(s32[10]{0:T(128)} %pad_add_fusion.1.refs_0_.info.who, ...), custom_call_target="tpu_custom_call" | custom-call | tf_op jit(solution)/shard_map/back/pallas_call | solution.py:797
  154.0 1.9 collective-permute-done.26
  155.9 1.8 fusion.10
  157.7 1.6 collective-permute-done.27
  159.3 1.5 collective-permute-start.28
  161.1 4.0 %split.2 = (bf16[4,96,576]{2,1,0:T(8,128)(2,1)}, bf16[4,96,576]{2,1,0:T(8,128)(2,1)}) custom-call(s32[10]{0:T(128)} %pad_add_fusion.1.refs_0_.info.who, bf16[1024,768]{1,0:T(8,128)(2,1)} %get-tuple-element.124.left, bf16[576,1024]{1,0:T(8,128)(2,1)} %get-tuple-element.154.right), custom_call_target="tpu_custom_call" | custom-call | tf_op jit(solution)/shard_map/split/pallas_call | solution.py:266
  170.7 2.8 %collective-permute-start.29 = (bf16[112,1024]{1,0:T(8,128)(2,1)S(1)}, bf16[112,1024]{1,0:T(8,128)(2,1)S(1)}, u32[]{:S(2)}, u32[]{:S(2)}) collective-permute-start(bf16[112,1024]{1,0:T(8,128)(2,1)S(1)} %get-tuple-element.211), channel_id=1, source_target_pairs={{0,16},{4,20},{8,24},{12,28},{16,0},{20,4},{24,8},{28,12},{1,17},{... | collective-permute-start | bytes 688136 | tf_op jit(solution)/shard_map/ppermute | solution.py:26
  173.6 11.1 %collective-permute-done.29 = bf16[112,1024]{1,0:T(8,128)(2,1)S(1)} collective-permute-done((bf16[112,1024]{1,0:T(8,128)(2,1)S(1)}, bf16[112,1024]{1,0:T(8,128)(2,1)S(1)}, u32[]{:S(2)}, u32[]{:S(2)}) %collective-permute-start.29) | collective-permute-done | bytes 229408 | tf_op jit(solution)/shard_map/ppermute | solution.py:26
  185.8 1.5 collective-permute-start.35
  187.3 2.9 %collective-permute-start.34 = (bf16[2,112,1024]{2,1,0:T(8,128)(2,1)S(1)}, bf16[2,112,1024]{2,1,0:T(8,128)(2,1)}, u32[]{:S(2)}, u32[]{:S(2)}) collective-permute-start(bf16[2,112,1024]{2,1,0:T(8,128)(2,1)S(1)} %pad_maximum_fusion.2.refs_1_), channel_id=1, source_target_pairs={{0,8},{4,12},{8,0},{12,4},{16,24},{20,28},{24,16},{28,20},{1,9},{5... | collective-permute-start | bytes 1376264 | tf_op jit(solution)/shard_map/ppermute | solution.py:26
  193.0 2.1 split.3
  195.1 2.3 collective-permute-done.35.refs_3_
  197.4 2.4 %collective-permute-done.34.refs_2_ = bf16[2,112,1024]{2,1,0:T(8,128)(2,1)} collective-permute-done((bf16[2,112,1024]{2,1,0:T(8,128)(2,1)S(1)}, bf16[2,112,1024]{2,1,0:T(8,128)(2,1)}, u32[]{:S(2)}, u32[]{:S(2)}) %collective-permute-start.34) | collective-permute-done | bytes 458784 | tf_op jit(solution)/shard_map/ppermute | solution.py:26
  204.9 4.3 %spread.2.refs_2_ = f32[96,1024]{1,0:T(8,128)} custom-call(s32[10]{0:T(128)} %pad_add_fusion.1.refs_0_.info.who, bf16[2,112,1024]{2,1,0:T(8,128)(2,1)} %copy-done.6, bf16[2,112,1024]{2,1,0:T(8,128)(2,1)} %collective-permute-done.34.refs_2_, bf16[2,112,1024]{2,1,0:T(8,128)(2,1)} %collective-permute-done.35.refs_3_), custom_call_target="tpu_custom_call" | custom-call | tf_op jit(solution)/shard_map/spread/pallas_call | solution.py:419
  209.2 1.5 add_convert_fusion.8
  212.6 2.8 %collective-permute-done.44 = bf16[96,1536]{1,0:T(8,128)(2,1)} collective-permute-done((bf16[96,1536]{1,0:T(8,128)(2,1)}, bf16[96,1536]{1,0:T(8,128)(2,1)}, u32[]{:S(2)}, u32[]{:S(2)}) %collective-permute-start.44) | collective-permute-done | bytes 294944 | tf_op jit(solution)/shard_map/ppermute | solution.py:26
  216.4 4.8 %collective-permute-done.37 = bf16[4,112,288]{2,1,0:T(8,128)(2,1)S(1)} collective-permute-done((bf16[4,112,288]{2,1,0:T(8,128)(2,1)}, bf16[4,112,288]{2,1,0:T(8,128)(2,1)S(1)}, u32[]{:S(2)}, u32[]{:S(2)}) %collective-permute-start.37) | collective-permute-done | bytes 258080 | tf_op jit(solution)/shard_map/ppermute | solution.py:26
  222.3 1.6 bitcast_add_fusion
  227.5 1.9 collective-permute-start.43
  231.9 2.7 %spread.3 = (f32[48,1024]{1,0:T(8,128)}, f32[48,1024]{1,0:T(8,128)}) custom-call(s32[10]{0:T(128)} %pad_add_fusion.1.refs_0_.info.who, bf16[2,112,1024]{2,1,0:T(8,128)(2,1)} %collective-permute-done.41.refs_1_, f32[96,1024]{1,0:T(8,128)} %spread.2.refs_2_), custom_call_target="tpu_custom_call" | custom-call | tf_op jit(solution)/shard_map/spread/pallas_call | solution.py:419
  234.7 2.6 %collective-permute-done.42.attn_come = bf16[96,576]{1,0:T(8,128)(2,1)S(1)} collective-permute-done((bf16[96,576]{1,0:T(8,128)(2,1)S(1)}, bf16[96,576]{1,0:T(8,128)(2,1)S(1)}, u32[]{:S(2)}, u32[]{:S(2)}) %collective-permute-start.42) | collective-permute-done | bytes 110624 | tf_op jit(solution)/shard_map/ppermute | solution.py:26
  237.9 1.9 finish.1
  (184 shorter events, 50.1 us)
Async XLA Ops:
  2.5 14.5 %collective-permute-start = (bf16[96,1152]{1,0:T(8,128)(2,1)}, bf16[96,1152]{1,0:T(8,128)(2,1)S(1)}, u32[]{:S(2)}, u32[]{:S(2)}) collective-permute-start(bf16[96,1152]{1,0:T(8,128)(2,1)} %pack_first.1), channel_id=1, source_target_pairs={{0,16},{4,20},{8,24},{12,28},{16,0},{20,4},{24,8},{28,12},{1,17},{... | collective-permute-start | bytes 663560 | tf_op jit(solution)/shard_map/ppermute | solution.py:26
  7.8 30.1 %copy-start = (bf16[2,256,768]{2,1,0:T(8,128)(2,1)}, bf16[2,256,768]{2,1,0:T(8,128)(2,1)S(1)}, u32[]{:S(2)}) copy-start(bf16[2,256,768]{2,1,0:T(8,128)(2,1)S(1)} %pad_maximum_fusion.emb0.cot0.refs_0_) | copy-start | bytes 2359300
  7.8 25.0 %collective-permute-start.4 = (bf16[2,256,768]{2,1,0:T(8,128)(2,1)S(1)}, bf16[2,256,768]{2,1,0:T(8,128)(2,1)S(1)}, u32[]{:S(2)}, u32[]{:S(2)}) collective-permute-start(bf16[2,256,768]{2,1,0:T(8,128)(2,1)S(1)} %pad_maximum_fusion.emb0.cot0.refs_0_), channel_id=1, source_target_pairs={{0,1},{1,0},{2,3},{3,2},{4,5},{5,4},{6,7},{7,6},{8,9},{9,8},{10,11... | collective-permute-start | bytes 2359304 | tf_op jit(solution)/shard_map/ppermute | solution.py:22
  17.1 12.1 %collective-permute-start.3 = (bf16[2,96,1152]{2,1,0:T(8,128)(2,1)S(1)}, bf16[2,96,1152]{2,1,0:T(8,128)(2,1)S(1)}, u32[]{:S(2)}, u32[]{:S(2)}) collective-permute-start(bf16[2,96,1152]{2,1,0:T(8,128)(2,1)S(1)} %pad_maximum_fusion.3.refs_2_.refs_3_), channel_id=1, source_target_pairs={{0,4},{4,0},{8,12},{12,8},{16,20},{20,16},{24,28},{28,24},{1,5},{5... | collective-permute-start | bytes 1327112 | tf_op jit(solution)/shard_map/ppermute | solution.py:26
  18.7 14.1 %collective-permute-start.2 = (bf16[2,96,1152]{2,1,0:T(8,128)(2,1)S(1)}, bf16[2,96,1152]{2,1,0:T(8,128)(2,1)}, u32[]{:S(2)}, u32[]{:S(2)}) collective-permute-start(bf16[2,96,1152]{2,1,0:T(8,128)(2,1)S(1)} %pad_maximum_fusion.3.refs_2_.refs_3_), channel_id=1, source_target_pairs={{0,8},{4,12},{8,0},{12,4},{16,24},{20,28},{24,16},{28,20},{1,9},{5... | collective-permute-start | bytes 1327112 | tf_op jit(solution)/shard_map/ppermute | solution.py:26
  19.4 31.8 %collective-permute-start.8 = (bf16[2,256,768]{2,1,0:T(8,128)(2,1)S(1)}, bf16[2,256,768]{2,1,0:T(8,128)(2,1)S(1)}, u32[]{:S(2)}, u32[]{:S(2)}) collective-permute-start(bf16[2,256,768]{2,1,0:T(8,128)(2,1)S(1)} %pad_maximum_fusion.emb0.cot0.refs_0_), channel_id=1, source_target_pairs={{0,2},{1,3},{2,0},{3,1},{4,6},{5,7},{6,4},{7,5},{8,10},{9,11},{10,... | collective-permute-start | bytes 2359304 | tf_op jit(solution)/shard_map/ppermute | solution.py:22
  21.0 16.8 %collective-permute-start.1 = (bf16[96,768]{1,0:T(8,128)(2,1)}, bf16[96,768]{1,0:T(8,128)(2,1)}, u32[]{:S(2)}, u32[]{:S(2)}) collective-permute-start(bf16[96,768]{1,0:T(8,128)(2,1)} %get-tuple-element.109), channel_id=1, source_target_pairs={{0,16},{4,20},{8,24},{12,28},{16,0},{20,4},{24,8},{28,12},{1,17},{... | collective-permute-start | bytes 442376 | tf_op jit(solution)/shard_map/ppermute | solution.py:26
  32.8 13.3 %collective-permute-start.7 = (bf16[2,96,1152]{2,1,0:T(8,128)(2,1)}, bf16[2,96,1152]{2,1,0:T(8,128)(2,1)S(1)}, u32[]{:S(2)}, u32[]{:S(2)}) collective-permute-start(bf16[2,96,1152]{2,1,0:T(8,128)(2,1)} %collective-permute-done.2.refs_2_.refs_4_), channel_id=1, source_target_pairs={{0,4},{4,0},{8,12},{12,8},{16,20},{20,16},{24,28},{28,24},{1,5},{5... | collective-permute-start | bytes 1327112 | tf_op jit(solution)/shard_map/ppermute | solution.py:26
  38.9 12.4 %collective-permute-start.6 = (bf16[2,96,768]{2,1,0:T(8,128)(2,1)S(1)}, bf16[2,96,768]{2,1,0:T(8,128)(2,1)}, u32[]{:S(2)}, u32[]{:S(2)}) collective-permute-start(bf16[2,96,768]{2,1,0:T(8,128)(2,1)S(1)} %pad_maximum_fusion.4.refs_0_), channel_id=1, source_target_pairs={{0,4},{4,0},{8,12},{12,8},{16,20},{20,16},{24,28},{28,24},{1,5},{5... | collective-permute-start | bytes 884744 | tf_op jit(solution)/shard_map/ppermute | solution.py:26
  40.2 12.9 %collective-permute-start.5 = (bf16[2,96,768]{2,1,0:T(8,128)(2,1)S(1)}, bf16[2,96,768]{2,1,0:T(8,128)(2,1)}, u32[]{:S(2)}, u32[]{:S(2)}) collective-permute-start(bf16[2,96,768]{2,1,0:T(8,128)(2,1)S(1)} %pad_maximum_fusion.4.refs_0_), channel_id=1, source_target_pairs={{0,8},{4,12},{8,0},{12,4},{16,24},{20,28},{24,16},{28,20},{1,9},{5... | collective-permute-start | bytes 884744 | tf_op jit(solution)/shard_map/ppermute | solution.py:26
  40.2 16.7 %collective-permute-start.14 = (bf16[96,1536]{1,0:T(8,128)(2,1)S(1)}, bf16[96,1536]{1,0:T(8,128)(2,1)}, u32[]{:S(2)}, u32[]{:S(2)}) collective-permute-start(bf16[96,1536]{1,0:T(8,128)(2,1)S(1)} %copy-done.31), channel_id=1, source_target_pairs={{0,16},{4,20},{8,24},{12,28},{16,0},{20,4},{24,8},{28,12},{1,17},{... | collective-permute-start | bytes 884744 | tf_op jit(solution)/shard_map/ppermute | solution.py:26
  53.1 15.8 %collective-permute-start.12 = (bf16[2,256,768]{2,1,0:T(8,128)(2,1)S(1)}, bf16[2,256,768]{2,1,0:T(8,128)(2,1)S(1)}, u32[]{:S(2)}, u32[]{:S(2)}) collective-permute-start(bf16[2,256,768]{2,1,0:T(8,128)(2,1)S(1)} %collective-permute-done.8.emb2.cot2.refs_2_), channel_id=1, source_target_pairs={{0,1},{1,0},{2,3},{3,2},{4,5},{5,4},{6,7},{7,6},{8,9},{9,8},{10,11... | collective-permute-start | bytes 2359304 | tf_op jit(solution)/shard_map/ppermute | solution.py:22
  53.1 12.3 %collective-permute-start.10 = (bf16[96,1792]{1,0:T(8,128)(2,1)}, bf16[96,1792]{1,0:T(8,128)(2,1)S(1)}, u32[]{:S(2)}, u32[]{:S(2)}) collective-permute-start(bf16[96,1792]{1,0:T(8,128)(2,1)} %lookup.5.set0), channel_id=1, source_target_pairs={{0,2},{1,3},{2,0},{3,1},{4,6},{5,7},{6,4},{7,5},{8,10},{9,11},{10,... | collective-permute-start | bytes 1032200 | tf_op jit(solution)/shard_map/ppermute | solution.py:22
  54.6 10.1 %collective-permute-start.13 = (bf16[2,96,768]{2,1,0:T(8,128)(2,1)}, bf16[2,96,768]{2,1,0:T(8,128)(2,1)S(1)}, u32[]{:S(2)}, u32[]{:S(2)}) collective-permute-start(bf16[2,96,768]{2,1,0:T(8,128)(2,1)} %collective-permute-done.5.refs_1_), channel_id=1, source_target_pairs={{0,4},{4,0},{8,12},{12,8},{16,20},{20,16},{24,28},{28,24},{1,5},{5... | collective-permute-start | bytes 884744 | tf_op jit(solution)/shard_map/ppermute | solution.py:26
  55.1 13.1 %collective-permute-start.9 = (bf16[96,1792]{1,0:T(8,128)(2,1)}, bf16[96,1792]{1,0:T(8,128)(2,1)S(1)}, u32[]{:S(2)}, u32[]{:S(2)}) collective-permute-start(bf16[96,1792]{1,0:T(8,128)(2,1)} %lookup.5.set0), channel_id=1, source_target_pairs={{0,1},{1,0},{2,3},{3,2},{4,5},{5,4},{6,7},{7,6},{8,9},{9,8},{10,11... | collective-permute-start | bytes 1032200 | tf_op jit(solution)/shard_map/ppermute | solution.py:22
  57.9 25.5 %copy-start.5 = (bf16[2,96,1536]{2,1,0:T(8,128)(2,1)}, bf16[2,96,1536]{2,1,0:T(8,128)(2,1)S(1)}, u32[]{:S(2)}) copy-start(bf16[2,96,1536]{2,1,0:T(8,128)(2,1)S(1)} %pad_maximum_fusion.1.ffn0) | copy-start | bytes 1769476
  57.9 27.0 %collective-permute-start.22 = (bf16[2,96,1536]{2,1,0:T(8,128)(2,1)S(1)}, bf16[2,96,1536]{2,1,0:T(8,128)(2,1)}, u32[]{:S(2)}, u32[]{:S(2)}) collective-permute-start(bf16[2,96,1536]{2,1,0:T(8,128)(2,1)S(1)} %pad_maximum_fusion.1.ffn0), channel_id=1, source_target_pairs={{0,4},{4,0},{8,12},{12,8},{16,20},{20,16},{24,28},{28,24},{1,5},{5... | collective-permute-start | bytes 1769480 | tf_op jit(solution)/shard_map/ppermute | solution.py:26
  64.7 20.3 %collective-permute-start.21 = (bf16[2,96,1536]{2,1,0:T(8,128)(2,1)S(1)}, bf16[2,96,1536]{2,1,0:T(8,128)(2,1)}, u32[]{:S(2)}, u32[]{:S(2)}) collective-permute-start(bf16[2,96,1536]{2,1,0:T(8,128)(2,1)S(1)} %pad_maximum_fusion.1.ffn0), channel_id=1, source_target_pairs={{0,8},{4,12},{8,0},{12,4},{16,24},{20,28},{24,16},{28,20},{1,9},{5... | collective-permute-start | bytes 1769480 | tf_op jit(solution)/shard_map/ppermute | solution.py:26
  65.4 3.5 %collective-permute-start.11 = (bf16[96,1792]{1,0:T(8,128)(2,1)S(1)}, bf16[96,1792]{1,0:T(8,128)(2,1)S(1)}, u32[]{:S(2)}, u32[]{:S(2)}) collective-permute-start(bf16[96,1792]{1,0:T(8,128)(2,1)S(1)} %collective-permute-done.10.set2), channel_id=1, source_target_pairs={{0,1},{1,0},{2,3},{3,2},{4,5},{5,4},{6,7},{7,6},{8,9},{9,8},{10,11... | collective-permute-start | bytes 1032200 | tf_op jit(solution)/shard_map/ppermute | solution.py:22
  68.2 15.1 %collective-permute-start.15 = (bf16[192,768]{1,0:T(8,128)(2,1)}, bf16[192,768]{1,0:T(8,128)(2,1)}, u32[]{:S(2)}, u32[]{:S(2)}) collective-permute-start(bf16[192,768]{1,0:T(8,128)(2,1)} %get-tuple-element.128.out0), channel_id=1, source_target_pairs={{0,2},{1,3},{2,0},{3,1},{4,6},{5,7},{6,4},{7,5},{8,10},{9,11},{10,... | collective-permute-start | bytes 884744 | tf_op jit(solution)/shard_map/ppermute | solution.py:22
  83.4 11.4 %collective-permute-start.17 = (bf16[192,1024]{1,0:T(8,128)(2,1)}, bf16[192,1024]{1,0:T(8,128)(2,1)S(1)}, u32[]{:S(2)}, u32[]{:S(2)}) collective-permute-start(bf16[192,1024]{1,0:T(8,128)(2,1)} %get-tuple-element.129.mix0.refs_4_.mixed), channel_id=1, source_target_pairs={{0,2},{1,3},{2,0},{3,1},{4,6},{5,7},{6,4},{7,5},{8,10},{9,11},{10,... | collective-permute-start | bytes 1179656 | tf_op jit(solution)/shard_map/ppermute | solution.py:22
  84.9 15.2 %collective-permute-start.23 = (bf16[2,96,1536]{2,1,0:T(8,128)(2,1)}, bf16[2,96,1536]{2,1,0:T(8,128)(2,1)S(1)}, u32[]{:S(2)}, u32[]{:S(2)}) collective-permute-start(bf16[2,96,1536]{2,1,0:T(8,128)(2,1)} %collective-permute-done.21.ffn1), channel_id=1, source_target_pairs={{0,4},{4,0},{8,12},{12,8},{16,20},{20,16},{24,28},{28,24},{1,5},{5... | collective-permute-start | bytes 1769480 | tf_op jit(solution)/shard_map/ppermute | solution.py:26
  85.4 12.1 %collective-permute-start.16 = (bf16[192,1024]{1,0:T(8,128)(2,1)}, bf16[192,1024]{1,0:T(8,128)(2,1)S(1)}, u32[]{:S(2)}, u32[]{:S(2)}) collective-permute-start(bf16[192,1024]{1,0:T(8,128)(2,1)} %get-tuple-element.129.mix0.refs_4_.mixed), channel_id=1, source_target_pairs={{0,1},{1,0},{2,3},{3,2},{4,5},{5,4},{6,7},{7,6},{8,9},{9,8},{10,11... | collective-permute-start | bytes 1179656 | tf_op jit(solution)/shard_map/ppermute | solution.py:22
  94.8 5.4 %collective-permute-start.18 = (bf16[192,1024]{1,0:T(8,128)(2,1)S(1)}, bf16[192,1024]{1,0:T(8,128)(2,1)S(1)}, u32[]{:S(2)}, u32[]{:S(2)}) collective-permute-start(bf16[192,1024]{1,0:T(8,128)(2,1)S(1)} %collective-permute-done.17.mix2.refs_6_), channel_id=1, source_target_pairs={{0,1},{1,0},{2,3},{3,2},{4,5},{5,4},{6,7},{7,6},{8,9},{9,8},{10,11... | collective-permute-start | bytes 1179656 | tf_op jit(solution)/shard_map/ppermute | solution.py:22
  94.8 2.2 collective-permute-start.19
  95.3 2.3 collective-permute-start.20
  117.4 2.6 %collective-permute-start.24 = (bf16[2,192,1024]{2,1,0:T(8,128)(2,1)}, bf16[2,192,1024]{2,1,0:T(8,128)(2,1)S(1)}, u32[]{:S(2)}, u32[]{:S(2)}) collective-permute-start(bf16[2,192,1024]{2,1,0:T(8,128)(2,1)} %get-tuple-element.135), channel_id=1, source_target_pairs={{0,1},{1,0},{2,3},{3,2},{4,5},{5,4},{6,7},{7,6},{8,9},{9,8},{10,11... | collective-permute-start | bytes 2359304 | tf_op jit(solution)/shard_map/ppermute | solution.py:22
  121.9 11.4 %collective-permute-start.25 = (bf16[192,1024]{1,0:T(8,128)(2,1)}, bf16[192,1024]{1,0:T(8,128)(2,1)S(1)}, u32[]{:S(2)}, u32[]{:S(2)}) collective-permute-start(bf16[192,1024]{1,0:T(8,128)(2,1)} %fusion.6), channel_id=1, source_target_pairs={{0,2},{1,3},{2,0},{3,1},{4,6},{5,7},{6,4},{7,5},{8,10},{9,11},{10,... | collective-permute-start | bytes 1179656 | tf_op jit(solution)/shard_map/ppermute | solution.py:22
  131.4 27.9 %collective-permute-start.27 = (bf16[4,96,1536]{2,1,0:T(8,128)(2,1)}, bf16[4,96,1536]{2,1,0:T(8,128)(2,1)S(1)}, u32[]{:S(2)}, u32[]{:S(2)}) collective-permute-start(bf16[4,96,1536]{2,1,0:T(8,128)(2,1)} %get-tuple-element.141), channel_id=1, source_target_pairs={{0,4},{4,0},{8,12},{12,8},{16,20},{20,16},{24,28},{28,24},{1,5},{5... | collective-permute-start | bytes 3538952 | tf_op jit(solution)/shard_map/ppermute | solution.py:26
  134.2 26.6 %copy-start.16 = (bf16[4,96,1536]{2,1,0:T(8,128)(2,1)S(1)}, bf16[4,96,1536]{2,1,0:T(8,128)(2,1)}, u32[]{:S(2)}) copy-start(bf16[4,96,1536]{2,1,0:T(8,128)(2,1)} %get-tuple-element.142) | copy-start | bytes 3538948
  153.9 2.0 collective-permute-start.26
  159.3 8.8 %collective-permute-start.31 = (bf16[2,304,768]{2,1,0:T(8,128)(2,1)}, bf16[2,304,768]{2,1,0:T(8,128)(2,1)}, u32[]{:S(2)}, u32[]{:S(2)}) collective-permute-start(bf16[2,304,768]{2,1,0:T(8,128)(2,1)} %get-tuple-element.160), channel_id=1, source_target_pairs={{0,1},{1,0},{2,3},{3,2},{4,5},{5,4},{6,7},{7,6},{8,9},{9,8},{10,11... | collective-permute-start | bytes 2801672 | tf_op jit(solution)/shard_map/ppermute | solution.py:22
  159.3 7.7 %collective-permute-start.28 = (bf16[96,1024]{1,0:T(8,128)(2,1)}, bf16[96,1024]{1,0:T(8,128)(2,1)}, u32[]{:S(2)}, u32[]{:S(2)}) collective-permute-start(bf16[96,1024]{1,0:T(8,128)(2,1)} %fusion.10), channel_id=1, source_target_pairs={{0,2},{1,3},{2,0},{3,1},{4,6},{5,7},{6,4},{7,5},{8,10},{9,11},{10,... | collective-permute-start | bytes 589832 | tf_op jit(solution)/shard_map/ppermute | solution.py:22
  165.2 19.6 %collective-permute-start.30 = (bf16[4,96,576]{2,1,0:T(8,128)(2,1)}, bf16[4,96,576]{2,1,0:T(8,128)(2,1)}, u32[]{:S(2)}, u32[]{:S(2)}) collective-permute-start(bf16[4,96,576]{2,1,0:T(8,128)(2,1)} %get-tuple-element.156), channel_id=1, source_target_pairs={{0,4},{4,0},{8,12},{12,8},{16,20},{20,16},{24,28},{28,24},{1,5},{5... | collective-permute-start | bytes 1327112 | tf_op jit(solution)/shard_map/ppermute | solution.py:26
  165.7 20.1 %collective-permute-start.33 = (bf16[2,96,1536]{2,1,0:T(8,128)(2,1)S(1)}, bf16[2,96,1536]{2,1,0:T(8,128)(2,1)S(1)}, u32[]{:S(2)}, u32[]{:S(2)}) collective-permute-start(bf16[2,96,1536]{2,1,0:T(8,128)(2,1)S(1)} %get-tuple-element.198), channel_id=1, source_target_pairs={{0,8},{4,12},{8,0},{12,4},{16,24},{20,28},{24,16},{28,20},{1,9},{5... | collective-permute-start | bytes 1769480 | tf_op jit(solution)/shard_map/ppermute | solution.py:26
  167.1 34.8 %collective-permute-start.38 = (bf16[2,512,768]{2,1,0:T(8,128)(2,1)}, bf16[2,512,768]{2,1,0:T(8,128)(2,1)}, u32[]{:S(2)}, u32[]{:S(2)}) collective-permute-start(bf16[2,512,768]{2,1,0:T(8,128)(2,1)} %get-tuple-element.175), channel_id=1, source_target_pairs={{0,1},{1,0},{2,3},{3,2},{4,5},{5,4},{6,7},{7,6},{8,9},{9,8},{10,11... | collective-permute-start | bytes 4718600 | tf_op jit(solution)/shard_map/ppermute | solution.py:22
  169.3 16.5 %collective-permute-start.32 = (bf16[304,768]{1,0:T(8,128)(2,1)S(1)}, bf16[304,768]{1,0:T(8,128)(2,1)S(1)}, u32[]{:S(2)}, u32[]{:S(2)}) collective-permute-start(bf16[304,768]{1,0:T(8,128)(2,1)S(1)} %fusion.4), channel_id=1, source_target_pairs={{0,2},{1,3},{2,0},{3,1},{4,6},{5,7},{6,4},{7,5},{8,10},{9,11},{10,... | collective-permute-start | bytes 1400840 | tf_op jit(solution)/shard_map/ppermute | solution.py:22
  170.7 13.9 %collective-permute-start.29 = (bf16[112,1024]{1,0:T(8,128)(2,1)S(1)}, bf16[112,1024]{1,0:T(8,128)(2,1)S(1)}, u32[]{:S(2)}, u32[]{:S(2)}) collective-permute-start(bf16[112,1024]{1,0:T(8,128)(2,1)S(1)} %get-tuple-element.211), channel_id=1, source_target_pairs={{0,16},{4,20},{8,24},{12,28},{16,0},{20,4},{24,8},{28,12},{1,17},{... | collective-permute-start | bytes 688136 | tf_op jit(solution)/shard_map/ppermute | solution.py:26
  185.8 11.6 %collective-permute-start.35 = (bf16[2,112,1024]{2,1,0:T(8,128)(2,1)S(1)}, bf16[2,112,1024]{2,1,0:T(8,128)(2,1)}, u32[]{:S(2)}, u32[]{:S(2)}) collective-permute-start(bf16[2,112,1024]{2,1,0:T(8,128)(2,1)S(1)} %pad_maximum_fusion.2.refs_1_), channel_id=1, source_target_pairs={{0,4},{4,0},{8,12},{12,8},{16,20},{20,16},{24,28},{28,24},{1,5},{5... | collective-permute-start | bytes 1376264 | tf_op jit(solution)/shard_map/ppermute | solution.py:26
  187.3 12.5 %collective-permute-start.34 = (bf16[2,112,1024]{2,1,0:T(8,128)(2,1)S(1)}, bf16[2,112,1024]{2,1,0:T(8,128)(2,1)}, u32[]{:S(2)}, u32[]{:S(2)}) collective-permute-start(bf16[2,112,1024]{2,1,0:T(8,128)(2,1)S(1)} %pad_maximum_fusion.2.refs_1_), channel_id=1, source_target_pairs={{0,8},{4,12},{8,0},{12,4},{16,24},{20,28},{24,16},{28,20},{1,9},{5... | collective-permute-start | bytes 1376264 | tf_op jit(solution)/shard_map/ppermute | solution.py:26
  200.6 14.7 %collective-permute-start.44 = (bf16[96,1536]{1,0:T(8,128)(2,1)}, bf16[96,1536]{1,0:T(8,128)(2,1)}, u32[]{:S(2)}, u32[]{:S(2)}) collective-permute-start(bf16[96,1536]{1,0:T(8,128)(2,1)} %fusion.9), channel_id=1, source_target_pairs={{0,16},{4,20},{8,24},{12,28},{16,0},{20,4},{24,8},{28,12},{1,17},{... | collective-permute-start | bytes 884744 | tf_op jit(solution)/shard_map/ppermute | solution.py:26
  203.2 18.0 %collective-permute-start.39 = (bf16[512,768]{1,0:T(8,128)(2,1)S(1)}, bf16[512,768]{1,0:T(8,128)(2,1)}, u32[]{:S(2)}, u32[]{:S(2)}) collective-permute-start(bf16[512,768]{1,0:T(8,128)(2,1)S(1)} %fusion.1), channel_id=1, source_target_pairs={{0,2},{1,3},{2,0},{3,1},{4,6},{5,7},{6,4},{7,5},{8,10},{9,11},{10,... | collective-permute-start | bytes 2359304 | tf_op jit(solution)/shard_map/ppermute | solution.py:22
  203.8 28.1 %collective-permute-start.41 = (bf16[2,112,1024]{2,1,0:T(8,128)(2,1)}, bf16[2,112,1024]{2,1,0:T(8,128)(2,1)}, u32[]{:S(2)}, u32[]{:S(2)}) collective-permute-start(bf16[2,112,1024]{2,1,0:T(8,128)(2,1)} %collective-permute-done.34.refs_2_), channel_id=1, source_target_pairs={{0,4},{4,0},{8,12},{12,8},{16,20},{20,16},{24,28},{28,24},{1,5},{5... | collective-permute-start | bytes 1376264 | tf_op jit(solution)/shard_map/ppermute | solution.py:26
  210.6 14.9 %collective-permute-start.36 = (bf16[2,96,576]{2,1,0:T(8,128)(2,1)S(1)}, bf16[2,96,576]{2,1,0:T(8,128)(2,1)S(1)}, u32[]{:S(2)}, u32[]{:S(2)}) collective-permute-start(bf16[2,96,576]{2,1,0:T(8,128)(2,1)S(1)} %get-tuple-element.200), channel_id=1, source_target_pairs={{0,8},{4,12},{8,0},{12,4},{16,24},{20,28},{24,16},{28,20},{1,9},{5... | collective-permute-start | bytes 663560 | tf_op jit(solution)/shard_map/ppermute | solution.py:26
  211.7 9.5 %collective-permute-start.37 = (bf16[4,112,288]{2,1,0:T(8,128)(2,1)}, bf16[4,112,288]{2,1,0:T(8,128)(2,1)S(1)}, u32[]{:S(2)}, u32[]{:S(2)}) collective-permute-start(bf16[4,112,288]{2,1,0:T(8,128)(2,1)} %get-tuple-element.172), channel_id=1, source_target_pairs={{0,4},{4,0},{8,12},{12,8},{16,20},{20,16},{24,28},{28,24},{1,5},{5... | collective-permute-start | bytes 774152 | tf_op jit(solution)/shard_map/ppermute | solution.py:26
  221.3 5.5 %collective-permute-start.40 = (bf16[2,112,288]{2,1,0:T(8,128)(2,1)S(1)}, bf16[2,112,288]{2,1,0:T(8,128)(2,1)S(1)}, u32[]{:S(2)}, u32[]{:S(2)}) collective-permute-start(bf16[2,112,288]{2,1,0:T(8,128)(2,1)S(1)} %get-tuple-element.202), channel_id=1, source_target_pairs={{0,8},{4,12},{8,0},{12,4},{16,24},{20,28},{24,16},{28,20},{1,9},{5... | collective-permute-start | bytes 387080 | tf_op jit(solution)/shard_map/ppermute | solution.py:26
  227.5 7.2 %collective-permute-start.43 = (bf16[112,288]{1,0:T(8,128)(2,1)S(1)}, bf16[112,288]{1,0:T(8,128)(2,1)S(1)}, u32[]{:S(2)}, u32[]{:S(2)}) collective-permute-start(bf16[112,288]{1,0:T(8,128)(2,1)S(1)} %get-tuple-element.208), channel_id=1, source_target_pairs={{0,16},{4,20},{8,24},{12,28},{16,0},{20,4},{24,8},{28,12},{1,17},{... | collective-permute-start | bytes 193544 | tf_op jit(solution)/shard_map/ppermute | solution.py:26
  230.1 7.2 %collective-permute-start.42 = (bf16[96,576]{1,0:T(8,128)(2,1)S(1)}, bf16[96,576]{1,0:T(8,128)(2,1)S(1)}, u32[]{:S(2)}, u32[]{:S(2)}) collective-permute-start(bf16[96,576]{1,0:T(8,128)(2,1)S(1)} %get-tuple-element.206), channel_id=1, source_target_pairs={{0,16},{4,20},{8,24},{12,28},{16,0},{20,4},{24,8},{28,12},{1,17},{... | collective-permute-start | bytes 331784 | tf_op jit(solution)/shard_map/ppermute | solution.py:26
  (38 other events, 254.8 us)

commit v5 on v4

--- a/solution.py
+++ b/solution.py
@@ -950,19 +950,25 @@
     if dp == 8:
         folded = gains.reshape(2 * dim // (2 * ng), 2 * ng)
         halves = turn(info, wide_grad, folded, dp, own_dim)
-        two, one, ffn_sum.second, halves = lax.optimization_barrier(
-            (xor_dp(zero, 2, dp), xor_dp(zero, 1, dp), ffn_sum.second, halves)
+        proj_sum = SumDp(halves, dp)
+        ffn_sum.between()
+        two, one, ffn_sum.third, proj_sum.first = lax.optimization_barrier(
+            (xor_dp(zero, 2, dp), xor_dp(zero, 1, dp), ffn_sum.third, proj_sum.first)
         )
         three = xor_dp(two, 1, dp)
-        proj_sum = SumDp(halves, dp)
-        ffn_sum.between()
         attn_sum.first = after(attn_sum.first, two)
         attn_sum.across()
+        proj_sum.across()
+        zero = after(zero, attn_sum.stay, proj_sum.stay)
         table_grad = spread(info, [zero, two, one], own_rows, ng, None, False)
-        proj_sum.first, token_far, table_grad = lax.optimization_barrier(
-            (proj_sum.first, token_far, table_grad)
+        attn_sum.second, proj_sum.second, token_far, table_grad = lax.optimization_barrier(
+            (attn_sum.second, proj_sum.second, token_far, table_grad)
         )
-        proj_sum.across()
+        attn_sum.between()
+        proj_sum.between()
+        token_far, ffn_sum.third = (
+            after(x, attn_sum.ours, proj_sum.ours) for x in (token_far, ffn_sum.third)
+        )
         ffn_total = ffn_sum.total()
         sums = total((stay[0], token_near[0], token_far))
         embed_grad = sums[:rows].astype(BF16)
@@ -970,13 +976,9 @@
         gate_grad, up_grad, down_grad = (
             ffn_total[:, i * units : (i + 1) * units] for i in range(3)
         )
-        attn_sum.second, proj_sum.second, embed_grad, output, table_grad = (
-            lax.optimization_barrier(
-                (attn_sum.second, proj_sum.second, embed_grad, output, table_grad)
-            )
+        embed_grad, output, table_grad = lax.optimization_barrier(
+            (embed_grad, output, table_grad)
         )
-        proj_sum.between()
-        attn_sum.between()
         table_grad = spread(info, [three], own_rows, ng, table_grad, True)
         *grads_done, folded = finish(attn_sum, proj_sum, ng)
         gains = folded.reshape(2, dim)

time: 243 us -> 238 us (0.979)
  waiting for transfers between devices: 67.5 us -> 62.5 us
  starting transfers between devices: 46.6 us -> 43.8 us
  other arithmetic: 23.4 us -> 26 us
    ppermute x25, waiting for transfers between devices: 50.4 us -> 45.5 us  [xor_dp(): return lax.ppermute(value, 'dp', [(i, i ^ step) for i in range(count)])]
    convert_element_type x11, other arithmetic: 11.4 us -> 14.1 us  [add_round(): return (one.astype(F32) + two.astype(F32)).astype(BF16)]
    unnamed x82 -> x86, local copies, waits for them, and re-layouts: 4.88 us -> 5.49 us
  transfers between devices with their start and end apart: 45 -> 45, of which waited for: 22 -> 19; matrix products, arithmetic and copies ran while one was open for 11% -> 12% of each run, Pallas kernels for 30% -> 30%
where the time goes in v5:
time: 238 us; the launch traced here: 237 us
  Pallas kernels  92.1 us (39%)
  waiting for transfers between devices  62.5 us (26%)
  starting transfers between devices  43.8 us (18%)
  other arithmetic  26 us (11%)
  local copies, waits for them, and re-layouts  11.9 us (5%)
    ppermute x25, waiting for transfers between devices, xor_dp(): return lax.ppermute(value, 'dp', [(i, i ^ step) for i in range(count)])  45.5 us
    ppermute x25, starting transfers between devices, xor_dp(): return lax.ppermute(value, 'dp', [(i, i ^ step) for i in range(count)])  34.5 us
    pallas_call x1, Pallas kernels, back(): pl.pallas_call(back_kernel, out_shape=[jax.ShapeDtypeStruct(shape, BF16)...  19.8 us
    ppermute x20, waiting for transfers between devices, xor_tensor(): return lax.ppermute(value, 'tensor', [(i, i ^ step) for i in range(4)])  17.1 us
    pallas_call x1, Pallas kernels, middle(): pl.pallas_call(middle_kernel, in_specs=[pl.BlockSpec(memory_space=pltpu.S...  16.2 us
    convert_element_type x11, other arithmetic, add_round(): return (one.astype(F32) + two.astype(F32)).astype(BF16)  14.1 us
    pallas_call x1, Pallas kernels, front(): pl.pallas_call(front_kernel, out_shape=[jax.ShapeDtypeStruct(*shape) for...  12.9 us
    pallas_call x3, Pallas kernels, lookup(): pl.pallas_call(functools.partial(lookup_kernel, owners, len(pieces), widt...  12.3 us
  transfers between devices with their start and end apart: 45, of which 19 were waited for; matrix products, arithmetic and copies ran while one was open for 12% of the time, Pallas kernels for 30%

profile of v5, /device:TPU:0, one launch (start us, length us, event | category | flops | bytes accessed | tf_op | source)
XLA Modules:
  0.0 237.4 jit_solution(5905033383349541351)
XLA Ops:
  0.7 1.8 pack_first.1
  2.5 4.0 %collective-permute-start = (bf16[96,1152]{1,0:T(8,128)(2,1)}, bf16[96,1152]{1,0:T(8,128)(2,1)S(1)}, u32[]{:S(2)}, u32[]{:S(2)}) collective-permute-start(bf16[96,1152]{1,0:T(8,128)(2,1)} %pack_first.1), channel_id=1, source_target_pairs={{0,16},{4,20},{8,24},{12,28},{16,0},{20,4},{24,8},{28,12},{1,17},{... | collective-permute-start | bytes 663560 | tf_op jit(solution)/shard_map/ppermute | solution.py:26
  10.4 2.1 pack.1
  13.2 3.8 %collective-permute-done = bf16[96,1152]{1,0:T(8,128)(2,1)S(1)} collective-permute-done((bf16[96,1152]{1,0:T(8,128)(2,1)}, bf16[96,1152]{1,0:T(8,128)(2,1)S(1)}, u32[]{:S(2)}, u32[]{:S(2)}) %collective-permute-start) | collective-permute-done | bytes 221216 | tf_op jit(solution)/shard_map/ppermute | solution.py:26
  17.1 1.6 collective-permute-start.3
  19.4 1.5 collective-permute-start.8
  21.0 3.3 %collective-permute-start.1 = (bf16[96,768]{1,0:T(8,128)(2,1)}, bf16[96,768]{1,0:T(8,128)(2,1)}, u32[]{:S(2)}, u32[]{:S(2)}) collective-permute-start(bf16[96,768]{1,0:T(8,128)(2,1)} %get-tuple-element.110), channel_id=1, source_target_pairs={{0,16},{4,20},{8,24},{12,28},{16,0},{20,4},{24,8},{28,12},{1,17},{... | collective-permute-start | bytes 442376 | tf_op jit(solution)/shard_map/ppermute | solution.py:26
  25.6 3.6 %lookup.3.refs_4_ = bf16[96,1024]{1,0:T(8,128)(2,1)} custom-call(s32[10]{0:T(128)} %pad_add_fusion.1.refs_0_.info.who, s32[2,1024]{1,0:T(2,128)} %pad_add_fusion.refs_1_, bf16[2,96,1152]{2,1,0:T(8,128)(2,1)} %copy-done.4), custom_call_target="tpu_custom_call" | custom-call | tf_op jit(solution)/shard_map/lookup/pallas_call | solution.py:373
  29.2 3.6 %collective-permute-done.2.refs_2_.refs_4_ = bf16[2,96,1152]{2,1,0:T(8,128)(2,1)} collective-permute-done((bf16[2,96,1152]{2,1,0:T(8,128)(2,1)S(1)}, bf16[2,96,1152]{2,1,0:T(8,128)(2,1)}, u32[]{:S(2)}, u32[]{:S(2)}) %collective-permute-start.2) | collective-permute-done | bytes 442400 | tf_op jit(solution)/shard_map/ppermute | solution.py:26
  33.5 4.3 %lookup.4.refs_7_ = bf16[96,1024]{1,0:T(8,128)(2,1)} custom-call(s32[10]{0:T(128)} %pad_add_fusion.1.refs_0_.info.who, s32[2,1024]{1,0:T(2,128)} %pad_add_fusion.refs_1_, bf16[2,96,1152]{2,1,0:T(8,128)(2,1)} %collective-permute-done.2.refs_2_.refs_4_, bf16[2,96,1152]{2,1,0:T(8,128)(2,1)} %copy-done.7, bf16[96,1024]{1,0:T(8,128)(2,1)} %lookup.3.refs_4_), custom_call_target="tpu_custom_call" | custom-call | tf_op jit(solution)/shard_map/lookup/pallas_call | solution.py:373
  40.2 5.0 %collective-permute-start.14 = (bf16[96,1536]{1,0:T(8,128)(2,1)S(1)}, bf16[96,1536]{1,0:T(8,128)(2,1)}, u32[]{:S(2)}, u32[]{:S(2)}) collective-permute-start(bf16[96,1536]{1,0:T(8,128)(2,1)S(1)} %copy-done.33), channel_id=1, source_target_pairs={{0,16},{4,20},{8,24},{12,28},{16,0},{20,4},{24,8},{28,12},{1,17},{... | collective-permute-start | bytes 884744 | tf_op jit(solution)/shard_map/ppermute | solution.py:26
  46.8 4.4 %lookup.5.set0 = bf16[96,1792]{1,0:T(8,128)(2,1)} custom-call(s32[10]{0:T(128)} %pad_add_fusion.1.refs_0_.info.who, s32[2,1024]{1,0:T(2,128)} %pad_add_fusion.refs_1_, bf16[2,96,1152]{2,1,0:T(8,128)(2,1)} %copy-done.8, bf16[2,96,1152]{2,1,0:T(8,128)(2,1)} %copy-done.4, bf16[2,96,1152]{2,1,0:T(8,128)(2,1)} %collective-permute-done.2.refs_2_.refs_4_, ...), custom_call_target="tpu_custom_call" | custom-call | tf_op jit(solution)/shard_map/lookup/pallas_call | solution.py:373
  51.3 1.8 collective-permute-done.5.refs_1_
  53.1 1.5 collective-permute-start.10
  55.1 1.7 collective-permute-done.14
  58.5 6.1 %collective-permute-done.13.refs_3_ = bf16[2,96,768]{2,1,0:T(8,128)(2,1)S(1)} collective-permute-done((bf16[2,96,768]{2,1,0:T(8,128)(2,1)}, bf16[2,96,768]{2,1,0:T(8,128)(2,1)S(1)}, u32[]{:S(2)}, u32[]{:S(2)}) %collective-permute-start.13) | collective-permute-done | bytes 294944 | tf_op jit(solution)/shard_map/ppermute | solution.py:26
  65.4 2.9 %assemble.1 = (bf16[576,768]{1,0:T(8,128)(2,1)}, bf16[192,768]{1,0:T(8,128)(2,1)}) custom-call(s32[10]{0:T(128)} %pad_add_fusion.1.refs_0_.info.who, bf16[2,96,768]{2,1,0:T(8,128)(2,1)} %copy-done.17, bf16[2,96,768]{2,1,0:T(8,128)(2,1)} %collective-permute-done.5.refs_1_, bf16[2,96,768]{2,1,0:T(8,128)(2,1)} %collective-permute-done.6.refs_2_, ...), custom_call_target="tpu_custom_call" | custom-call | tf_op jit(solution)/shard_map/assemble/pallas_call | solution.py:125
  70.5 12.9 %front.1 = (f32[1024,768]{1,0:T(8,128)}, bf16[1024,768]{1,0:T(8,128)(2,1)}, bf16[576,1024]{1,0:T(8,128)(2,1)}, bf16[192,1024]{1,0:T(8,128)(2,1)}, f32[8,1024]{1,0:T(8,128)}) custom-call(s32[10]{0:T(128)} %pad_add_fusion.1.refs_0_.info.who, bf16[96,1792]{1,0:T(8,128)(2,1)} %lookup.5.set0, bf16[96,1792]{1,0:T(8,128)(2,1)} %copy-done.14, ...), custom_call_target="tpu_custom_call" | custom-call | tf_op jit(solution)/shard_map/front/pallas_call | solution.py:534
  83.4 1.6 collective-permute-start.17
  85.4 9.3 %collective-permute-done.17.mix2.refs_6_ = bf16[192,1024]{1,0:T(8,128)(2,1)S(1)} collective-permute-done((bf16[192,1024]{1,0:T(8,128)(2,1)}, bf16[192,1024]{1,0:T(8,128)(2,1)S(1)}, u32[]{:S(2)}, u32[]{:S(2)}) %collective-permute-start.17) | collective-permute-done | bytes 393248 | tf_op jit(solution)/shard_map/ppermute | solution.py:22
  95.3 1.7 collective-permute-done.19.out1
  97.5 2.6 %collective-permute-done.23.ffn3 = bf16[2,96,1536]{2,1,0:T(8,128)(2,1)S(1)} collective-permute-done((bf16[2,96,1536]{2,1,0:T(8,128)(2,1)}, bf16[2,96,1536]{2,1,0:T(8,128)(2,1)S(1)}, u32[]{:S(2)}, u32[]{:S(2)}) %collective-permute-start.23) | collective-permute-done | bytes 589856 | tf_op jit(solution)/shard_map/ppermute | solution.py:26
  101.2 16.2 %middle.1 = (bf16[2,256,768]{2,1,0:T(8,128)(2,1)}, bf16[2,256,768]{2,1,0:T(8,128)(2,1)}, f32[256,768]{1,0:T(8,128)}, bf16[1024,768]{1,0:T(8,128)(2,1)}, bf16[102...) custom-call(s32[10]{0:T(128)} %pad_add_fusion.1.refs_0_.info.who, ...), custom_call_target="tpu_custom_call" | custom-call | tf_op jit(solution)/shard_map/middle/pallas_call | solution.py:654
  117.5 2.5 %collective-permute-done.24 = bf16[2,192,1024]{2,1,0:T(8,128)(2,1)S(1)} collective-permute-done((bf16[2,192,1024]{2,1,0:T(8,128)(2,1)}, bf16[2,192,1024]{2,1,0:T(8,128)(2,1)S(1)}, u32[]{:S(2)}, u32[]{:S(2)}) %collective-permute-start.24) | collective-permute-done | bytes 786464 | tf_op jit(solution)/shard_map/ppermute | solution.py:22
  120.0 1.9 fusion.6
  122.4 9.0 %weigh.1 = (bf16[4,96,1536]{2,1,0:T(8,128)(2,1)}, bf16[4,96,1536]{2,1,0:T(8,128)(2,1)}, bf16[2,192,768]{2,1,0:T(8,128)(2,1)}, bf16[2,192,768]{2,1,0:T(8,128)(2,1)}) custom-call(s32[10]{0:T(128)} %pad_add_fusion.1.refs_0_.info.who, bf16[1024,512]{1,0:T(8,128)(2,1)} %get-tuple-element.137.hidden, bf16[1024,768]{1,0:T(8,128)(2,1)} %get-tuple-element.138.norm, ...), custom_call_target="tpu_custom_call" | custom-call | tf_op jit(solution)/shard_map/weigh/pallas_call | solution.py:231
  134.2 19.8 %back.1 = (bf16[576,1024]{1,0:T(8,128)(2,1)}, bf16[2,512,768]{2,1,0:T(8,128)(2,1)}, bf16[2,512,768]{2,1,0:T(8,128)(2,1)}, bf16[2,304,768]{2,1,0:T(8,128)(2,1)}, ...) custom-call(s32[10]{0:T(128)} %pad_add_fusion.1.refs_0_.info.who, ...), custom_call_target="tpu_custom_call" | custom-call | tf_op jit(solution)/shard_map/back/pallas_call | solution.py:797
  154.0 1.9 collective-permute-done.26
  156.0 1.7 fusion.10
  157.6 1.7 collective-permute-done.27
  159.4 1.5 collective-permute-start.28
  162.0 4.1 %split.2 = (bf16[4,96,576]{2,1,0:T(8,128)(2,1)}, bf16[4,96,576]{2,1,0:T(8,128)(2,1)}) custom-call(s32[10]{0:T(128)} %pad_add_fusion.1.refs_0_.info.who, bf16[1024,768]{1,0:T(8,128)(2,1)} %get-tuple-element.155.left, bf16[576,1024]{1,0:T(8,128)(2,1)} %get-tuple-element.157.right), custom_call_target="tpu_custom_call" | custom-call | tf_op jit(solution)/shard_map/split/pallas_call | solution.py:266
  166.6 1.4 collective-permute-start.34
  171.1 2.5 %collective-permute-start.30 = (bf16[112,1024]{1,0:T(8,128)(2,1)S(1)}, bf16[112,1024]{1,0:T(8,128)(2,1)S(1)}, u32[]{:S(2)}, u32[]{:S(2)}) collective-permute-start(bf16[112,1024]{1,0:T(8,128)(2,1)S(1)} %get-tuple-element.213), channel_id=1, source_target_pairs={{0,16},{4,20},{8,24},{12,28},{16,0},{20,4},{24,8},{28,12},{1,17},{... | collective-permute-start | bytes 688136 | tf_op jit(solution)/shard_map/ppermute | solution.py:26
  173.6 12.0 %collective-permute-done.30 = bf16[112,1024]{1,0:T(8,128)(2,1)S(1)} collective-permute-done((bf16[112,1024]{1,0:T(8,128)(2,1)S(1)}, bf16[112,1024]{1,0:T(8,128)(2,1)S(1)}, u32[]{:S(2)}, u32[]{:S(2)}) %collective-permute-start.30) | collective-permute-done | bytes 229408 | tf_op jit(solution)/shard_map/ppermute | solution.py:26
  186.7 1.5 collective-permute-start.36
  188.2 2.9 %collective-permute-start.35 = (bf16[2,112,1024]{2,1,0:T(8,128)(2,1)S(1)}, bf16[2,112,1024]{2,1,0:T(8,128)(2,1)}, u32[]{:S(2)}, u32[]{:S(2)}) collective-permute-start(bf16[2,112,1024]{2,1,0:T(8,128)(2,1)S(1)} %pad_maximum_fusion.2.refs_1_), channel_id=1, source_target_pairs={{0,8},{4,12},{8,0},{12,4},{16,24},{20,28},{24,16},{28,20},{1,9},{5... | collective-permute-start | bytes 1376264 | tf_op jit(solution)/shard_map/ppermute | solution.py:26
  195.2 2.1 split.3
  197.8 2.3 fusion.1
  200.6 5.1 %collective-permute-done.38 = bf16[4,112,288]{2,1,0:T(8,128)(2,1)S(1)} collective-permute-done((bf16[4,112,288]{2,1,0:T(8,128)(2,1)}, bf16[4,112,288]{2,1,0:T(8,128)(2,1)S(1)}, u32[]{:S(2)}, u32[]{:S(2)}) %collective-permute-start.38) | collective-permute-done | bytes 258080 | tf_op jit(solution)/shard_map/ppermute | solution.py:26
  205.8 4.1 %collective-permute-done.37 = bf16[96,1536]{1,0:T(8,128)(2,1)} collective-permute-done((bf16[96,1536]{1,0:T(8,128)(2,1)}, bf16[96,1536]{1,0:T(8,128)(2,1)}, u32[]{:S(2)}, u32[]{:S(2)}) %collective-permute-start.37) | collective-permute-done | bytes 294944 | tf_op jit(solution)/shard_map/ppermute | solution.py:26
  211.4 2.0 collective-permute-start.40
  213.9 4.3 %spread.2.refs_2_ = f32[96,1024]{1,0:T(8,128)} custom-call(s32[10]{0:T(128)} %pad_add_fusion.1.refs_0_.info.who, bf16[2,112,1024]{2,1,0:T(8,128)(2,1)} %copy-done.6, bf16[2,112,1024]{2,1,0:T(8,128)(2,1)} %collective-permute-done.35.refs_2_, bf16[2,112,1024]{2,1,0:T(8,128)(2,1)} %collective-permute-done.36.refs_3_), custom_call_target="tpu_custom_call" | custom-call | tf_op jit(solution)/shard_map/spread/pallas_call | solution.py:419
  219.8 1.6 fusion.14
  223.8 1.6 collective-permute-start.43
  225.4 1.6 bitcast_add_fusion
  229.5 2.7 %spread.3 = (f32[48,1024]{1,0:T(8,128)}, f32[48,1024]{1,0:T(8,128)}) custom-call(s32[10]{0:T(128)} %pad_add_fusion.1.refs_0_.info.who, bf16[2,112,1024]{2,1,0:T(8,128)(2,1)} %collective-permute-done.42.refs_1_, f32[96,1024]{1,0:T(8,128)} %spread.2.refs_2_), custom_call_target="tpu_custom_call" | custom-call | tf_op jit(solution)/shard_map/spread/pallas_call | solution.py:419
  233.5 1.9 finish.1
  (188 shorter events, 45.0 us)
Async XLA Ops:
  2.5 14.5 %collective-permute-start = (bf16[96,1152]{1,0:T(8,128)(2,1)}, bf16[96,1152]{1,0:T(8,128)(2,1)S(1)}, u32[]{:S(2)}, u32[]{:S(2)}) collective-permute-start(bf16[96,1152]{1,0:T(8,128)(2,1)} %pack_first.1), channel_id=1, source_target_pairs={{0,16},{4,20},{8,24},{12,28},{16,0},{20,4},{24,8},{28,12},{1,17},{... | collective-permute-start | bytes 663560 | tf_op jit(solution)/shard_map/ppermute | solution.py:26
  7.8 30.1 %copy-start = (bf16[2,256,768]{2,1,0:T(8,128)(2,1)}, bf16[2,256,768]{2,1,0:T(8,128)(2,1)S(1)}, u32[]{:S(2)}) copy-start(bf16[2,256,768]{2,1,0:T(8,128)(2,1)S(1)} %pad_maximum_fusion.emb0.cot0.refs_0_) | copy-start | bytes 2359300
  7.8 25.0 %collective-permute-start.4 = (bf16[2,256,768]{2,1,0:T(8,128)(2,1)S(1)}, bf16[2,256,768]{2,1,0:T(8,128)(2,1)S(1)}, u32[]{:S(2)}, u32[]{:S(2)}) collective-permute-start(bf16[2,256,768]{2,1,0:T(8,128)(2,1)S(1)} %pad_maximum_fusion.emb0.cot0.refs_0_), channel_id=1, source_target_pairs={{0,1},{1,0},{2,3},{3,2},{4,5},{5,4},{6,7},{7,6},{8,9},{9,8},{10,11... | collective-permute-start | bytes 2359304 | tf_op jit(solution)/shard_map/ppermute | solution.py:22
  17.1 12.1 %collective-permute-start.3 = (bf16[2,96,1152]{2,1,0:T(8,128)(2,1)S(1)}, bf16[2,96,1152]{2,1,0:T(8,128)(2,1)S(1)}, u32[]{:S(2)}, u32[]{:S(2)}) collective-permute-start(bf16[2,96,1152]{2,1,0:T(8,128)(2,1)S(1)} %pad_maximum_fusion.3.refs_2_.refs_3_), channel_id=1, source_target_pairs={{0,4},{4,0},{8,12},{12,8},{16,20},{20,16},{24,28},{28,24},{1,5},{5... | collective-permute-start | bytes 1327112 | tf_op jit(solution)/shard_map/ppermute | solution.py:26
  18.7 14.1 %collective-permute-start.2 = (bf16[2,96,1152]{2,1,0:T(8,128)(2,1)S(1)}, bf16[2,96,1152]{2,1,0:T(8,128)(2,1)}, u32[]{:S(2)}, u32[]{:S(2)}) collective-permute-start(bf16[2,96,1152]{2,1,0:T(8,128)(2,1)S(1)} %pad_maximum_fusion.3.refs_2_.refs_3_), channel_id=1, source_target_pairs={{0,8},{4,12},{8,0},{12,4},{16,24},{20,28},{24,16},{28,20},{1,9},{5... | collective-permute-start | bytes 1327112 | tf_op jit(solution)/shard_map/ppermute | solution.py:26
  19.4 31.8 %collective-permute-start.8 = (bf16[2,256,768]{2,1,0:T(8,128)(2,1)S(1)}, bf16[2,256,768]{2,1,0:T(8,128)(2,1)S(1)}, u32[]{:S(2)}, u32[]{:S(2)}) collective-permute-start(bf16[2,256,768]{2,1,0:T(8,128)(2,1)S(1)} %pad_maximum_fusion.emb0.cot0.refs_0_), channel_id=1, source_target_pairs={{0,2},{1,3},{2,0},{3,1},{4,6},{5,7},{6,4},{7,5},{8,10},{9,11},{10,... | collective-permute-start | bytes 2359304 | tf_op jit(solution)/shard_map/ppermute | solution.py:22
  21.0 16.8 %collective-permute-start.1 = (bf16[96,768]{1,0:T(8,128)(2,1)}, bf16[96,768]{1,0:T(8,128)(2,1)}, u32[]{:S(2)}, u32[]{:S(2)}) collective-permute-start(bf16[96,768]{1,0:T(8,128)(2,1)} %get-tuple-element.110), channel_id=1, source_target_pairs={{0,16},{4,20},{8,24},{12,28},{16,0},{20,4},{24,8},{28,12},{1,17},{... | collective-permute-start | bytes 442376 | tf_op jit(solution)/shard_map/ppermute | solution.py:26
  32.8 13.3 %collective-permute-start.7 = (bf16[2,96,1152]{2,1,0:T(8,128)(2,1)}, bf16[2,96,1152]{2,1,0:T(8,128)(2,1)S(1)}, u32[]{:S(2)}, u32[]{:S(2)}) collective-permute-start(bf16[2,96,1152]{2,1,0:T(8,128)(2,1)} %collective-permute-done.2.refs_2_.refs_4_), channel_id=1, source_target_pairs={{0,4},{4,0},{8,12},{12,8},{16,20},{20,16},{24,28},{28,24},{1,5},{5... | collective-permute-start | bytes 1327112 | tf_op jit(solution)/shard_map/ppermute | solution.py:26
  38.9 12.4 %collective-permute-start.6 = (bf16[2,96,768]{2,1,0:T(8,128)(2,1)S(1)}, bf16[2,96,768]{2,1,0:T(8,128)(2,1)}, u32[]{:S(2)}, u32[]{:S(2)}) collective-permute-start(bf16[2,96,768]{2,1,0:T(8,128)(2,1)S(1)} %pad_maximum_fusion.4.refs_0_), channel_id=1, source_target_pairs={{0,4},{4,0},{8,12},{12,8},{16,20},{20,16},{24,28},{28,24},{1,5},{5... | collective-permute-start | bytes 884744 | tf_op jit(solution)/shard_map/ppermute | solution.py:26
  40.2 12.9 %collective-permute-start.5 = (bf16[2,96,768]{2,1,0:T(8,128)(2,1)S(1)}, bf16[2,96,768]{2,1,0:T(8,128)(2,1)}, u32[]{:S(2)}, u32[]{:S(2)}) collective-permute-start(bf16[2,96,768]{2,1,0:T(8,128)(2,1)S(1)} %pad_maximum_fusion.4.refs_0_), channel_id=1, source_target_pairs={{0,8},{4,12},{8,0},{12,4},{16,24},{20,28},{24,16},{28,20},{1,9},{5... | collective-permute-start | bytes 884744 | tf_op jit(solution)/shard_map/ppermute | solution.py:26
  40.2 16.7 %collective-permute-start.14 = (bf16[96,1536]{1,0:T(8,128)(2,1)S(1)}, bf16[96,1536]{1,0:T(8,128)(2,1)}, u32[]{:S(2)}, u32[]{:S(2)}) collective-permute-start(bf16[96,1536]{1,0:T(8,128)(2,1)S(1)} %copy-done.33), channel_id=1, source_target_pairs={{0,16},{4,20},{8,24},{12,28},{16,0},{20,4},{24,8},{28,12},{1,17},{... | collective-permute-start | bytes 884744 | tf_op jit(solution)/shard_map/ppermute | solution.py:26
  53.1 15.8 %collective-permute-start.12 = (bf16[2,256,768]{2,1,0:T(8,128)(2,1)S(1)}, bf16[2,256,768]{2,1,0:T(8,128)(2,1)S(1)}, u32[]{:S(2)}, u32[]{:S(2)}) collective-permute-start(bf16[2,256,768]{2,1,0:T(8,128)(2,1)S(1)} %collective-permute-done.8.emb2.cot2.refs_2_), channel_id=1, source_target_pairs={{0,1},{1,0},{2,3},{3,2},{4,5},{5,4},{6,7},{7,6},{8,9},{9,8},{10,11... | collective-permute-start | bytes 2359304 | tf_op jit(solution)/shard_map/ppermute | solution.py:22
  53.1 12.3 %collective-permute-start.10 = (bf16[96,1792]{1,0:T(8,128)(2,1)}, bf16[96,1792]{1,0:T(8,128)(2,1)S(1)}, u32[]{:S(2)}, u32[]{:S(2)}) collective-permute-start(bf16[96,1792]{1,0:T(8,128)(2,1)} %lookup.5.set0), channel_id=1, source_target_pairs={{0,2},{1,3},{2,0},{3,1},{4,6},{5,7},{6,4},{7,5},{8,10},{9,11},{10,... | collective-permute-start | bytes 1032200 | tf_op jit(solution)/shard_map/ppermute | solution.py:22
  54.6 10.1 %collective-permute-start.13 = (bf16[2,96,768]{2,1,0:T(8,128)(2,1)}, bf16[2,96,768]{2,1,0:T(8,128)(2,1)S(1)}, u32[]{:S(2)}, u32[]{:S(2)}) collective-permute-start(bf16[2,96,768]{2,1,0:T(8,128)(2,1)} %collective-permute-done.5.refs_1_), channel_id=1, source_target_pairs={{0,4},{4,0},{8,12},{12,8},{16,20},{20,16},{24,28},{28,24},{1,5},{5... | collective-permute-start | bytes 884744 | tf_op jit(solution)/shard_map/ppermute | solution.py:26
  55.1 13.1 %collective-permute-start.9 = (bf16[96,1792]{1,0:T(8,128)(2,1)}, bf16[96,1792]{1,0:T(8,128)(2,1)S(1)}, u32[]{:S(2)}, u32[]{:S(2)}) collective-permute-start(bf16[96,1792]{1,0:T(8,128)(2,1)} %lookup.5.set0), channel_id=1, source_target_pairs={{0,1},{1,0},{2,3},{3,2},{4,5},{5,4},{6,7},{7,6},{8,9},{9,8},{10,11... | collective-permute-start | bytes 1032200 | tf_op jit(solution)/shard_map/ppermute | solution.py:22
  57.9 25.5 %copy-start.5 = (bf16[2,96,1536]{2,1,0:T(8,128)(2,1)}, bf16[2,96,1536]{2,1,0:T(8,128)(2,1)S(1)}, u32[]{:S(2)}) copy-start(bf16[2,96,1536]{2,1,0:T(8,128)(2,1)S(1)} %pad_maximum_fusion.1.ffn0) | copy-start | bytes 1769476
  57.9 27.0 %collective-permute-start.22 = (bf16[2,96,1536]{2,1,0:T(8,128)(2,1)S(1)}, bf16[2,96,1536]{2,1,0:T(8,128)(2,1)}, u32[]{:S(2)}, u32[]{:S(2)}) collective-permute-start(bf16[2,96,1536]{2,1,0:T(8,128)(2,1)S(1)} %pad_maximum_fusion.1.ffn0), channel_id=1, source_target_pairs={{0,4},{4,0},{8,12},{12,8},{16,20},{20,16},{24,28},{28,24},{1,5},{5... | collective-permute-start | bytes 1769480 | tf_op jit(solution)/shard_map/ppermute | solution.py:26
  64.7 20.3 %collective-permute-start.21 = (bf16[2,96,1536]{2,1,0:T(8,128)(2,1)S(1)}, bf16[2,96,1536]{2,1,0:T(8,128)(2,1)}, u32[]{:S(2)}, u32[]{:S(2)}) collective-permute-start(bf16[2,96,1536]{2,1,0:T(8,128)(2,1)S(1)} %pad_maximum_fusion.1.ffn0), channel_id=1, source_target_pairs={{0,8},{4,12},{8,0},{12,4},{16,24},{20,28},{24,16},{28,20},{1,9},{5... | collective-permute-start | bytes 1769480 | tf_op jit(solution)/shard_map/ppermute | solution.py:26
  65.4 3.5 %collective-permute-start.11 = (bf16[96,1792]{1,0:T(8,128)(2,1)S(1)}, bf16[96,1792]{1,0:T(8,128)(2,1)S(1)}, u32[]{:S(2)}, u32[]{:S(2)}) collective-permute-start(bf16[96,1792]{1,0:T(8,128)(2,1)S(1)} %collective-permute-done.10.set2), channel_id=1, source_target_pairs={{0,1},{1,0},{2,3},{3,2},{4,5},{5,4},{6,7},{7,6},{8,9},{9,8},{10,11... | collective-permute-start | bytes 1032200 | tf_op jit(solution)/shard_map/ppermute | solution.py:22
  68.2 15.1 %collective-permute-start.15 = (bf16[192,768]{1,0:T(8,128)(2,1)}, bf16[192,768]{1,0:T(8,128)(2,1)}, u32[]{:S(2)}, u32[]{:S(2)}) collective-permute-start(bf16[192,768]{1,0:T(8,128)(2,1)} %get-tuple-element.128.out0), channel_id=1, source_target_pairs={{0,2},{1,3},{2,0},{3,1},{4,6},{5,7},{6,4},{7,5},{8,10},{9,11},{10,... | collective-permute-start | bytes 884744 | tf_op jit(solution)/shard_map/ppermute | solution.py:22
  83.4 11.4 %collective-permute-start.17 = (bf16[192,1024]{1,0:T(8,128)(2,1)}, bf16[192,1024]{1,0:T(8,128)(2,1)S(1)}, u32[]{:S(2)}, u32[]{:S(2)}) collective-permute-start(bf16[192,1024]{1,0:T(8,128)(2,1)} %get-tuple-element.129.mix0.refs_4_.mixed), channel_id=1, source_target_pairs={{0,2},{1,3},{2,0},{3,1},{4,6},{5,7},{6,4},{7,5},{8,10},{9,11},{10,... | collective-permute-start | bytes 1179656 | tf_op jit(solution)/shard_map/ppermute | solution.py:22
  84.9 15.2 %collective-permute-start.23 = (bf16[2,96,1536]{2,1,0:T(8,128)(2,1)}, bf16[2,96,1536]{2,1,0:T(8,128)(2,1)S(1)}, u32[]{:S(2)}, u32[]{:S(2)}) collective-permute-start(bf16[2,96,1536]{2,1,0:T(8,128)(2,1)} %collective-permute-done.21.ffn1), channel_id=1, source_target_pairs={{0,4},{4,0},{8,12},{12,8},{16,20},{20,16},{24,28},{28,24},{1,5},{5... | collective-permute-start | bytes 1769480 | tf_op jit(solution)/shard_map/ppermute | solution.py:26
  85.4 12.1 %collective-permute-start.16 = (bf16[192,1024]{1,0:T(8,128)(2,1)}, bf16[192,1024]{1,0:T(8,128)(2,1)S(1)}, u32[]{:S(2)}, u32[]{:S(2)}) collective-permute-start(bf16[192,1024]{1,0:T(8,128)(2,1)} %get-tuple-element.129.mix0.refs_4_.mixed), channel_id=1, source_target_pairs={{0,1},{1,0},{2,3},{3,2},{4,5},{5,4},{6,7},{7,6},{8,9},{9,8},{10,11... | collective-permute-start | bytes 1179656 | tf_op jit(solution)/shard_map/ppermute | solution.py:22
  94.8 5.4 %collective-permute-start.18 = (bf16[192,1024]{1,0:T(8,128)(2,1)S(1)}, bf16[192,1024]{1,0:T(8,128)(2,1)S(1)}, u32[]{:S(2)}, u32[]{:S(2)}) collective-permute-start(bf16[192,1024]{1,0:T(8,128)(2,1)S(1)} %collective-permute-done.17.mix2.refs_6_), channel_id=1, source_target_pairs={{0,1},{1,0},{2,3},{3,2},{4,5},{5,4},{6,7},{7,6},{8,9},{9,8},{10,11... | collective-permute-start | bytes 1179656 | tf_op jit(solution)/shard_map/ppermute | solution.py:22
  94.8 2.2 collective-permute-start.19
  95.3 2.3 collective-permute-start.20
  117.4 2.6 %collective-permute-start.24 = (bf16[2,192,1024]{2,1,0:T(8,128)(2,1)}, bf16[2,192,1024]{2,1,0:T(8,128)(2,1)S(1)}, u32[]{:S(2)}, u32[]{:S(2)}) collective-permute-start(bf16[2,192,1024]{2,1,0:T(8,128)(2,1)} %get-tuple-element.135), channel_id=1, source_target_pairs={{0,1},{1,0},{2,3},{3,2},{4,5},{5,4},{6,7},{7,6},{8,9},{9,8},{10,11... | collective-permute-start | bytes 2359304 | tf_op jit(solution)/shard_map/ppermute | solution.py:22
  121.9 11.4 %collective-permute-start.25 = (bf16[192,1024]{1,0:T(8,128)(2,1)}, bf16[192,1024]{1,0:T(8,128)(2,1)S(1)}, u32[]{:S(2)}, u32[]{:S(2)}) collective-permute-start(bf16[192,1024]{1,0:T(8,128)(2,1)} %fusion.6), channel_id=1, source_target_pairs={{0,2},{1,3},{2,0},{3,1},{4,6},{5,7},{6,4},{7,5},{8,10},{9,11},{10,... | collective-permute-start | bytes 1179656 | tf_op jit(solution)/shard_map/ppermute | solution.py:22
  131.4 27.9 %collective-permute-start.27 = (bf16[4,96,1536]{2,1,0:T(8,128)(2,1)}, bf16[4,96,1536]{2,1,0:T(8,128)(2,1)S(1)}, u32[]{:S(2)}, u32[]{:S(2)}) collective-permute-start(bf16[4,96,1536]{2,1,0:T(8,128)(2,1)} %get-tuple-element.141), channel_id=1, source_target_pairs={{0,4},{4,0},{8,12},{12,8},{16,20},{20,16},{24,28},{28,24},{1,5},{5... | collective-permute-start | bytes 3538952 | tf_op jit(solution)/shard_map/ppermute | solution.py:26
  134.2 26.7 %copy-start.16 = (bf16[4,96,1536]{2,1,0:T(8,128)(2,1)S(1)}, bf16[4,96,1536]{2,1,0:T(8,128)(2,1)}, u32[]{:S(2)}) copy-start(bf16[4,96,1536]{2,1,0:T(8,128)(2,1)} %get-tuple-element.142) | copy-start | bytes 3538948
  154.0 2.0 collective-permute-start.26
  159.4 9.6 %collective-permute-start.32 = (bf16[2,304,768]{2,1,0:T(8,128)(2,1)}, bf16[2,304,768]{2,1,0:T(8,128)(2,1)}, u32[]{:S(2)}, u32[]{:S(2)}) collective-permute-start(bf16[2,304,768]{2,1,0:T(8,128)(2,1)} %get-tuple-element.164), channel_id=1, source_target_pairs={{0,1},{1,0},{2,3},{3,2},{4,5},{5,4},{6,7},{7,6},{8,9},{9,8},{10,11... | collective-permute-start | bytes 2801672 | tf_op jit(solution)/shard_map/ppermute | solution.py:22
  159.4 8.6 %collective-permute-start.28 = (bf16[96,1024]{1,0:T(8,128)(2,1)}, bf16[96,1024]{1,0:T(8,128)(2,1)}, u32[]{:S(2)}, u32[]{:S(2)}) collective-permute-start(bf16[96,1024]{1,0:T(8,128)(2,1)} %fusion.10), channel_id=1, source_target_pairs={{0,2},{1,3},{2,0},{3,1},{4,6},{5,7},{6,4},{7,5},{8,10},{9,11},{10,... | collective-permute-start | bytes 589832 | tf_op jit(solution)/shard_map/ppermute | solution.py:22
  166.1 19.6 %collective-permute-start.31 = (bf16[4,96,576]{2,1,0:T(8,128)(2,1)}, bf16[4,96,576]{2,1,0:T(8,128)(2,1)S(1)}, u32[]{:S(2)}, u32[]{:S(2)}) collective-permute-start(bf16[4,96,576]{2,1,0:T(8,128)(2,1)} %get-tuple-element.158), channel_id=1, source_target_pairs={{0,4},{4,0},{8,12},{12,8},{16,20},{20,16},{24,28},{28,24},{1,5},{5... | collective-permute-start | bytes 1327112 | tf_op jit(solution)/shard_map/ppermute | solution.py:26
  166.6 20.1 %collective-permute-start.34 = (bf16[2,96,1536]{2,1,0:T(8,128)(2,1)S(1)}, bf16[2,96,1536]{2,1,0:T(8,128)(2,1)S(1)}, u32[]{:S(2)}, u32[]{:S(2)}) collective-permute-start(bf16[2,96,1536]{2,1,0:T(8,128)(2,1)S(1)} %copy-done.23), channel_id=1, source_target_pairs={{0,8},{4,12},{8,0},{12,4},{16,24},{20,28},{24,16},{28,20},{1,9},{5... | collective-permute-start | bytes 1769480 | tf_op jit(solution)/shard_map/ppermute | solution.py:26
  168.0 29.9 %collective-permute-start.29 = (bf16[2,512,768]{2,1,0:T(8,128)(2,1)}, bf16[2,512,768]{2,1,0:T(8,128)(2,1)}, u32[]{:S(2)}, u32[]{:S(2)}) collective-permute-start(bf16[2,512,768]{2,1,0:T(8,128)(2,1)} %get-tuple-element.161), channel_id=1, source_target_pairs={{0,1},{1,0},{2,3},{3,2},{4,5},{5,4},{6,7},{7,6},{8,9},{9,8},{10,11... | collective-permute-start | bytes 4718600 | tf_op jit(solution)/shard_map/ppermute | solution.py:22
  170.1 16.5 %collective-permute-start.33 = (bf16[304,768]{1,0:T(8,128)(2,1)S(1)}, bf16[304,768]{1,0:T(8,128)(2,1)S(1)}, u32[]{:S(2)}, u32[]{:S(2)}) collective-permute-start(bf16[304,768]{1,0:T(8,128)(2,1)S(1)} %fusion.4), channel_id=1, source_target_pairs={{0,2},{1,3},{2,0},{3,1},{4,6},{5,7},{6,4},{7,5},{8,10},{9,11},{10,... | collective-permute-start | bytes 1400840 | tf_op jit(solution)/shard_map/ppermute | solution.py:22
  171.1 14.5 %collective-permute-start.30 = (bf16[112,1024]{1,0:T(8,128)(2,1)S(1)}, bf16[112,1024]{1,0:T(8,128)(2,1)S(1)}, u32[]{:S(2)}, u32[]{:S(2)}) collective-permute-start(bf16[112,1024]{1,0:T(8,128)(2,1)S(1)} %get-tuple-element.213), channel_id=1, source_target_pairs={{0,16},{4,20},{8,24},{12,28},{16,0},{20,4},{24,8},{28,12},{1,17},{... | collective-permute-start | bytes 688136 | tf_op jit(solution)/shard_map/ppermute | solution.py:26
  186.7 23.2 %collective-permute-start.36 = (bf16[2,112,1024]{2,1,0:T(8,128)(2,1)S(1)}, bf16[2,112,1024]{2,1,0:T(8,128)(2,1)}, u32[]{:S(2)}, u32[]{:S(2)}) collective-permute-start(bf16[2,112,1024]{2,1,0:T(8,128)(2,1)S(1)} %pad_maximum_fusion.2.refs_1_), channel_id=1, source_target_pairs={{0,4},{4,0},{8,12},{12,8},{16,20},{20,16},{24,28},{28,24},{1,5},{5... | collective-permute-start | bytes 1376264 | tf_op jit(solution)/shard_map/ppermute | solution.py:26
  188.2 21.7 %collective-permute-start.35 = (bf16[2,112,1024]{2,1,0:T(8,128)(2,1)S(1)}, bf16[2,112,1024]{2,1,0:T(8,128)(2,1)}, u32[]{:S(2)}, u32[]{:S(2)}) collective-permute-start(bf16[2,112,1024]{2,1,0:T(8,128)(2,1)S(1)} %pad_maximum_fusion.2.refs_1_), channel_id=1, source_target_pairs={{0,8},{4,12},{8,0},{12,4},{16,24},{20,28},{24,16},{28,20},{1,9},{5... | collective-permute-start | bytes 1376264 | tf_op jit(solution)/shard_map/ppermute | solution.py:26
  194.7 15.1 %collective-permute-start.37 = (bf16[96,1536]{1,0:T(8,128)(2,1)}, bf16[96,1536]{1,0:T(8,128)(2,1)}, u32[]{:S(2)}, u32[]{:S(2)}) collective-permute-start(bf16[96,1536]{1,0:T(8,128)(2,1)} %fusion.8), channel_id=1, source_target_pairs={{0,16},{4,20},{8,24},{12,28},{16,0},{20,4},{24,8},{28,12},{1,17},{... | collective-permute-start | bytes 884744 | tf_op jit(solution)/shard_map/ppermute | solution.py:26
  197.3 8.4 %collective-permute-start.38 = (bf16[4,112,288]{2,1,0:T(8,128)(2,1)}, bf16[4,112,288]{2,1,0:T(8,128)(2,1)S(1)}, u32[]{:S(2)}, u32[]{:S(2)}) collective-permute-start(bf16[4,112,288]{2,1,0:T(8,128)(2,1)} %get-tuple-element.171), channel_id=1, source_target_pairs={{0,4},{4,0},{8,12},{12,8},{16,20},{20,16},{24,28},{28,24},{1,5},{5... | collective-permute-start | bytes 774152 | tf_op jit(solution)/shard_map/ppermute | solution.py:26
  200.1 19.0 %collective-permute-start.41 = (bf16[512,768]{1,0:T(8,128)(2,1)}, bf16[512,768]{1,0:T(8,128)(2,1)}, u32[]{:S(2)}, u32[]{:S(2)}) collective-permute-start(bf16[512,768]{1,0:T(8,128)(2,1)} %fusion.1), channel_id=1, source_target_pairs={{0,2},{1,3},{2,0},{3,1},{4,6},{5,7},{6,4},{7,5},{8,10},{9,11},{10,... | collective-permute-start | bytes 2359304 | tf_op jit(solution)/shard_map/ppermute | solution.py:22
  210.7 8.4 %collective-permute-start.39 = (bf16[2,96,576]{2,1,0:T(8,128)(2,1)}, bf16[2,96,576]{2,1,0:T(8,128)(2,1)S(1)}, u32[]{:S(2)}, u32[]{:S(2)}) collective-permute-start(bf16[2,96,576]{2,1,0:T(8,128)(2,1)} %get-tuple-element.202), channel_id=1, source_target_pairs={{0,8},{4,12},{8,0},{12,4},{16,24},{20,28},{24,16},{28,20},{1,9},{5... | collective-permute-start | bytes 663560 | tf_op jit(solution)/shard_map/ppermute | solution.py:26
  211.4 7.6 %collective-permute-start.40 = (bf16[2,112,288]{2,1,0:T(8,128)(2,1)}, bf16[2,112,288]{2,1,0:T(8,128)(2,1)}, u32[]{:S(2)}, u32[]{:S(2)}) collective-permute-start(bf16[2,112,288]{2,1,0:T(8,128)(2,1)} %get-tuple-element.204), channel_id=1, source_target_pairs={{0,8},{4,12},{8,0},{12,4},{16,24},{20,28},{24,16},{28,20},{1,9},{5... | collective-permute-start | bytes 387080 | tf_op jit(solution)/shard_map/ppermute | solution.py:26
  213.5 16.0 %collective-permute-start.42 = (bf16[2,112,1024]{2,1,0:T(8,128)(2,1)}, bf16[2,112,1024]{2,1,0:T(8,128)(2,1)}, u32[]{:S(2)}, u32[]{:S(2)}) collective-permute-start(bf16[2,112,1024]{2,1,0:T(8,128)(2,1)} %collective-permute-done.35.refs_2_), channel_id=1, source_target_pairs={{0,4},{4,0},{8,12},{12,8},{16,20},{20,16},{24,28},{28,24},{1,5},{5... | collective-permute-start | bytes 1376264 | tf_op jit(solution)/shard_map/ppermute | solution.py:26
  222.4 9.8 %collective-permute-start.44 = (bf16[112,288]{1,0:T(8,128)(2,1)S(1)}, bf16[112,288]{1,0:T(8,128)(2,1)S(1)}, u32[]{:S(2)}, u32[]{:S(2)}) collective-permute-start(bf16[112,288]{1,0:T(8,128)(2,1)S(1)} %get-tuple-element.210), channel_id=1, source_target_pairs={{0,16},{4,20},{8,24},{12,28},{16,0},{20,4},{24,8},{28,12},{1,17},{... | collective-permute-start | bytes 193544 | tf_op jit(solution)/shard_map/ppermute | solution.py:26
  223.8 8.5 %collective-permute-start.43 = (bf16[96,576]{1,0:T(8,128)(2,1)S(1)}, bf16[96,576]{1,0:T(8,128)(2,1)S(1)}, u32[]{:S(2)}, u32[]{:S(2)}) collective-permute-start(bf16[96,576]{1,0:T(8,128)(2,1)S(1)} %get-tuple-element.208), channel_id=1, source_target_pairs={{0,16},{4,20},{8,24},{12,28},{16,0},{20,4},{24,8},{28,12},{1,17},{... | collective-permute-start | bytes 331784 | tf_op jit(solution)/shard_map/ppermute | solution.py:26
  (40 other events, 279.5 us)

commit v6 on v5

--- a/solution.py
+++ b/solution.py
@@ -285,7 +285,10 @@
     )
 
 
-def finish_kernel(attn, attn_come, wide, wide_come, query, key, value, two, three, output, gains):
+def finish_kernel(
+    attn, attn_come, wide, wide_come, ffn, ffn_come,
+    query, key, value, two, three, output, gains, gate, up, down,
+):
     width, ng = query.shape[1], two.shape[0]
     rows = query.shape[0]
     sums = attn[...].astype(F32) + attn_come[...].astype(F32)
@@ -297,20 +300,26 @@
     three[...] = turned[ng : 2 * ng]
     output[...] = turned[2 * ng :]
     gains[...] = sums[rows:, : gains.shape[1]]
-
-
-def finish(attn_sum, wide_sum, ng):
+    units = gate.shape[1]
+    for i, out in enumerate((gate, up, down)):
+        cut = slice(i * units, (i + 1) * units)
+        out[...] = ffn[:, cut].astype(F32) + ffn_come[:, cut].astype(F32)
+
+
+def finish(attn_sum, wide_sum, ffn_sum, ng):
     rows, cols = attn_sum.ours.shape
     width = cols // 3
     operands = [attn_sum.ours, attn_sum.third, wide_sum.ours, wide_sum.third]
+    operands += [ffn_sum.ours, ffn_sum.third]
     below = wide_sum.ours.shape[0] - rows
     shapes = [(rows, width)] * 3 + [(ng, rows)] * 2 + [(width, rows), (below, 2 * ng)]
+    shapes += [(rows, ffn_sum.ours.shape[1] // 3)] * 3
     vm = pl.BlockSpec(memory_space=VMEM)
     return pl.pallas_call(
         finish_kernel,
         out_shape=[jax.ShapeDtypeStruct(shape, F32) for shape in shapes],
-        in_specs=[vm] * 4,
-        out_specs=[vm] * 7,
+        in_specs=[vm] * len(operands),
+        out_specs=[vm] * len(shapes),
         name="finish",
     )(*operands)
 
@@ -969,18 +978,16 @@
         token_far, ffn_sum.third = (
             after(x, attn_sum.ours, proj_sum.ours) for x in (token_far, ffn_sum.third)
         )
-        ffn_total = ffn_sum.total()
         sums = total((stay[0], token_near[0], token_far))
         embed_grad = sums[:rows].astype(BF16)
         output = (resid_own + sums[rows:]).astype(BF16)
-        gate_grad, up_grad, down_grad = (
-            ffn_total[:, i * units : (i + 1) * units] for i in range(3)
-        )
         embed_grad, output, table_grad = lax.optimization_barrier(
             (embed_grad, output, table_grad)
         )
         table_grad = spread(info, [three], own_rows, ng, table_grad, True)
-        *grads_done, folded = finish(attn_sum, proj_sum, ng)
+        *grads_done, folded, gate_grad, up_grad, down_grad = finish(
+            attn_sum, proj_sum, ffn_sum, ng
+        )
         gains = folded.reshape(2, dim)
     else:
         every = lax.all_gather(row_pack, "dp", axis=0)

time: 238 us -> 235 us (0.987)
  other arithmetic: 26 us -> 22 us
    convert_element_type x11, other arithmetic: 14.1 us -> 11.1 us  [add_round(): return (one.astype(F32) + two.astype(F32)).astype(BF16)]
    unnamed x86 -> x88, local copies, waits for them, and re-layouts: 5.49 us -> 6.35 us
  transfers between devices with their start and end apart: 45 -> 45, of which waited for: 19 -> 19; matrix products, arithmetic and copies ran while one was open for 12% -> 10% of each run, Pallas kernels for 30% -> 31%
where the time goes in v6:
time: 235 us; the launch traced here: 234 us
  Pallas kernels  92.4 us (39%)
  waiting for transfers between devices  61.9 us (26%)
  starting transfers between devices  44.7 us (19%)
  other arithmetic  22 us (9%)
  local copies, waits for them, and re-layouts  12 us (5%)
    ppermute x25, waiting for transfers between devices, xor_dp(): return lax.ppermute(value, 'dp', [(i, i ^ step) for i in range(count)])  45 us
    ppermute x25, starting transfers between devices, xor_dp(): return lax.ppermute(value, 'dp', [(i, i ^ step) for i in range(count)])  34.8 us
    pallas_call x1, Pallas kernels, back(): pl.pallas_call(back_kernel, out_shape=[jax.ShapeDtypeStruct(shape, BF16)...  19.8 us
    ppermute x20, waiting for transfers between devices, xor_tensor(): return lax.ppermute(value, 'tensor', [(i, i ^ step) for i in range(4)])  16.9 us
    pallas_call x1, Pallas kernels, middle(): pl.pallas_call(middle_kernel, in_specs=[pl.BlockSpec(memory_space=pltpu.S...  16.2 us
    pallas_call x1, Pallas kernels, front(): pl.pallas_call(front_kernel, out_shape=[jax.ShapeDtypeStruct(*shape) for...  12.8 us
    pallas_call x3, Pallas kernels, lookup(): pl.pallas_call(functools.partial(lookup_kernel, owners, len(pieces), widt...  12.3 us
    convert_element_type x11, other arithmetic, add_round(): return (one.astype(F32) + two.astype(F32)).astype(BF16)  11.1 us
  transfers between devices with their start and end apart: 45, of which 19 were waited for; matrix products, arithmetic and copies ran while one was open for 10% of the time, Pallas kernels for 31%

profile of v6, /device:TPU:0, one launch (start us, length us, event | category | flops | bytes accessed | tf_op | source)
XLA Modules:
  0.0 234.1 jit_solution(13432316684772091860)
XLA Ops:
  0.7 1.8 pack_first.1
  2.5 4.0 %collective-permute-start = (bf16[96,1152]{1,0:T(8,128)(2,1)}, bf16[96,1152]{1,0:T(8,128)(2,1)S(1)}, u32[]{:S(2)}, u32[]{:S(2)}) collective-permute-start(bf16[96,1152]{1,0:T(8,128)(2,1)} %pack_first.1), channel_id=1, source_target_pairs={{0,16},{4,20},{8,24},{12,28},{16,0},{20,4},{24,8},{28,12},{1,17},{... | collective-permute-start | bytes 663560 | tf_op jit(solution)/shard_map/ppermute | solution.py:26
  10.4 2.1 pack.1
  13.2 3.8 %collective-permute-done = bf16[96,1152]{1,0:T(8,128)(2,1)S(1)} collective-permute-done((bf16[96,1152]{1,0:T(8,128)(2,1)}, bf16[96,1152]{1,0:T(8,128)(2,1)S(1)}, u32[]{:S(2)}, u32[]{:S(2)}) %collective-permute-start) | collective-permute-done | bytes 221216 | tf_op jit(solution)/shard_map/ppermute | solution.py:26
  17.1 1.6 collective-permute-start.3
  19.4 1.5 collective-permute-start.8
  21.0 3.3 %collective-permute-start.1 = (bf16[96,768]{1,0:T(8,128)(2,1)}, bf16[96,768]{1,0:T(8,128)(2,1)}, u32[]{:S(2)}, u32[]{:S(2)}) collective-permute-start(bf16[96,768]{1,0:T(8,128)(2,1)} %get-tuple-element.113), channel_id=1, source_target_pairs={{0,16},{4,20},{8,24},{12,28},{16,0},{20,4},{24,8},{28,12},{1,17},{... | collective-permute-start | bytes 442376 | tf_op jit(solution)/shard_map/ppermute | solution.py:26
  25.6 3.6 %lookup.3.refs_4_ = bf16[96,1024]{1,0:T(8,128)(2,1)} custom-call(s32[10]{0:T(128)} %pad_add_fusion.1.refs_0_.info.who, s32[2,1024]{1,0:T(2,128)} %pad_add_fusion.refs_1_, bf16[2,96,1152]{2,1,0:T(8,128)(2,1)} %copy-done.4), custom_call_target="tpu_custom_call" | custom-call | tf_op jit(solution)/shard_map/lookup/pallas_call | solution.py:382
  29.2 3.6 %collective-permute-done.2.refs_2_.refs_4_ = bf16[2,96,1152]{2,1,0:T(8,128)(2,1)} collective-permute-done((bf16[2,96,1152]{2,1,0:T(8,128)(2,1)S(1)}, bf16[2,96,1152]{2,1,0:T(8,128)(2,1)}, u32[]{:S(2)}, u32[]{:S(2)}) %collective-permute-start.2) | collective-permute-done | bytes 442400 | tf_op jit(solution)/shard_map/ppermute | solution.py:26
  33.5 4.3 %lookup.4.refs_7_ = bf16[96,1024]{1,0:T(8,128)(2,1)} custom-call(s32[10]{0:T(128)} %pad_add_fusion.1.refs_0_.info.who, s32[2,1024]{1,0:T(2,128)} %pad_add_fusion.refs_1_, bf16[2,96,1152]{2,1,0:T(8,128)(2,1)} %collective-permute-done.2.refs_2_.refs_4_, bf16[2,96,1152]{2,1,0:T(8,128)(2,1)} %copy-done.7, bf16[96,1024]{1,0:T(8,128)(2,1)} %lookup.3.refs_4_), custom_call_target="tpu_custom_call" | custom-call | tf_op jit(solution)/shard_map/lookup/pallas_call | solution.py:382
  38.8 1.3 collective-permute-start.6
  40.2 5.0 %collective-permute-start.14 = (bf16[96,1536]{1,0:T(8,128)(2,1)S(1)}, bf16[96,1536]{1,0:T(8,128)(2,1)}, u32[]{:S(2)}, u32[]{:S(2)}) collective-permute-start(bf16[96,1536]{1,0:T(8,128)(2,1)S(1)} %copy-done.34), channel_id=1, source_target_pairs={{0,16},{4,20},{8,24},{12,28},{16,0},{20,4},{24,8},{28,12},{1,17},{... | collective-permute-start | bytes 884744 | tf_op jit(solution)/shard_map/ppermute | solution.py:26
  46.8 4.4 %lookup.5.set0 = bf16[96,1792]{1,0:T(8,128)(2,1)} custom-call(s32[10]{0:T(128)} %pad_add_fusion.1.refs_0_.info.who, s32[2,1024]{1,0:T(2,128)} %pad_add_fusion.refs_1_, bf16[2,96,1152]{2,1,0:T(8,128)(2,1)} %copy-done.8, bf16[2,96,1152]{2,1,0:T(8,128)(2,1)} %copy-done.4, bf16[2,96,1152]{2,1,0:T(8,128)(2,1)} %collective-permute-done.2.refs_2_.refs_4_, ...), custom_call_target="tpu_custom_call" | custom-call | tf_op jit(solution)/shard_map/lookup/pallas_call | solution.py:382
  51.2 1.9 collective-permute-done.5.refs_1_
  53.1 1.5 collective-permute-start.10
  55.1 1.7 collective-permute-done.14
  58.5 6.1 %collective-permute-done.13.refs_3_ = bf16[2,96,768]{2,1,0:T(8,128)(2,1)S(1)} collective-permute-done((bf16[2,96,768]{2,1,0:T(8,128)(2,1)}, bf16[2,96,768]{2,1,0:T(8,128)(2,1)S(1)}, u32[]{:S(2)}, u32[]{:S(2)}) %collective-permute-start.13) | collective-permute-done | bytes 294944 | tf_op jit(solution)/shard_map/ppermute | solution.py:26
  65.4 2.8 %assemble.1 = (bf16[576,768]{1,0:T(8,128)(2,1)}, bf16[192,768]{1,0:T(8,128)(2,1)}) custom-call(s32[10]{0:T(128)} %pad_add_fusion.1.refs_0_.info.who, bf16[2,96,768]{2,1,0:T(8,128)(2,1)} %copy-done.17, bf16[2,96,768]{2,1,0:T(8,128)(2,1)} %collective-permute-done.5.refs_1_, bf16[2,96,768]{2,1,0:T(8,128)(2,1)} %collective-permute-done.6.refs_2_, ...), custom_call_target="tpu_custom_call" | custom-call | tf_op jit(solution)/shard_map/assemble/pallas_call | solution.py:125
  70.5 12.8 %front.1 = (f32[1024,768]{1,0:T(8,128)}, bf16[1024,768]{1,0:T(8,128)(2,1)}, bf16[576,1024]{1,0:T(8,128)(2,1)}, bf16[192,1024]{1,0:T(8,128)(2,1)}, f32[8,1024]{1,0:T(8,128)}) custom-call(s32[10]{0:T(128)} %pad_add_fusion.1.refs_0_.info.who, bf16[96,1792]{1,0:T(8,128)(2,1)} %lookup.5.set0, bf16[96,1792]{1,0:T(8,128)(2,1)} %copy-done.14, ...), custom_call_target="tpu_custom_call" | custom-call | tf_op jit(solution)/shard_map/front/pallas_call | solution.py:543
  83.3 1.6 collective-permute-start.17
  85.4 9.3 %collective-permute-done.17.mix2.refs_6_ = bf16[192,1024]{1,0:T(8,128)(2,1)S(1)} collective-permute-done((bf16[192,1024]{1,0:T(8,128)(2,1)}, bf16[192,1024]{1,0:T(8,128)(2,1)S(1)}, u32[]{:S(2)}, u32[]{:S(2)}) %collective-permute-start.17) | collective-permute-done | bytes 393248 | tf_op jit(solution)/shard_map/ppermute | solution.py:22
  95.2 1.7 collective-permute-done.19.out1
  97.5 2.6 %collective-permute-done.23.ffn3 = bf16[2,96,1536]{2,1,0:T(8,128)(2,1)S(1)} collective-permute-done((bf16[2,96,1536]{2,1,0:T(8,128)(2,1)}, bf16[2,96,1536]{2,1,0:T(8,128)(2,1)S(1)}, u32[]{:S(2)}, u32[]{:S(2)}) %collective-permute-start.23) | collective-permute-done | bytes 589856 | tf_op jit(solution)/shard_map/ppermute | solution.py:26
  101.2 16.2 %middle.1 = (bf16[2,256,768]{2,1,0:T(8,128)(2,1)}, bf16[2,256,768]{2,1,0:T(8,128)(2,1)}, f32[256,768]{1,0:T(8,128)}, bf16[1024,768]{1,0:T(8,128)(2,1)}, bf16[102...) custom-call(s32[10]{0:T(128)} %pad_add_fusion.1.refs_0_.info.who, ...), custom_call_target="tpu_custom_call" | custom-call | tf_op jit(solution)/shard_map/middle/pallas_call | solution.py:663
  117.4 2.5 %collective-permute-done.24 = bf16[2,192,1024]{2,1,0:T(8,128)(2,1)S(1)} collective-permute-done((bf16[2,192,1024]{2,1,0:T(8,128)(2,1)}, bf16[2,192,1024]{2,1,0:T(8,128)(2,1)S(1)}, u32[]{:S(2)}, u32[]{:S(2)}) %collective-permute-start.24) | collective-permute-done | bytes 786464 | tf_op jit(solution)/shard_map/ppermute | solution.py:22
  121.7 9.0 %weigh.1 = (bf16[4,96,1536]{2,1,0:T(8,128)(2,1)}, bf16[4,96,1536]{2,1,0:T(8,128)(2,1)}, bf16[2,192,768]{2,1,0:T(8,128)(2,1)}, bf16[2,192,768]{2,1,0:T(8,128)(2,1)}) custom-call(s32[10]{0:T(128)} %pad_add_fusion.1.refs_0_.info.who, bf16[1024,512]{1,0:T(8,128)(2,1)} %get-tuple-element.140.hidden, bf16[1024,768]{1,0:T(8,128)(2,1)} %get-tuple-element.141.norm, ...), custom_call_target="tpu_custom_call" | custom-call | tf_op jit(solution)/shard_map/weigh/pallas_call | solution.py:231
  133.2 19.8 %back.1 = (bf16[576,1024]{1,0:T(8,128)(2,1)}, bf16[2,512,768]{2,1,0:T(8,128)(2,1)}, bf16[2,512,768]{2,1,0:T(8,128)(2,1)}, bf16[2,304,768]{2,1,0:T(8,128)(2,1)}, ...) custom-call(s32[10]{0:T(128)} %pad_add_fusion.1.refs_0_.info.who, ...), custom_call_target="tpu_custom_call" | custom-call | tf_op jit(solution)/shard_map/back/pallas_call | solution.py:806
  153.1 1.9 collective-permute-done.26
  155.0 1.8 fusion.10
  156.8 1.8 collective-permute-done.27
  158.6 1.5 collective-permute-start.28
  160.4 4.1 %split.2 = (bf16[4,96,576]{2,1,0:T(8,128)(2,1)}, bf16[4,96,576]{2,1,0:T(8,128)(2,1)}) custom-call(s32[10]{0:T(128)} %pad_add_fusion.1.refs_0_.info.who, bf16[1024,768]{1,0:T(8,128)(2,1)} %get-tuple-element.158.left, bf16[576,1024]{1,0:T(8,128)(2,1)} %get-tuple-element.160.right), custom_call_target="tpu_custom_call" | custom-call | tf_op jit(solution)/shard_map/split/pallas_call | solution.py:266
  165.0 1.4 collective-permute-start.34
  168.6 1.4 collective-permute-start.33
  170.0 2.8 %collective-permute-start.30 = (bf16[112,1024]{1,0:T(8,128)(2,1)S(1)}, bf16[112,1024]{1,0:T(8,128)(2,1)S(1)}, u32[]{:S(2)}, u32[]{:S(2)}) collective-permute-start(bf16[112,1024]{1,0:T(8,128)(2,1)S(1)} %get-tuple-element.218), channel_id=1, source_target_pairs={{0,16},{4,20},{8,24},{12,28},{16,0},{20,4},{24,8},{28,12},{1,17},{... | collective-permute-start | bytes 688136 | tf_op jit(solution)/shard_map/ppermute | solution.py:26
  172.8 11.2 %collective-permute-done.30 = bf16[112,1024]{1,0:T(8,128)(2,1)S(1)} collective-permute-done((bf16[112,1024]{1,0:T(8,128)(2,1)S(1)}, bf16[112,1024]{1,0:T(8,128)(2,1)S(1)}, u32[]{:S(2)}, u32[]{:S(2)}) %collective-permute-start.30) | collective-permute-done | bytes 229408 | tf_op jit(solution)/shard_map/ppermute | solution.py:26
  185.1 1.5 collective-permute-start.36
  186.6 2.9 %collective-permute-start.35 = (bf16[2,112,1024]{2,1,0:T(8,128)(2,1)S(1)}, bf16[2,112,1024]{2,1,0:T(8,128)(2,1)}, u32[]{:S(2)}, u32[]{:S(2)}) collective-permute-start(bf16[2,112,1024]{2,1,0:T(8,128)(2,1)S(1)} %pad_maximum_fusion.2.refs_1_), channel_id=1, source_target_pairs={{0,8},{4,12},{8,0},{12,4},{16,24},{20,28},{24,16},{28,20},{1,9},{5... | collective-permute-start | bytes 1376264 | tf_op jit(solution)/shard_map/ppermute | solution.py:26
  193.8 2.1 split.3
  196.4 2.2 fusion.1
  199.2 5.1 %collective-permute-done.38 = bf16[4,112,288]{2,1,0:T(8,128)(2,1)S(1)} collective-permute-done((bf16[4,112,288]{2,1,0:T(8,128)(2,1)}, bf16[4,112,288]{2,1,0:T(8,128)(2,1)S(1)}, u32[]{:S(2)}, u32[]{:S(2)}) %collective-permute-start.38) | collective-permute-done | bytes 258080 | tf_op jit(solution)/shard_map/ppermute | solution.py:26
  204.3 3.9 %collective-permute-done.37.ffn_come = bf16[96,1536]{1,0:T(8,128)(2,1)S(1)} collective-permute-done((bf16[96,1536]{1,0:T(8,128)(2,1)}, bf16[96,1536]{1,0:T(8,128)(2,1)S(1)}, u32[]{:S(2)}, u32[]{:S(2)}) %collective-permute-start.37) | collective-permute-done | bytes 294944 | tf_op jit(solution)/shard_map/ppermute | solution.py:26
  209.9 2.1 collective-permute-start.40
  212.5 4.3 %spread.2.refs_2_ = f32[96,1024]{1,0:T(8,128)} custom-call(s32[10]{0:T(128)} %pad_add_fusion.1.refs_0_.info.who, bf16[2,112,1024]{2,1,0:T(8,128)(2,1)} %copy-done.6, bf16[2,112,1024]{2,1,0:T(8,128)(2,1)} %collective-permute-done.35.refs_2_, bf16[2,112,1024]{2,1,0:T(8,128)(2,1)} %collective-permute-done.36.refs_3_), custom_call_target="tpu_custom_call" | custom-call | tf_op jit(solution)/shard_map/spread/pallas_call | solution.py:428
  220.6 1.8 collective-permute-start.43
  222.4 1.6 bitcast_add_fusion
  226.4 2.7 %spread.3 = (f32[48,1024]{1,0:T(8,128)}, f32[48,1024]{1,0:T(8,128)}) custom-call(s32[10]{0:T(128)} %pad_add_fusion.1.refs_0_.info.who, bf16[2,112,1024]{2,1,0:T(8,128)(2,1)} %copy-done.26, f32[96,1024]{1,0:T(8,128)} %spread.2.refs_2_), custom_call_target="tpu_custom_call" | custom-call | tf_op jit(solution)/shard_map/spread/pallas_call | solution.py:428
  229.8 2.3 finish.1
  (188 shorter events, 42.5 us)
Async XLA Ops:
  2.5 14.5 %collective-permute-start = (bf16[96,1152]{1,0:T(8,128)(2,1)}, bf16[96,1152]{1,0:T(8,128)(2,1)S(1)}, u32[]{:S(2)}, u32[]{:S(2)}) collective-permute-start(bf16[96,1152]{1,0:T(8,128)(2,1)} %pack_first.1), channel_id=1, source_target_pairs={{0,16},{4,20},{8,24},{12,28},{16,0},{20,4},{24,8},{28,12},{1,17},{... | collective-permute-start | bytes 663560 | tf_op jit(solution)/shard_map/ppermute | solution.py:26
  7.8 30.1 %copy-start = (bf16[2,256,768]{2,1,0:T(8,128)(2,1)}, bf16[2,256,768]{2,1,0:T(8,128)(2,1)S(1)}, u32[]{:S(2)}) copy-start(bf16[2,256,768]{2,1,0:T(8,128)(2,1)S(1)} %pad_maximum_fusion.emb0.cot0.refs_0_) | copy-start | bytes 2359300
  7.8 25.0 %collective-permute-start.4 = (bf16[2,256,768]{2,1,0:T(8,128)(2,1)S(1)}, bf16[2,256,768]{2,1,0:T(8,128)(2,1)S(1)}, u32[]{:S(2)}, u32[]{:S(2)}) collective-permute-start(bf16[2,256,768]{2,1,0:T(8,128)(2,1)S(1)} %pad_maximum_fusion.emb0.cot0.refs_0_), channel_id=1, source_target_pairs={{0,1},{1,0},{2,3},{3,2},{4,5},{5,4},{6,7},{7,6},{8,9},{9,8},{10,11... | collective-permute-start | bytes 2359304 | tf_op jit(solution)/shard_map/ppermute | solution.py:22
  17.1 12.1 %collective-permute-start.3 = (bf16[2,96,1152]{2,1,0:T(8,128)(2,1)S(1)}, bf16[2,96,1152]{2,1,0:T(8,128)(2,1)S(1)}, u32[]{:S(2)}, u32[]{:S(2)}) collective-permute-start(bf16[2,96,1152]{2,1,0:T(8,128)(2,1)S(1)} %pad_maximum_fusion.3.refs_2_.refs_3_), channel_id=1, source_target_pairs={{0,4},{4,0},{8,12},{12,8},{16,20},{20,16},{24,28},{28,24},{1,5},{5... | collective-permute-start | bytes 1327112 | tf_op jit(solution)/shard_map/ppermute | solution.py:26
  18.7 14.1 %collective-permute-start.2 = (bf16[2,96,1152]{2,1,0:T(8,128)(2,1)S(1)}, bf16[2,96,1152]{2,1,0:T(8,128)(2,1)}, u32[]{:S(2)}, u32[]{:S(2)}) collective-permute-start(bf16[2,96,1152]{2,1,0:T(8,128)(2,1)S(1)} %pad_maximum_fusion.3.refs_2_.refs_3_), channel_id=1, source_target_pairs={{0,8},{4,12},{8,0},{12,4},{16,24},{20,28},{24,16},{28,20},{1,9},{5... | collective-permute-start | bytes 1327112 | tf_op jit(solution)/shard_map/ppermute | solution.py:26
  19.4 31.8 %collective-permute-start.8 = (bf16[2,256,768]{2,1,0:T(8,128)(2,1)S(1)}, bf16[2,256,768]{2,1,0:T(8,128)(2,1)S(1)}, u32[]{:S(2)}, u32[]{:S(2)}) collective-permute-start(bf16[2,256,768]{2,1,0:T(8,128)(2,1)S(1)} %pad_maximum_fusion.emb0.cot0.refs_0_), channel_id=1, source_target_pairs={{0,2},{1,3},{2,0},{3,1},{4,6},{5,7},{6,4},{7,5},{8,10},{9,11},{10,... | collective-permute-start | bytes 2359304 | tf_op jit(solution)/shard_map/ppermute | solution.py:22
  21.0 16.8 %collective-permute-start.1 = (bf16[96,768]{1,0:T(8,128)(2,1)}, bf16[96,768]{1,0:T(8,128)(2,1)}, u32[]{:S(2)}, u32[]{:S(2)}) collective-permute-start(bf16[96,768]{1,0:T(8,128)(2,1)} %get-tuple-element.113), channel_id=1, source_target_pairs={{0,16},{4,20},{8,24},{12,28},{16,0},{20,4},{24,8},{28,12},{1,17},{... | collective-permute-start | bytes 442376 | tf_op jit(solution)/shard_map/ppermute | solution.py:26
  32.8 13.3 %collective-permute-start.7 = (bf16[2,96,1152]{2,1,0:T(8,128)(2,1)}, bf16[2,96,1152]{2,1,0:T(8,128)(2,1)S(1)}, u32[]{:S(2)}, u32[]{:S(2)}) collective-permute-start(bf16[2,96,1152]{2,1,0:T(8,128)(2,1)} %collective-permute-done.2.refs_2_.refs_4_), channel_id=1, source_target_pairs={{0,4},{4,0},{8,12},{12,8},{16,20},{20,16},{24,28},{28,24},{1,5},{5... | collective-permute-start | bytes 1327112 | tf_op jit(solution)/shard_map/ppermute | solution.py:26
  38.8 12.4 %collective-permute-start.6 = (bf16[2,96,768]{2,1,0:T(8,128)(2,1)S(1)}, bf16[2,96,768]{2,1,0:T(8,128)(2,1)}, u32[]{:S(2)}, u32[]{:S(2)}) collective-permute-start(bf16[2,96,768]{2,1,0:T(8,128)(2,1)S(1)} %pad_maximum_fusion.4.refs_0_), channel_id=1, source_target_pairs={{0,4},{4,0},{8,12},{12,8},{16,20},{20,16},{24,28},{28,24},{1,5},{5... | collective-permute-start | bytes 884744 | tf_op jit(solution)/shard_map/ppermute | solution.py:26
  40.2 12.9 %collective-permute-start.5 = (bf16[2,96,768]{2,1,0:T(8,128)(2,1)S(1)}, bf16[2,96,768]{2,1,0:T(8,128)(2,1)}, u32[]{:S(2)}, u32[]{:S(2)}) collective-permute-start(bf16[2,96,768]{2,1,0:T(8,128)(2,1)S(1)} %pad_maximum_fusion.4.refs_0_), channel_id=1, source_target_pairs={{0,8},{4,12},{8,0},{12,4},{16,24},{20,28},{24,16},{28,20},{1,9},{5... | collective-permute-start | bytes 884744 | tf_op jit(solution)/shard_map/ppermute | solution.py:26
  40.2 16.7 %collective-permute-start.14 = (bf16[96,1536]{1,0:T(8,128)(2,1)S(1)}, bf16[96,1536]{1,0:T(8,128)(2,1)}, u32[]{:S(2)}, u32[]{:S(2)}) collective-permute-start(bf16[96,1536]{1,0:T(8,128)(2,1)S(1)} %copy-done.34), channel_id=1, source_target_pairs={{0,16},{4,20},{8,24},{12,28},{16,0},{20,4},{24,8},{28,12},{1,17},{... | collective-permute-start | bytes 884744 | tf_op jit(solution)/shard_map/ppermute | solution.py:26
  53.1 15.7 %collective-permute-start.12 = (bf16[2,256,768]{2,1,0:T(8,128)(2,1)S(1)}, bf16[2,256,768]{2,1,0:T(8,128)(2,1)S(1)}, u32[]{:S(2)}, u32[]{:S(2)}) collective-permute-start(bf16[2,256,768]{2,1,0:T(8,128)(2,1)S(1)} %collective-permute-done.8.emb2.cot2.refs_2_), channel_id=1, source_target_pairs={{0,1},{1,0},{2,3},{3,2},{4,5},{5,4},{6,7},{7,6},{8,9},{9,8},{10,11... | collective-permute-start | bytes 2359304 | tf_op jit(solution)/shard_map/ppermute | solution.py:22
  53.1 12.3 %collective-permute-start.10 = (bf16[96,1792]{1,0:T(8,128)(2,1)}, bf16[96,1792]{1,0:T(8,128)(2,1)S(1)}, u32[]{:S(2)}, u32[]{:S(2)}) collective-permute-start(bf16[96,1792]{1,0:T(8,128)(2,1)} %lookup.5.set0), channel_id=1, source_target_pairs={{0,2},{1,3},{2,0},{3,1},{4,6},{5,7},{6,4},{7,5},{8,10},{9,11},{10,... | collective-permute-start | bytes 1032200 | tf_op jit(solution)/shard_map/ppermute | solution.py:22
  54.6 10.1 %collective-permute-start.13 = (bf16[2,96,768]{2,1,0:T(8,128)(2,1)}, bf16[2,96,768]{2,1,0:T(8,128)(2,1)S(1)}, u32[]{:S(2)}, u32[]{:S(2)}) collective-permute-start(bf16[2,96,768]{2,1,0:T(8,128)(2,1)} %collective-permute-done.5.refs_1_), channel_id=1, source_target_pairs={{0,4},{4,0},{8,12},{12,8},{16,20},{20,16},{24,28},{28,24},{1,5},{5... | collective-permute-start | bytes 884744 | tf_op jit(solution)/shard_map/ppermute | solution.py:26
  55.1 13.1 %collective-permute-start.9 = (bf16[96,1792]{1,0:T(8,128)(2,1)}, bf16[96,1792]{1,0:T(8,128)(2,1)S(1)}, u32[]{:S(2)}, u32[]{:S(2)}) collective-permute-start(bf16[96,1792]{1,0:T(8,128)(2,1)} %lookup.5.set0), channel_id=1, source_target_pairs={{0,1},{1,0},{2,3},{3,2},{4,5},{5,4},{6,7},{7,6},{8,9},{9,8},{10,11... | collective-permute-start | bytes 1032200 | tf_op jit(solution)/shard_map/ppermute | solution.py:22
  57.9 25.4 %copy-start.5 = (bf16[2,96,1536]{2,1,0:T(8,128)(2,1)}, bf16[2,96,1536]{2,1,0:T(8,128)(2,1)S(1)}, u32[]{:S(2)}) copy-start(bf16[2,96,1536]{2,1,0:T(8,128)(2,1)S(1)} %pad_maximum_fusion.1.ffn0) | copy-start | bytes 1769476
  57.9 27.0 %collective-permute-start.22 = (bf16[2,96,1536]{2,1,0:T(8,128)(2,1)S(1)}, bf16[2,96,1536]{2,1,0:T(8,128)(2,1)}, u32[]{:S(2)}, u32[]{:S(2)}) collective-permute-start(bf16[2,96,1536]{2,1,0:T(8,128)(2,1)S(1)} %pad_maximum_fusion.1.ffn0), channel_id=1, source_target_pairs={{0,4},{4,0},{8,12},{12,8},{16,20},{20,16},{24,28},{28,24},{1,5},{5... | collective-permute-start | bytes 1769480 | tf_op jit(solution)/shard_map/ppermute | solution.py:26
  64.7 20.2 %collective-permute-start.21 = (bf16[2,96,1536]{2,1,0:T(8,128)(2,1)S(1)}, bf16[2,96,1536]{2,1,0:T(8,128)(2,1)}, u32[]{:S(2)}, u32[]{:S(2)}) collective-permute-start(bf16[2,96,1536]{2,1,0:T(8,128)(2,1)S(1)} %pad_maximum_fusion.1.ffn0), channel_id=1, source_target_pairs={{0,8},{4,12},{8,0},{12,4},{16,24},{20,28},{24,16},{28,20},{1,9},{5... | collective-permute-start | bytes 1769480 | tf_op jit(solution)/shard_map/ppermute | solution.py:26
  65.4 3.5 %collective-permute-start.11 = (bf16[96,1792]{1,0:T(8,128)(2,1)S(1)}, bf16[96,1792]{1,0:T(8,128)(2,1)S(1)}, u32[]{:S(2)}, u32[]{:S(2)}) collective-permute-start(bf16[96,1792]{1,0:T(8,128)(2,1)S(1)} %collective-permute-done.10.set2), channel_id=1, source_target_pairs={{0,1},{1,0},{2,3},{3,2},{4,5},{5,4},{6,7},{7,6},{8,9},{9,8},{10,11... | collective-permute-start | bytes 1032200 | tf_op jit(solution)/shard_map/ppermute | solution.py:22
  68.2 15.1 %collective-permute-start.15 = (bf16[192,768]{1,0:T(8,128)(2,1)}, bf16[192,768]{1,0:T(8,128)(2,1)}, u32[]{:S(2)}, u32[]{:S(2)}) collective-permute-start(bf16[192,768]{1,0:T(8,128)(2,1)} %get-tuple-element.131.out0), channel_id=1, source_target_pairs={{0,2},{1,3},{2,0},{3,1},{4,6},{5,7},{6,4},{7,5},{8,10},{9,11},{10,... | collective-permute-start | bytes 884744 | tf_op jit(solution)/shard_map/ppermute | solution.py:22
  83.3 11.4 %collective-permute-start.17 = (bf16[192,1024]{1,0:T(8,128)(2,1)}, bf16[192,1024]{1,0:T(8,128)(2,1)S(1)}, u32[]{:S(2)}, u32[]{:S(2)}) collective-permute-start(bf16[192,1024]{1,0:T(8,128)(2,1)} %get-tuple-element.132.mix0.refs_4_.mixed), channel_id=1, source_target_pairs={{0,2},{1,3},{2,0},{3,1},{4,6},{5,7},{6,4},{7,5},{8,10},{9,11},{10,... | collective-permute-start | bytes 1179656 | tf_op jit(solution)/shard_map/ppermute | solution.py:22
  84.9 15.2 %collective-permute-start.23 = (bf16[2,96,1536]{2,1,0:T(8,128)(2,1)}, bf16[2,96,1536]{2,1,0:T(8,128)(2,1)S(1)}, u32[]{:S(2)}, u32[]{:S(2)}) collective-permute-start(bf16[2,96,1536]{2,1,0:T(8,128)(2,1)} %collective-permute-done.21.ffn1), channel_id=1, source_target_pairs={{0,4},{4,0},{8,12},{12,8},{16,20},{20,16},{24,28},{28,24},{1,5},{5... | collective-permute-start | bytes 1769480 | tf_op jit(solution)/shard_map/ppermute | solution.py:26
  85.4 12.1 %collective-permute-start.16 = (bf16[192,1024]{1,0:T(8,128)(2,1)}, bf16[192,1024]{1,0:T(8,128)(2,1)S(1)}, u32[]{:S(2)}, u32[]{:S(2)}) collective-permute-start(bf16[192,1024]{1,0:T(8,128)(2,1)} %get-tuple-element.132.mix0.refs_4_.mixed), channel_id=1, source_target_pairs={{0,1},{1,0},{2,3},{3,2},{4,5},{5,4},{6,7},{7,6},{8,9},{9,8},{10,11... | collective-permute-start | bytes 1179656 | tf_op jit(solution)/shard_map/ppermute | solution.py:22
  94.7 5.4 %collective-permute-start.18 = (bf16[192,1024]{1,0:T(8,128)(2,1)S(1)}, bf16[192,1024]{1,0:T(8,128)(2,1)S(1)}, u32[]{:S(2)}, u32[]{:S(2)}) collective-permute-start(bf16[192,1024]{1,0:T(8,128)(2,1)S(1)} %collective-permute-done.17.mix2.refs_6_), channel_id=1, source_target_pairs={{0,1},{1,0},{2,3},{3,2},{4,5},{5,4},{6,7},{7,6},{8,9},{9,8},{10,11... | collective-permute-start | bytes 1179656 | tf_op jit(solution)/shard_map/ppermute | solution.py:22
  94.7 2.2 collective-permute-start.19
  95.2 2.3 collective-permute-start.20
  117.4 2.6 %collective-permute-start.24 = (bf16[2,192,1024]{2,1,0:T(8,128)(2,1)}, bf16[2,192,1024]{2,1,0:T(8,128)(2,1)S(1)}, u32[]{:S(2)}, u32[]{:S(2)}) collective-permute-start(bf16[2,192,1024]{2,1,0:T(8,128)(2,1)} %get-tuple-element.138), channel_id=1, source_target_pairs={{0,1},{1,0},{2,3},{3,2},{4,5},{5,4},{6,7},{7,6},{8,9},{9,8},{10,11... | collective-permute-start | bytes 2359304 | tf_op jit(solution)/shard_map/ppermute | solution.py:22
  121.1 11.2 %collective-permute-start.25 = (bf16[192,1024]{1,0:T(8,128)(2,1)S(1)}, bf16[192,1024]{1,0:T(8,128)(2,1)S(1)}, u32[]{:S(2)}, u32[]{:S(2)}) collective-permute-start(bf16[192,1024]{1,0:T(8,128)(2,1)S(1)} %fusion.6), channel_id=1, source_target_pairs={{0,2},{1,3},{2,0},{3,1},{4,6},{5,7},{6,4},{7,5},{8,10},{9,11},{10,... | collective-permute-start | bytes 1179656 | tf_op jit(solution)/shard_map/ppermute | solution.py:22
  130.7 27.9 %collective-permute-start.27 = (bf16[4,96,1536]{2,1,0:T(8,128)(2,1)}, bf16[4,96,1536]{2,1,0:T(8,128)(2,1)S(1)}, u32[]{:S(2)}, u32[]{:S(2)}) collective-permute-start(bf16[4,96,1536]{2,1,0:T(8,128)(2,1)} %get-tuple-element.144), channel_id=1, source_target_pairs={{0,4},{4,0},{8,12},{12,8},{16,20},{20,16},{24,28},{28,24},{1,5},{5... | collective-permute-start | bytes 3538952 | tf_op jit(solution)/shard_map/ppermute | solution.py:26
  133.2 26.9 %copy-start.16 = (bf16[4,96,1536]{2,1,0:T(8,128)(2,1)S(1)}, bf16[4,96,1536]{2,1,0:T(8,128)(2,1)}, u32[]{:S(2)}) copy-start(bf16[4,96,1536]{2,1,0:T(8,128)(2,1)} %get-tuple-element.145) | copy-start | bytes 3538948
  153.0 2.0 collective-permute-start.26
  158.6 8.8 %collective-permute-start.32 = (bf16[2,304,768]{2,1,0:T(8,128)(2,1)}, bf16[2,304,768]{2,1,0:T(8,128)(2,1)}, u32[]{:S(2)}, u32[]{:S(2)}) collective-permute-start(bf16[2,304,768]{2,1,0:T(8,128)(2,1)} %get-tuple-element.167), channel_id=1, source_target_pairs={{0,1},{1,0},{2,3},{3,2},{4,5},{5,4},{6,7},{7,6},{8,9},{9,8},{10,11... | collective-permute-start | bytes 2801672 | tf_op jit(solution)/shard_map/ppermute | solution.py:22
  158.6 7.8 %collective-permute-start.28 = (bf16[96,1024]{1,0:T(8,128)(2,1)}, bf16[96,1024]{1,0:T(8,128)(2,1)}, u32[]{:S(2)}, u32[]{:S(2)}) collective-permute-start(bf16[96,1024]{1,0:T(8,128)(2,1)} %fusion.10), channel_id=1, source_target_pairs={{0,2},{1,3},{2,0},{3,1},{4,6},{5,7},{6,4},{7,5},{8,10},{9,11},{10,... | collective-permute-start | bytes 589832 | tf_op jit(solution)/shard_map/ppermute | solution.py:22
  164.5 19.6 %collective-permute-start.31 = (bf16[4,96,576]{2,1,0:T(8,128)(2,1)}, bf16[4,96,576]{2,1,0:T(8,128)(2,1)S(1)}, u32[]{:S(2)}, u32[]{:S(2)}) collective-permute-start(bf16[4,96,576]{2,1,0:T(8,128)(2,1)} %get-tuple-element.161), channel_id=1, source_target_pairs={{0,4},{4,0},{8,12},{12,8},{16,20},{20,16},{24,28},{28,24},{1,5},{5... | collective-permute-start | bytes 1327112 | tf_op jit(solution)/shard_map/ppermute | solution.py:26
  165.0 20.1 %collective-permute-start.34 = (bf16[2,96,1536]{2,1,0:T(8,128)(2,1)S(1)}, bf16[2,96,1536]{2,1,0:T(8,128)(2,1)S(1)}, u32[]{:S(2)}, u32[]{:S(2)}) collective-permute-start(bf16[2,96,1536]{2,1,0:T(8,128)(2,1)S(1)} %get-tuple-element.206), channel_id=1, source_target_pairs={{0,8},{4,12},{8,0},{12,4},{16,24},{20,28},{24,16},{28,20},{1,9},{5... | collective-permute-start | bytes 1769480 | tf_op jit(solution)/shard_map/ppermute | solution.py:26
  166.4 30.0 %collective-permute-start.29 = (bf16[2,512,768]{2,1,0:T(8,128)(2,1)}, bf16[2,512,768]{2,1,0:T(8,128)(2,1)}, u32[]{:S(2)}, u32[]{:S(2)}) collective-permute-start(bf16[2,512,768]{2,1,0:T(8,128)(2,1)} %get-tuple-element.164), channel_id=1, source_target_pairs={{0,1},{1,0},{2,3},{3,2},{4,5},{5,4},{6,7},{7,6},{8,9},{9,8},{10,11... | collective-permute-start | bytes 4718600 | tf_op jit(solution)/shard_map/ppermute | solution.py:22
  168.6 16.5 %collective-permute-start.33 = (bf16[304,768]{1,0:T(8,128)(2,1)S(1)}, bf16[304,768]{1,0:T(8,128)(2,1)S(1)}, u32[]{:S(2)}, u32[]{:S(2)}) collective-permute-start(bf16[304,768]{1,0:T(8,128)(2,1)S(1)} %fusion.4), channel_id=1, source_target_pairs={{0,2},{1,3},{2,0},{3,1},{4,6},{5,7},{6,4},{7,5},{8,10},{9,11},{10,... | collective-permute-start | bytes 1400840 | tf_op jit(solution)/shard_map/ppermute | solution.py:22
  170.0 14.0 %collective-permute-start.30 = (bf16[112,1024]{1,0:T(8,128)(2,1)S(1)}, bf16[112,1024]{1,0:T(8,128)(2,1)S(1)}, u32[]{:S(2)}, u32[]{:S(2)}) collective-permute-start(bf16[112,1024]{1,0:T(8,128)(2,1)S(1)} %get-tuple-element.218), channel_id=1, source_target_pairs={{0,16},{4,20},{8,24},{12,28},{16,0},{20,4},{24,8},{28,12},{1,17},{... | collective-permute-start | bytes 688136 | tf_op jit(solution)/shard_map/ppermute | solution.py:26
  185.1 23.2 %collective-permute-start.36 = (bf16[2,112,1024]{2,1,0:T(8,128)(2,1)S(1)}, bf16[2,112,1024]{2,1,0:T(8,128)(2,1)}, u32[]{:S(2)}, u32[]{:S(2)}) collective-permute-start(bf16[2,112,1024]{2,1,0:T(8,128)(2,1)S(1)} %pad_maximum_fusion.2.refs_1_), channel_id=1, source_target_pairs={{0,4},{4,0},{8,12},{12,8},{16,20},{20,16},{24,28},{28,24},{1,5},{5... | collective-permute-start | bytes 1376264 | tf_op jit(solution)/shard_map/ppermute | solution.py:26
  186.6 22.4 %collective-permute-start.35 = (bf16[2,112,1024]{2,1,0:T(8,128)(2,1)S(1)}, bf16[2,112,1024]{2,1,0:T(8,128)(2,1)}, u32[]{:S(2)}, u32[]{:S(2)}) collective-permute-start(bf16[2,112,1024]{2,1,0:T(8,128)(2,1)S(1)} %pad_maximum_fusion.2.refs_1_), channel_id=1, source_target_pairs={{0,8},{4,12},{8,0},{12,4},{16,24},{20,28},{24,16},{28,20},{1,9},{5... | collective-permute-start | bytes 1376264 | tf_op jit(solution)/shard_map/ppermute | solution.py:26
  193.3 14.9 %collective-permute-start.37 = (bf16[96,1536]{1,0:T(8,128)(2,1)}, bf16[96,1536]{1,0:T(8,128)(2,1)S(1)}, u32[]{:S(2)}, u32[]{:S(2)}) collective-permute-start(bf16[96,1536]{1,0:T(8,128)(2,1)} %get-tuple-element.208), channel_id=1, source_target_pairs={{0,16},{4,20},{8,24},{12,28},{16,0},{20,4},{24,8},{28,12},{1,17},{... | collective-permute-start | bytes 884744 | tf_op jit(solution)/shard_map/ppermute | solution.py:26
  195.9 8.4 %collective-permute-start.38 = (bf16[4,112,288]{2,1,0:T(8,128)(2,1)}, bf16[4,112,288]{2,1,0:T(8,128)(2,1)S(1)}, u32[]{:S(2)}, u32[]{:S(2)}) collective-permute-start(bf16[4,112,288]{2,1,0:T(8,128)(2,1)} %get-tuple-element.174), channel_id=1, source_target_pairs={{0,4},{4,0},{8,12},{12,8},{16,20},{20,16},{24,28},{28,24},{1,5},{5... | collective-permute-start | bytes 774152 | tf_op jit(solution)/shard_map/ppermute | solution.py:26
  198.7 19.4 %collective-permute-start.41 = (bf16[512,768]{1,0:T(8,128)(2,1)}, bf16[512,768]{1,0:T(8,128)(2,1)}, u32[]{:S(2)}, u32[]{:S(2)}) collective-permute-start(bf16[512,768]{1,0:T(8,128)(2,1)} %fusion.1), channel_id=1, source_target_pairs={{0,2},{1,3},{2,0},{3,1},{4,6},{5,7},{6,4},{7,5},{8,10},{9,11},{10,... | collective-permute-start | bytes 2359304 | tf_op jit(solution)/shard_map/ppermute | solution.py:22
  209.8 8.3 %collective-permute-start.39 = (bf16[2,96,576]{2,1,0:T(8,128)(2,1)}, bf16[2,96,576]{2,1,0:T(8,128)(2,1)S(1)}, u32[]{:S(2)}, u32[]{:S(2)}) collective-permute-start(bf16[2,96,576]{2,1,0:T(8,128)(2,1)} %get-tuple-element.210), channel_id=1, source_target_pairs={{0,8},{4,12},{8,0},{12,4},{16,24},{20,28},{24,16},{28,20},{1,9},{5... | collective-permute-start | bytes 663560 | tf_op jit(solution)/shard_map/ppermute | solution.py:26
  209.9 8.2 %collective-permute-start.40 = (bf16[2,112,288]{2,1,0:T(8,128)(2,1)S(1)}, bf16[2,112,288]{2,1,0:T(8,128)(2,1)S(1)}, u32[]{:S(2)}, u32[]{:S(2)}) collective-permute-start(bf16[2,112,288]{2,1,0:T(8,128)(2,1)S(1)} %get-tuple-element.212), channel_id=1, source_target_pairs={{0,8},{4,12},{8,0},{12,4},{16,24},{20,28},{24,16},{28,20},{1,9},{5... | collective-permute-start | bytes 387080 | tf_op jit(solution)/shard_map/ppermute | solution.py:26
  212.0 13.6 %collective-permute-start.42 = (bf16[2,112,1024]{2,1,0:T(8,128)(2,1)}, bf16[2,112,1024]{2,1,0:T(8,128)(2,1)S(1)}, u32[]{:S(2)}, u32[]{:S(2)}) collective-permute-start(bf16[2,112,1024]{2,1,0:T(8,128)(2,1)} %collective-permute-done.35.refs_2_), channel_id=1, source_target_pairs={{0,4},{4,0},{8,12},{12,8},{16,20},{20,16},{24,28},{28,24},{1,5},{5... | collective-permute-start | bytes 1376264 | tf_op jit(solution)/shard_map/ppermute | solution.py:26
  219.5 9.7 %collective-permute-start.44 = (bf16[112,288]{1,0:T(8,128)(2,1)S(1)}, bf16[112,288]{1,0:T(8,128)(2,1)S(1)}, u32[]{:S(2)}, u32[]{:S(2)}) collective-permute-start(bf16[112,288]{1,0:T(8,128)(2,1)S(1)} %get-tuple-element.215), channel_id=1, source_target_pairs={{0,16},{4,20},{8,24},{12,28},{16,0},{20,4},{24,8},{28,12},{1,17},{... | collective-permute-start | bytes 193544 | tf_op jit(solution)/shard_map/ppermute | solution.py:26
  220.6 8.5 %collective-permute-start.43 = (bf16[96,576]{1,0:T(8,128)(2,1)S(1)}, bf16[96,576]{1,0:T(8,128)(2,1)S(1)}, u32[]{:S(2)}, u32[]{:S(2)}) collective-permute-start(bf16[96,576]{1,0:T(8,128)(2,1)S(1)} %get-tuple-element.213), channel_id=1, source_target_pairs={{0,16},{4,20},{8,24},{12,28},{16,0},{20,4},{24,8},{28,12},{1,17},{... | collective-permute-start | bytes 331784 | tf_op jit(solution)/shard_map/ppermute | solution.py:26
  (41 other events, 276.3 us)

commit v7 on v6

--- a/solution.py
+++ b/solution.py
@@ -287,7 +287,7 @@
 
 def finish_kernel(
     attn, attn_come, wide, wide_come, ffn, ffn_come,
-    query, key, value, two, three, output, gains, gate, up, down,
+    query, key, value, two, three, output, gain, other_gain, gate, up, down,
 ):
     width, ng = query.shape[1], two.shape[0]
     rows = query.shape[0]
@@ -299,7 +299,9 @@
     two[...] = turned[:ng]
     three[...] = turned[ng : 2 * ng]
     output[...] = turned[2 * ng :]
-    gains[...] = sums[rows:, : gains.shape[1]]
+    lines, lanes = gain.shape
+    gain[...] = sums[rows : rows + lines, :lanes]
+    other_gain[...] = sums[rows + lines :, :lanes]
     units = gate.shape[1]
     for i, out in enumerate((gate, up, down)):
         cut = slice(i * units, (i + 1) * units)
@@ -312,7 +314,7 @@
     operands = [attn_sum.ours, attn_sum.third, wide_sum.ours, wide_sum.third]
     operands += [ffn_sum.ours, ffn_sum.third]
     below = wide_sum.ours.shape[0] - rows
-    shapes = [(rows, width)] * 3 + [(ng, rows)] * 2 + [(width, rows), (below, 2 * ng)]
+    shapes = [(rows, width)] * 3 + [(ng, rows)] * 2 + [(width, rows)] + [(below // 2, 2 * ng)] * 2
     shapes += [(rows, ffn_sum.ours.shape[1] // 3)] * 3
     vm = pl.BlockSpec(memory_space=VMEM)
     return pl.pallas_call(
@@ -985,10 +987,10 @@
             (embed_grad, output, table_grad)
         )
         table_grad = spread(info, [three], own_rows, ng, table_grad, True)
-        *grads_done, folded, gate_grad, up_grad, down_grad = finish(
+        *grads_done, gain, other_gain, gate_grad, up_grad, down_grad = finish(
             attn_sum, proj_sum, ffn_sum, ng
         )
-        gains = folded.reshape(2, dim)
+        gains = gain.reshape(dim), other_gain.reshape(dim)
     else:
         every = lax.all_gather(row_pack, "dp", axis=0)
 

time: 235 us -> 236 us (level)
    reshape x0 -> x2, local copies, waits for them, and re-layouts: none -> 2.7 us  [shards(): gains = (gain.reshape(dim), other_gain.reshape(dim))]
where the time goes in v7:
time: 236 us; the launch traced here: 235 us
  Pallas kernels  92.4 us (39%)
  waiting for transfers between devices  61.8 us (26%)
  starting transfers between devices  44.7 us (19%)
  other arithmetic  22 us (9%)
  local copies, waits for them, and re-layouts  12.7 us (5%)
    ppermute x25, waiting for transfers between devices, xor_dp(): return lax.ppermute(value, 'dp', [(i, i ^ step) for i in range(count)])  44.9 us
    ppermute x25, starting transfers between devices, xor_dp(): return lax.ppermute(value, 'dp', [(i, i ^ step) for i in range(count)])  34.8 us
    pallas_call x1, Pallas kernels, back(): pl.pallas_call(back_kernel, out_shape=[jax.ShapeDtypeStruct(shape, BF16)...  19.8 us
    ppermute x20, waiting for transfers between devices, xor_tensor(): return lax.ppermute(value, 'tensor', [(i, i ^ step) for i in range(4)])  16.9 us
    pallas_call x1, Pallas kernels, middle(): pl.pallas_call(middle_kernel, in_specs=[pl.BlockSpec(memory_space=pltpu.S...  16.2 us
    pallas_call x1, Pallas kernels, front(): pl.pallas_call(front_kernel, out_shape=[jax.ShapeDtypeStruct(*shape) for...  12.9 us
    pallas_call x3, Pallas kernels, lookup(): pl.pallas_call(functools.partial(lookup_kernel, owners, len(pieces), widt...  12.3 us
    convert_element_type x11, other arithmetic, add_round(): return (one.astype(F32) + two.astype(F32)).astype(BF16)  11.1 us
  transfers between devices with their start and end apart: 45, of which 19 were waited for; matrix products, arithmetic and copies ran while one was open for 10% of the time, Pallas kernels for 31%

profile of v7, /device:TPU:0, one launch (start us, length us, event | category | flops | bytes accessed | tf_op | source)
XLA Modules:
  0.0 234.8 jit_solution(11308748622056015588)
XLA Ops:
  0.7 1.8 pack_first.1
  2.5 4.0 %collective-permute-start = (bf16[96,1152]{1,0:T(8,128)(2,1)}, bf16[96,1152]{1,0:T(8,128)(2,1)S(1)}, u32[]{:S(2)}, u32[]{:S(2)}) collective-permute-start(bf16[96,1152]{1,0:T(8,128)(2,1)} %pack_first.1), channel_id=1, source_target_pairs={{0,16},{4,20},{8,24},{12,28},{16,0},{20,4},{24,8},{28,12},{1,17},{... | collective-permute-start | bytes 663560 | tf_op jit(solution)/shard_map/ppermute | solution.py:26
  10.4 2.1 pack.1
  13.2 3.8 %collective-permute-done = bf16[96,1152]{1,0:T(8,128)(2,1)S(1)} collective-permute-done((bf16[96,1152]{1,0:T(8,128)(2,1)}, bf16[96,1152]{1,0:T(8,128)(2,1)S(1)}, u32[]{:S(2)}, u32[]{:S(2)}) %collective-permute-start) | collective-permute-done | bytes 221216 | tf_op jit(solution)/shard_map/ppermute | solution.py:26
  17.1 1.6 collective-permute-start.3
  19.4 1.5 collective-permute-start.8
  21.0 3.3 %collective-permute-start.1 = (bf16[96,768]{1,0:T(8,128)(2,1)}, bf16[96,768]{1,0:T(8,128)(2,1)}, u32[]{:S(2)}, u32[]{:S(2)}) collective-permute-start(bf16[96,768]{1,0:T(8,128)(2,1)} %get-tuple-element.114), channel_id=1, source_target_pairs={{0,16},{4,20},{8,24},{12,28},{16,0},{20,4},{24,8},{28,12},{1,17},{... | collective-permute-start | bytes 442376 | tf_op jit(solution)/shard_map/ppermute | solution.py:26
  25.6 3.6 %lookup.3.refs_4_ = bf16[96,1024]{1,0:T(8,128)(2,1)} custom-call(s32[10]{0:T(128)} %pad_add_fusion.1.refs_0_.info.who, s32[2,1024]{1,0:T(2,128)} %pad_add_fusion.refs_1_, bf16[2,96,1152]{2,1,0:T(8,128)(2,1)} %copy-done.4), custom_call_target="tpu_custom_call" | custom-call | tf_op jit(solution)/shard_map/lookup/pallas_call | solution.py:384
  29.2 3.6 %collective-permute-done.2.refs_2_.refs_4_ = bf16[2,96,1152]{2,1,0:T(8,128)(2,1)} collective-permute-done((bf16[2,96,1152]{2,1,0:T(8,128)(2,1)S(1)}, bf16[2,96,1152]{2,1,0:T(8,128)(2,1)}, u32[]{:S(2)}, u32[]{:S(2)}) %collective-permute-start.2) | collective-permute-done | bytes 442400 | tf_op jit(solution)/shard_map/ppermute | solution.py:26
  33.5 4.3 %lookup.4.refs_7_ = bf16[96,1024]{1,0:T(8,128)(2,1)} custom-call(s32[10]{0:T(128)} %pad_add_fusion.1.refs_0_.info.who, s32[2,1024]{1,0:T(2,128)} %pad_add_fusion.refs_1_, bf16[2,96,1152]{2,1,0:T(8,128)(2,1)} %collective-permute-done.2.refs_2_.refs_4_, bf16[2,96,1152]{2,1,0:T(8,128)(2,1)} %copy-done.7, bf16[96,1024]{1,0:T(8,128)(2,1)} %lookup.3.refs_4_), custom_call_target="tpu_custom_call" | custom-call | tf_op jit(solution)/shard_map/lookup/pallas_call | solution.py:384
  40.2 5.0 %collective-permute-start.14 = (bf16[96,1536]{1,0:T(8,128)(2,1)S(1)}, bf16[96,1536]{1,0:T(8,128)(2,1)}, u32[]{:S(2)}, u32[]{:S(2)}) collective-permute-start(bf16[96,1536]{1,0:T(8,128)(2,1)S(1)} %copy-done.34), channel_id=1, source_target_pairs={{0,16},{4,20},{8,24},{12,28},{16,0},{20,4},{24,8},{28,12},{1,17},{... | collective-permute-start | bytes 884744 | tf_op jit(solution)/shard_map/ppermute | solution.py:26
  46.8 4.4 %lookup.5.set0 = bf16[96,1792]{1,0:T(8,128)(2,1)} custom-call(s32[10]{0:T(128)} %pad_add_fusion.1.refs_0_.info.who, s32[2,1024]{1,0:T(2,128)} %pad_add_fusion.refs_1_, bf16[2,96,1152]{2,1,0:T(8,128)(2,1)} %copy-done.8, bf16[2,96,1152]{2,1,0:T(8,128)(2,1)} %copy-done.4, bf16[2,96,1152]{2,1,0:T(8,128)(2,1)} %collective-permute-done.2.refs_2_.refs_4_, ...), custom_call_target="tpu_custom_call" | custom-call | tf_op jit(solution)/shard_map/lookup/pallas_call | solution.py:384
  51.2 1.9 collective-permute-done.5.refs_1_
  53.1 1.5 collective-permute-start.10
  55.1 1.7 collective-permute-done.14
  58.5 6.1 %collective-permute-done.13.refs_3_ = bf16[2,96,768]{2,1,0:T(8,128)(2,1)S(1)} collective-permute-done((bf16[2,96,768]{2,1,0:T(8,128)(2,1)}, bf16[2,96,768]{2,1,0:T(8,128)(2,1)S(1)}, u32[]{:S(2)}, u32[]{:S(2)}) %collective-permute-start.13) | collective-permute-done | bytes 294944 | tf_op jit(solution)/shard_map/ppermute | solution.py:26
  65.4 2.9 %assemble.1 = (bf16[576,768]{1,0:T(8,128)(2,1)}, bf16[192,768]{1,0:T(8,128)(2,1)}) custom-call(s32[10]{0:T(128)} %pad_add_fusion.1.refs_0_.info.who, bf16[2,96,768]{2,1,0:T(8,128)(2,1)} %copy-done.17, bf16[2,96,768]{2,1,0:T(8,128)(2,1)} %collective-permute-done.5.refs_1_, bf16[2,96,768]{2,1,0:T(8,128)(2,1)} %collective-permute-done.6.refs_2_, ...), custom_call_target="tpu_custom_call" | custom-call | tf_op jit(solution)/shard_map/assemble/pallas_call | solution.py:125
  70.5 12.9 %front.1 = (f32[1024,768]{1,0:T(8,128)}, bf16[1024,768]{1,0:T(8,128)(2,1)}, bf16[576,1024]{1,0:T(8,128)(2,1)}, bf16[192,1024]{1,0:T(8,128)(2,1)}, f32[8,1024]{1,0:T(8,128)}) custom-call(s32[10]{0:T(128)} %pad_add_fusion.1.refs_0_.info.who, bf16[96,1792]{1,0:T(8,128)(2,1)} %lookup.5.set0, bf16[96,1792]{1,0:T(8,128)(2,1)} %copy-done.14, ...), custom_call_target="tpu_custom_call" | custom-call | tf_op jit(solution)/shard_map/front/pallas_call | solution.py:545
  83.4 1.6 collective-permute-start.17
  85.4 9.3 %collective-permute-done.17.mix2.refs_6_ = bf16[192,1024]{1,0:T(8,128)(2,1)S(1)} collective-permute-done((bf16[192,1024]{1,0:T(8,128)(2,1)}, bf16[192,1024]{1,0:T(8,128)(2,1)S(1)}, u32[]{:S(2)}, u32[]{:S(2)}) %collective-permute-start.17) | collective-permute-done | bytes 393248 | tf_op jit(solution)/shard_map/ppermute | solution.py:22
  95.3 1.7 collective-permute-done.19.out1
  97.5 2.6 %collective-permute-done.23.ffn3 = bf16[2,96,1536]{2,1,0:T(8,128)(2,1)S(1)} collective-permute-done((bf16[2,96,1536]{2,1,0:T(8,128)(2,1)}, bf16[2,96,1536]{2,1,0:T(8,128)(2,1)S(1)}, u32[]{:S(2)}, u32[]{:S(2)}) %collective-permute-start.23) | collective-permute-done | bytes 589856 | tf_op jit(solution)/shard_map/ppermute | solution.py:26
  101.2 16.2 %middle.1 = (bf16[2,256,768]{2,1,0:T(8,128)(2,1)}, bf16[2,256,768]{2,1,0:T(8,128)(2,1)}, f32[256,768]{1,0:T(8,128)}, bf16[1024,768]{1,0:T(8,128)(2,1)}, bf16[102...) custom-call(s32[10]{0:T(128)} %pad_add_fusion.1.refs_0_.info.who, ...), custom_call_target="tpu_custom_call" | custom-call | tf_op jit(solution)/shard_map/middle/pallas_call | solution.py:665
  117.5 2.5 %collective-permute-done.24 = bf16[2,192,1024]{2,1,0:T(8,128)(2,1)S(1)} collective-permute-done((bf16[2,192,1024]{2,1,0:T(8,128)(2,1)}, bf16[2,192,1024]{2,1,0:T(8,128)(2,1)S(1)}, u32[]{:S(2)}, u32[]{:S(2)}) %collective-permute-start.24) | collective-permute-done | bytes 786464 | tf_op jit(solution)/shard_map/ppermute | solution.py:22
  121.7 9.0 %weigh.1 = (bf16[4,96,1536]{2,1,0:T(8,128)(2,1)}, bf16[4,96,1536]{2,1,0:T(8,128)(2,1)}, bf16[2,192,768]{2,1,0:T(8,128)(2,1)}, bf16[2,192,768]{2,1,0:T(8,128)(2,1)}) custom-call(s32[10]{0:T(128)} %pad_add_fusion.1.refs_0_.info.who, bf16[1024,512]{1,0:T(8,128)(2,1)} %get-tuple-element.141.hidden, bf16[1024,768]{1,0:T(8,128)(2,1)} %get-tuple-element.142.norm, ...), custom_call_target="tpu_custom_call" | custom-call | tf_op jit(solution)/shard_map/weigh/pallas_call | solution.py:231
  133.3 19.8 %back.1 = (bf16[576,1024]{1,0:T(8,128)(2,1)}, bf16[2,512,768]{2,1,0:T(8,128)(2,1)}, bf16[2,512,768]{2,1,0:T(8,128)(2,1)}, bf16[2,304,768]{2,1,0:T(8,128)(2,1)}, ...) custom-call(s32[10]{0:T(128)} %pad_add_fusion.1.refs_0_.info.who, ...), custom_call_target="tpu_custom_call" | custom-call | tf_op jit(solution)/shard_map/back/pallas_call | solution.py:808
  153.1 1.9 collective-permute-done.26
  155.1 1.8 fusion.10
  156.9 1.8 collective-permute-done.27
  158.7 1.5 collective-permute-start.28
  160.5 4.1 %split.2 = (bf16[4,96,576]{2,1,0:T(8,128)(2,1)}, bf16[4,96,576]{2,1,0:T(8,128)(2,1)}) custom-call(s32[10]{0:T(128)} %pad_add_fusion.1.refs_0_.info.who, bf16[1024,768]{1,0:T(8,128)(2,1)} %get-tuple-element.159.left, bf16[576,1024]{1,0:T(8,128)(2,1)} %get-tuple-element.161.right), custom_call_target="tpu_custom_call" | custom-call | tf_op jit(solution)/shard_map/split/pallas_call | solution.py:266
  165.0 1.4 collective-permute-start.34
  168.6 1.4 collective-permute-start.33
  170.1 2.8 %collective-permute-start.30 = (bf16[112,1024]{1,0:T(8,128)(2,1)S(1)}, bf16[112,1024]{1,0:T(8,128)(2,1)S(1)}, u32[]{:S(2)}, u32[]{:S(2)}) collective-permute-start(bf16[112,1024]{1,0:T(8,128)(2,1)S(1)} %get-tuple-element.220), channel_id=1, source_target_pairs={{0,16},{4,20},{8,24},{12,28},{16,0},{20,4},{24,8},{28,12},{1,17},{... | collective-permute-start | bytes 688136 | tf_op jit(solution)/shard_map/ppermute | solution.py:26
  172.8 11.2 %collective-permute-done.30 = bf16[112,1024]{1,0:T(8,128)(2,1)S(1)} collective-permute-done((bf16[112,1024]{1,0:T(8,128)(2,1)S(1)}, bf16[112,1024]{1,0:T(8,128)(2,1)S(1)}, u32[]{:S(2)}, u32[]{:S(2)}) %collective-permute-start.30) | collective-permute-done | bytes 229408 | tf_op jit(solution)/shard_map/ppermute | solution.py:26
  185.1 1.5 collective-permute-start.36
  186.6 2.9 %collective-permute-start.35 = (bf16[2,112,1024]{2,1,0:T(8,128)(2,1)S(1)}, bf16[2,112,1024]{2,1,0:T(8,128)(2,1)}, u32[]{:S(2)}, u32[]{:S(2)}) collective-permute-start(bf16[2,112,1024]{2,1,0:T(8,128)(2,1)S(1)} %pad_maximum_fusion.2.refs_1_), channel_id=1, source_target_pairs={{0,8},{4,12},{8,0},{12,4},{16,24},{20,28},{24,16},{28,20},{1,9},{5... | collective-permute-start | bytes 1376264 | tf_op jit(solution)/shard_map/ppermute | solution.py:26
  193.8 2.1 split.3
  196.5 2.3 fusion.1
  199.2 5.1 %collective-permute-done.38 = bf16[4,112,288]{2,1,0:T(8,128)(2,1)S(1)} collective-permute-done((bf16[4,112,288]{2,1,0:T(8,128)(2,1)}, bf16[4,112,288]{2,1,0:T(8,128)(2,1)S(1)}, u32[]{:S(2)}, u32[]{:S(2)}) %collective-permute-start.38) | collective-permute-done | bytes 258080 | tf_op jit(solution)/shard_map/ppermute | solution.py:26
  204.4 3.9 %collective-permute-done.37.ffn_come = bf16[96,1536]{1,0:T(8,128)(2,1)S(1)} collective-permute-done((bf16[96,1536]{1,0:T(8,128)(2,1)}, bf16[96,1536]{1,0:T(8,128)(2,1)S(1)}, u32[]{:S(2)}, u32[]{:S(2)}) %collective-permute-start.37) | collective-permute-done | bytes 294944 | tf_op jit(solution)/shard_map/ppermute | solution.py:26
  209.9 2.1 collective-permute-start.40
  212.5 4.3 %spread.2.refs_2_ = f32[96,1024]{1,0:T(8,128)} custom-call(s32[10]{0:T(128)} %pad_add_fusion.1.refs_0_.info.who, bf16[2,112,1024]{2,1,0:T(8,128)(2,1)} %copy-done.6, bf16[2,112,1024]{2,1,0:T(8,128)(2,1)} %collective-permute-done.35.refs_2_, bf16[2,112,1024]{2,1,0:T(8,128)(2,1)} %collective-permute-done.36.refs_3_), custom_call_target="tpu_custom_call" | custom-call | tf_op jit(solution)/shard_map/spread/pallas_call | solution.py:430
  220.6 1.8 collective-permute-start.43
  222.4 1.6 bitcast_add_fusion
  226.4 2.7 %spread.3 = (f32[48,1024]{1,0:T(8,128)}, f32[48,1024]{1,0:T(8,128)}) custom-call(s32[10]{0:T(128)} %pad_add_fusion.1.refs_0_.info.who, bf16[2,112,1024]{2,1,0:T(8,128)(2,1)} %copy-done.26, f32[96,1024]{1,0:T(8,128)} %spread.2.refs_2_), custom_call_target="tpu_custom_call" | custom-call | tf_op jit(solution)/shard_map/spread/pallas_call | solution.py:430
  229.9 2.3 finish.1
  232.1 1.4 reshape.114
  (187 shorter events, 43.2 us)
Async XLA Ops:
  2.5 14.5 %collective-permute-start = (bf16[96,1152]{1,0:T(8,128)(2,1)}, bf16[96,1152]{1,0:T(8,128)(2,1)S(1)}, u32[]{:S(2)}, u32[]{:S(2)}) collective-permute-start(bf16[96,1152]{1,0:T(8,128)(2,1)} %pack_first.1), channel_id=1, source_target_pairs={{0,16},{4,20},{8,24},{12,28},{16,0},{20,4},{24,8},{28,12},{1,17},{... | collective-permute-start | bytes 663560 | tf_op jit(solution)/shard_map/ppermute | solution.py:26
  7.8 30.1 %copy-start = (bf16[2,256,768]{2,1,0:T(8,128)(2,1)}, bf16[2,256,768]{2,1,0:T(8,128)(2,1)S(1)}, u32[]{:S(2)}) copy-start(bf16[2,256,768]{2,1,0:T(8,128)(2,1)S(1)} %pad_maximum_fusion.emb0.cot0.refs_0_) | copy-start | bytes 2359300
  7.8 25.0 %collective-permute-start.4 = (bf16[2,256,768]{2,1,0:T(8,128)(2,1)S(1)}, bf16[2,256,768]{2,1,0:T(8,128)(2,1)S(1)}, u32[]{:S(2)}, u32[]{:S(2)}) collective-permute-start(bf16[2,256,768]{2,1,0:T(8,128)(2,1)S(1)} %pad_maximum_fusion.emb0.cot0.refs_0_), channel_id=1, source_target_pairs={{0,1},{1,0},{2,3},{3,2},{4,5},{5,4},{6,7},{7,6},{8,9},{9,8},{10,11... | collective-permute-start | bytes 2359304 | tf_op jit(solution)/shard_map/ppermute | solution.py:22
  17.1 12.1 %collective-permute-start.3 = (bf16[2,96,1152]{2,1,0:T(8,128)(2,1)S(1)}, bf16[2,96,1152]{2,1,0:T(8,128)(2,1)S(1)}, u32[]{:S(2)}, u32[]{:S(2)}) collective-permute-start(bf16[2,96,1152]{2,1,0:T(8,128)(2,1)S(1)} %pad_maximum_fusion.3.refs_2_.refs_3_), channel_id=1, source_target_pairs={{0,4},{4,0},{8,12},{12,8},{16,20},{20,16},{24,28},{28,24},{1,5},{5... | collective-permute-start | bytes 1327112 | tf_op jit(solution)/shard_map/ppermute | solution.py:26
  18.7 14.1 %collective-permute-start.2 = (bf16[2,96,1152]{2,1,0:T(8,128)(2,1)S(1)}, bf16[2,96,1152]{2,1,0:T(8,128)(2,1)}, u32[]{:S(2)}, u32[]{:S(2)}) collective-permute-start(bf16[2,96,1152]{2,1,0:T(8,128)(2,1)S(1)} %pad_maximum_fusion.3.refs_2_.refs_3_), channel_id=1, source_target_pairs={{0,8},{4,12},{8,0},{12,4},{16,24},{20,28},{24,16},{28,20},{1,9},{5... | collective-permute-start | bytes 1327112 | tf_op jit(solution)/shard_map/ppermute | solution.py:26
  19.4 31.8 %collective-permute-start.8 = (bf16[2,256,768]{2,1,0:T(8,128)(2,1)S(1)}, bf16[2,256,768]{2,1,0:T(8,128)(2,1)S(1)}, u32[]{:S(2)}, u32[]{:S(2)}) collective-permute-start(bf16[2,256,768]{2,1,0:T(8,128)(2,1)S(1)} %pad_maximum_fusion.emb0.cot0.refs_0_), channel_id=1, source_target_pairs={{0,2},{1,3},{2,0},{3,1},{4,6},{5,7},{6,4},{7,5},{8,10},{9,11},{10,... | collective-permute-start | bytes 2359304 | tf_op jit(solution)/shard_map/ppermute | solution.py:22
  21.0 16.8 %collective-permute-start.1 = (bf16[96,768]{1,0:T(8,128)(2,1)}, bf16[96,768]{1,0:T(8,128)(2,1)}, u32[]{:S(2)}, u32[]{:S(2)}) collective-permute-start(bf16[96,768]{1,0:T(8,128)(2,1)} %get-tuple-element.114), channel_id=1, source_target_pairs={{0,16},{4,20},{8,24},{12,28},{16,0},{20,4},{24,8},{28,12},{1,17},{... | collective-permute-start | bytes 442376 | tf_op jit(solution)/shard_map/ppermute | solution.py:26
  32.8 13.3 %collective-permute-start.7 = (bf16[2,96,1152]{2,1,0:T(8,128)(2,1)}, bf16[2,96,1152]{2,1,0:T(8,128)(2,1)S(1)}, u32[]{:S(2)}, u32[]{:S(2)}) collective-permute-start(bf16[2,96,1152]{2,1,0:T(8,128)(2,1)} %collective-permute-done.2.refs_2_.refs_4_), channel_id=1, source_target_pairs={{0,4},{4,0},{8,12},{12,8},{16,20},{20,16},{24,28},{28,24},{1,5},{5... | collective-permute-start | bytes 1327112 | tf_op jit(solution)/shard_map/ppermute | solution.py:26
  38.8 12.4 %collective-permute-start.6 = (bf16[2,96,768]{2,1,0:T(8,128)(2,1)S(1)}, bf16[2,96,768]{2,1,0:T(8,128)(2,1)}, u32[]{:S(2)}, u32[]{:S(2)}) collective-permute-start(bf16[2,96,768]{2,1,0:T(8,128)(2,1)S(1)} %pad_maximum_fusion.4.refs_0_), channel_id=1, source_target_pairs={{0,4},{4,0},{8,12},{12,8},{16,20},{20,16},{24,28},{28,24},{1,5},{5... | collective-permute-start | bytes 884744 | tf_op jit(solution)/shard_map/ppermute | solution.py:26
  40.2 12.9 %collective-permute-start.5 = (bf16[2,96,768]{2,1,0:T(8,128)(2,1)S(1)}, bf16[2,96,768]{2,1,0:T(8,128)(2,1)}, u32[]{:S(2)}, u32[]{:S(2)}) collective-permute-start(bf16[2,96,768]{2,1,0:T(8,128)(2,1)S(1)} %pad_maximum_fusion.4.refs_0_), channel_id=1, source_target_pairs={{0,8},{4,12},{8,0},{12,4},{16,24},{20,28},{24,16},{28,20},{1,9},{5... | collective-permute-start | bytes 884744 | tf_op jit(solution)/shard_map/ppermute | solution.py:26
  40.2 16.7 %collective-permute-start.14 = (bf16[96,1536]{1,0:T(8,128)(2,1)S(1)}, bf16[96,1536]{1,0:T(8,128)(2,1)}, u32[]{:S(2)}, u32[]{:S(2)}) collective-permute-start(bf16[96,1536]{1,0:T(8,128)(2,1)S(1)} %copy-done.34), channel_id=1, source_target_pairs={{0,16},{4,20},{8,24},{12,28},{16,0},{20,4},{24,8},{28,12},{1,17},{... | collective-permute-start | bytes 884744 | tf_op jit(solution)/shard_map/ppermute | solution.py:26
  53.1 15.8 %collective-permute-start.12 = (bf16[2,256,768]{2,1,0:T(8,128)(2,1)S(1)}, bf16[2,256,768]{2,1,0:T(8,128)(2,1)S(1)}, u32[]{:S(2)}, u32[]{:S(2)}) collective-permute-start(bf16[2,256,768]{2,1,0:T(8,128)(2,1)S(1)} %collective-permute-done.8.emb2.cot2.refs_2_), channel_id=1, source_target_pairs={{0,1},{1,0},{2,3},{3,2},{4,5},{5,4},{6,7},{7,6},{8,9},{9,8},{10,11... | collective-permute-start | bytes 2359304 | tf_op jit(solution)/shard_map/ppermute | solution.py:22
  53.1 12.3 %collective-permute-start.10 = (bf16[96,1792]{1,0:T(8,128)(2,1)}, bf16[96,1792]{1,0:T(8,128)(2,1)S(1)}, u32[]{:S(2)}, u32[]{:S(2)}) collective-permute-start(bf16[96,1792]{1,0:T(8,128)(2,1)} %lookup.5.set0), channel_id=1, source_target_pairs={{0,2},{1,3},{2,0},{3,1},{4,6},{5,7},{6,4},{7,5},{8,10},{9,11},{10,... | collective-permute-start | bytes 1032200 | tf_op jit(solution)/shard_map/ppermute | solution.py:22
  54.6 10.1 %collective-permute-start.13 = (bf16[2,96,768]{2,1,0:T(8,128)(2,1)}, bf16[2,96,768]{2,1,0:T(8,128)(2,1)S(1)}, u32[]{:S(2)}, u32[]{:S(2)}) collective-permute-start(bf16[2,96,768]{2,1,0:T(8,128)(2,1)} %collective-permute-done.5.refs_1_), channel_id=1, source_target_pairs={{0,4},{4,0},{8,12},{12,8},{16,20},{20,16},{24,28},{28,24},{1,5},{5... | collective-permute-start | bytes 884744 | tf_op jit(solution)/shard_map/ppermute | solution.py:26
  55.1 13.1 %collective-permute-start.9 = (bf16[96,1792]{1,0:T(8,128)(2,1)}, bf16[96,1792]{1,0:T(8,128)(2,1)S(1)}, u32[]{:S(2)}, u32[]{:S(2)}) collective-permute-start(bf16[96,1792]{1,0:T(8,128)(2,1)} %lookup.5.set0), channel_id=1, source_target_pairs={{0,1},{1,0},{2,3},{3,2},{4,5},{5,4},{6,7},{7,6},{8,9},{9,8},{10,11... | collective-permute-start | bytes 1032200 | tf_op jit(solution)/shard_map/ppermute | solution.py:22
  57.9 25.5 %copy-start.5 = (bf16[2,96,1536]{2,1,0:T(8,128)(2,1)}, bf16[2,96,1536]{2,1,0:T(8,128)(2,1)S(1)}, u32[]{:S(2)}) copy-start(bf16[2,96,1536]{2,1,0:T(8,128)(2,1)S(1)} %pad_maximum_fusion.1.ffn0) | copy-start | bytes 1769476
  57.9 27.0 %collective-permute-start.22 = (bf16[2,96,1536]{2,1,0:T(8,128)(2,1)S(1)}, bf16[2,96,1536]{2,1,0:T(8,128)(2,1)}, u32[]{:S(2)}, u32[]{:S(2)}) collective-permute-start(bf16[2,96,1536]{2,1,0:T(8,128)(2,1)S(1)} %pad_maximum_fusion.1.ffn0), channel_id=1, source_target_pairs={{0,4},{4,0},{8,12},{12,8},{16,20},{20,16},{24,28},{28,24},{1,5},{5... | collective-permute-start | bytes 1769480 | tf_op jit(solution)/shard_map/ppermute | solution.py:26
  64.7 20.3 %collective-permute-start.21 = (bf16[2,96,1536]{2,1,0:T(8,128)(2,1)S(1)}, bf16[2,96,1536]{2,1,0:T(8,128)(2,1)}, u32[]{:S(2)}, u32[]{:S(2)}) collective-permute-start(bf16[2,96,1536]{2,1,0:T(8,128)(2,1)S(1)} %pad_maximum_fusion.1.ffn0), channel_id=1, source_target_pairs={{0,8},{4,12},{8,0},{12,4},{16,24},{20,28},{24,16},{28,20},{1,9},{5... | collective-permute-start | bytes 1769480 | tf_op jit(solution)/shard_map/ppermute | solution.py:26
  65.4 3.5 %collective-permute-start.11 = (bf16[96,1792]{1,0:T(8,128)(2,1)S(1)}, bf16[96,1792]{1,0:T(8,128)(2,1)S(1)}, u32[]{:S(2)}, u32[]{:S(2)}) collective-permute-start(bf16[96,1792]{1,0:T(8,128)(2,1)S(1)} %collective-permute-done.10.set2), channel_id=1, source_target_pairs={{0,1},{1,0},{2,3},{3,2},{4,5},{5,4},{6,7},{7,6},{8,9},{9,8},{10,11... | collective-permute-start | bytes 1032200 | tf_op jit(solution)/shard_map/ppermute | solution.py:22
  68.2 15.1 %collective-permute-start.15 = (bf16[192,768]{1,0:T(8,128)(2,1)}, bf16[192,768]{1,0:T(8,128)(2,1)}, u32[]{:S(2)}, u32[]{:S(2)}) collective-permute-start(bf16[192,768]{1,0:T(8,128)(2,1)} %get-tuple-element.132.out0), channel_id=1, source_target_pairs={{0,2},{1,3},{2,0},{3,1},{4,6},{5,7},{6,4},{7,5},{8,10},{9,11},{10,... | collective-permute-start | bytes 884744 | tf_op jit(solution)/shard_map/ppermute | solution.py:22
  83.4 11.4 %collective-permute-start.17 = (bf16[192,1024]{1,0:T(8,128)(2,1)}, bf16[192,1024]{1,0:T(8,128)(2,1)S(1)}, u32[]{:S(2)}, u32[]{:S(2)}) collective-permute-start(bf16[192,1024]{1,0:T(8,128)(2,1)} %get-tuple-element.133.mix0.refs_4_.mixed), channel_id=1, source_target_pairs={{0,2},{1,3},{2,0},{3,1},{4,6},{5,7},{6,4},{7,5},{8,10},{9,11},{10,... | collective-permute-start | bytes 1179656 | tf_op jit(solution)/shard_map/ppermute | solution.py:22
  84.9 15.2 %collective-permute-start.23 = (bf16[2,96,1536]{2,1,0:T(8,128)(2,1)}, bf16[2,96,1536]{2,1,0:T(8,128)(2,1)S(1)}, u32[]{:S(2)}, u32[]{:S(2)}) collective-permute-start(bf16[2,96,1536]{2,1,0:T(8,128)(2,1)} %collective-permute-done.21.ffn1), channel_id=1, source_target_pairs={{0,4},{4,0},{8,12},{12,8},{16,20},{20,16},{24,28},{28,24},{1,5},{5... | collective-permute-start | bytes 1769480 | tf_op jit(solution)/shard_map/ppermute | solution.py:26
  85.4 12.1 %collective-permute-start.16 = (bf16[192,1024]{1,0:T(8,128)(2,1)}, bf16[192,1024]{1,0:T(8,128)(2,1)S(1)}, u32[]{:S(2)}, u32[]{:S(2)}) collective-permute-start(bf16[192,1024]{1,0:T(8,128)(2,1)} %get-tuple-element.133.mix0.refs_4_.mixed), channel_id=1, source_target_pairs={{0,1},{1,0},{2,3},{3,2},{4,5},{5,4},{6,7},{7,6},{8,9},{9,8},{10,11... | collective-permute-start | bytes 1179656 | tf_op jit(solution)/shard_map/ppermute | solution.py:22
  94.8 5.4 %collective-permute-start.18 = (bf16[192,1024]{1,0:T(8,128)(2,1)S(1)}, bf16[192,1024]{1,0:T(8,128)(2,1)S(1)}, u32[]{:S(2)}, u32[]{:S(2)}) collective-permute-start(bf16[192,1024]{1,0:T(8,128)(2,1)S(1)} %collective-permute-done.17.mix2.refs_6_), channel_id=1, source_target_pairs={{0,1},{1,0},{2,3},{3,2},{4,5},{5,4},{6,7},{7,6},{8,9},{9,8},{10,11... | collective-permute-start | bytes 1179656 | tf_op jit(solution)/shard_map/ppermute | solution.py:22
  94.8 2.2 collective-permute-start.19
  95.3 2.3 collective-permute-start.20
  117.4 2.6 %collective-permute-start.24 = (bf16[2,192,1024]{2,1,0:T(8,128)(2,1)}, bf16[2,192,1024]{2,1,0:T(8,128)(2,1)S(1)}, u32[]{:S(2)}, u32[]{:S(2)}) collective-permute-start(bf16[2,192,1024]{2,1,0:T(8,128)(2,1)} %get-tuple-element.139), channel_id=1, source_target_pairs={{0,1},{1,0},{2,3},{3,2},{4,5},{5,4},{6,7},{7,6},{8,9},{9,8},{10,11... | collective-permute-start | bytes 2359304 | tf_op jit(solution)/shard_map/ppermute | solution.py:22
  121.1 11.2 %collective-permute-start.25 = (bf16[192,1024]{1,0:T(8,128)(2,1)S(1)}, bf16[192,1024]{1,0:T(8,128)(2,1)S(1)}, u32[]{:S(2)}, u32[]{:S(2)}) collective-permute-start(bf16[192,1024]{1,0:T(8,128)(2,1)S(1)} %fusion.6), channel_id=1, source_target_pairs={{0,2},{1,3},{2,0},{3,1},{4,6},{5,7},{6,4},{7,5},{8,10},{9,11},{10,... | collective-permute-start | bytes 1179656 | tf_op jit(solution)/shard_map/ppermute | solution.py:22
  130.7 27.9 %collective-permute-start.27 = (bf16[4,96,1536]{2,1,0:T(8,128)(2,1)}, bf16[4,96,1536]{2,1,0:T(8,128)(2,1)S(1)}, u32[]{:S(2)}, u32[]{:S(2)}) collective-permute-start(bf16[4,96,1536]{2,1,0:T(8,128)(2,1)} %get-tuple-element.145), channel_id=1, source_target_pairs={{0,4},{4,0},{8,12},{12,8},{16,20},{20,16},{24,28},{28,24},{1,5},{5... | collective-permute-start | bytes 3538952 | tf_op jit(solution)/shard_map/ppermute | solution.py:26
  133.3 26.9 %copy-start.16 = (bf16[4,96,1536]{2,1,0:T(8,128)(2,1)S(1)}, bf16[4,96,1536]{2,1,0:T(8,128)(2,1)}, u32[]{:S(2)}) copy-start(bf16[4,96,1536]{2,1,0:T(8,128)(2,1)} %get-tuple-element.146) | copy-start | bytes 3538948
  153.1 2.0 collective-permute-start.26
  158.7 8.8 %collective-permute-start.32 = (bf16[2,304,768]{2,1,0:T(8,128)(2,1)}, bf16[2,304,768]{2,1,0:T(8,128)(2,1)}, u32[]{:S(2)}, u32[]{:S(2)}) collective-permute-start(bf16[2,304,768]{2,1,0:T(8,128)(2,1)} %get-tuple-element.168), channel_id=1, source_target_pairs={{0,1},{1,0},{2,3},{3,2},{4,5},{5,4},{6,7},{7,6},{8,9},{9,8},{10,11... | collective-permute-start | bytes 2801672 | tf_op jit(solution)/shard_map/ppermute | solution.py:22
  158.7 7.8 %collective-permute-start.28 = (bf16[96,1024]{1,0:T(8,128)(2,1)}, bf16[96,1024]{1,0:T(8,128)(2,1)}, u32[]{:S(2)}, u32[]{:S(2)}) collective-permute-start(bf16[96,1024]{1,0:T(8,128)(2,1)} %fusion.10), channel_id=1, source_target_pairs={{0,2},{1,3},{2,0},{3,1},{4,6},{5,7},{6,4},{7,5},{8,10},{9,11},{10,... | collective-permute-start | bytes 589832 | tf_op jit(solution)/shard_map/ppermute | solution.py:22
  164.5 19.6 %collective-permute-start.31 = (bf16[4,96,576]{2,1,0:T(8,128)(2,1)}, bf16[4,96,576]{2,1,0:T(8,128)(2,1)S(1)}, u32[]{:S(2)}, u32[]{:S(2)}) collective-permute-start(bf16[4,96,576]{2,1,0:T(8,128)(2,1)} %get-tuple-element.162), channel_id=1, source_target_pairs={{0,4},{4,0},{8,12},{12,8},{16,20},{20,16},{24,28},{28,24},{1,5},{5... | collective-permute-start | bytes 1327112 | tf_op jit(solution)/shard_map/ppermute | solution.py:26
  165.0 20.1 %collective-permute-start.34 = (bf16[2,96,1536]{2,1,0:T(8,128)(2,1)S(1)}, bf16[2,96,1536]{2,1,0:T(8,128)(2,1)S(1)}, u32[]{:S(2)}, u32[]{:S(2)}) collective-permute-start(bf16[2,96,1536]{2,1,0:T(8,128)(2,1)S(1)} %get-tuple-element.208), channel_id=1, source_target_pairs={{0,8},{4,12},{8,0},{12,4},{16,24},{20,28},{24,16},{28,20},{1,9},{5... | collective-permute-start | bytes 1769480 | tf_op jit(solution)/shard_map/ppermute | solution.py:26
  166.4 30.0 %collective-permute-start.29 = (bf16[2,512,768]{2,1,0:T(8,128)(2,1)}, bf16[2,512,768]{2,1,0:T(8,128)(2,1)}, u32[]{:S(2)}, u32[]{:S(2)}) collective-permute-start(bf16[2,512,768]{2,1,0:T(8,128)(2,1)} %get-tuple-element.165), channel_id=1, source_target_pairs={{0,1},{1,0},{2,3},{3,2},{4,5},{5,4},{6,7},{7,6},{8,9},{9,8},{10,11... | collective-permute-start | bytes 4718600 | tf_op jit(solution)/shard_map/ppermute | solution.py:22
  168.6 16.5 %collective-permute-start.33 = (bf16[304,768]{1,0:T(8,128)(2,1)S(1)}, bf16[304,768]{1,0:T(8,128)(2,1)S(1)}, u32[]{:S(2)}, u32[]{:S(2)}) collective-permute-start(bf16[304,768]{1,0:T(8,128)(2,1)S(1)} %fusion.4), channel_id=1, source_target_pairs={{0,2},{1,3},{2,0},{3,1},{4,6},{5,7},{6,4},{7,5},{8,10},{9,11},{10,... | collective-permute-start | bytes 1400840 | tf_op jit(solution)/shard_map/ppermute | solution.py:22
  170.1 14.0 %collective-permute-start.30 = (bf16[112,1024]{1,0:T(8,128)(2,1)S(1)}, bf16[112,1024]{1,0:T(8,128)(2,1)S(1)}, u32[]{:S(2)}, u32[]{:S(2)}) collective-permute-start(bf16[112,1024]{1,0:T(8,128)(2,1)S(1)} %get-tuple-element.220), channel_id=1, source_target_pairs={{0,16},{4,20},{8,24},{12,28},{16,0},{20,4},{24,8},{28,12},{1,17},{... | collective-permute-start | bytes 688136 | tf_op jit(solution)/shard_map/ppermute | solution.py:26
  185.1 23.2 %collective-permute-start.36 = (bf16[2,112,1024]{2,1,0:T(8,128)(2,1)S(1)}, bf16[2,112,1024]{2,1,0:T(8,128)(2,1)}, u32[]{:S(2)}, u32[]{:S(2)}) collective-permute-start(bf16[2,112,1024]{2,1,0:T(8,128)(2,1)S(1)} %pad_maximum_fusion.2.refs_1_), channel_id=1, source_target_pairs={{0,4},{4,0},{8,12},{12,8},{16,20},{20,16},{24,28},{28,24},{1,5},{5... | collective-permute-start | bytes 1376264 | tf_op jit(solution)/shard_map/ppermute | solution.py:26
  186.6 22.4 %collective-permute-start.35 = (bf16[2,112,1024]{2,1,0:T(8,128)(2,1)S(1)}, bf16[2,112,1024]{2,1,0:T(8,128)(2,1)}, u32[]{:S(2)}, u32[]{:S(2)}) collective-permute-start(bf16[2,112,1024]{2,1,0:T(8,128)(2,1)S(1)} %pad_maximum_fusion.2.refs_1_), channel_id=1, source_target_pairs={{0,8},{4,12},{8,0},{12,4},{16,24},{20,28},{24,16},{28,20},{1,9},{5... | collective-permute-start | bytes 1376264 | tf_op jit(solution)/shard_map/ppermute | solution.py:26
  193.4 14.9 %collective-permute-start.37 = (bf16[96,1536]{1,0:T(8,128)(2,1)}, bf16[96,1536]{1,0:T(8,128)(2,1)S(1)}, u32[]{:S(2)}, u32[]{:S(2)}) collective-permute-start(bf16[96,1536]{1,0:T(8,128)(2,1)} %get-tuple-element.210), channel_id=1, source_target_pairs={{0,16},{4,20},{8,24},{12,28},{16,0},{20,4},{24,8},{28,12},{1,17},{... | collective-permute-start | bytes 884744 | tf_op jit(solution)/shard_map/ppermute | solution.py:26
  195.9 8.4 %collective-permute-start.38 = (bf16[4,112,288]{2,1,0:T(8,128)(2,1)}, bf16[4,112,288]{2,1,0:T(8,128)(2,1)S(1)}, u32[]{:S(2)}, u32[]{:S(2)}) collective-permute-start(bf16[4,112,288]{2,1,0:T(8,128)(2,1)} %get-tuple-element.175), channel_id=1, source_target_pairs={{0,4},{4,0},{8,12},{12,8},{16,20},{20,16},{24,28},{28,24},{1,5},{5... | collective-permute-start | bytes 774152 | tf_op jit(solution)/shard_map/ppermute | solution.py:26
  198.7 19.4 %collective-permute-start.41 = (bf16[512,768]{1,0:T(8,128)(2,1)}, bf16[512,768]{1,0:T(8,128)(2,1)}, u32[]{:S(2)}, u32[]{:S(2)}) collective-permute-start(bf16[512,768]{1,0:T(8,128)(2,1)} %fusion.1), channel_id=1, source_target_pairs={{0,2},{1,3},{2,0},{3,1},{4,6},{5,7},{6,4},{7,5},{8,10},{9,11},{10,... | collective-permute-start | bytes 2359304 | tf_op jit(solution)/shard_map/ppermute | solution.py:22
  209.8 8.3 %collective-permute-start.39 = (bf16[2,96,576]{2,1,0:T(8,128)(2,1)}, bf16[2,96,576]{2,1,0:T(8,128)(2,1)S(1)}, u32[]{:S(2)}, u32[]{:S(2)}) collective-permute-start(bf16[2,96,576]{2,1,0:T(8,128)(2,1)} %get-tuple-element.212), channel_id=1, source_target_pairs={{0,8},{4,12},{8,0},{12,4},{16,24},{20,28},{24,16},{28,20},{1,9},{5... | collective-permute-start | bytes 663560 | tf_op jit(solution)/shard_map/ppermute | solution.py:26
  209.9 8.2 %collective-permute-start.40 = (bf16[2,112,288]{2,1,0:T(8,128)(2,1)S(1)}, bf16[2,112,288]{2,1,0:T(8,128)(2,1)S(1)}, u32[]{:S(2)}, u32[]{:S(2)}) collective-permute-start(bf16[2,112,288]{2,1,0:T(8,128)(2,1)S(1)} %get-tuple-element.214), channel_id=1, source_target_pairs={{0,8},{4,12},{8,0},{12,4},{16,24},{20,28},{24,16},{28,20},{1,9},{5... | collective-permute-start | bytes 387080 | tf_op jit(solution)/shard_map/ppermute | solution.py:26
  212.0 13.6 %collective-permute-start.42 = (bf16[2,112,1024]{2,1,0:T(8,128)(2,1)}, bf16[2,112,1024]{2,1,0:T(8,128)(2,1)S(1)}, u32[]{:S(2)}, u32[]{:S(2)}) collective-permute-start(bf16[2,112,1024]{2,1,0:T(8,128)(2,1)} %collective-permute-done.35.refs_2_), channel_id=1, source_target_pairs={{0,4},{4,0},{8,12},{12,8},{16,20},{20,16},{24,28},{28,24},{1,5},{5... | collective-permute-start | bytes 1376264 | tf_op jit(solution)/shard_map/ppermute | solution.py:26
  219.5 9.7 %collective-permute-start.44 = (bf16[112,288]{1,0:T(8,128)(2,1)S(1)}, bf16[112,288]{1,0:T(8,128)(2,1)S(1)}, u32[]{:S(2)}, u32[]{:S(2)}) collective-permute-start(bf16[112,288]{1,0:T(8,128)(2,1)S(1)} %get-tuple-element.217), channel_id=1, source_target_pairs={{0,16},{4,20},{8,24},{12,28},{16,0},{20,4},{24,8},{28,12},{1,17},{... | collective-permute-start | bytes 193544 | tf_op jit(solution)/shard_map/ppermute | solution.py:26
  220.6 8.6 %collective-permute-start.43 = (bf16[96,576]{1,0:T(8,128)(2,1)S(1)}, bf16[96,576]{1,0:T(8,128)(2,1)S(1)}, u32[]{:S(2)}, u32[]{:S(2)}) collective-permute-start(bf16[96,576]{1,0:T(8,128)(2,1)S(1)} %get-tuple-element.215), channel_id=1, source_target_pairs={{0,16},{4,20},{8,24},{12,28},{16,0},{20,4},{24,8},{28,12},{1,17},{... | collective-permute-start | bytes 331784 | tf_op jit(solution)/shard_map/ppermute | solution.py:26
  (41 other events, 276.3 us)
